TPU v7x, 256 devices: a whole 4x4x8 slice. The times are simulated.
256 devices in a mesh: section: 8 (over z), dp: 32 (over x, y, core).
Axes of the slice: x: 4, y: 4, z: 8, core: 2. Of those that a mesh axis runs over, the one named last changes fastest.
Arguments:
- stream: float32 [2, 256, 16, 16, 128], P(None, 'dp'), may hold values from -6 to 6
- cotangent: float32 [2, 256, 16, 16, 128], P(None, 'dp'), may hold values from -6 to 6
- weights: bfloat16 [8, 2304, 128], P('section'), may hold values from -0.09375 to 0.09375
- master: float32 [8, 2304, 128], P('section', 'dp'), may hold values from -0.09375 to 0.09375
- momentum: float32 [8, 2304, 128], P('section', 'dp'), may hold values from -6 to 6
Outputs:
- new_master: float32 [8, 2304, 128], P('section', 'dp')
- new_momentum: float32 [8, 2304, 128], P('section', 'dp')
- new_weights: bfloat16 [8, 2304, 128], P('section')
All inputs are finite; a program needn't handle non-finite values.
Results may differ from a plain program's by a relative error of at most 0.014.
Values may be sent and summed in bfloat16 or wider, within the bound.
No kernel may reach another device: no remote copies, remote signals or barrier semaphores. Data moves between devices by JAX's collectives and lax.ppermute only.
A program may use at most 64 MiB of HBM per device.

v0:
```python
import jax
import jax.numpy as jnp
from jax import lax
from jax.sharding import PartitionSpec as P

MICRO = 8
LAYERS = 1


step_size = 0.1
inertia = 0.9


def shifted_2(value, axis, by):
    devices = lax.axis_size(axis)
    pairs = [(i, i + by) for i in range(devices) if 0 <= i + by < devices]
    return lax.ppermute(value, axis, pairs)


def shortened(value):
    return jax.tree.map(lambda a: a.astype(jnp.bfloat16) if a.dtype == jnp.float32 else a, value)


def split_up(value, dim, devices):
    before, after = (value.shape[:dim], value.shape[dim + 1 :])
    return jnp.moveaxis(value.reshape(*before, devices, -1, *after), dim, 0)


def summed_on_arrival(value, axis, dim):
    devices = lax.axis_size(axis)
    tiles = lax.all_to_all(split_up(value, dim, devices), axis, 0, 0, tiled=True)
    return jnp.sum(tiles.astype(jnp.float32), axis=0)


def columns(field):
    height = field.shape[1]
    breadth = field.shape[2]
    padded = jnp.pad(jax.nn.silu(field).astype(jnp.bfloat16), ((0, 0), (1, 1), (1, 1), (0, 0)))
    shifted = [
        padded[:, row_tap : row_tap + height, col_tap : col_tap + breadth, :]
        for row_tap in range(3)
        for col_tap in range(3)
    ]
    return jnp.concatenate(shifted, axis=3).reshape(-1, 9 * field.shape[3])


def convolve(patches, weight, template):
    return jnp.dot(patches, weight, preferred_element_type=jnp.float32).reshape(template.shape)


def spread(rounded, weight, template):
    height, breadth, channels = (template.shape[1], template.shape[2], template.shape[3])
    spread_cols = lax.dot_general(
        rounded, weight, (((1,), (1,)), ((), ())), preferred_element_type=jnp.float32
    )
    spread_cols = spread_cols.reshape(template.shape[0], height, breadth, 9 * channels)
    padded = jnp.pad(spread_cols, ((0, 0), (1, 1), (1, 1), (0, 0)))
    summed = jnp.zeros(template.shape, jnp.float32)
    for row_tap in range(3):
        for col_tap in range(3):
            tap_index = 3 * row_tap + col_tap
            summed = (
                summed
                + padded[
                    :,
                    2 - row_tap : 2 - row_tap + height,
                    2 - col_tap : 2 - col_tap + breadth,
                    tap_index * channels : (tap_index + 1) * channels,
                ]
            )
    return summed


def weight_grad(patches, rounded):
    return lax.dot_general(
        patches, rounded, (((0,), (0,)), ((), ())), preferred_element_type=jnp.float32
    )


def silu_slope(field):
    logistic = jax.nn.sigmoid(field)
    return logistic * (1.0 + field * (1.0 - logistic))


def coupling_forward(first, second, weight_f, weight_g):
    patch_f = columns(second)
    out_first = first + convolve(patch_f, weight_f, second)
    patch_g = columns(out_first)
    out_second = second + convolve(patch_g, weight_g, out_first)
    return (out_first, out_second, patch_f, patch_g)


def coupling_grads(
    patch_f, second, patch_g, out_first, grad_first, grad_second, weight_f, weight_g
):
    channels = out_first.shape[3]
    round_second = grad_second.astype(jnp.bfloat16).reshape(-1, channels)
    wgrad_g = weight_grad(patch_g, round_second)
    grad_first = grad_first + spread(round_second, weight_g, out_first) * silu_slope(out_first)
    round_first = grad_first.astype(jnp.bfloat16).reshape(-1, channels)
    wgrad_f = weight_grad(patch_f, round_first)
    grad_second = grad_second + spread(round_first, weight_f, second) * silu_slope(second)
    return (grad_first, grad_second, wgrad_f, wgrad_g)


def relay_grads(stream, cotangent, weights):
    section_index = lax.axis_index("section")
    sections = lax.axis_size("section")
    channels = weights.shape[2]
    blocks = weights.reshape(LAYERS, 2, 9 * channels, channels)
    per_batch = stream.shape[1] // MICRO
    steps_total = MICRO + sections - 1
    piece_shape = (2, per_batch) + stream.shape[2:]
    last_section = section_index == sections - 1

    def run_section(streams):
        first, second = (streams[0], streams[1])
        first, second, patch_f, patch_g = coupling_forward(
            first, second, blocks[0, 0], blocks[0, 1]
        )
        return jnp.stack([first, second])

    def forward_step(step_idx, carry):
        received, finals, kept_inputs = carry
        micro_idx = step_idx - section_index
        active = (micro_idx >= 0) & (micro_idx < MICRO)
        slot_idx = jnp.clip(micro_idx, 0, MICRO - 1)
        incoming = lax.dynamic_slice_in_dim(
            stream, jnp.minimum(step_idx, MICRO - 1) * per_batch, per_batch, 1
        )
        entering = jnp.where(section_index == 0, incoming, received)
        result = lax.cond(active, run_section, lambda streams: streams, entering)
        kept_inputs = jnp.where(
            active, lax.dynamic_update_index_in_dim(kept_inputs, entering, slot_idx, 0), kept_inputs
        )
        received = shifted_2(result, "section", 1)
        return (received, finals, kept_inputs)

    holder = jnp.zeros((MICRO,) + piece_shape, jnp.float32)
    received, finals, kept_inputs = lax.fori_loop(
        0, steps_total, forward_step, (jnp.zeros(piece_shape, jnp.float32), holder, holder)
    )

    def replay_section(state, stored):
        first, second = (stored[0], stored[1])
        coupling = 0
        out_first, out_second, patch_f, patch_g = coupling_forward(
            first, second, blocks[coupling, 0], blocks[coupling, 1]
        )
        saved = [(patch_f, second, patch_g, out_first)]
        grad_first, grad_second = (state[0], state[1])
        pieces = []
        for coupling in reversed(range(LAYERS)):
            patch_f, second_in, patch_g, first_out = saved[coupling]
            grad_first, grad_second, wgrad_f, wgrad_g = coupling_grads(
                patch_f,
                second_in,
                patch_g,
                first_out,
                grad_first,
                grad_second,
                blocks[coupling, 0],
                blocks[coupling, 1],
            )
            pieces.append(jnp.stack([wgrad_f, wgrad_g]))
        pieces = pieces[::-1]
        return (jnp.stack([grad_first, grad_second]), jnp.stack(pieces))

    grads_zero = jnp.zeros((LAYERS, 2, 9 * channels, channels), jnp.float32)

    def backward_step(step_idx, carry):
        received, grads = carry
        micro_idx = step_idx - (sections - 1 - section_index)
        active = (micro_idx >= 0) & (micro_idx < MICRO)
        slot_idx = jnp.clip(micro_idx, 0, MICRO - 1)
        seed_grad = lax.dynamic_slice_in_dim(cotangent, slot_idx * per_batch, per_batch, 1)
        stored = lax.dynamic_index_in_dim(kept_inputs, slot_idx, 0, keepdims=False)
        state = jnp.where(last_section, seed_grad, received)
        process = lambda state_in: replay_section(state_in, stored)
        outgoing, contrib = lax.cond(
            active, process, lambda state_in: (state_in, grads_zero), state
        )
        grads = grads + jnp.where(active, contrib, 0.0)
        received = shifted_2(shortened(outgoing), "section", -1).astype(outgoing.dtype)
        return (received, grads)

    leading = 2
    start_state = jnp.zeros((leading,) + piece_shape[1:], jnp.float32)
    received, grads = lax.fori_loop(0, steps_total, backward_step, (start_state, grads_zero))
    return summed_on_arrival(grads.reshape(-1, channels).astype(jnp.bfloat16), "dp", 0)


def on_device(stream, cotangent, weights, master, momentum):
    summed = relay_grads(stream, cotangent, weights)
    images = stream.shape[1] * lax.axis_size("dp")
    gradient = summed / images
    new_momentum = inertia * momentum[0] + gradient
    new_master = master[0] - step_size * new_momentum
    new_weights = lax.all_gather(new_master.astype(jnp.bfloat16), "dp", axis=0, tiled=True)
    return (new_master[None], new_momentum[None], new_weights[None])


def solution(mesh):
    placed = (
        P(None, "dp", None, None, None),
        P(None, "dp", None, None, None),
        P("section", None, None),
        P("section", "dp", None),
        P("section", "dp", None),
    )
    return jax.shard_map(
        on_device,
        mesh=mesh,
        in_specs=placed,
        out_specs=(P("section", "dp", None), P("section", "dp", None), P("section", None, None)),
        check_vma=False,
    )
```

profile of v0, /device:TPU:1, one launch (start us, length us, event | category | flops | bytes accessed | tf_op | source)
XLA Modules:
  0.0 478.1 jit_solution(9952069645770203905)
XLA Ops:
  2.3 169.9 %while.34 = (s32[]{:T(128)}, f32[2,1,16,16,128]{4,3,2,1,0:T(8,128)S(1)}, f32[8,2,1,16,16,128]{5,4,3,1,2,0:T(8,128)}, s32[]{:T(128)}, pred[]{:T(512)}, /*index=5*...) while((s32[]{:T(128)}, ...), condition=%wide.region_3.4_spmd, body=%wide.region_0.3_spmd.sunk | while | flops 151912464 | bytes 8061730 | solution.py:140
  8.5 4.2 collective-permute-done
  15.9 4.3 collective-permute-start
  20.2 3.3 collective-permute-done
  26.7 4.3 collective-permute-start
  37.5 3.8 collective-permute-start
  47.8 3.8 collective-permute-start
  58.2 4.9 %collective-permute-start = (f32[2,1,16,16,128]{4,3,2,1,0:T(8,128)S(1)}, f32[2,1,16,16,128]{4,3,2,1,0:T(8,128)S(1)}, u32[]{:S(2)}, u32[]{:S(2)}) collective-permute-start(f32[2,1,16,16,128]{4,3,2,1,0:T(8,128)S(1)} %get-tuple-element.631), channel_id=1, source_target_pairs={{0,32},{32,64},{64,96},{96,128},{128,160},{160,192},{192,224},{1,3... | collective-permute-start | bytes 786440 | tf_op jit(solution)/shard_map/while/body/eval_jaxpr/ppermute | solution.py:17
  69.6 3.8 collective-permute-start
  79.9 4.8 %collective-permute-start = (f32[2,1,16,16,128]{4,3,2,1,0:T(8,128)S(1)}, f32[2,1,16,16,128]{4,3,2,1,0:T(8,128)S(1)}, u32[]{:S(2)}, u32[]{:S(2)}) collective-permute-start(f32[2,1,16,16,128]{4,3,2,1,0:T(8,128)S(1)} %get-tuple-element.631), channel_id=1, source_target_pairs={{0,32},{32,64},{64,96},{96,128},{128,160},{160,192},{192,224},{1,3... | collective-permute-start | bytes 786440 | tf_op jit(solution)/shard_map/while/body/eval_jaxpr/ppermute | solution.py:17
  89.8 6.5 %collective-permute-start = (f32[2,1,16,16,128]{4,3,2,1,0:T(8,128)S(1)}, f32[2,1,16,16,128]{4,3,2,1,0:T(8,128)S(1)}, u32[]{:S(2)}, u32[]{:S(2)}) collective-permute-start(f32[2,1,16,16,128]{4,3,2,1,0:T(8,128)S(1)} %get-tuple-element.631), channel_id=1, source_target_pairs={{0,32},{32,64},{64,96},{96,128},{128,160},{160,192},{192,224},{1,3... | collective-permute-start | bytes 786440 | tf_op jit(solution)/shard_map/while/body/eval_jaxpr/ppermute | solution.py:17
  101.4 5.0 %collective-permute-start = (f32[2,1,16,16,128]{4,3,2,1,0:T(8,128)S(1)}, f32[2,1,16,16,128]{4,3,2,1,0:T(8,128)S(1)}, u32[]{:S(2)}, u32[]{:S(2)}) collective-permute-start(f32[2,1,16,16,128]{4,3,2,1,0:T(8,128)S(1)} %get-tuple-element.631), channel_id=1, source_target_pairs={{0,32},{32,64},{64,96},{96,128},{128,160},{160,192},{192,224},{1,3... | collective-permute-start | bytes 786440 | tf_op jit(solution)/shard_map/while/body/eval_jaxpr/ppermute | solution.py:17
  106.4 4.9 %collective-permute-done = f32[2,1,16,16,128]{4,3,2,1,0:T(8,128)S(1)} collective-permute-done((f32[2,1,16,16,128]{4,3,2,1,0:T(8,128)S(1)}, f32[2,1,16,16,128]{4,3,2,1,0:T(8,128)S(1)}, u32[]{:S(2)}, u32[]{:S(2)}) %collective-permute-start) | collective-permute-done | bytes 262176 | tf_op jit(solution)/shard_map/while/body/eval_jaxpr/ppermute | solution.py:17
  113.1 5.3 %collective-permute-start = (f32[2,1,16,16,128]{4,3,2,1,0:T(8,128)S(1)}, f32[2,1,16,16,128]{4,3,2,1,0:T(8,128)S(1)}, u32[]{:S(2)}, u32[]{:S(2)}) collective-permute-start(f32[2,1,16,16,128]{4,3,2,1,0:T(8,128)S(1)} %get-tuple-element.631), channel_id=1, source_target_pairs={{0,32},{32,64},{64,96},{96,128},{128,160},{160,192},{192,224},{1,3... | collective-permute-start | bytes 786440 | tf_op jit(solution)/shard_map/while/body/eval_jaxpr/ppermute | solution.py:17
  118.4 4.6 collective-permute-done
  124.8 6.6 %collective-permute-start = (f32[2,1,16,16,128]{4,3,2,1,0:T(8,128)S(1)}, f32[2,1,16,16,128]{4,3,2,1,0:T(8,128)S(1)}, u32[]{:S(2)}, u32[]{:S(2)}) collective-permute-start(f32[2,1,16,16,128]{4,3,2,1,0:T(8,128)S(1)} %get-tuple-element.631), channel_id=1, source_target_pairs={{0,32},{32,64},{64,96},{96,128},{128,160},{160,192},{192,224},{1,3... | collective-permute-start | bytes 786440 | tf_op jit(solution)/shard_map/while/body/eval_jaxpr/ppermute | solution.py:17
  131.4 5.0 %collective-permute-done = f32[2,1,16,16,128]{4,3,2,1,0:T(8,128)S(1)} collective-permute-done((f32[2,1,16,16,128]{4,3,2,1,0:T(8,128)S(1)}, f32[2,1,16,16,128]{4,3,2,1,0:T(8,128)S(1)}, u32[]{:S(2)}, u32[]{:S(2)}) %collective-permute-start) | collective-permute-done | bytes 262176 | tf_op jit(solution)/shard_map/while/body/eval_jaxpr/ppermute | solution.py:17
  138.2 7.1 %collective-permute-start = (f32[2,1,16,16,128]{4,3,2,1,0:T(8,128)S(1)}, f32[2,1,16,16,128]{4,3,2,1,0:T(8,128)S(1)}, u32[]{:S(2)}, u32[]{:S(2)}) collective-permute-start(f32[2,1,16,16,128]{4,3,2,1,0:T(8,128)S(1)} %get-tuple-element.631), channel_id=1, source_target_pairs={{0,32},{32,64},{64,96},{96,128},{128,160},{160,192},{192,224},{1,3... | collective-permute-start | bytes 786440 | tf_op jit(solution)/shard_map/while/body/eval_jaxpr/ppermute | solution.py:17
  145.4 5.4 %collective-permute-done = f32[2,1,16,16,128]{4,3,2,1,0:T(8,128)S(1)} collective-permute-done((f32[2,1,16,16,128]{4,3,2,1,0:T(8,128)S(1)}, f32[2,1,16,16,128]{4,3,2,1,0:T(8,128)S(1)}, u32[]{:S(2)}, u32[]{:S(2)}) %collective-permute-start) | collective-permute-done | bytes 262176 | tf_op jit(solution)/shard_map/while/body/eval_jaxpr/ppermute | solution.py:17
  152.6 4.1 collective-permute-start
  156.7 4.5 collective-permute-done
  163.0 5.8 %collective-permute-start = (f32[2,1,16,16,128]{4,3,2,1,0:T(8,128)S(1)}, f32[2,1,16,16,128]{4,3,2,1,0:T(8,128)S(1)}, u32[]{:S(2)}, u32[]{:S(2)}) collective-permute-start(f32[2,1,16,16,128]{4,3,2,1,0:T(8,128)S(1)} %get-tuple-element.631), channel_id=1, source_target_pairs={{0,32},{32,64},{64,96},{96,128},{128,160},{160,192},{192,224},{1,3... | collective-permute-start | bytes 786440 | tf_op jit(solution)/shard_map/while/body/eval_jaxpr/ppermute | solution.py:17
  172.1 232.1 %while.35 = (s32[]{:T(128)}, f32[2,1,16,16,128]{4,3,2,1,0:T(8,128)S(1)}, f32[1,2,1152,128]{3,2,1,0:T(8,128)S(1)}, s32[]{:T(128)}, pred[]{:T(512)}, /*index=5*/f3...) while((s32[]{:T(128)}, ...), condition=%wide.region_7.8_spmd.clone, body=%wide.region_4.7_spmd.clone.sunk | while | flops 381026304 | bytes 22774092 | solution.py:189
  174.9 4.8 collective-permute-done.1
  182.6 5.0 %collective-permute-done.1 = bf16[2,1,16,16,128]{4,3,2,1,0:T(8,128)(2,1)S(1)} collective-permute-done((bf16[2,1,16,16,128]{4,3,2,1,0:T(8,128)(2,1)S(1)}, bf16[2,1,16,16,128]{4,3,2,1,0:T(8,128)(2,1)S(1)}, u32[]{:S(2)}, u32[]{:S(2)}) %collective-permute-start.1) | collective-permute-done | bytes 131104 | tf_op jit(solution)/shard_map/while/body/eval_jaxpr/ppermute | solution.py:17
  190.4 6.3 %collective-permute-done.1 = bf16[2,1,16,16,128]{4,3,2,1,0:T(8,128)(2,1)S(1)} collective-permute-done((bf16[2,1,16,16,128]{4,3,2,1,0:T(8,128)(2,1)S(1)}, bf16[2,1,16,16,128]{4,3,2,1,0:T(8,128)(2,1)S(1)}, u32[]{:S(2)}, u32[]{:S(2)}) %collective-permute-start.1) | collective-permute-done | bytes 131104 | tf_op jit(solution)/shard_map/while/body/eval_jaxpr/ppermute | solution.py:17
  199.6 7.3 %collective-permute-done.1 = bf16[2,1,16,16,128]{4,3,2,1,0:T(8,128)(2,1)S(1)} collective-permute-done((bf16[2,1,16,16,128]{4,3,2,1,0:T(8,128)(2,1)S(1)}, bf16[2,1,16,16,128]{4,3,2,1,0:T(8,128)(2,1)S(1)}, u32[]{:S(2)}, u32[]{:S(2)}) %collective-permute-start.1) | collective-permute-done | bytes 131104 | tf_op jit(solution)/shard_map/while/body/eval_jaxpr/ppermute | solution.py:17
  209.8 5.3 %collective-permute-done.1 = bf16[2,1,16,16,128]{4,3,2,1,0:T(8,128)(2,1)S(1)} collective-permute-done((bf16[2,1,16,16,128]{4,3,2,1,0:T(8,128)(2,1)S(1)}, bf16[2,1,16,16,128]{4,3,2,1,0:T(8,128)(2,1)S(1)}, u32[]{:S(2)}, u32[]{:S(2)}) %collective-permute-start.1) | collective-permute-done | bytes 131104 | tf_op jit(solution)/shard_map/while/body/eval_jaxpr/ppermute | solution.py:17
  217.9 4.0 collective-permute-done.1
  224.8 53.0 %collective-permute-done.1 = bf16[2,1,16,16,128]{4,3,2,1,0:T(8,128)(2,1)S(1)} collective-permute-done((bf16[2,1,16,16,128]{4,3,2,1,0:T(8,128)(2,1)S(1)}, bf16[2,1,16,16,128]{4,3,2,1,0:T(8,128)(2,1)S(1)}, u32[]{:S(2)}, u32[]{:S(2)}) %collective-permute-start.1) | collective-permute-done | bytes 131104 | tf_op jit(solution)/shard_map/while/body/eval_jaxpr/ppermute | solution.py:17
  278.9 7.7 %conditional.6 = (f32[2,1,16,16,128]{4,3,2,1,0:T(8,128)S(1)}, f32[1,2,1152,128]{3,2,1,0:T(8,128)S(1)}) conditional(s32[]{:T(128)} %convert_element_type.166, f32[2,1,16,16,128]{4,3,2,1,0:T(8,128)S(1)} %select_select_fusion.2, (f32[2,1,16,16,128]{4,3,2,1,0:T(8,128)S(1)}, bf16[1,2,1152,128]{3,2,1,0:T(8,128)(2,1)S(1)}, ...), branch_computations={%region_5.5_spmd, %region_6.6_spmd} | conditional | flops 379879424 | bytes 17137728 | solution.py:180
  288.3 7.3 %collective-permute-done.1 = bf16[2,1,16,16,128]{4,3,2,1,0:T(8,128)(2,1)S(1)} collective-permute-done((bf16[2,1,16,16,128]{4,3,2,1,0:T(8,128)(2,1)S(1)}, bf16[2,1,16,16,128]{4,3,2,1,0:T(8,128)(2,1)S(1)}, u32[]{:S(2)}, u32[]{:S(2)}) %collective-permute-start.1) | collective-permute-done | bytes 131104 | tf_op jit(solution)/shard_map/while/body/eval_jaxpr/ppermute | solution.py:17
  296.7 7.7 %conditional.6 = (f32[2,1,16,16,128]{4,3,2,1,0:T(8,128)S(1)}, f32[1,2,1152,128]{3,2,1,0:T(8,128)S(1)}) conditional(s32[]{:T(128)} %convert_element_type.166, f32[2,1,16,16,128]{4,3,2,1,0:T(8,128)S(1)} %select_select_fusion.2, (f32[2,1,16,16,128]{4,3,2,1,0:T(8,128)S(1)}, bf16[1,2,1152,128]{3,2,1,0:T(8,128)(2,1)S(1)}, ...), branch_computations={%region_5.5_spmd, %region_6.6_spmd} | conditional | flops 379879424 | bytes 17137728 | solution.py:180
  306.1 5.2 %collective-permute-done.1 = bf16[2,1,16,16,128]{4,3,2,1,0:T(8,128)(2,1)S(1)} collective-permute-done((bf16[2,1,16,16,128]{4,3,2,1,0:T(8,128)(2,1)S(1)}, bf16[2,1,16,16,128]{4,3,2,1,0:T(8,128)(2,1)S(1)}, u32[]{:S(2)}, u32[]{:S(2)}) %collective-permute-start.1) | collective-permute-done | bytes 131104 | tf_op jit(solution)/shard_map/while/body/eval_jaxpr/ppermute | solution.py:17
  312.4 7.7 %conditional.6 = (f32[2,1,16,16,128]{4,3,2,1,0:T(8,128)S(1)}, f32[1,2,1152,128]{3,2,1,0:T(8,128)S(1)}) conditional(s32[]{:T(128)} %convert_element_type.166, f32[2,1,16,16,128]{4,3,2,1,0:T(8,128)S(1)} %select_select_fusion.2, (f32[2,1,16,16,128]{4,3,2,1,0:T(8,128)S(1)}, bf16[1,2,1152,128]{3,2,1,0:T(8,128)(2,1)S(1)}, ...), branch_computations={%region_5.5_spmd, %region_6.6_spmd} | conditional | flops 379879424 | bytes 17137728 | solution.py:180
  321.8 5.2 %collective-permute-done.1 = bf16[2,1,16,16,128]{4,3,2,1,0:T(8,128)(2,1)S(1)} collective-permute-done((bf16[2,1,16,16,128]{4,3,2,1,0:T(8,128)(2,1)S(1)}, bf16[2,1,16,16,128]{4,3,2,1,0:T(8,128)(2,1)S(1)}, u32[]{:S(2)}, u32[]{:S(2)}) %collective-permute-start.1) | collective-permute-done | bytes 131104 | tf_op jit(solution)/shard_map/while/body/eval_jaxpr/ppermute | solution.py:17
  328.1 7.7 %conditional.6 = (f32[2,1,16,16,128]{4,3,2,1,0:T(8,128)S(1)}, f32[1,2,1152,128]{3,2,1,0:T(8,128)S(1)}) conditional(s32[]{:T(128)} %convert_element_type.166, f32[2,1,16,16,128]{4,3,2,1,0:T(8,128)S(1)} %select_select_fusion.2, (f32[2,1,16,16,128]{4,3,2,1,0:T(8,128)S(1)}, bf16[1,2,1152,128]{3,2,1,0:T(8,128)(2,1)S(1)}, ...), branch_computations={%region_5.5_spmd, %region_6.6_spmd} | conditional | flops 379879424 | bytes 17137728 | solution.py:180
  337.5 5.2 %collective-permute-done.1 = bf16[2,1,16,16,128]{4,3,2,1,0:T(8,128)(2,1)S(1)} collective-permute-done((bf16[2,1,16,16,128]{4,3,2,1,0:T(8,128)(2,1)S(1)}, bf16[2,1,16,16,128]{4,3,2,1,0:T(8,128)(2,1)S(1)}, u32[]{:S(2)}, u32[]{:S(2)}) %collective-permute-start.1) | collective-permute-done | bytes 131104 | tf_op jit(solution)/shard_map/while/body/eval_jaxpr/ppermute | solution.py:17
  343.7 7.7 %conditional.6 = (f32[2,1,16,16,128]{4,3,2,1,0:T(8,128)S(1)}, f32[1,2,1152,128]{3,2,1,0:T(8,128)S(1)}) conditional(s32[]{:T(128)} %convert_element_type.166, f32[2,1,16,16,128]{4,3,2,1,0:T(8,128)S(1)} %select_select_fusion.2, (f32[2,1,16,16,128]{4,3,2,1,0:T(8,128)S(1)}, bf16[1,2,1152,128]{3,2,1,0:T(8,128)(2,1)S(1)}, ...), branch_computations={%region_5.5_spmd, %region_6.6_spmd} | conditional | flops 379879424 | bytes 17137728 | solution.py:180
  353.1 5.2 %collective-permute-done.1 = bf16[2,1,16,16,128]{4,3,2,1,0:T(8,128)(2,1)S(1)} collective-permute-done((bf16[2,1,16,16,128]{4,3,2,1,0:T(8,128)(2,1)S(1)}, bf16[2,1,16,16,128]{4,3,2,1,0:T(8,128)(2,1)S(1)}, u32[]{:S(2)}, u32[]{:S(2)}) %collective-permute-start.1) | collective-permute-done | bytes 131104 | tf_op jit(solution)/shard_map/while/body/eval_jaxpr/ppermute | solution.py:17
  359.4 7.7 %conditional.6 = (f32[2,1,16,16,128]{4,3,2,1,0:T(8,128)S(1)}, f32[1,2,1152,128]{3,2,1,0:T(8,128)S(1)}) conditional(s32[]{:T(128)} %convert_element_type.166, f32[2,1,16,16,128]{4,3,2,1,0:T(8,128)S(1)} %select_select_fusion.2, (f32[2,1,16,16,128]{4,3,2,1,0:T(8,128)S(1)}, bf16[1,2,1152,128]{3,2,1,0:T(8,128)(2,1)S(1)}, ...), branch_computations={%region_5.5_spmd, %region_6.6_spmd} | conditional | flops 379879424 | bytes 17137728 | solution.py:180
  368.8 5.2 %collective-permute-done.1 = bf16[2,1,16,16,128]{4,3,2,1,0:T(8,128)(2,1)S(1)} collective-permute-done((bf16[2,1,16,16,128]{4,3,2,1,0:T(8,128)(2,1)S(1)}, bf16[2,1,16,16,128]{4,3,2,1,0:T(8,128)(2,1)S(1)}, u32[]{:S(2)}, u32[]{:S(2)}) %collective-permute-start.1) | collective-permute-done | bytes 131104 | tf_op jit(solution)/shard_map/while/body/eval_jaxpr/ppermute | solution.py:17
  375.1 7.7 %conditional.6 = (f32[2,1,16,16,128]{4,3,2,1,0:T(8,128)S(1)}, f32[1,2,1152,128]{3,2,1,0:T(8,128)S(1)}) conditional(s32[]{:T(128)} %convert_element_type.166, f32[2,1,16,16,128]{4,3,2,1,0:T(8,128)S(1)} %select_select_fusion.2, (f32[2,1,16,16,128]{4,3,2,1,0:T(8,128)S(1)}, bf16[1,2,1152,128]{3,2,1,0:T(8,128)(2,1)S(1)}, ...), branch_computations={%region_5.5_spmd, %region_6.6_spmd} | conditional | flops 379879424 | bytes 17137728 | solution.py:180
  384.5 5.2 %collective-permute-done.1 = bf16[2,1,16,16,128]{4,3,2,1,0:T(8,128)(2,1)S(1)} collective-permute-done((bf16[2,1,16,16,128]{4,3,2,1,0:T(8,128)(2,1)S(1)}, bf16[2,1,16,16,128]{4,3,2,1,0:T(8,128)(2,1)S(1)}, u32[]{:S(2)}, u32[]{:S(2)}) %collective-permute-start.1) | collective-permute-done | bytes 131104 | tf_op jit(solution)/shard_map/while/body/eval_jaxpr/ppermute | solution.py:17
  390.8 7.7 %conditional.6 = (f32[2,1,16,16,128]{4,3,2,1,0:T(8,128)S(1)}, f32[1,2,1152,128]{3,2,1,0:T(8,128)S(1)}) conditional(s32[]{:T(128)} %convert_element_type.166, f32[2,1,16,16,128]{4,3,2,1,0:T(8,128)S(1)} %select_select_fusion.2, (f32[2,1,16,16,128]{4,3,2,1,0:T(8,128)S(1)}, bf16[1,2,1152,128]{3,2,1,0:T(8,128)(2,1)S(1)}, ...), branch_computations={%region_5.5_spmd, %region_6.6_spmd} | conditional | flops 379879424 | bytes 17137728 | solution.py:180
  400.2 4.0 collective-permute-done.1
  404.3 49.2 %all_to_all.5 = bf16[32,72,128]{2,1,0:T(8,128)(2,1)S(1)} all-to-all(bf16[32,72,128]{2,1,0:T(8,128)(2,1)S(1)} %bitcast.271), channel_id=1, replica_groups=mesh['section'=8,'dp'=32] {'dp'}, dimensions={0} | all-to-all | bytes 1179648 | tf_op jit(solution)/shard_map/all_to_all | solution.py:31
  454.3 23.0 %all_gather.3 = bf16[2304,128]{1,0:T(8,128)(2,1)S(1)} all-gather(bf16[72,128]{1,0:T(8,128)(2,1)S(1)} %fusion.106), channel_id=1, replica_groups=mesh['section'=8,'dp'=32] {'dp'}, dimensions={0}, use_global_device_ids=true | all-gather | bytes 608256 | tf_op jit(solution)/shard_map/all_gather | solution.py:199
  (623 shorter events, 183.3 us)
Async XLA Ops:
  0.7 1.6 copy-start
  5.5 7.2 %collective-permute-start = (f32[2,1,16,16,128]{4,3,2,1,0:T(8,128)S(1)}, f32[2,1,16,16,128]{4,3,2,1,0:T(8,128)S(1)}, u32[]{:S(2)}, u32[]{:S(2)}) collective-permute-start(f32[2,1,16,16,128]{4,3,2,1,0:T(8,128)S(1)} %get-tuple-element.631), channel_id=1, source_target_pairs={{0,32},{32,64},{64,96},{96,128},{128,160},{160,192},{192,224},{1,3... | collective-permute-start | bytes 786440 | tf_op jit(solution)/shard_map/while/body/eval_jaxpr/ppermute | solution.py:17
  15.9 7.6 %collective-permute-start = (f32[2,1,16,16,128]{4,3,2,1,0:T(8,128)S(1)}, f32[2,1,16,16,128]{4,3,2,1,0:T(8,128)S(1)}, u32[]{:S(2)}, u32[]{:S(2)}) collective-permute-start(f32[2,1,16,16,128]{4,3,2,1,0:T(8,128)S(1)} %get-tuple-element.631), channel_id=1, source_target_pairs={{0,32},{32,64},{64,96},{96,128},{128,160},{160,192},{192,224},{1,3... | collective-permute-start | bytes 786440 | tf_op jit(solution)/shard_map/while/body/eval_jaxpr/ppermute | solution.py:17
  26.7 7.6 %collective-permute-start = (f32[2,1,16,16,128]{4,3,2,1,0:T(8,128)S(1)}, f32[2,1,16,16,128]{4,3,2,1,0:T(8,128)S(1)}, u32[]{:S(2)}, u32[]{:S(2)}) collective-permute-start(f32[2,1,16,16,128]{4,3,2,1,0:T(8,128)S(1)} %get-tuple-element.631), channel_id=1, source_target_pairs={{0,32},{32,64},{64,96},{96,128},{128,160},{160,192},{192,224},{1,3... | collective-permute-start | bytes 786440 | tf_op jit(solution)/shard_map/while/body/eval_jaxpr/ppermute | solution.py:17
  37.5 7.1 %collective-permute-start = (f32[2,1,16,16,128]{4,3,2,1,0:T(8,128)S(1)}, f32[2,1,16,16,128]{4,3,2,1,0:T(8,128)S(1)}, u32[]{:S(2)}, u32[]{:S(2)}) collective-permute-start(f32[2,1,16,16,128]{4,3,2,1,0:T(8,128)S(1)} %get-tuple-element.631), channel_id=1, source_target_pairs={{0,32},{32,64},{64,96},{96,128},{128,160},{160,192},{192,224},{1,3... | collective-permute-start | bytes 786440 | tf_op jit(solution)/shard_map/while/body/eval_jaxpr/ppermute | solution.py:17
  47.8 7.1 %collective-permute-start = (f32[2,1,16,16,128]{4,3,2,1,0:T(8,128)S(1)}, f32[2,1,16,16,128]{4,3,2,1,0:T(8,128)S(1)}, u32[]{:S(2)}, u32[]{:S(2)}) collective-permute-start(f32[2,1,16,16,128]{4,3,2,1,0:T(8,128)S(1)} %get-tuple-element.631), channel_id=1, source_target_pairs={{0,32},{32,64},{64,96},{96,128},{128,160},{160,192},{192,224},{1,3... | collective-permute-start | bytes 786440 | tf_op jit(solution)/shard_map/while/body/eval_jaxpr/ppermute | solution.py:17
  58.2 8.2 %collective-permute-start = (f32[2,1,16,16,128]{4,3,2,1,0:T(8,128)S(1)}, f32[2,1,16,16,128]{4,3,2,1,0:T(8,128)S(1)}, u32[]{:S(2)}, u32[]{:S(2)}) collective-permute-start(f32[2,1,16,16,128]{4,3,2,1,0:T(8,128)S(1)} %get-tuple-element.631), channel_id=1, source_target_pairs={{0,32},{32,64},{64,96},{96,128},{128,160},{160,192},{192,224},{1,3... | collective-permute-start | bytes 786440 | tf_op jit(solution)/shard_map/while/body/eval_jaxpr/ppermute | solution.py:17
  69.6 7.1 %collective-permute-start = (f32[2,1,16,16,128]{4,3,2,1,0:T(8,128)S(1)}, f32[2,1,16,16,128]{4,3,2,1,0:T(8,128)S(1)}, u32[]{:S(2)}, u32[]{:S(2)}) collective-permute-start(f32[2,1,16,16,128]{4,3,2,1,0:T(8,128)S(1)} %get-tuple-element.631), channel_id=1, source_target_pairs={{0,32},{32,64},{64,96},{96,128},{128,160},{160,192},{192,224},{1,3... | collective-permute-start | bytes 786440 | tf_op jit(solution)/shard_map/while/body/eval_jaxpr/ppermute | solution.py:17
  79.9 8.1 %collective-permute-start = (f32[2,1,16,16,128]{4,3,2,1,0:T(8,128)S(1)}, f32[2,1,16,16,128]{4,3,2,1,0:T(8,128)S(1)}, u32[]{:S(2)}, u32[]{:S(2)}) collective-permute-start(f32[2,1,16,16,128]{4,3,2,1,0:T(8,128)S(1)} %get-tuple-element.631), channel_id=1, source_target_pairs={{0,32},{32,64},{64,96},{96,128},{128,160},{160,192},{192,224},{1,3... | collective-permute-start | bytes 786440 | tf_op jit(solution)/shard_map/while/body/eval_jaxpr/ppermute | solution.py:17
  89.8 9.7 %collective-permute-start = (f32[2,1,16,16,128]{4,3,2,1,0:T(8,128)S(1)}, f32[2,1,16,16,128]{4,3,2,1,0:T(8,128)S(1)}, u32[]{:S(2)}, u32[]{:S(2)}) collective-permute-start(f32[2,1,16,16,128]{4,3,2,1,0:T(8,128)S(1)} %get-tuple-element.631), channel_id=1, source_target_pairs={{0,32},{32,64},{64,96},{96,128},{128,160},{160,192},{192,224},{1,3... | collective-permute-start | bytes 786440 | tf_op jit(solution)/shard_map/while/body/eval_jaxpr/ppermute | solution.py:17
  101.4 10.0 %collective-permute-start = (f32[2,1,16,16,128]{4,3,2,1,0:T(8,128)S(1)}, f32[2,1,16,16,128]{4,3,2,1,0:T(8,128)S(1)}, u32[]{:S(2)}, u32[]{:S(2)}) collective-permute-start(f32[2,1,16,16,128]{4,3,2,1,0:T(8,128)S(1)} %get-tuple-element.631), channel_id=1, source_target_pairs={{0,32},{32,64},{64,96},{96,128},{128,160},{160,192},{192,224},{1,3... | collective-permute-start | bytes 786440 | tf_op jit(solution)/shard_map/while/body/eval_jaxpr/ppermute | solution.py:17
  113.1 9.9 %collective-permute-start = (f32[2,1,16,16,128]{4,3,2,1,0:T(8,128)S(1)}, f32[2,1,16,16,128]{4,3,2,1,0:T(8,128)S(1)}, u32[]{:S(2)}, u32[]{:S(2)}) collective-permute-start(f32[2,1,16,16,128]{4,3,2,1,0:T(8,128)S(1)} %get-tuple-element.631), channel_id=1, source_target_pairs={{0,32},{32,64},{64,96},{96,128},{128,160},{160,192},{192,224},{1,3... | collective-permute-start | bytes 786440 | tf_op jit(solution)/shard_map/while/body/eval_jaxpr/ppermute | solution.py:17
  124.8 11.6 %collective-permute-start = (f32[2,1,16,16,128]{4,3,2,1,0:T(8,128)S(1)}, f32[2,1,16,16,128]{4,3,2,1,0:T(8,128)S(1)}, u32[]{:S(2)}, u32[]{:S(2)}) collective-permute-start(f32[2,1,16,16,128]{4,3,2,1,0:T(8,128)S(1)} %get-tuple-element.631), channel_id=1, source_target_pairs={{0,32},{32,64},{64,96},{96,128},{128,160},{160,192},{192,224},{1,3... | collective-permute-start | bytes 786440 | tf_op jit(solution)/shard_map/while/body/eval_jaxpr/ppermute | solution.py:17
  138.2 12.6 %collective-permute-start = (f32[2,1,16,16,128]{4,3,2,1,0:T(8,128)S(1)}, f32[2,1,16,16,128]{4,3,2,1,0:T(8,128)S(1)}, u32[]{:S(2)}, u32[]{:S(2)}) collective-permute-start(f32[2,1,16,16,128]{4,3,2,1,0:T(8,128)S(1)} %get-tuple-element.631), channel_id=1, source_target_pairs={{0,32},{32,64},{64,96},{96,128},{128,160},{160,192},{192,224},{1,3... | collective-permute-start | bytes 786440 | tf_op jit(solution)/shard_map/while/body/eval_jaxpr/ppermute | solution.py:17
  152.6 8.6 %collective-permute-start = (f32[2,1,16,16,128]{4,3,2,1,0:T(8,128)S(1)}, f32[2,1,16,16,128]{4,3,2,1,0:T(8,128)S(1)}, u32[]{:S(2)}, u32[]{:S(2)}) collective-permute-start(f32[2,1,16,16,128]{4,3,2,1,0:T(8,128)S(1)} %get-tuple-element.631), channel_id=1, source_target_pairs={{0,32},{32,64},{64,96},{96,128},{128,160},{160,192},{192,224},{1,3... | collective-permute-start | bytes 786440 | tf_op jit(solution)/shard_map/while/body/eval_jaxpr/ppermute | solution.py:17
  163.0 9.1 %collective-permute-start = (f32[2,1,16,16,128]{4,3,2,1,0:T(8,128)S(1)}, f32[2,1,16,16,128]{4,3,2,1,0:T(8,128)S(1)}, u32[]{:S(2)}, u32[]{:S(2)}) collective-permute-start(f32[2,1,16,16,128]{4,3,2,1,0:T(8,128)S(1)} %get-tuple-element.631), channel_id=1, source_target_pairs={{0,32},{32,64},{64,96},{96,128},{128,160},{160,192},{192,224},{1,3... | collective-permute-start | bytes 786440 | tf_op jit(solution)/shard_map/while/body/eval_jaxpr/ppermute | solution.py:17
  173.2 6.5 %collective-permute-start.1 = (bf16[2,1,16,16,128]{4,3,2,1,0:T(8,128)(2,1)S(1)}, bf16[2,1,16,16,128]{4,3,2,1,0:T(8,128)(2,1)S(1)}, u32[]{:S(2)}, u32[]{:S(2)}) collective-permute-start(bf16[2,1,16,16,128]{4,3,2,1,0:T(8,128)(2,1)S(1)} %convert_element_type.167), channel_id=1, source_target_pairs={{32,0},{64,32},{96,64},{128,96},{160,128},{192,160},{224,192},{33,... | collective-permute-start | bytes 393224 | tf_op jit(solution)/shard_map/while/body/eval_jaxpr/ppermute | solution.py:17
  180.9 6.6 %collective-permute-start.1 = (bf16[2,1,16,16,128]{4,3,2,1,0:T(8,128)(2,1)S(1)}, bf16[2,1,16,16,128]{4,3,2,1,0:T(8,128)(2,1)S(1)}, u32[]{:S(2)}, u32[]{:S(2)}) collective-permute-start(bf16[2,1,16,16,128]{4,3,2,1,0:T(8,128)(2,1)S(1)} %convert_element_type.167), channel_id=1, source_target_pairs={{32,0},{64,32},{96,64},{128,96},{160,128},{192,160},{224,192},{33,... | collective-permute-start | bytes 393224 | tf_op jit(solution)/shard_map/while/body/eval_jaxpr/ppermute | solution.py:17
  188.7 8.0 %collective-permute-start.1 = (bf16[2,1,16,16,128]{4,3,2,1,0:T(8,128)(2,1)S(1)}, bf16[2,1,16,16,128]{4,3,2,1,0:T(8,128)(2,1)S(1)}, u32[]{:S(2)}, u32[]{:S(2)}) collective-permute-start(bf16[2,1,16,16,128]{4,3,2,1,0:T(8,128)(2,1)S(1)} %convert_element_type.167), channel_id=1, source_target_pairs={{32,0},{64,32},{96,64},{128,96},{160,128},{192,160},{224,192},{33,... | collective-permute-start | bytes 393224 | tf_op jit(solution)/shard_map/while/body/eval_jaxpr/ppermute | solution.py:17
  197.9 9.0 %collective-permute-start.1 = (bf16[2,1,16,16,128]{4,3,2,1,0:T(8,128)(2,1)S(1)}, bf16[2,1,16,16,128]{4,3,2,1,0:T(8,128)(2,1)S(1)}, u32[]{:S(2)}, u32[]{:S(2)}) collective-permute-start(bf16[2,1,16,16,128]{4,3,2,1,0:T(8,128)(2,1)S(1)} %convert_element_type.167), channel_id=1, source_target_pairs={{32,0},{64,32},{96,64},{128,96},{160,128},{192,160},{224,192},{33,... | collective-permute-start | bytes 393224 | tf_op jit(solution)/shard_map/while/body/eval_jaxpr/ppermute | solution.py:17
  208.1 7.0 %collective-permute-start.1 = (bf16[2,1,16,16,128]{4,3,2,1,0:T(8,128)(2,1)S(1)}, bf16[2,1,16,16,128]{4,3,2,1,0:T(8,128)(2,1)S(1)}, u32[]{:S(2)}, u32[]{:S(2)}) collective-permute-start(bf16[2,1,16,16,128]{4,3,2,1,0:T(8,128)(2,1)S(1)} %convert_element_type.167), channel_id=1, source_target_pairs={{32,0},{64,32},{96,64},{128,96},{160,128},{192,160},{224,192},{33,... | collective-permute-start | bytes 393224 | tf_op jit(solution)/shard_map/while/body/eval_jaxpr/ppermute | solution.py:17
  216.2 5.7 %collective-permute-start.1 = (bf16[2,1,16,16,128]{4,3,2,1,0:T(8,128)(2,1)S(1)}, bf16[2,1,16,16,128]{4,3,2,1,0:T(8,128)(2,1)S(1)}, u32[]{:S(2)}, u32[]{:S(2)}) collective-permute-start(bf16[2,1,16,16,128]{4,3,2,1,0:T(8,128)(2,1)S(1)} %convert_element_type.167), channel_id=1, source_target_pairs={{32,0},{64,32},{96,64},{128,96},{160,128},{192,160},{224,192},{33,... | collective-permute-start | bytes 393224 | tf_op jit(solution)/shard_map/while/body/eval_jaxpr/ppermute | solution.py:17
  223.1 54.7 %collective-permute-start.1 = (bf16[2,1,16,16,128]{4,3,2,1,0:T(8,128)(2,1)S(1)}, bf16[2,1,16,16,128]{4,3,2,1,0:T(8,128)(2,1)S(1)}, u32[]{:S(2)}, u32[]{:S(2)}) collective-permute-start(bf16[2,1,16,16,128]{4,3,2,1,0:T(8,128)(2,1)S(1)} %convert_element_type.167), channel_id=1, source_target_pairs={{32,0},{64,32},{96,64},{128,96},{160,128},{192,160},{224,192},{33,... | collective-permute-start | bytes 393224 | tf_op jit(solution)/shard_map/while/body/eval_jaxpr/ppermute | solution.py:17
  286.6 9.0 %collective-permute-start.1 = (bf16[2,1,16,16,128]{4,3,2,1,0:T(8,128)(2,1)S(1)}, bf16[2,1,16,16,128]{4,3,2,1,0:T(8,128)(2,1)S(1)}, u32[]{:S(2)}, u32[]{:S(2)}) collective-permute-start(bf16[2,1,16,16,128]{4,3,2,1,0:T(8,128)(2,1)S(1)} %convert_element_type.167), channel_id=1, source_target_pairs={{32,0},{64,32},{96,64},{128,96},{160,128},{192,160},{224,192},{33,... | collective-permute-start | bytes 393224 | tf_op jit(solution)/shard_map/while/body/eval_jaxpr/ppermute | solution.py:17
  304.4 6.9 %collective-permute-start.1 = (bf16[2,1,16,16,128]{4,3,2,1,0:T(8,128)(2,1)S(1)}, bf16[2,1,16,16,128]{4,3,2,1,0:T(8,128)(2,1)S(1)}, u32[]{:S(2)}, u32[]{:S(2)}) collective-permute-start(bf16[2,1,16,16,128]{4,3,2,1,0:T(8,128)(2,1)S(1)} %convert_element_type.167), channel_id=1, source_target_pairs={{32,0},{64,32},{96,64},{128,96},{160,128},{192,160},{224,192},{33,... | collective-permute-start | bytes 393224 | tf_op jit(solution)/shard_map/while/body/eval_jaxpr/ppermute | solution.py:17
  320.1 6.9 %collective-permute-start.1 = (bf16[2,1,16,16,128]{4,3,2,1,0:T(8,128)(2,1)S(1)}, bf16[2,1,16,16,128]{4,3,2,1,0:T(8,128)(2,1)S(1)}, u32[]{:S(2)}, u32[]{:S(2)}) collective-permute-start(bf16[2,1,16,16,128]{4,3,2,1,0:T(8,128)(2,1)S(1)} %convert_element_type.167), channel_id=1, source_target_pairs={{32,0},{64,32},{96,64},{128,96},{160,128},{192,160},{224,192},{33,... | collective-permute-start | bytes 393224 | tf_op jit(solution)/shard_map/while/body/eval_jaxpr/ppermute | solution.py:17
  335.8 6.9 %collective-permute-start.1 = (bf16[2,1,16,16,128]{4,3,2,1,0:T(8,128)(2,1)S(1)}, bf16[2,1,16,16,128]{4,3,2,1,0:T(8,128)(2,1)S(1)}, u32[]{:S(2)}, u32[]{:S(2)}) collective-permute-start(bf16[2,1,16,16,128]{4,3,2,1,0:T(8,128)(2,1)S(1)} %convert_element_type.167), channel_id=1, source_target_pairs={{32,0},{64,32},{96,64},{128,96},{160,128},{192,160},{224,192},{33,... | collective-permute-start | bytes 393224 | tf_op jit(solution)/shard_map/while/body/eval_jaxpr/ppermute | solution.py:17
  351.4 6.9 %collective-permute-start.1 = (bf16[2,1,16,16,128]{4,3,2,1,0:T(8,128)(2,1)S(1)}, bf16[2,1,16,16,128]{4,3,2,1,0:T(8,128)(2,1)S(1)}, u32[]{:S(2)}, u32[]{:S(2)}) collective-permute-start(bf16[2,1,16,16,128]{4,3,2,1,0:T(8,128)(2,1)S(1)} %convert_element_type.167), channel_id=1, source_target_pairs={{32,0},{64,32},{96,64},{128,96},{160,128},{192,160},{224,192},{33,... | collective-permute-start | bytes 393224 | tf_op jit(solution)/shard_map/while/body/eval_jaxpr/ppermute | solution.py:17
  367.1 6.9 %collective-permute-start.1 = (bf16[2,1,16,16,128]{4,3,2,1,0:T(8,128)(2,1)S(1)}, bf16[2,1,16,16,128]{4,3,2,1,0:T(8,128)(2,1)S(1)}, u32[]{:S(2)}, u32[]{:S(2)}) collective-permute-start(bf16[2,1,16,16,128]{4,3,2,1,0:T(8,128)(2,1)S(1)} %convert_element_type.167), channel_id=1, source_target_pairs={{32,0},{64,32},{96,64},{128,96},{160,128},{192,160},{224,192},{33,... | collective-permute-start | bytes 393224 | tf_op jit(solution)/shard_map/while/body/eval_jaxpr/ppermute | solution.py:17
  382.8 6.9 %collective-permute-start.1 = (bf16[2,1,16,16,128]{4,3,2,1,0:T(8,128)(2,1)S(1)}, bf16[2,1,16,16,128]{4,3,2,1,0:T(8,128)(2,1)S(1)}, u32[]{:S(2)}, u32[]{:S(2)}) collective-permute-start(bf16[2,1,16,16,128]{4,3,2,1,0:T(8,128)(2,1)S(1)} %convert_element_type.167), channel_id=1, source_target_pairs={{32,0},{64,32},{96,64},{128,96},{160,128},{192,160},{224,192},{33,... | collective-permute-start | bytes 393224 | tf_op jit(solution)/shard_map/while/body/eval_jaxpr/ppermute | solution.py:17
  398.5 5.7 %collective-permute-start.1 = (bf16[2,1,16,16,128]{4,3,2,1,0:T(8,128)(2,1)S(1)}, bf16[2,1,16,16,128]{4,3,2,1,0:T(8,128)(2,1)S(1)}, u32[]{:S(2)}, u32[]{:S(2)}) collective-permute-start(bf16[2,1,16,16,128]{4,3,2,1,0:T(8,128)(2,1)S(1)} %convert_element_type.167), channel_id=1, source_target_pairs={{32,0},{64,32},{96,64},{128,96},{160,128},{192,160},{224,192},{33,... | collective-permute-start | bytes 393224 | tf_op jit(solution)/shard_map/while/body/eval_jaxpr/ppermute | solution.py:17
  404.3 49.3 %copy-start.1 = (f32[1,72,128]{2,1,0:T(8,128)S(1)}, f32[1,72,128]{2,1,0:T(8,128)}, u32[]{:S(2)}) copy-start(f32[1,72,128]{2,1,0:T(8,128)} %param.16) | copy-start | bytes 110596
  404.3 49.3 %copy-start.2 = (f32[1,72,128]{2,1,0:T(8,128)S(1)}, f32[1,72,128]{2,1,0:T(8,128)}, u32[]{:S(2)}) copy-start(f32[1,72,128]{2,1,0:T(8,128)} %param.17) | copy-start | bytes 110596
where the time goes:
time: 481 us; the launch traced here: 478 us
  waiting for transfers between devices  187 us (39%)
  starting transfers between devices  92.5 us (19%)
  other arithmetic  84 us (17%)
  blocking collectives  72.1 us (15%)
  matrix products  26.4 us (5%)
  local copies, waits for them, and re-layouts  12.2 us (3%)
    ppermute x30, waiting for transfers between devices, shifted_2(): return lax.ppermute(value, axis, pairs)  187 us
    ppermute x30, starting transfers between devices, shifted_2(): return lax.ppermute(value, axis, pairs)  92.5 us
    all_to_all x1, blocking collectives, summed_on_arrival(): lax.all_to_all(split_up(value, dim, devices), axis, 0, 0, tiled=True)  49.2 us
    select_n x15, other arithmetic, forward_step(): jnp.where(active, lax.dynamic_update_index_in_dim(kept_inputs, entering,...  26.8 us
    all_gather x1, blocking collectives, on_device(): lax.all_gather(new_master.astype(jnp.bfloat16), 'dp', axis=0, tiled=True)  23 us
    cond x40, other arithmetic  17.1 us
    dot_general x24, matrix products, convolve(): jnp.dot(patches, weight, preferred_element_type=jnp.float32)  15.4 us
    select_n x15, other arithmetic, backward_step(): state = jnp.where(last_section, seed_grad, received)  14.9 us
  transfers between devices with their start and end apart: 30, of which 30 were waited for; matrix products, arithmetic and copies ran while one was open for 1% of the time, Pallas kernels for 0%

commit v1 on v0

v1 whole, which is shorter than its diff:
```python
import jax
import jax.numpy as jnp
from jax import lax
from jax.experimental import pallas as pl
from jax.experimental.pallas import tpu as pltpu
from jax.sharding import PartitionSpec as P

STEP_SIZE = 0.1
INERTIA = 0.9
ROUND = jnp.bfloat16


def image_step(sections, side, rows, slot, stream, cotangent, weights, grads, x_in, d_in, w_all, g_all,
               saved_p, slopes, fwd_pad, bwd_pad, x_sem, w_sem, g_sem):
    channels = stream.shape[-1]
    pixels = side * side
    half = rows // 2
    x_copy = pltpu.make_async_copy(stream.at[:, slot[0]], x_in, x_sem.at[0])
    d_copy = pltpu.make_async_copy(cotangent.at[:, slot[0]], d_in, x_sem.at[1])
    x_copy.start()

    def w_copy(s):
        part = pl.ds(s * rows, rows)
        return pltpu.make_async_copy(weights.at[part, :], w_all.at[part, :], w_sem.at[s])

    def g_copy(s):
        part = pl.ds(s * rows, rows)
        return pltpu.make_async_copy(g_all.at[part, :], grads.at[part, :], g_sem.at[s])

    for s in range(sections):
        w_copy(s).start()
    d_copy.start()
    edge = jnp.zeros((side, 3 * channels), ROUND)
    for pad in (fwd_pad, bwd_pad):
        for k in range(2):
            pad[k, 0:side, :] = edge
            pad[k, side + pixels : 2 * side + pixels, :] = edge

    column = lax.broadcasted_iota(jnp.int32, (pixels, channels), 0) & (side - 1)
    not_first = column > 0
    not_last = column < side - 1

    def before(v):
        return jnp.where(not_first, pltpu.roll(v, 1, 0), 0.0).astype(ROUND)

    def after(v):
        return jnp.where(not_last, pltpu.roll(v, pixels - 1, 0), 0.0).astype(ROUND)

    def band(pad, k, low, mid, high):
        body = pl.ds(side, pixels)
        pad[k, body, 0:channels] = low
        pad[k, body, channels : 2 * channels] = mid
        pad[k, body, 2 * channels : 3 * channels] = high

    def conv(pad, k, w):
        taps = jnp.concatenate([pad[k, a * side : a * side + pixels, :] for a in range(3)], axis=1)
        return jnp.dot(taps, w, preferred_element_type=jnp.float32)

    def activate(v, at):
        logistic = 1.0 / (1.0 + jnp.exp(-v))
        p = v * logistic
        slopes[at] = logistic + p * (1.0 - logistic)
        saved_p[at] = p.T.astype(ROUND)
        return p

    def forward(s, pair):
        x1, x2 = pair
        w_copy(s).wait()
        base = pl.multiple_of(s * rows, rows)
        p = activate(x2, 2 * s)
        band(fwd_pad, 0, before(p), p.astype(ROUND), after(p))
        y1 = x1 + conv(fwd_pad, 0, w_all[pl.ds(base, half), :])
        p = activate(y1, 2 * s + 1)
        band(fwd_pad, 1, before(p), p.astype(ROUND), after(p))
        y2 = x2 + conv(fwd_pad, 1, w_all[pl.ds(base + half, half), :])
        return y1, y2

    x_copy.wait()
    lax.fori_loop(0, sections, forward, (x_in[0], x_in[1]))

    def spread(k, e, base, at):
        band(bwd_pad, k, after(e), e.astype(ROUND), before(e))
        total = None
        pieces = []
        for a in range(3):
            lines = bwd_pad[k, (2 - a) * side : (2 - a) * side + pixels, :]
            pieces.append(lines)
            for b in range(3):
                w = w_all[pl.ds(base + (3 * a + b) * channels, channels), :]
                part = lax.dot_general(
                    lines[:, b * channels : (b + 1) * channels], w, (((1,), (1,)), ((), ())),
                    preferred_element_type=jnp.float32,
                )
                total = part if total is None else total + part
        wgrad = jnp.dot(
            saved_p[at], jnp.concatenate(pieces, axis=1), preferred_element_type=jnp.float32
        ).astype(ROUND)
        for tap in range(9):
            g_all[pl.ds(base + tap * channels, channels), :] = wgrad[:, tap * channels : (tap + 1) * channels]
        return total * slopes[at]

    def backward(step, pair):
        d1, d2 = pair
        s = sections - 1 - step
        base = pl.multiple_of(s * rows, rows)
        d1 = d1 + spread(0, d2, base + half, 2 * s + 1)
        d2 = d2 + spread(1, d1, base, 2 * s)
        g_copy(s).start()
        return d1, d2

    d_copy.wait()
    lax.fori_loop(0, sections, backward, (d_in[0], d_in[1]))
    for s in range(sections):
        g_copy(s).wait()


def image_grads(stream, cotangent, weights, which, sections):
    side, channels = stream.shape[2], stream.shape[4]
    pixels = side * side
    images = stream.shape[1]
    rows = weights.shape[0] // sections
    flat = (2, images, pixels, channels)
    far = pl.BlockSpec(memory_space=pltpu.HBM)
    kernel = lambda *refs: image_step(sections, side, rows, *refs)
    return pl.pallas_call(
        kernel,
        out_shape=jax.ShapeDtypeStruct(weights.shape, ROUND),
        grid_spec=pltpu.PrefetchScalarGridSpec(
            num_scalar_prefetch=1,
            grid=(1,),
            in_specs=[far, far, far],
            out_specs=far,
            scratch_shapes=[
                pltpu.VMEM((2, pixels, channels), jnp.float32),
                pltpu.VMEM((2, pixels, channels), jnp.float32),
                pltpu.VMEM(weights.shape, ROUND),
                pltpu.VMEM(weights.shape, ROUND),
                pltpu.VMEM((2 * sections, channels, pixels), ROUND),
                pltpu.VMEM((2 * sections, pixels, channels), jnp.float32),
                pltpu.VMEM((2, pixels + 2 * side, 3 * channels), ROUND),
                pltpu.VMEM((2, pixels + 2 * side, 3 * channels), ROUND),
                pltpu.SemaphoreType.DMA((2,)),
                pltpu.SemaphoreType.DMA((sections,)),
                pltpu.SemaphoreType.DMA((sections,)),
            ],
        ),
        compiler_params=pltpu.CompilerParams(vmem_limit_bytes=60 << 20),
        name="image_step",
    )(which, stream.reshape(flat), cotangent.reshape(flat), weights)


def on_device(stream, cotangent, weights, master, momentum):
    sections = lax.axis_size("section")
    dp = lax.axis_size("dp")
    images = stream.shape[1] * dp
    share = weights.shape[1] // dp
    channels = weights.shape[2]
    every = lax.all_gather(weights[0], "section", axis=0, tiled=True)
    which = lax.axis_index("section").astype(jnp.int32).reshape(1)
    grads = image_grads(stream, cotangent, every, which, sections)
    own = lax.psum_scatter(grads, "section", scatter_dimension=0, tiled=True)
    tiles = lax.all_to_all(own.reshape(dp, share, channels), "dp", 0, 0, tiled=True)
    gradient = jnp.sum(tiles.astype(jnp.float32), axis=0) / images
    new_momentum = INERTIA * momentum[0] + gradient
    new_master = master[0] - STEP_SIZE * new_momentum
    copies = jnp.broadcast_to(new_master.astype(ROUND)[None], (dp, share, channels))
    new_weights = lax.all_to_all(copies, "dp", 0, 0, tiled=True).reshape(dp * share, channels)
    return (new_master[None], new_momentum[None], new_weights[None])


def solution(mesh):
    placed = (
        P(None, "dp", None, None, None),
        P(None, "dp", None, None, None),
        P("section", None, None),
        P("section", "dp", None),
        P("section", "dp", None),
    )
    return jax.shard_map(
        on_device,
        mesh=mesh,
        in_specs=placed,
        out_specs=(P("section", "dp", None), P("section", "dp", None), P("section", None, None)),
        check_vma=False,
    )
```

time: 481 us -> 193 us (0.40)
  starting transfers between devices: 92.5 us -> 0.08 us
  other arithmetic: 84 us -> 0.73 us
  waiting for transfers between devices: 187 us -> 125 us
  blocking collectives: 72.1 us -> 35.5 us
  matrix products: 26.4 us -> 0 us
  Pallas kernels: 0 us -> 16.2 us
  between operations: 0.73 us -> 14.1 us
  local copies, waits for them, and re-layouts: 12.2 us -> 0.9 us
    ppermute x30 -> x0, waiting for transfers between devices: 187 us -> none  [shifted_2(): return lax.ppermute(value, axis, pairs)]
    ppermute x30 -> x0, starting transfers between devices: 92.5 us -> none  [shifted_2(): return lax.ppermute(value, axis, pairs)]
    all_gather x0 -> x1, waiting for transfers between devices: none -> 65.4 us  [on_device(): every = lax.all_gather(weights[0], 'section', axis=0, tiled=True)]
    reduce_scatter x0 -> x1, waiting for transfers between devices: none -> 59.1 us  [on_device(): own = lax.psum_scatter(grads, 'section', scatter_dimension=0, tiled=True)]
    select_n x30 -> x0, other arithmetic: 41.7 us -> none  [the longest x15 26.8 us: forward_step(): jnp.where(active, lax.dynamic_update_index_in_dim(kept_inputs, entering,...]
    dot_general x56 -> x0, matrix products: 26.4 us -> none  [the longest x24 15.4 us: convolve(): jnp.dot(patches, weight, preferred_element_type=jnp.float32)]
    all_gather x1 -> x0, blocking collectives: 23 us -> none  [on_device(): lax.all_gather(new_master.astype(jnp.bfloat16), 'dp', axis=0, tiled=True)]
    cond x40 -> x0, other arithmetic: 17.1 us -> none
  transfers between devices with their start and end apart: 30 -> 2, of which waited for: 30 -> 2; matrix products, arithmetic and copies ran while one was open for 1% -> 0% of each run, Pallas kernels for 0% -> 0%
where the time goes in v1:
time: 193 us
  waiting for transfers between devices  125 us (65%)
  blocking collectives  35.5 us (18%)
  Pallas kernels  16.2 us (8%)
  between operations  14.1 us (7%)
    all_gather x1, waiting for transfers between devices, on_device(): every = lax.all_gather(weights[0], 'section', axis=0, tiled=True)  65.4 us
    reduce_scatter x1, waiting for transfers between devices, on_device(): own = lax.psum_scatter(grads, 'section', scatter_dimension=0, tiled=True)  59.1 us
    all_to_all x1, blocking collectives, on_device(): lax.all_to_all(own.reshape(dp, share, channels), 'dp', 0, 0, tiled=True)  19.8 us
    pallas_call x1, Pallas kernels, image_grads(): pl.pallas_call(kernel, out_shape=jax.ShapeDtypeStruct(weights.shape, ROUN...  16.2 us
    all_to_all x1, blocking collectives, on_device(): lax.all_to_all(copies, 'dp', 0, 0, tiled=True).reshape(dp * share, channels)  15.8 us
  transfers between devices with their start and end apart: 2, of which 2 were waited for; matrix products, arithmetic and copies ran while one was open for 0% of the time, Pallas kernels for 0%

profile of v1, /device:TPU:1, one launch (start us, length us, event | category | flops | bytes accessed | tf_op | source)
XLA Modules:
  0.0 192.7 jit_solution(8324358998602107714)
XLA Ops:
  7.2 0.0 all-gather.3.cloned.1.call-start
  7.2 0.7 all-gather.3.cloned.1.call-update
  7.9 0.0 reduce-scatter.2.cloned.1.call-start
  7.9 65.4 %all-gather.3.cloned.1.call-done = bf16[1,18432,128]{2,1,0:T(8,128)(2,1)} async-done(((bf16[1,2304,128]{2,1,0:T(8,128)(2,1)}), bf16[1,18432,128]{2,1,0:T(8,128)(2,1)}) %all-gather.3.cloned.1.call-update) | async-done | bytes 4718608 | tf_op jit(solution)/shard_map/all_gather | solution.py:158
  73.4 16.2 %image_step.1 = bf16[18432,128]{1,0:T(8,128)(2,1)} custom-call(s32[1]{0:T(128)} %bitcast.refs_0_, f32[2,8,256,128]{3,2,1,0:T(8,128)} %bitcast.13, f32[2,8,256,128]{3,2,1,0:T(8,128)} %bitcast.14, bf16[18432,128]{1,0:T(8,128)(2,1)} %bitcast.11), custom_call_target="tpu_custom_call" | custom-call | tf_op jit(solution)/shard_map/image_step/pallas_call | solution.py:125
  89.6 0.0 copy-start
  89.6 0.0 copy-start.1
  89.6 0.0 reduce-scatter.2.cloned.1.call-update
  89.6 59.1 %reduce-scatter.2.cloned.1.call-done = bf16[2304,128]{1,0:T(8,128)(2,1)} async-done(((bf16[18432,128]{1,0:T(8,128)(2,1)}), bf16[2304,128]{1,0:T(8,128)(2,1)}) %reduce-scatter.2.cloned.1.call-update) | async-done | bytes 589840 | tf_op jit(solution)/shard_map/reduce_scatter | solution.py:161
  148.7 19.8 %all_to_all.10 = bf16[32,72,128]{2,1,0:T(8,128)(2,1)S(1)} all-to-all(bf16[32,72,128]{2,1,0:T(8,128)(2,1)} %bitcast.15), channel_id=1, replica_groups=mesh['section'=8,'dp'=32] {'dp'}, dimensions={0} | all-to-all | bytes 1179648 | tf_op jit(solution)/shard_map/all_to_all | solution.py:162
  168.5 0.1 convert_reduce_fusion
  168.6 0.0 copy-done
  168.6 0.0 copy-done.1
  168.6 0.6 convert_bitcast_fusion
  169.2 0.1 broadcast_in_dim.5
  169.3 15.8 %all_to_all.11 = bf16[32,72,128]{2,1,0:T(8,128)(2,1)S(1)} all-to-all(bf16[32,72,128]{2,1,0:T(8,128)(2,1)S(1)} %broadcast_in_dim.5), channel_id=1, replica_groups=mesh['section'=8,'dp'=32] {'dp'}, dimensions={0} | all-to-all | bytes 1179648 | tf_op jit(solution)/shard_map/all_to_all | solution.py:167
  185.0 0.8 copy.9
Async XLA Ops:
  7.2 66.2 %all-gather.3.cloned.1.call-start = ((), (), s32[]{:S(2)}) async-start(), calls=%async_computation.4 | async-start | bytes 5308416 | tf_op jit(solution)/shard_map/all_gather | solution.py:158
  7.9 140.8 %reduce-scatter.2.cloned.1.call-start = ((), (), s32[]{:S(2)}) async-start(), calls=%async_computation.3 | async-start | bytes 5308416 | tf_op jit(solution)/shard_map/reduce_scatter | solution.py:161
  89.6 79.0 %copy-start = (f32[1,72,128]{2,1,0:T(8,128)S(1)}, f32[1,72,128]{2,1,0:T(8,128)}, u32[]{:S(2)}) copy-start(f32[1,72,128]{2,1,0:T(8,128)} %param.8) | copy-start | bytes 110596
  89.6 79.0 %copy-start.1 = (f32[1,72,128]{2,1,0:T(8,128)S(1)}, f32[1,72,128]{2,1,0:T(8,128)}, u32[]{:S(2)}) copy-start(f32[1,72,128]{2,1,0:T(8,128)} %param.9) | copy-start | bytes 110596
Sparse Core Ops, SparseCore 0:
  9.8 63.5 all-gather.2
  89.8 58.9 reduce-scatter.1

commit v2 on v1

v2 whole, which is shorter than its diff:
```python
import jax
import jax.numpy as jnp
from jax import lax
from jax.experimental import pallas as pl
from jax.experimental.pallas import tpu as pltpu
from jax.sharding import PartitionSpec as P

STEP_SIZE = 0.1
INERTIA = 0.9
ROUND = jnp.bfloat16


def chip(role, first, second):
    return jnp.where(role == 0, second, first), jnp.where(role == 0, first, second)


def image_step(sides, sections, side, share, place, stream, cotangent, *refs):
    gathered, refs = refs[:10], refs[10:]
    kept, passed, refs = refs[0], refs[1:5], refs[5:]
    x_in, d_in, w_all, g_all, saved_p, slopes, fwd_pad, bwd_pad, x_sem, w_sem, g_sem = refs
    z, x, y, core = place[0], place[1], place[2], place[3]
    channels = stream.shape[-1]
    pixels = side * side
    rows = w_all.shape[1]
    half = rows // 2
    x_copy = pltpu.make_async_copy(stream.at[:, z], x_in, x_sem.at[0])
    d_copy = pltpu.make_async_copy(cotangent.at[:, z], d_in, x_sem.at[1])

    def block(role, at_first, at_second):
        first = jnp.where(role == 0, y, x)
        second = jnp.where(role == 0, x, y)
        px, py = chip(role, lax.rem(first + at_first + sides, sides), lax.rem(second + at_second + sides, sides))
        return pl.ds(pl.multiple_of(((px * sides + py) * 2 + role) * share, 8), share)

    copies = []
    for which in range(2):
        role = core if which == 0 else 1 - core
        near, low, high, far_a, far_b = gathered[5 * which : 5 * which + 5]
        for i in range(sides):
            far = far_a.at[i] if i < sides // 2 else far_b.at[i - sides // 2]
            for j, source in enumerate((near.at[i], low.at[i], far, high.at[i])):
                target = w_all.at[:, block(role, -i, -j), :]
                copies.append(pltpu.make_async_copy(source, target, w_sem.at[len(copies)]))
    x_copy.start()
    for copy in copies:
        copy.start()
    d_copy.start()
    edge = jnp.zeros((side, 3 * channels), ROUND)
    for pad in (fwd_pad, bwd_pad):
        for k in range(2):
            pad[k, 0:side, :] = edge
            pad[k, side + pixels : 2 * side + pixels, :] = edge

    column = lax.broadcasted_iota(jnp.int32, (pixels, channels), 0) & (side - 1)
    not_first = column > 0
    not_last = column < side - 1

    def before(v):
        return jnp.where(not_first, pltpu.roll(v, 1, 0), 0.0).astype(ROUND)

    def after(v):
        return jnp.where(not_last, pltpu.roll(v, pixels - 1, 0), 0.0).astype(ROUND)

    def band(pad, k, low, mid, high):
        body = pl.ds(side, pixels)
        pad[k, body, 0:channels] = low
        pad[k, body, channels : 2 * channels] = mid
        pad[k, body, 2 * channels : 3 * channels] = high

    def conv(pad, k, w):
        taps = jnp.concatenate([pad[k, a * side : a * side + pixels, :] for a in range(3)], axis=1)
        return jnp.dot(taps, w, preferred_element_type=jnp.float32)

    def activate(v, at):
        logistic = 1.0 / (1.0 + jnp.exp(-v))
        p = v * logistic
        slopes[at] = logistic + p * (1.0 - logistic)
        saved_p[at] = p.T.astype(ROUND)
        return p

    def forward(s, pair):
        x1, x2 = pair
        w = w_all.at[lax.rem(z - s + sections, sections)]
        p = activate(x2, 2 * s)
        band(fwd_pad, 0, before(p), p.astype(ROUND), after(p))
        y1 = x1 + conv(fwd_pad, 0, w[0:half, :])
        p = activate(y1, 2 * s + 1)
        band(fwd_pad, 1, before(p), p.astype(ROUND), after(p))
        y2 = x2 + conv(fwd_pad, 1, w[half:rows, :])
        return y1, y2

    x_copy.wait()
    for copy in copies:
        copy.wait()
    lax.fori_loop(0, sections, forward, (x_in[0], x_in[1]))

    def spread(k, e, w, g, base, at):
        band(bwd_pad, k, after(e), e.astype(ROUND), before(e))
        total = None
        pieces = []
        for a in range(3):
            lines = bwd_pad[k, (2 - a) * side : (2 - a) * side + pixels, :]
            pieces.append(lines)
            for b in range(3):
                first = base + (3 * a + b) * channels
                part = lax.dot_general(
                    lines[:, b * channels : (b + 1) * channels], w[first : first + channels, :],
                    (((1,), (1,)), ((), ())), preferred_element_type=jnp.float32,
                )
                total = part if total is None else total + part
        wgrad = jnp.dot(
            saved_p[at], jnp.concatenate(pieces, axis=1), preferred_element_type=jnp.float32
        ).astype(ROUND)
        for tap in range(9):
            first = base + tap * channels
            g[first : first + channels, :] = wgrad[:, tap * channels : (tap + 1) * channels]
        return total * slopes[at]

    def backward(step, pair):
        d1, d2 = pair
        s = sections - 1 - step
        w = w_all.at[lax.rem(z - s + sections, sections)]
        g = g_all.at[lax.rem(s - z + sections, sections)]
        d1 = d1 + spread(0, d2, w, g, half, 2 * s + 1)
        d2 = d2 + spread(1, d1, w, g, 0, 2 * s)
        return d1, d2

    d_copy.wait()
    lax.fori_loop(0, sections, backward, (d_in[0], d_in[1]))
    copies = []
    for j in (2, 1, 3, 0):
        for i in range(sides):
            for role, target in ((1 - core, passed[j].at[i]), (core, kept.at[j, i])):
                source = g_all.at[:, block(role, i, j), :]
                copies.append(pltpu.make_async_copy(source, target, g_sem.at[len(copies)]))
    for copy in copies:
        copy.start()
    for copy in copies:
        copy.wait()


def image_grads(stream, cotangent, gathered, place, sides):
    side, channels = stream.shape[2], stream.shape[4]
    pixels = side * side
    images = stream.shape[1]
    sections, share = gathered[0].shape[1:3]
    rows = share * 2 * sides * sides
    flat = (2, images, pixels, channels)
    far = pl.BlockSpec(memory_space=pltpu.HBM)
    kernel = lambda *refs: image_step(sides, sections, side, share, *refs)
    piece = (sides, sections, share, channels)
    return pl.pallas_call(
        kernel,
        out_shape=[jax.ShapeDtypeStruct((sides, *piece), ROUND)] + [jax.ShapeDtypeStruct(piece, ROUND)] * sides,
        grid_spec=pltpu.PrefetchScalarGridSpec(
            num_scalar_prefetch=1,
            grid=(1,),
            in_specs=[far] * 12,
            out_specs=[far] * 5,
            scratch_shapes=[
                pltpu.VMEM((2, pixels, channels), jnp.float32),
                pltpu.VMEM((2, pixels, channels), jnp.float32),
                pltpu.VMEM((sections, rows, channels), ROUND),
                pltpu.VMEM((sections, rows, channels), ROUND),
                pltpu.VMEM((2 * sections, channels, pixels), ROUND),
                pltpu.VMEM((2 * sections, pixels, channels), jnp.float32),
                pltpu.VMEM((2, pixels + 2 * side, 3 * channels), ROUND),
                pltpu.VMEM((2, pixels + 2 * side, 3 * channels), ROUND),
                pltpu.SemaphoreType.DMA((2,)),
                pltpu.SemaphoreType.DMA((2 * sides * sides,)),
                pltpu.SemaphoreType.DMA((2 * sides * sides,)),
            ],
        ),
        compiler_params=pltpu.CompilerParams(vmem_limit_bytes=60 << 20),
        name="image_step",
    )(place, stream.reshape(flat), cotangent.reshape(flat), *gathered)


def along_z(value, by):
    n = lax.axis_size("section")
    return lax.ppermute(value, "section", [(i, (i + by) % n) for i in range(n)])


def in_plane(sides, value, to):
    pairs = []
    for x in range(sides):
        for y in range(sides):
            for core in range(2):
                px, py, pc = to(x, y, core)
                pairs.append(((x * sides + y) * 2 + core, ((px % sides) * sides + py % sides) * 2 + pc))
    return lax.ppermute(value, "dp", pairs)


def along_first(sides, value, by):
    return in_plane(sides, value, lambda x, y, c: (x, y + by, c) if c == 0 else (x + by, y, c))


def along_second(sides, value, by):
    return in_plane(sides, value, lambda x, y, c: (x + by, y, c) if c == 0 else (x, y + by, c))


def swapped(sides, value):
    return in_plane(sides, value, lambda x, y, c: (x, y, 1 - c))


def gather_weights(mine, sections, sides):
    line = jnp.stack([mine] + [along_z(mine, k) for k in range(1, sections)])
    near = jnp.stack([line] + [along_first(sides, line, i) for i in range(1, sides)])
    middle = sides // 2
    low = along_second(sides, near, 1)
    high = along_second(sides, near, -1)
    far_a = along_second(sides, low[:middle], 1)
    far_b = along_second(sides, high[middle:], -1)
    own = [near, low, high, far_a, far_b]
    return own + [swapped(sides, block) for block in own]


def wide(value):
    return value.astype(jnp.float32)


def scatter_grads(kept, passed, sections, sides):
    middle = sides // 2
    came = {j: swapped(sides, passed[j]) for j in (2, 1, 3, 0)}
    opposite = wide(kept[2]) + wide(came[2])
    opposite = opposite.astype(ROUND)
    a_in = along_second(sides, opposite[:middle], 1)
    b_in = along_second(sides, opposite[middle:], -1)
    one, three = kept[1], kept[3]
    one_b = (wide(one[middle:]) + wide(came[1][middle:])).astype(ROUND)
    three_a = (wide(three[:middle]) + wide(came[3][:middle])).astype(ROUND)
    low_b = along_second(sides, one_b, 1)
    high_a = along_second(sides, three_a, -1)
    one_a = (wide(one[:middle]) + wide(came[1][:middle]) + wide(a_in)).astype(ROUND)
    three_b = (wide(three[middle:]) + wide(came[3][middle:]) + wide(b_in)).astype(ROUND)
    low_a = along_second(sides, one_a, 1)
    high_b = along_second(sides, three_b, -1)
    low = jnp.concatenate([low_a, low_b])
    high = jnp.concatenate([high_a, high_b])
    mine = (wide(kept[0]) + wide(came[0]) + wide(low) + wide(high)).astype(ROUND)
    line = wide(mine[0])
    for i in range(1, sides):
        line = line + wide(along_first(sides, mine[i], i))
    line = line.astype(ROUND)
    total = wide(line[0])
    for k in range(1, sections):
        total = total + wide(along_z(line[k], k))
    return total


def on_device(stream, cotangent, weights, master, momentum):
    sections = lax.axis_size("section")
    dp = lax.axis_size("dp")
    sides = int(round((dp // 2) ** 0.5))
    images = stream.shape[1] * dp
    share = weights.shape[1] // dp
    channels = weights.shape[2]
    z, at = lax.axis_index("section"), lax.axis_index("dp")
    place = jnp.stack([z, at // (2 * sides), at // 2 % sides, at % 2]).astype(jnp.int32)
    mine = lax.dynamic_slice_in_dim(weights[0], at * share, share, 0)
    gathered = gather_weights(mine, sections, sides)
    kept, *passed = image_grads(stream, cotangent, gathered, place, sides)
    gradient = scatter_grads(kept, passed, sections, sides) / images
    new_momentum = INERTIA * momentum[0] + gradient
    new_master = master[0] - STEP_SIZE * new_momentum
    copies = jnp.broadcast_to(new_master.astype(ROUND)[None], (dp, share, channels))
    new_weights = lax.all_to_all(copies, "dp", 0, 0, tiled=True).reshape(dp * share, channels)
    return (new_master[None], new_momentum[None], new_weights[None])


def solution(mesh):
    placed = (
        P(None, "dp", None, None, None),
        P(None, "dp", None, None, None),
        P("section", None, None),
        P("section", "dp", None),
        P("section", "dp", None),
    )
    return jax.shard_map(
        on_device,
        mesh=mesh,
        in_specs=placed,
        out_specs=(P("section", "dp", None), P("section", "dp", None), P("section", None, None)),
        check_vma=False,
    )
```

time: 193 us -> 158 us (0.82)
  starting transfers between devices: 0.08 us -> 78.5 us
  waiting for transfers between devices: 125 us -> 52 us
  blocking collectives: 35.5 us -> 0 us
  between operations: 14.1 us -> 0.9 us
  Pallas kernels: 16.2 us -> 19.2 us
  other arithmetic: 0.73 us -> 3.48 us
  local copies, waits for them, and re-layouts: 0.9 us -> 3.49 us
    ppermute x0 -> x39, starting transfers between devices: none -> 66.4 us  [the longest x25 41.3 us: in_plane(): return lax.ppermute(value, 'dp', pairs)]
    all_gather x1 -> x0, waiting for transfers between devices: 65.4 us -> none  [on_device(): every = lax.all_gather(weights[0], 'section', axis=0, tiled=True)]
    reduce_scatter x1 -> x0, waiting for transfers between devices: 59.1 us -> none  [on_device(): own = lax.psum_scatter(grads, 'section', scatter_dimension=0, tiled=True)]
    ppermute x0 -> x39, waiting for transfers between devices: none -> 40.4 us  [the longest x25 27.3 us: in_plane(): return lax.ppermute(value, 'dp', pairs)]
    all_to_all x2 -> x0, blocking collectives: 35.5 us -> none  [the longest x1 19.8 us: on_device(): lax.all_to_all(own.reshape(dp, share, channels), 'dp', 0, 0, tiled=True)]
    all_to_all x0 -> x1, starting transfers between devices: none -> 12.1 us  [on_device(): lax.all_to_all(copies, 'dp', 0, 0, tiled=True).reshape(dp * share, channels)]
    all_to_all x0 -> x1, waiting for transfers between devices: none -> 11.7 us  [on_device(): lax.all_to_all(copies, 'dp', 0, 0, tiled=True).reshape(dp * share, channels)]
    pallas_call x1, Pallas kernels: 16.2 us -> 19.2 us  [image_grads(): pl.pallas_call(kernel, out_shape=[jax.ShapeDtypeStruct((sides, *piece), R...]
  transfers between devices with their start and end apart: 2 -> 40, of which waited for: 2 -> 19; matrix products, arithmetic and copies ran while one was open for 0% -> 2% of each run, Pallas kernels for 0% -> 0%
where the time goes in v2:
time: 158 us
  starting transfers between devices  78.5 us (50%)
  waiting for transfers between devices  52 us (33%)
  Pallas kernels  19.2 us (12%)
  local copies, waits for them, and re-layouts  3.49 us (2%)
  other arithmetic  3.48 us (2%)
    ppermute x25, starting transfers between devices, in_plane(): return lax.ppermute(value, 'dp', pairs)  41.3 us
    ppermute x25, waiting for transfers between devices, in_plane(): return lax.ppermute(value, 'dp', pairs)  27.3 us
    ppermute x14, starting transfers between devices, along_z(): return lax.ppermute(value, 'section', [(i, (i + by) % n) for i in range(n)])  25.1 us
    pallas_call x1, Pallas kernels, image_grads(): pl.pallas_call(kernel, out_shape=[jax.ShapeDtypeStruct((sides, *piece), R...  19.2 us
    ppermute x14, waiting for transfers between devices, along_z(): return lax.ppermute(value, 'section', [(i, (i + by) % n) for i in range(n)])  13.1 us
    all_to_all x1, starting transfers between devices, on_device(): lax.all_to_all(copies, 'dp', 0, 0, tiled=True).reshape(dp * share, channels)  12.1 us
    all_to_all x1, waiting for transfers between devices, on_device(): lax.all_to_all(copies, 'dp', 0, 0, tiled=True).reshape(dp * share, channels)  11.7 us
  transfers between devices with their start and end apart: 40, of which 19 were waited for; matrix products, arithmetic and copies ran while one was open for 2% of the time, Pallas kernels for 0%

profile of v2, /device:TPU:1, one launch (start us, length us, event | category | flops | bytes accessed | tf_op | source)
XLA Modules:
  0.0 157.6 jit_solution(7922596639662931390)
XLA Ops:
  0.6 0.7 dynamic-slice_bitcast_fusion
  1.4 2.5 %collective-permute-start = (bf16[72,128]{1,0:T(8,128)(2,1)S(1)}, bf16[72,128]{1,0:T(8,128)(2,1)S(1)}, u32[]{:S(2)}, u32[]{:S(2)}) collective-permute-start(bf16[72,128]{1,0:T(8,128)(2,1)S(1)} %get-tuple-element.26), channel_id=1, source_target_pairs={{0,32},{32,64},{64,96},{96,128},{128,160},{160,192},{192,224},{224... | collective-permute-start | bytes 55304 | tf_op jit(solution)/shard_map/ppermute | solution.py:181
  3.8 4.0 %collective-permute-start.6 = (bf16[72,128]{1,0:T(8,128)(2,1)S(1)}, bf16[72,128]{1,0:T(8,128)(2,1)S(1)}, u32[]{:S(2)}, u32[]{:S(2)}) collective-permute-start(bf16[72,128]{1,0:T(8,128)(2,1)S(1)} %get-tuple-element.26), channel_id=1, source_target_pairs={{0,224},{32,0},{64,32},{96,64},{128,96},{160,128},{192,160},{224,1... | collective-permute-start | bytes 55304 | tf_op jit(solution)/shard_map/ppermute | solution.py:181
  7.8 1.8 %collective-permute-start.5 = (bf16[72,128]{1,0:T(8,128)(2,1)S(1)}, bf16[72,128]{1,0:T(8,128)(2,1)S(1)}, u32[]{:S(2)}, u32[]{:S(2)}) collective-permute-start(bf16[72,128]{1,0:T(8,128)(2,1)S(1)} %get-tuple-element.26), channel_id=1, source_target_pairs={{0,192},{32,224},{64,0},{96,32},{128,64},{160,96},{192,128},{224,1... | collective-permute-start | bytes 55304 | tf_op jit(solution)/shard_map/ppermute | solution.py:181
  9.7 2.1 %collective-permute-start.4 = (bf16[72,128]{1,0:T(8,128)(2,1)S(1)}, bf16[72,128]{1,0:T(8,128)(2,1)S(1)}, u32[]{:S(2)}, u32[]{:S(2)}) collective-permute-start(bf16[72,128]{1,0:T(8,128)(2,1)S(1)} %get-tuple-element.26), channel_id=1, source_target_pairs={{0,160},{32,192},{64,224},{96,0},{128,32},{160,64},{192,96},{224,1... | collective-permute-start | bytes 55304 | tf_op jit(solution)/shard_map/ppermute | solution.py:181
  11.8 2.8 %collective-permute-start.3 = (bf16[72,128]{1,0:T(8,128)(2,1)S(1)}, bf16[72,128]{1,0:T(8,128)(2,1)S(1)}, u32[]{:S(2)}, u32[]{:S(2)}) collective-permute-start(bf16[72,128]{1,0:T(8,128)(2,1)S(1)} %get-tuple-element.26), channel_id=1, source_target_pairs={{0,128},{32,160},{64,192},{96,224},{128,0},{160,32},{192,64},{224,... | collective-permute-start | bytes 55304 | tf_op jit(solution)/shard_map/ppermute | solution.py:181
  14.6 4.8 %collective-permute-done.1 = bf16[72,128]{1,0:T(8,128)(2,1)S(1)} collective-permute-done((bf16[72,128]{1,0:T(8,128)(2,1)S(1)}, bf16[72,128]{1,0:T(8,128)(2,1)S(1)}, u32[]{:S(2)}, u32[]{:S(2)}) %collective-permute-start.1) | collective-permute-done | bytes 18464 | tf_op jit(solution)/shard_map/ppermute | solution.py:181
  19.5 5.6 %collective-permute-done.2 = bf16[72,128]{1,0:T(8,128)(2,1)S(1)} collective-permute-done((bf16[72,128]{1,0:T(8,128)(2,1)S(1)}, bf16[72,128]{1,0:T(8,128)(2,1)S(1)}, u32[]{:S(2)}, u32[]{:S(2)}) %collective-permute-start.2) | collective-permute-done | bytes 18464 | tf_op jit(solution)/shard_map/ppermute | solution.py:181
  25.2 2.6 %collective-permute-start.9 = (bf16[8,72,128]{2,1,0:T(8,128)(2,1)S(1)}, bf16[8,72,128]{2,1,0:T(8,128)(2,1)S(1)}, u32[]{:S(2)}, u32[]{:S(2)}) collective-permute-start(bf16[8,72,128]{2,1,0:T(8,128)(2,1)S(1)} %constant_dynamic-update-slice_fusion), channel_id=1, source_target_pairs={{0,6},{1,25},{2,0},{3,27},{4,2},{5,29},{6,4},{7,31},{8,14},{9,1},{... | collective-permute-start | bytes 442376 | tf_op jit(solution)/shard_map/ppermute | solution.py:191
  28.3 0.6 collective-permute-start.7
  28.9 2.5 %collective-permute-done.9 = bf16[8,72,128]{2,1,0:T(8,128)(2,1)S(1)} collective-permute-done((bf16[8,72,128]{2,1,0:T(8,128)(2,1)S(1)}, bf16[8,72,128]{2,1,0:T(8,128)(2,1)S(1)}, u32[]{:S(2)}, u32[]{:S(2)}) %collective-permute-start.9) | collective-permute-done | bytes 147488 | tf_op jit(solution)/shard_map/ppermute | solution.py:191
  31.5 1.9 %collective-permute-done.8 = bf16[8,72,128]{2,1,0:T(8,128)(2,1)S(1)} collective-permute-done((bf16[8,72,128]{2,1,0:T(8,128)(2,1)S(1)}, bf16[8,72,128]{2,1,0:T(8,128)(2,1)S(1)}, u32[]{:S(2)}, u32[]{:S(2)}) %collective-permute-start.8) | collective-permute-done | bytes 147488 | tf_op jit(solution)/shard_map/ppermute | solution.py:191
  33.4 1.5 collective-permute-done.7
  35.0 3.1 %collective-permute-start.11 = (bf16[4,8,72,128]{3,2,1,0:T(8,128)(2,1)S(1)}, bf16[4,8,72,128]{3,2,1,0:T(8,128)(2,1)S(1)}, u32[]{:S(2)}, u32[]{:S(2)}) collective-permute-start(bf16[4,8,72,128]{3,2,1,0:T(8,128)(2,1)S(1)} %pad_maximum_fusion.refs_3_), channel_id=1, source_target_pairs={{0,24},{1,7},{2,26},{3,1},{4,28},{5,3},{6,30},{7,5},{8,0},{9,15},{... | collective-permute-start | bytes 1769480 | tf_op jit(solution)/shard_map/ppermute | solution.py:191
  38.1 6.4 %collective-permute-start.14 = (bf16[4,8,72,128]{3,2,1,0:T(8,128)(2,1)S(1)}, bf16[4,8,72,128]{3,2,1,0:T(8,128)(2,1)S(1)}, u32[]{:S(2)}, u32[]{:S(2)}) collective-permute-start(bf16[4,8,72,128]{3,2,1,0:T(8,128)(2,1)S(1)} %pad_maximum_fusion.refs_3_), channel_id=1, source_target_pairs={{0,1},{1,0},{2,3},{3,2},{4,5},{5,4},{6,7},{7,6},{8,9},{9,8},{10,11... | collective-permute-start | bytes 1769480 | tf_op jit(solution)/shard_map/ppermute | solution.py:191
  44.9 3.2 %collective-permute-start.13 = (bf16[2,8,72,128]{3,2,1,0:T(8,128)(2,1)S(1)}, bf16[2,8,72,128]{3,2,1,0:T(8,128)(2,1)}, u32[]{:S(2)}, u32[]{:S(2)}) collective-permute-start(bf16[2,8,72,128]{3,2,1,0:T(8,128)(2,1)S(1)} %slice.115), channel_id=1, source_target_pairs={{0,24},{1,7},{2,26},{3,1},{4,28},{5,3},{6,30},{7,5},{8,0},{9,15},{... | collective-permute-start | bytes 884744 | tf_op jit(solution)/shard_map/ppermute | solution.py:191
  48.2 7.7 %collective-permute-start.16 = (bf16[4,8,72,128]{3,2,1,0:T(8,128)(2,1)S(1)}, bf16[4,8,72,128]{3,2,1,0:T(8,128)(2,1)S(1)}, u32[]{:S(2)}, u32[]{:S(2)}) collective-permute-start(bf16[4,8,72,128]{3,2,1,0:T(8,128)(2,1)S(1)} %collective-permute-done.11.refs_5_), channel_id=1, source_target_pairs={{0,1},{1,0},{2,3},{3,2},{4,5},{5,4},{6,7},{7,6},{8,9},{9,8},{10,11... | collective-permute-start | bytes 1769480 | tf_op jit(solution)/shard_map/ppermute | solution.py:191
  56.0 3.9 %collective-permute-start.18 = (bf16[2,8,72,128]{3,2,1,0:T(8,128)(2,1)}, bf16[2,8,72,128]{3,2,1,0:T(8,128)(2,1)}, u32[]{:S(2)}, u32[]{:S(2)}) collective-permute-start(bf16[2,8,72,128]{3,2,1,0:T(8,128)(2,1)} %collective-permute-done.13.refs_7_), channel_id=1, source_target_pairs={{0,1},{1,0},{2,3},{3,2},{4,5},{5,4},{6,7},{7,6},{8,9},{9,8},{10,11... | collective-permute-start | bytes 884744 | tf_op jit(solution)/shard_map/ppermute | solution.py:191
  60.0 3.9 %collective-permute-start.17 = (bf16[2,8,72,128]{3,2,1,0:T(8,128)(2,1)}, bf16[2,8,72,128]{3,2,1,0:T(8,128)(2,1)}, u32[]{:S(2)}, u32[]{:S(2)}) collective-permute-start(bf16[2,8,72,128]{3,2,1,0:T(8,128)(2,1)} %collective-permute-done.12.refs_6_), channel_id=1, source_target_pairs={{0,1},{1,0},{2,3},{3,2},{4,5},{5,4},{6,7},{7,6},{8,9},{9,8},{10,11... | collective-permute-start | bytes 884744 | tf_op jit(solution)/shard_map/ppermute | solution.py:191
  64.5 0.9 collective-permute-done.17.refs_11_
  65.5 0.8 copy-done.6
  66.2 19.2 %image_step.1 = (bf16[4,4,8,72,128]{4,3,2,1,0:T(8,128)(2,1)}, bf16[4,8,72,128]{3,2,1,0:T(8,128)(2,1)}, bf16[4,8,72,128]{3,2,1,0:T(8,128)(2,1)}, bf16[4,8,72,128]{3,2,1,0:T(8,128)(2,1)}, bf16[4,8,72,128]{3,2,1,0:T(8,128)(2,1)}) custom-call(s32[4]{0:T(128)} %pad_add_fusion.refs_0_, f32[2,8,256,128]{3,2,1,0:T(8,128)} %bitcast.89, f32[2,8,256,128]{3,2,1,0:T(8,128)} %bitcast.90, ...), custom_call_target="tpu_custom_call" | custom-call | tf_op jit(solution)/shard_map/image_step/pallas_call | solution.py:152
  86.4 1.3 collective-permute-done.21
  87.8 1.4 fusion
  89.2 1.1 collective-permute-start.27
  90.8 0.9 collective-permute-start.19
  91.7 3.5 %collective-permute-done.27 = bf16[2,8,72,128]{3,2,1,0:T(8,128)(2,1)S(1)} collective-permute-done((bf16[2,8,72,128]{3,2,1,0:T(8,128)(2,1)S(1)}, bf16[2,8,72,128]{3,2,1,0:T(8,128)(2,1)S(1)}, u32[]{:S(2)}, u32[]{:S(2)}) %collective-permute-start.27) | collective-permute-done | bytes 294944 | tf_op jit(solution)/shard_map/ppermute | solution.py:191
  95.2 2.2 %collective-permute-done.22 = bf16[2,8,72,128]{3,2,1,0:T(8,128)(2,1)S(1)} collective-permute-done((bf16[2,8,72,128]{3,2,1,0:T(8,128)(2,1)S(1)}, bf16[2,8,72,128]{3,2,1,0:T(8,128)(2,1)S(1)}, u32[]{:S(2)}, u32[]{:S(2)}) %collective-permute-start.22) | collective-permute-done | bytes 294944 | tf_op jit(solution)/shard_map/ppermute | solution.py:191
  98.0 1.5 collective-permute-start.24
  99.4 1.4 collective-permute-start.23
  100.8 2.9 %collective-permute-done.26 = bf16[2,8,72,128]{3,2,1,0:T(8,128)(2,1)S(1)} collective-permute-done((bf16[2,8,72,128]{3,2,1,0:T(8,128)(2,1)S(1)}, bf16[2,8,72,128]{3,2,1,0:T(8,128)(2,1)S(1)}, u32[]{:S(2)}, u32[]{:S(2)}) %collective-permute-start.26) | collective-permute-done | bytes 294944 | tf_op jit(solution)/shard_map/ppermute | solution.py:191
  103.7 3.2 %collective-permute-done.28 = bf16[2,8,72,128]{3,2,1,0:T(8,128)(2,1)S(1)} collective-permute-done((bf16[2,8,72,128]{3,2,1,0:T(8,128)(2,1)S(1)}, bf16[2,8,72,128]{3,2,1,0:T(8,128)(2,1)S(1)}, u32[]{:S(2)}, u32[]{:S(2)}) %collective-permute-start.28) | collective-permute-done | bytes 294944 | tf_op jit(solution)/shard_map/ppermute | solution.py:191
  106.9 1.4 collective-permute-done.23
  108.8 2.7 %collective-permute-start.31 = (bf16[8,72,128]{2,1,0:T(8,128)(2,1)S(1)}, bf16[8,72,128]{2,1,0:T(8,128)(2,1)S(1)}, u32[]{:S(2)}, u32[]{:S(2)}) collective-permute-start(bf16[8,72,128]{2,1,0:T(8,128)(2,1)S(1)} %get-tuple-element.22), channel_id=1, source_target_pairs={{0,6},{1,25},{2,0},{3,27},{4,2},{5,29},{6,4},{7,31},{8,14},{9,1},{... | collective-permute-start | bytes 442376 | tf_op jit(solution)/shard_map/ppermute | solution.py:191
  111.4 2.5 %collective-permute-done.29 = bf16[8,72,128]{2,1,0:T(8,128)(2,1)S(1)} collective-permute-done((bf16[8,72,128]{2,1,0:T(8,128)(2,1)S(1)}, bf16[8,72,128]{2,1,0:T(8,128)(2,1)S(1)}, u32[]{:S(2)}, u32[]{:S(2)}) %collective-permute-start.29) | collective-permute-done | bytes 147488 | tf_op jit(solution)/shard_map/ppermute | solution.py:191
  114.0 1.1 collective-permute-done.31
  115.1 1.8 %collective-permute-done.30 = bf16[8,72,128]{2,1,0:T(8,128)(2,1)S(1)} collective-permute-done((bf16[8,72,128]{2,1,0:T(8,128)(2,1)S(1)}, bf16[8,72,128]{2,1,0:T(8,128)(2,1)S(1)}, u32[]{:S(2)}, u32[]{:S(2)}) %collective-permute-start.30) | collective-permute-done | bytes 147488 | tf_op jit(solution)/shard_map/ppermute | solution.py:191
  117.1 2.7 %collective-permute-start.38 = (bf16[72,128]{1,0:T(8,128)(2,1)S(1)}, bf16[72,128]{1,0:T(8,128)(2,1)S(1)}, u32[]{:S(2)}, u32[]{:S(2)}) collective-permute-start(bf16[72,128]{1,0:T(8,128)(2,1)S(1)} %get-tuple-element.29), channel_id=1, source_target_pairs={{0,224},{32,0},{64,32},{96,64},{128,96},{160,128},{192,160},{224,1... | collective-permute-start | bytes 55304 | tf_op jit(solution)/shard_map/ppermute | solution.py:181
  120.3 1.6 %collective-permute-start.36 = (bf16[72,128]{1,0:T(8,128)(2,1)S(1)}, bf16[72,128]{1,0:T(8,128)(2,1)S(1)}, u32[]{:S(2)}, u32[]{:S(2)}) collective-permute-start(bf16[72,128]{1,0:T(8,128)(2,1)S(1)} %get-tuple-element.31), channel_id=1, source_target_pairs={{0,160},{32,192},{64,224},{96,0},{128,32},{160,64},{192,96},{224,1... | collective-permute-start | bytes 55304 | tf_op jit(solution)/shard_map/ppermute | solution.py:181
  121.9 3.2 %collective-permute-start.35 = (bf16[72,128]{1,0:T(8,128)(2,1)S(1)}, bf16[72,128]{1,0:T(8,128)(2,1)S(1)}, u32[]{:S(2)}, u32[]{:S(2)}) collective-permute-start(bf16[72,128]{1,0:T(8,128)(2,1)S(1)} %get-tuple-element.32), channel_id=1, source_target_pairs={{0,128},{32,160},{64,192},{96,224},{128,0},{160,32},{192,64},{224,... | collective-permute-start | bytes 55304 | tf_op jit(solution)/shard_map/ppermute | solution.py:181
  125.2 3.6 %collective-permute-start.33 = (bf16[72,128]{1,0:T(8,128)(2,1)S(1)}, bf16[72,128]{1,0:T(8,128)(2,1)S(1)}, u32[]{:S(2)}, u32[]{:S(2)}) collective-permute-start(bf16[72,128]{1,0:T(8,128)(2,1)S(1)} %get-tuple-element.34), channel_id=1, source_target_pairs={{0,64},{32,96},{64,128},{96,160},{128,192},{160,224},{192,0},{224,... | collective-permute-start | bytes 55304 | tf_op jit(solution)/shard_map/ppermute | solution.py:181
  128.8 2.0 %collective-permute-done.34 = bf16[72,128]{1,0:T(8,128)(2,1)S(1)} collective-permute-done((bf16[72,128]{1,0:T(8,128)(2,1)S(1)}, bf16[72,128]{1,0:T(8,128)(2,1)S(1)}, u32[]{:S(2)}, u32[]{:S(2)}) %collective-permute-start.34) | collective-permute-done | bytes 18464 | tf_op jit(solution)/shard_map/ppermute | solution.py:181
  130.8 0.7 collective-permute-done.33
  131.5 0.9 broadcast_in_dim.14
  132.4 12.1 %all-to-all-start = ((bf16[32,72,128]{2,1,0:T(8,128)(2,1)}), bf16[32,72,128]{2,1,0:T(8,128)(2,1)S(1)}, u32[]{:S(2)}, u32[]{:S(2)}) async-start(bf16[32,72,128]{2,1,0:T(8,128)(2,1)} %broadcast_in_dim.14), calls=%async_computation | async-start | bytes 1179648 | tf_op jit(solution)/shard_map/all_to_all | solution.py:267
  144.5 0.6 fusion.22
  145.2 11.7 %all-to-all-done = bf16[32,72,128]{2,1,0:T(8,128)(2,1)S(1)} async-done(((bf16[32,72,128]{2,1,0:T(8,128)(2,1)}), bf16[32,72,128]{2,1,0:T(8,128)(2,1)S(1)}, u32[]{:S(2)}, u32[]{:S(2)}) %all-to-all-start) | async-done | bytes 589856 | tf_op jit(solution)/shard_map/all_to_all | solution.py:267
  156.8 0.8 copy.16
  (78 shorter events, 5.3 us)
Async XLA Ops:
  1.4 13.2 %collective-permute-start = (bf16[72,128]{1,0:T(8,128)(2,1)S(1)}, bf16[72,128]{1,0:T(8,128)(2,1)S(1)}, u32[]{:S(2)}, u32[]{:S(2)}) collective-permute-start(bf16[72,128]{1,0:T(8,128)(2,1)S(1)} %get-tuple-element.26), channel_id=1, source_target_pairs={{0,32},{32,64},{64,96},{96,128},{128,160},{160,192},{192,224},{224... | collective-permute-start | bytes 55304 | tf_op jit(solution)/shard_map/ppermute | solution.py:181
  3.8 21.4 %collective-permute-start.6 = (bf16[72,128]{1,0:T(8,128)(2,1)S(1)}, bf16[72,128]{1,0:T(8,128)(2,1)S(1)}, u32[]{:S(2)}, u32[]{:S(2)}) collective-permute-start(bf16[72,128]{1,0:T(8,128)(2,1)S(1)} %get-tuple-element.26), channel_id=1, source_target_pairs={{0,224},{32,0},{64,32},{96,64},{128,96},{160,128},{192,160},{224,1... | collective-permute-start | bytes 55304 | tf_op jit(solution)/shard_map/ppermute | solution.py:181
  7.8 17.3 %collective-permute-start.5 = (bf16[72,128]{1,0:T(8,128)(2,1)S(1)}, bf16[72,128]{1,0:T(8,128)(2,1)S(1)}, u32[]{:S(2)}, u32[]{:S(2)}) collective-permute-start(bf16[72,128]{1,0:T(8,128)(2,1)S(1)} %get-tuple-element.26), channel_id=1, source_target_pairs={{0,192},{32,224},{64,0},{96,32},{128,64},{160,96},{192,128},{224,1... | collective-permute-start | bytes 55304 | tf_op jit(solution)/shard_map/ppermute | solution.py:181
  9.7 15.5 %collective-permute-start.4 = (bf16[72,128]{1,0:T(8,128)(2,1)S(1)}, bf16[72,128]{1,0:T(8,128)(2,1)S(1)}, u32[]{:S(2)}, u32[]{:S(2)}) collective-permute-start(bf16[72,128]{1,0:T(8,128)(2,1)S(1)} %get-tuple-element.26), channel_id=1, source_target_pairs={{0,160},{32,192},{64,224},{96,0},{128,32},{160,64},{192,96},{224,1... | collective-permute-start | bytes 55304 | tf_op jit(solution)/shard_map/ppermute | solution.py:181
  11.8 13.4 %collective-permute-start.3 = (bf16[72,128]{1,0:T(8,128)(2,1)S(1)}, bf16[72,128]{1,0:T(8,128)(2,1)S(1)}, u32[]{:S(2)}, u32[]{:S(2)}) collective-permute-start(bf16[72,128]{1,0:T(8,128)(2,1)S(1)} %get-tuple-element.26), channel_id=1, source_target_pairs={{0,128},{32,160},{64,192},{96,224},{128,0},{160,32},{192,64},{224,... | collective-permute-start | bytes 55304 | tf_op jit(solution)/shard_map/ppermute | solution.py:181
  14.6 4.8 %collective-permute-start.1 = (bf16[72,128]{1,0:T(8,128)(2,1)S(1)}, bf16[72,128]{1,0:T(8,128)(2,1)S(1)}, u32[]{:S(2)}, u32[]{:S(2)}) collective-permute-start(bf16[72,128]{1,0:T(8,128)(2,1)S(1)} %get-tuple-element.26), channel_id=1, source_target_pairs={{0,64},{32,96},{64,128},{96,160},{128,192},{160,224},{192,0},{224,... | collective-permute-start | bytes 55304 | tf_op jit(solution)/shard_map/ppermute | solution.py:181
  19.4 5.7 %collective-permute-start.2 = (bf16[72,128]{1,0:T(8,128)(2,1)S(1)}, bf16[72,128]{1,0:T(8,128)(2,1)S(1)}, u32[]{:S(2)}, u32[]{:S(2)}) collective-permute-start(bf16[72,128]{1,0:T(8,128)(2,1)S(1)} %get-tuple-element.26), channel_id=1, source_target_pairs={{0,96},{32,128},{64,160},{96,192},{128,224},{160,0},{192,32},{224,... | collective-permute-start | bytes 55304 | tf_op jit(solution)/shard_map/ppermute | solution.py:181
  25.2 6.2 %collective-permute-start.9 = (bf16[8,72,128]{2,1,0:T(8,128)(2,1)S(1)}, bf16[8,72,128]{2,1,0:T(8,128)(2,1)S(1)}, u32[]{:S(2)}, u32[]{:S(2)}) collective-permute-start(bf16[8,72,128]{2,1,0:T(8,128)(2,1)S(1)} %constant_dynamic-update-slice_fusion), channel_id=1, source_target_pairs={{0,6},{1,25},{2,0},{3,27},{4,2},{5,29},{6,4},{7,31},{8,14},{9,1},{... | collective-permute-start | bytes 442376 | tf_op jit(solution)/shard_map/ppermute | solution.py:191
  27.8 5.6 %collective-permute-start.8 = (bf16[8,72,128]{2,1,0:T(8,128)(2,1)S(1)}, bf16[8,72,128]{2,1,0:T(8,128)(2,1)S(1)}, u32[]{:S(2)}, u32[]{:S(2)}) collective-permute-start(bf16[8,72,128]{2,1,0:T(8,128)(2,1)S(1)} %constant_dynamic-update-slice_fusion), channel_id=1, source_target_pairs={{0,4},{1,17},{2,6},{3,19},{4,0},{5,21},{6,2},{7,23},{8,12},{9,25},... | collective-permute-start | bytes 442376 | tf_op jit(solution)/shard_map/ppermute | solution.py:191
  28.3 6.6 %collective-permute-start.7 = (bf16[8,72,128]{2,1,0:T(8,128)(2,1)S(1)}, bf16[8,72,128]{2,1,0:T(8,128)(2,1)S(1)}, u32[]{:S(2)}, u32[]{:S(2)}) collective-permute-start(bf16[8,72,128]{2,1,0:T(8,128)(2,1)S(1)} %constant_dynamic-update-slice_fusion), channel_id=1, source_target_pairs={{0,2},{1,9},{2,4},{3,11},{4,6},{5,13},{6,0},{7,15},{8,10},{9,17},{... | collective-permute-start | bytes 442376 | tf_op jit(solution)/shard_map/ppermute | solution.py:191
  34.9 30.5 %copy-start = (bf16[4,8,72,128]{3,2,1,0:T(8,128)(2,1)}, bf16[4,8,72,128]{3,2,1,0:T(8,128)(2,1)S(1)}, u32[]{:S(2)}) copy-start(bf16[4,8,72,128]{3,2,1,0:T(8,128)(2,1)S(1)} %pad_maximum_fusion.refs_3_) | copy-start | bytes 1769476
  35.0 9.9 %collective-permute-start.11 = (bf16[4,8,72,128]{3,2,1,0:T(8,128)(2,1)S(1)}, bf16[4,8,72,128]{3,2,1,0:T(8,128)(2,1)S(1)}, u32[]{:S(2)}, u32[]{:S(2)}) collective-permute-start(bf16[4,8,72,128]{3,2,1,0:T(8,128)(2,1)S(1)} %pad_maximum_fusion.refs_3_), channel_id=1, source_target_pairs={{0,24},{1,7},{2,26},{3,1},{4,28},{5,3},{6,30},{7,5},{8,0},{9,15},{... | collective-permute-start | bytes 1769480 | tf_op jit(solution)/shard_map/ppermute | solution.py:191
  38.1 10.1 %collective-permute-start.10 = (bf16[4,8,72,128]{3,2,1,0:T(8,128)(2,1)S(1)}, bf16[4,8,72,128]{3,2,1,0:T(8,128)(2,1)S(1)}, u32[]{:S(2)}, u32[]{:S(2)}) collective-permute-start(bf16[4,8,72,128]{3,2,1,0:T(8,128)(2,1)S(1)} %pad_maximum_fusion.refs_3_), channel_id=1, source_target_pairs={{0,8},{1,3},{2,10},{3,5},{4,12},{5,7},{6,14},{7,1},{8,16},{9,11},{... | collective-permute-start | bytes 1769480 | tf_op jit(solution)/shard_map/ppermute | solution.py:191
  38.1 26.4 %collective-permute-start.14 = (bf16[4,8,72,128]{3,2,1,0:T(8,128)(2,1)S(1)}, bf16[4,8,72,128]{3,2,1,0:T(8,128)(2,1)S(1)}, u32[]{:S(2)}, u32[]{:S(2)}) collective-permute-start(bf16[4,8,72,128]{3,2,1,0:T(8,128)(2,1)S(1)} %pad_maximum_fusion.refs_3_), channel_id=1, source_target_pairs={{0,1},{1,0},{2,3},{3,2},{4,5},{5,4},{6,7},{7,6},{8,9},{9,8},{10,11... | collective-permute-start | bytes 1769480 | tf_op jit(solution)/shard_map/ppermute | solution.py:191
  44.9 20.5 %copy-start.2 = (bf16[4,8,72,128]{3,2,1,0:T(8,128)(2,1)}, bf16[4,8,72,128]{3,2,1,0:T(8,128)(2,1)S(1)}, u32[]{:S(2)}) copy-start(bf16[4,8,72,128]{3,2,1,0:T(8,128)(2,1)S(1)} %collective-permute-done.11.refs_5_) | copy-start | bytes 1769476
  44.9 11.1 %collective-permute-start.13 = (bf16[2,8,72,128]{3,2,1,0:T(8,128)(2,1)S(1)}, bf16[2,8,72,128]{3,2,1,0:T(8,128)(2,1)}, u32[]{:S(2)}, u32[]{:S(2)}) collective-permute-start(bf16[2,8,72,128]{3,2,1,0:T(8,128)(2,1)S(1)} %slice.115), channel_id=1, source_target_pairs={{0,24},{1,7},{2,26},{3,1},{4,28},{5,3},{6,30},{7,5},{8,0},{9,15},{... | collective-permute-start | bytes 884744 | tf_op jit(solution)/shard_map/ppermute | solution.py:191
  48.1 17.3 %copy-start.3 = (bf16[4,8,72,128]{3,2,1,0:T(8,128)(2,1)}, bf16[4,8,72,128]{3,2,1,0:T(8,128)(2,1)S(1)}, u32[]{:S(2)}) copy-start(bf16[4,8,72,128]{3,2,1,0:T(8,128)(2,1)S(1)} %collective-permute-done.10.refs_4_) | copy-start | bytes 1769476
  48.1 11.8 %collective-permute-start.12 = (bf16[2,8,72,128]{3,2,1,0:T(8,128)(2,1)S(1)}, bf16[2,8,72,128]{3,2,1,0:T(8,128)(2,1)}, u32[]{:S(2)}, u32[]{:S(2)}) collective-permute-start(bf16[2,8,72,128]{3,2,1,0:T(8,128)(2,1)S(1)} %slice.114), channel_id=1, source_target_pairs={{0,8},{1,3},{2,10},{3,5},{4,12},{5,7},{6,14},{7,1},{8,16},{9,11},{... | collective-permute-start | bytes 884744 | tf_op jit(solution)/shard_map/ppermute | solution.py:191
  48.2 16.2 %collective-permute-start.16 = (bf16[4,8,72,128]{3,2,1,0:T(8,128)(2,1)S(1)}, bf16[4,8,72,128]{3,2,1,0:T(8,128)(2,1)S(1)}, u32[]{:S(2)}, u32[]{:S(2)}) collective-permute-start(bf16[4,8,72,128]{3,2,1,0:T(8,128)(2,1)S(1)} %collective-permute-done.11.refs_5_), channel_id=1, source_target_pairs={{0,1},{1,0},{2,3},{3,2},{4,5},{5,4},{6,7},{7,6},{8,9},{9,8},{10,11... | collective-permute-start | bytes 1769480 | tf_op jit(solution)/shard_map/ppermute | solution.py:191
  55.9 9.5 %collective-permute-start.15 = (bf16[4,8,72,128]{3,2,1,0:T(8,128)(2,1)S(1)}, bf16[4,8,72,128]{3,2,1,0:T(8,128)(2,1)S(1)}, u32[]{:S(2)}, u32[]{:S(2)}) collective-permute-start(bf16[4,8,72,128]{3,2,1,0:T(8,128)(2,1)S(1)} %collective-permute-done.10.refs_4_), channel_id=1, source_target_pairs={{0,1},{1,0},{2,3},{3,2},{4,5},{5,4},{6,7},{7,6},{8,9},{9,8},{10,11... | collective-permute-start | bytes 1769480 | tf_op jit(solution)/shard_map/ppermute | solution.py:191
  56.0 8.4 %collective-permute-start.18 = (bf16[2,8,72,128]{3,2,1,0:T(8,128)(2,1)}, bf16[2,8,72,128]{3,2,1,0:T(8,128)(2,1)}, u32[]{:S(2)}, u32[]{:S(2)}) collective-permute-start(bf16[2,8,72,128]{3,2,1,0:T(8,128)(2,1)} %collective-permute-done.13.refs_7_), channel_id=1, source_target_pairs={{0,1},{1,0},{2,3},{3,2},{4,5},{5,4},{6,7},{7,6},{8,9},{9,8},{10,11... | collective-permute-start | bytes 884744 | tf_op jit(solution)/shard_map/ppermute | solution.py:191
  60.0 5.5 %collective-permute-start.17 = (bf16[2,8,72,128]{3,2,1,0:T(8,128)(2,1)}, bf16[2,8,72,128]{3,2,1,0:T(8,128)(2,1)}, u32[]{:S(2)}, u32[]{:S(2)}) collective-permute-start(bf16[2,8,72,128]{3,2,1,0:T(8,128)(2,1)} %collective-permute-done.12.refs_6_), channel_id=1, source_target_pairs={{0,1},{1,0},{2,3},{3,2},{4,5},{5,4},{6,7},{7,6},{8,9},{9,8},{10,11... | collective-permute-start | bytes 884744 | tf_op jit(solution)/shard_map/ppermute | solution.py:191
  85.5 2.3 %collective-permute-start.21 = (bf16[4,8,72,128]{3,2,1,0:T(8,128)(2,1)}, bf16[4,8,72,128]{3,2,1,0:T(8,128)(2,1)S(1)}, u32[]{:S(2)}, u32[]{:S(2)}) collective-permute-start(bf16[4,8,72,128]{3,2,1,0:T(8,128)(2,1)} %get-tuple-element.11), channel_id=1, source_target_pairs={{0,1},{1,0},{2,3},{3,2},{4,5},{5,4},{6,7},{7,6},{8,9},{9,8},{10,11... | collective-permute-start | bytes 1769480 | tf_op jit(solution)/shard_map/ppermute | solution.py:191
  85.9 5.8 %collective-permute-start.20 = (bf16[4,8,72,128]{3,2,1,0:T(8,128)(2,1)}, bf16[4,8,72,128]{3,2,1,0:T(8,128)(2,1)S(1)}, u32[]{:S(2)}, u32[]{:S(2)}) collective-permute-start(bf16[4,8,72,128]{3,2,1,0:T(8,128)(2,1)} %get-tuple-element.10), channel_id=1, source_target_pairs={{0,1},{1,0},{2,3},{3,2},{4,5},{5,4},{6,7},{7,6},{8,9},{9,8},{10,11... | collective-permute-start | bytes 1769480 | tf_op jit(solution)/shard_map/ppermute | solution.py:191
  86.1 5.6 %collective-permute-start.25 = (bf16[4,8,72,128]{3,2,1,0:T(8,128)(2,1)}, bf16[4,8,72,128]{3,2,1,0:T(8,128)(2,1)S(1)}, u32[]{:S(2)}, u32[]{:S(2)}) collective-permute-start(bf16[4,8,72,128]{3,2,1,0:T(8,128)(2,1)} %get-tuple-element.12), channel_id=1, source_target_pairs={{0,1},{1,0},{2,3},{3,2},{4,5},{5,4},{6,7},{7,6},{8,9},{9,8},{10,11... | collective-permute-start | bytes 1769480 | tf_op jit(solution)/shard_map/ppermute | solution.py:191
  87.8 3.0 %copy-start.10 = (bf16[4,8,72,128]{3,2,1,0:T(8,128)(2,1)S(1)}, bf16[4,8,72,128]{3,2,1,0:T(8,128)(2,1)}, u32[]{:S(2)}) copy-start(bf16[4,8,72,128]{3,2,1,0:T(8,128)(2,1)} %get-tuple-element.9) | copy-start | bytes 1769476
  87.8 9.6 %copy-start.1 = (bf16[4,4,8,72,128]{4,3,2,1,0:T(8,128)(2,1)S(1)}, bf16[4,4,8,72,128]{4,3,2,1,0:T(8,128)(2,1)}, u32[]{:S(2)}) copy-start(bf16[4,4,8,72,128]{4,3,2,1,0:T(8,128)(2,1)} %get-tuple-element.8) | copy-start | bytes 7077892
  89.2 5.9 %collective-permute-start.27 = (bf16[2,8,72,128]{3,2,1,0:T(8,128)(2,1)S(1)}, bf16[2,8,72,128]{3,2,1,0:T(8,128)(2,1)S(1)}, u32[]{:S(2)}, u32[]{:S(2)}) collective-permute-start(bf16[2,8,72,128]{3,2,1,0:T(8,128)(2,1)S(1)} %get-tuple-element.24), channel_id=1, source_target_pairs={{0,24},{1,7},{2,26},{3,1},{4,28},{5,3},{6,30},{7,5},{8,0},{9,15},{... | collective-permute-start | bytes 884744 | tf_op jit(solution)/shard_map/ppermute | solution.py:191
  90.3 7.1 %collective-permute-start.22 = (bf16[2,8,72,128]{3,2,1,0:T(8,128)(2,1)S(1)}, bf16[2,8,72,128]{3,2,1,0:T(8,128)(2,1)S(1)}, u32[]{:S(2)}, u32[]{:S(2)}) collective-permute-start(bf16[2,8,72,128]{3,2,1,0:T(8,128)(2,1)S(1)} %get-tuple-element.25), channel_id=1, source_target_pairs={{0,8},{1,3},{2,10},{3,5},{4,12},{5,7},{6,14},{7,1},{8,16},{9,11},{... | collective-permute-start | bytes 884744 | tf_op jit(solution)/shard_map/ppermute | solution.py:191
  90.8 10.0 %collective-permute-start.19 = (bf16[4,8,72,128]{3,2,1,0:T(8,128)(2,1)S(1)}, bf16[4,8,72,128]{3,2,1,0:T(8,128)(2,1)S(1)}, u32[]{:S(2)}, u32[]{:S(2)}) collective-permute-start(bf16[4,8,72,128]{3,2,1,0:T(8,128)(2,1)S(1)} %copy-done.10), channel_id=1, source_target_pairs={{0,1},{1,0},{2,3},{3,2},{4,5},{5,4},{6,7},{7,6},{8,9},{9,8},{10,11... | collective-permute-start | bytes 1769480 | tf_op jit(solution)/shard_map/ppermute | solution.py:191
  97.8 5.9 %collective-permute-start.26 = (bf16[2,8,72,128]{3,2,1,0:T(8,128)(2,1)S(1)}, bf16[2,8,72,128]{3,2,1,0:T(8,128)(2,1)S(1)}, u32[]{:S(2)}, u32[]{:S(2)}) collective-permute-start(bf16[2,8,72,128]{3,2,1,0:T(8,128)(2,1)S(1)} %get-tuple-element.15), channel_id=1, source_target_pairs={{0,24},{1,7},{2,26},{3,1},{4,28},{5,3},{6,30},{7,5},{8,0},{9,15},{... | collective-permute-start | bytes 884744 | tf_op jit(solution)/shard_map/ppermute | solution.py:191
  97.9 9.0 %collective-permute-start.28 = (bf16[2,8,72,128]{3,2,1,0:T(8,128)(2,1)S(1)}, bf16[2,8,72,128]{3,2,1,0:T(8,128)(2,1)S(1)}, u32[]{:S(2)}, u32[]{:S(2)}) collective-permute-start(bf16[2,8,72,128]{3,2,1,0:T(8,128)(2,1)S(1)} %get-tuple-element.16), channel_id=1, source_target_pairs={{0,24},{1,7},{2,26},{3,1},{4,28},{5,3},{6,30},{7,5},{8,0},{9,15},{... | collective-permute-start | bytes 884744 | tf_op jit(solution)/shard_map/ppermute | solution.py:191
  98.0 8.9 %collective-permute-start.24 = (bf16[2,8,72,128]{3,2,1,0:T(8,128)(2,1)S(1)}, bf16[2,8,72,128]{3,2,1,0:T(8,128)(2,1)S(1)}, u32[]{:S(2)}, u32[]{:S(2)}) collective-permute-start(bf16[2,8,72,128]{3,2,1,0:T(8,128)(2,1)S(1)} %get-tuple-element.19), channel_id=1, source_target_pairs={{0,8},{1,3},{2,10},{3,5},{4,12},{5,7},{6,14},{7,1},{8,16},{9,11},{... | collective-permute-start | bytes 884744 | tf_op jit(solution)/shard_map/ppermute | solution.py:191
  99.4 8.9 %collective-permute-start.23 = (bf16[2,8,72,128]{3,2,1,0:T(8,128)(2,1)S(1)}, bf16[2,8,72,128]{3,2,1,0:T(8,128)(2,1)S(1)}, u32[]{:S(2)}, u32[]{:S(2)}) collective-permute-start(bf16[2,8,72,128]{3,2,1,0:T(8,128)(2,1)S(1)} %get-tuple-element.20), channel_id=1, source_target_pairs={{0,8},{1,3},{2,10},{3,5},{4,12},{5,7},{6,14},{7,1},{8,16},{9,11},{... | collective-permute-start | bytes 884744 | tf_op jit(solution)/shard_map/ppermute | solution.py:191
  108.6 22.9 %copy-start.7 = (f32[1,72,128]{2,1,0:T(8,128)S(1)}, f32[1,72,128]{2,1,0:T(8,128)}, u32[]{:S(2)}) copy-start(f32[1,72,128]{2,1,0:T(8,128)} %param.8) | copy-start | bytes 110596
  108.6 22.9 %copy-start.9 = (f32[1,72,128]{2,1,0:T(8,128)S(1)}, f32[1,72,128]{2,1,0:T(8,128)}, u32[]{:S(2)}) copy-start(f32[1,72,128]{2,1,0:T(8,128)} %param.9) | copy-start | bytes 110596
  108.7 5.3 %collective-permute-start.29 = (bf16[8,72,128]{2,1,0:T(8,128)(2,1)S(1)}, bf16[8,72,128]{2,1,0:T(8,128)(2,1)S(1)}, u32[]{:S(2)}, u32[]{:S(2)}) collective-permute-start(bf16[8,72,128]{2,1,0:T(8,128)(2,1)S(1)} %get-tuple-element.21), channel_id=1, source_target_pairs={{0,2},{1,9},{2,4},{3,11},{4,6},{5,13},{6,0},{7,15},{8,10},{9,17},{... | collective-permute-start | bytes 442376 | tf_op jit(solution)/shard_map/ppermute | solution.py:191
  108.8 6.3 %collective-permute-start.31 = (bf16[8,72,128]{2,1,0:T(8,128)(2,1)S(1)}, bf16[8,72,128]{2,1,0:T(8,128)(2,1)S(1)}, u32[]{:S(2)}, u32[]{:S(2)}) collective-permute-start(bf16[8,72,128]{2,1,0:T(8,128)(2,1)S(1)} %get-tuple-element.22), channel_id=1, source_target_pairs={{0,6},{1,25},{2,0},{3,27},{4,2},{5,29},{6,4},{7,31},{8,14},{9,1},{... | collective-permute-start | bytes 442376 | tf_op jit(solution)/shard_map/ppermute | solution.py:191
  111.4 5.5 %collective-permute-start.30 = (bf16[8,72,128]{2,1,0:T(8,128)(2,1)S(1)}, bf16[8,72,128]{2,1,0:T(8,128)(2,1)S(1)}, u32[]{:S(2)}, u32[]{:S(2)}) collective-permute-start(bf16[8,72,128]{2,1,0:T(8,128)(2,1)S(1)} %get-tuple-element.23), channel_id=1, source_target_pairs={{0,4},{1,17},{2,6},{3,19},{4,0},{5,21},{6,2},{7,23},{8,12},{9,25},... | collective-permute-start | bytes 442376 | tf_op jit(solution)/shard_map/ppermute | solution.py:191
  117.0 8.1 %collective-permute-start.32 = (bf16[72,128]{1,0:T(8,128)(2,1)S(1)}, bf16[72,128]{1,0:T(8,128)(2,1)S(1)}, u32[]{:S(2)}, u32[]{:S(2)}) collective-permute-start(bf16[72,128]{1,0:T(8,128)(2,1)S(1)} %get-tuple-element.28), channel_id=1, source_target_pairs={{0,32},{32,64},{64,96},{96,128},{128,160},{160,192},{192,224},{224... | collective-permute-start | bytes 55304 | tf_op jit(solution)/shard_map/ppermute | solution.py:181
  117.1 8.1 %collective-permute-start.38 = (bf16[72,128]{1,0:T(8,128)(2,1)S(1)}, bf16[72,128]{1,0:T(8,128)(2,1)S(1)}, u32[]{:S(2)}, u32[]{:S(2)}) collective-permute-start(bf16[72,128]{1,0:T(8,128)(2,1)S(1)} %get-tuple-element.29), channel_id=1, source_target_pairs={{0,224},{32,0},{64,32},{96,64},{128,96},{160,128},{192,160},{224,1... | collective-permute-start | bytes 55304 | tf_op jit(solution)/shard_map/ppermute | solution.py:181
  119.8 9.0 %collective-permute-start.37 = (bf16[72,128]{1,0:T(8,128)(2,1)S(1)}, bf16[72,128]{1,0:T(8,128)(2,1)S(1)}, u32[]{:S(2)}, u32[]{:S(2)}) collective-permute-start(bf16[72,128]{1,0:T(8,128)(2,1)S(1)} %get-tuple-element.30), channel_id=1, source_target_pairs={{0,192},{32,224},{64,0},{96,32},{128,64},{160,96},{192,128},{224,1... | collective-permute-start | bytes 55304 | tf_op jit(solution)/shard_map/ppermute | solution.py:181
  120.3 8.5 %collective-permute-start.36 = (bf16[72,128]{1,0:T(8,128)(2,1)S(1)}, bf16[72,128]{1,0:T(8,128)(2,1)S(1)}, u32[]{:S(2)}, u32[]{:S(2)}) collective-permute-start(bf16[72,128]{1,0:T(8,128)(2,1)S(1)} %get-tuple-element.31), channel_id=1, source_target_pairs={{0,160},{32,192},{64,224},{96,0},{128,32},{160,64},{192,96},{224,1... | collective-permute-start | bytes 55304 | tf_op jit(solution)/shard_map/ppermute | solution.py:181
  121.9 6.9 %collective-permute-start.35 = (bf16[72,128]{1,0:T(8,128)(2,1)S(1)}, bf16[72,128]{1,0:T(8,128)(2,1)S(1)}, u32[]{:S(2)}, u32[]{:S(2)}) collective-permute-start(bf16[72,128]{1,0:T(8,128)(2,1)S(1)} %get-tuple-element.32), channel_id=1, source_target_pairs={{0,128},{32,160},{64,192},{96,224},{128,0},{160,32},{192,64},{224,... | collective-permute-start | bytes 55304 | tf_op jit(solution)/shard_map/ppermute | solution.py:181
  125.2 5.6 %collective-permute-start.34 = (bf16[72,128]{1,0:T(8,128)(2,1)S(1)}, bf16[72,128]{1,0:T(8,128)(2,1)S(1)}, u32[]{:S(2)}, u32[]{:S(2)}) collective-permute-start(bf16[72,128]{1,0:T(8,128)(2,1)S(1)} %get-tuple-element.33), channel_id=1, source_target_pairs={{0,96},{32,128},{64,160},{96,192},{128,224},{160,0},{192,32},{224,... | collective-permute-start | bytes 55304 | tf_op jit(solution)/shard_map/ppermute | solution.py:181
  125.2 6.3 %collective-permute-start.33 = (bf16[72,128]{1,0:T(8,128)(2,1)S(1)}, bf16[72,128]{1,0:T(8,128)(2,1)S(1)}, u32[]{:S(2)}, u32[]{:S(2)}) collective-permute-start(bf16[72,128]{1,0:T(8,128)(2,1)S(1)} %get-tuple-element.34), channel_id=1, source_target_pairs={{0,64},{32,96},{64,128},{96,160},{128,192},{160,224},{192,0},{224,... | collective-permute-start | bytes 55304 | tf_op jit(solution)/shard_map/ppermute | solution.py:181
  131.5 26.1 %copy-start.8 = (f32[72,128]{1,0:T(8,128)}, f32[72,128]{1,0:T(8,128)S(1)}, u32[]{:S(2)}) copy-start(f32[72,128]{1,0:T(8,128)S(1)} %get-tuple-element.14) | copy-start | bytes 110596
  132.4 24.4 %all-to-all-start = ((bf16[32,72,128]{2,1,0:T(8,128)(2,1)}), bf16[32,72,128]{2,1,0:T(8,128)(2,1)S(1)}, u32[]{:S(2)}, u32[]{:S(2)}) async-start(bf16[32,72,128]{2,1,0:T(8,128)(2,1)} %broadcast_in_dim.14), calls=%async_computation | async-start | bytes 1179648 | tf_op jit(solution)/shard_map/all_to_all | solution.py:267
  (3 other events, 2.8 us)

commit v3 on v2

v3 whole, which is shorter than its diff:
```python
import jax
import jax.numpy as jnp
from jax import lax
from jax.experimental import pallas as pl
from jax.experimental.pallas import tpu as pltpu
from jax.sharding import PartitionSpec as P

STEP_SIZE = 0.1
INERTIA = 0.9
ROUND = jnp.bfloat16
VMEM = 24


ORDERS = ((0, 1, 3, 2), (0, 3, 1, 2))
FIRST = ORDERS[0]


def reversed_bits(r):
    return ((r & 1) << 2) | (r & 2) | (r >> 2)


def image_step(sides, sections, side, share, place, stream, cotangent, *refs):
    gathered, refs = refs[:10], refs[10:]
    outs, refs = refs[:8], refs[8:]
    x_in, d_in, w_all, g_all, saved_p, slopes, fwd_pad, bwd_pad, x_sem, w_sem, g_sem = refs
    z, x, y, core = place[0], place[1], place[2], place[3]
    channels = stream.shape[-1]
    pixels = side * side
    rows = w_all.shape[1]
    half = rows // 2
    slots = sections // 2
    x_copy = pltpu.make_async_copy(stream, x_in, x_sem.at[0])
    d_copy = pltpu.make_async_copy(cotangent, d_in, x_sem.at[1])

    def block(role, part, i, j):
        first, second = FIRST[i], ORDERS[part][j]
        px = x ^ jnp.where(role == 0, second, first)
        py = y ^ jnp.where(role == 0, first, second)
        start = pl.multiple_of(((px * sides + py) * 2 + role) * share, 8)
        return pl.ds(part * slots, slots), pl.ds(start, share)

    copies = []
    for which in range(2):
        role = core if which == 0 else 1 - core
        near, one_a, one_b, two_a, two_b = gathered[5 * which : 5 * which + 5]
        for part, (one, two) in enumerate(((one_a, two_a), (one_b, two_b))):
            for i in range(sides):
                for j, source in enumerate((near.at[part, i], one.at[i], two.at[0, i], two.at[1, i])):
                    where, lines = block(role, part, i, j)
                    target = w_all.at[where, lines, :]
                    copies.append(pltpu.make_async_copy(source, target, w_sem.at[len(copies)]))
    x_copy.start()
    for copy in copies:
        copy.start()
    d_copy.start()
    edge = jnp.zeros((side, 3 * channels), ROUND)
    for pad in (fwd_pad, bwd_pad):
        for k in range(2):
            pad[k, 0:side, :] = edge
            pad[k, side + pixels : 2 * side + pixels, :] = edge

    column = lax.broadcasted_iota(jnp.int32, (pixels, channels), 0) & (side - 1)
    not_first = column > 0
    not_last = column < side - 1

    def before(v):
        return jnp.where(not_first, pltpu.roll(v, 1, 0), 0.0).astype(ROUND)

    def after(v):
        return jnp.where(not_last, pltpu.roll(v, pixels - 1, 0), 0.0).astype(ROUND)

    def band(pad, k, low, mid, high):
        body = pl.ds(side, pixels)
        pad[k, body, 0:channels] = low
        pad[k, body, channels : 2 * channels] = mid
        pad[k, body, 2 * channels : 3 * channels] = high

    def conv(pad, k, w):
        taps = jnp.concatenate([pad[k, a * side : a * side + pixels, :] for a in range(3)], axis=1)
        return jnp.dot(taps, w, preferred_element_type=jnp.float32)

    def activate(v, at):
        logistic = 1.0 / (1.0 + jnp.exp(-v))
        p = v * logistic
        slopes[at] = logistic + p * (1.0 - logistic)
        saved_p[at] = p.T.astype(ROUND)
        return p

    def forward(s, pair):
        x1, x2 = pair
        w = w_all.at[reversed_bits(z ^ s)]
        p = activate(x2, 2 * s)
        band(fwd_pad, 0, before(p), p.astype(ROUND), after(p))
        y1 = x1 + conv(fwd_pad, 0, w[0:half, :])
        p = activate(y1, 2 * s + 1)
        band(fwd_pad, 1, before(p), p.astype(ROUND), after(p))
        y2 = x2 + conv(fwd_pad, 1, w[half:rows, :])
        return y1, y2

    x_copy.wait()
    for copy in copies:
        copy.wait()
    lax.fori_loop(0, sections, forward, (x_in[0], x_in[1]))

    def spread(k, e, w, g, base, at):
        band(bwd_pad, k, after(e), e.astype(ROUND), before(e))
        total = None
        pieces = []
        for a in range(3):
            lines = bwd_pad[k, (2 - a) * side : (2 - a) * side + pixels, :]
            pieces.append(lines)
            for b in range(3):
                first = base + (3 * a + b) * channels
                part = lax.dot_general(
                    lines[:, b * channels : (b + 1) * channels], w[first : first + channels, :],
                    (((1,), (1,)), ((), ())), preferred_element_type=jnp.float32,
                )
                total = part if total is None else total + part
        wgrad = jnp.dot(
            saved_p[at], jnp.concatenate(pieces, axis=1), preferred_element_type=jnp.float32
        ).astype(ROUND)
        for tap in range(9):
            first = base + tap * channels
            g[first : first + channels, :] = wgrad[:, tap * channels : (tap + 1) * channels]
        return total * slopes[at]

    def backward(step, pair):
        d1, d2 = pair
        s = sections - 1 - step
        w = w_all.at[reversed_bits(z ^ s)]
        g = g_all.at[reversed_bits(z ^ s)]
        d1 = d1 + spread(0, d2, w, g, half, 2 * s + 1)
        d2 = d2 + spread(1, d1, w, g, 0, 2 * s)
        return d1, d2

    d_copy.wait()
    lax.fori_loop(0, sections, backward, (d_in[0], d_in[1]))
    copies = []
    for first_j in (2, 0):
        for part in range(2):
            passed, kept = outs[2 * part + 1 - first_j // 2], outs[4 + 2 * part + 1 - first_j // 2]
            for i in range(sides):
                for j in range(2):
                    for role, target in ((1 - core, passed.at[j, i]), (core, kept.at[j, i])):
                        where, lines = block(role, part, i, first_j + j)
                        source = g_all.at[where, lines, :]
                        copies.append(pltpu.make_async_copy(source, target, g_sem.at[len(copies)]))
    for copy in copies:
        copy.start()
    for copy in copies:
        copy.wait()


def image_grads(stream, cotangent, gathered, place, sides):
    pixels, channels = stream.shape[1:]
    side = int(round(pixels**0.5))
    share = gathered[0].shape[3]
    sections = 2 * gathered[0].shape[2]
    rows = share * 2 * sides * sides
    far = pl.BlockSpec(memory_space=pl.ANY)
    kernel = lambda *refs: image_step(sides, sections, side, share, *refs)
    pair = (2, sides, sections // 2, share, channels)
    return pl.pallas_call(
        kernel,
        out_shape=[jax.ShapeDtypeStruct(pair, ROUND)] * 8,
        grid_spec=pltpu.PrefetchScalarGridSpec(
            num_scalar_prefetch=1,
            grid=(1,),
            in_specs=[far] * 12,
            out_specs=[far] * 8,
            scratch_shapes=[
                pltpu.VMEM((2, pixels, channels), jnp.float32),
                pltpu.VMEM((2, pixels, channels), jnp.float32),
                pltpu.VMEM((sections, rows, channels), ROUND),
                pltpu.VMEM((sections, rows, channels), ROUND),
                pltpu.VMEM((2 * sections, channels, pixels), ROUND),
                pltpu.VMEM((2 * sections, pixels, channels), jnp.float32),
                pltpu.VMEM((2, pixels + 2 * side, 3 * channels), ROUND),
                pltpu.VMEM((2, pixels + 2 * side, 3 * channels), ROUND),
                pltpu.SemaphoreType.DMA((2,)),
                pltpu.SemaphoreType.DMA((4 * sides * sides,)),
                pltpu.SemaphoreType.DMA((4 * sides * sides,)),
            ],
        ),
        compiler_params=pltpu.CompilerParams(vmem_limit_bytes=VMEM << 20),
        name="image_step",
    )(place, stream, cotangent, *gathered)


def along_z(value, mask):
    n = lax.axis_size("section")
    return lax.ppermute(value, "section", [(i, i ^ mask) for i in range(n)])


def in_plane(sides, value, to):
    pairs = []
    for x in range(sides):
        for y in range(sides):
            for core in range(2):
                px, py, pc = to(x, y, core)
                pairs.append(((x * sides + y) * 2 + core, (px * sides + py) * 2 + pc))
    return lax.ppermute(value, "dp", pairs)


def along_first(sides, value, mask):
    return in_plane(sides, value, lambda x, y, c: (x, y ^ mask, c) if c == 0 else (x ^ mask, y, c))


def along_second(sides, value, mask):
    return in_plane(sides, value, lambda x, y, c: (x ^ mask, y, c) if c == 0 else (x, y ^ mask, c))


def swapped(sides, value):
    return in_plane(sides, value, lambda x, y, c: (x, y, 1 - c))


def gather_weights(mine, sides):
    line = mine[None]
    for mask in (4, 2):
        line = jnp.concatenate([line, along_z(line, mask)])
    line = jnp.stack([line, along_z(line, 1)])[:, None]
    for mask in (1, 3):
        line = jnp.concatenate([line, along_first(sides, line, mask)], axis=1)
    zero_a, zero_b = line[0], line[1]
    one_a = along_second(sides, zero_a, 1)
    one_b = along_second(sides, zero_b, 3)
    two_a = along_second(sides, jnp.stack([zero_a, one_a]), 3)
    two_b = along_second(sides, jnp.stack([zero_b, one_b]), 1)
    own = [line, one_a, one_b, two_a, two_b]
    return own + [swapped(sides, block) for block in own]


def wide(value):
    return value.astype(jnp.float32)


def scatter_grads(blocks, sides):
    passed, kept = blocks[:4], blocks[4:]
    late = [None, None]
    for part in range(2):
        late[part] = swapped(sides, passed[2 * part])
    soon = [None, None]
    for part in range(2):
        soon[part] = swapped(sides, passed[2 * part + 1])
    came = []
    for part in range(2):
        out = (wide(kept[2 * part]) + wide(late[part])).astype(ROUND)
        came.append(along_second(sides, out, (3, 1)[part]))
    parts = []
    for part in range(2):
        near = kept[2 * part + 1]
        out = (wide(near[1]) + wide(soon[part][1]) + wide(came[part][1])).astype(ROUND)
        last = along_second(sides, out, (1, 3)[part])
        parts.append(wide(near[0]) + wide(soon[part][0]) + wide(came[part][0]) + wide(last))
    line = jnp.stack(parts).astype(ROUND)
    got = along_first(sides, line[:, 2:], 3)
    line = wide(line[:, :2]) + wide(got)
    got = along_first(sides, line[:, 1].astype(ROUND), 1)
    line = line[:, 0] + wide(got)
    got = along_z(line[1].astype(ROUND), 1)
    line = line[0] + wide(got)
    for mask in (2, 4):
        middle = line.shape[0] // 2
        got = along_z(line[middle:].astype(ROUND), mask)
        line = line[:middle] + wide(got)
    return line[0]


def on_device(stream, cotangent, weights, master, momentum):
    dp = lax.axis_size("dp")
    sides = int(round((dp // 2) ** 0.5))
    images = stream.shape[1] * dp
    share = weights.shape[1] // dp
    channels = weights.shape[2]
    z, at = lax.axis_index("section"), lax.axis_index("dp")
    place = jnp.stack([z, at // (2 * sides), at // 2 % sides, at % 2]).astype(jnp.int32)
    mine = lax.dynamic_slice_in_dim(weights[0], at * share, share, 0)
    gathered = gather_weights(mine, sides)
    pair = (2, stream.shape[2] * stream.shape[3], channels)
    first, last = (lax.dynamic_slice_in_dim(v, z, 1, 1).reshape(pair) for v in (stream, cotangent))
    blocks = image_grads(first, last, gathered, place, sides)
    gradient = scatter_grads(blocks, sides) / images
    new_momentum = INERTIA * momentum[0] + gradient
    new_master = master[0] - STEP_SIZE * new_momentum
    copies = jnp.broadcast_to(new_master.astype(ROUND)[None], (dp, share, channels))
    new_weights = lax.all_to_all(copies, "dp", 0, 0, tiled=True).reshape(dp * share, channels)
    return (new_master[None], new_momentum[None], new_weights[None])


def solution(mesh):
    placed = (
        P(None, "dp", None, None, None),
        P(None, "dp", None, None, None),
        P("section", None, None),
        P("section", "dp", None),
        P("section", "dp", None),
    )
    return jax.shard_map(
        on_device,
        mesh=mesh,
        in_specs=placed,
        out_specs=(P("section", "dp", None), P("section", "dp", None), P("section", None, None)),
        check_vma=False,
    )
```

time: 158 us -> 154 us (0.975)
  starting transfers between devices: 78.5 us -> 51.6 us
  blocking collectives: 0 us -> 24.5 us
    all_to_all x0 -> x1, blocking collectives: none -> 24.5 us  [on_device(): lax.all_to_all(copies, 'dp', 0, 0, tiled=True).reshape(dp * share, channels)]
    ppermute x25 -> x21, waiting for transfers between devices: 27.3 us -> 40 us  [in_plane(): return lax.ppermute(value, 'dp', pairs)]
    all_to_all x1 -> x0, starting transfers between devices: 12.1 us -> none  [on_device(): lax.all_to_all(copies, 'dp', 0, 0, tiled=True).reshape(dp * share, channels)]
    all_to_all x1 -> x0, waiting for transfers between devices: 11.7 us -> none  [on_device(): lax.all_to_all(copies, 'dp', 0, 0, tiled=True).reshape(dp * share, channels)]
    ppermute x25 -> x21, starting transfers between devices: 41.3 us -> 32.7 us  [in_plane(): return lax.ppermute(value, 'dp', pairs)]
    ppermute x14 -> x6, starting transfers between devices: 25.1 us -> 19 us  [along_z(): return lax.ppermute(value, 'section', [(i, i ^ mask) for i in range(n)])]
    convert_element_type x5 -> x4, other arithmetic: 2.19 us -> 0.55 us  [the longest x2 0.31 us: scatter_grads(): out = (wide(kept[2 * part]) + wide(late[part])).astype(ROUND)]
    ppermute x14 -> x6, waiting for transfers between devices: 13.1 us -> 11.5 us  [along_z(): return lax.ppermute(value, 'section', [(i, i ^ mask) for i in range(n)])]
  transfers between devices with their start and end apart: 40 -> 27, of which waited for: 19 -> 18; matrix products, arithmetic and copies ran while one was open for 2% -> 1% of each run, Pallas kernels for 0% -> 0%
where the time goes in v3:
time: 154 us
  starting transfers between devices  51.6 us (34%)
  waiting for transfers between devices  51.6 us (34%)
  blocking collectives  24.5 us (16%)
  Pallas kernels  19.9 us (13%)
  local copies, waits for them, and re-layouts  3.23 us (2%)
  other arithmetic  1.97 us (1%)
    ppermute x21, waiting for transfers between devices, in_plane(): return lax.ppermute(value, 'dp', pairs)  40 us
    ppermute x21, starting transfers between devices, in_plane(): return lax.ppermute(value, 'dp', pairs)  32.7 us
    all_to_all x1, blocking collectives, on_device(): lax.all_to_all(copies, 'dp', 0, 0, tiled=True).reshape(dp * share, channels)  24.5 us
    pallas_call x1, Pallas kernels, image_grads(): pl.pallas_call(kernel, out_shape=[jax.ShapeDtypeStruct(pair, ROUND)] * 8,...  19.9 us
    ppermute x6, starting transfers between devices, along_z(): return lax.ppermute(value, 'section', [(i, i ^ mask) for i in range(n)])  19 us
    ppermute x6, waiting for transfers between devices, along_z(): return lax.ppermute(value, 'section', [(i, i ^ mask) for i in range(n)])  11.5 us
  transfers between devices with their start and end apart: 27, of which 18 were waited for; matrix products, arithmetic and copies ran while one was open for 1% of the time, Pallas kernels for 0%

profile of v3, /device:TPU:1, one launch (start us, length us, event | category | flops | bytes accessed | tf_op | source)
XLA Modules:
  0.0 153.6 jit_solution(12126431860966793305)
XLA Ops:
  0.7 1.0 copy-done
  1.7 7.7 %collective-permute-start = (bf16[1,72,128]{2,1,0:T(8,128)(2,1)S(1)}, bf16[1,72,128]{2,1,0:T(8,128)(2,1)S(1)}, u32[]{:S(2)}, u32[]{:S(2)}) collective-permute-start(bf16[1,72,128]{2,1,0:T(8,128)(2,1)S(1)} %constant_dynamic-slice_fusion), channel_id=1, source_target_pairs={{0,128},{32,160},{64,192},{96,224},{128,0},{160,32},{192,64},{224,... | collective-permute-start | bytes 55304 | tf_op jit(solution)/shard_map/ppermute | solution.py:192
  9.4 1.1 collective-permute-done
  10.6 1.5 collective-permute-start.1
  12.1 2.3 %collective-permute-done.1 = bf16[2,72,128]{2,1,0:T(8,128)(2,1)S(1)} collective-permute-done((bf16[2,72,128]{2,1,0:T(8,128)(2,1)S(1)}, bf16[2,72,128]{2,1,0:T(8,128)(2,1)S(1)}, u32[]{:S(2)}, u32[]{:S(2)}) %collective-permute-start.1) | collective-permute-done | bytes 36896 | tf_op jit(solution)/shard_map/ppermute | solution.py:192
  14.3 0.8 collective-permute-start.2
  15.2 2.8 %collective-permute-done.2 = bf16[4,72,128]{2,1,0:T(8,128)(2,1)S(1)} collective-permute-done((bf16[4,72,128]{2,1,0:T(8,128)(2,1)S(1)}, bf16[4,72,128]{2,1,0:T(8,128)(2,1)S(1)}, u32[]{:S(2)}, u32[]{:S(2)}) %collective-permute-start.2) | collective-permute-done | bytes 73760 | tf_op jit(solution)/shard_map/ppermute | solution.py:192
  18.0 1.0 collective-permute-start.3
  18.9 3.1 %collective-permute-done.3 = bf16[2,1,4,72,128]{4,3,2,1,0:T(8,128)(2,1)S(1)} collective-permute-done((bf16[2,1,4,72,128]{4,3,2,1,0:T(8,128)(2,1)S(1)}, bf16[2,1,4,72,128]{4,3,2,1,0:T(8,128)(2,1)S(1)}, u32[]{:S(2)}, u32[]{:S(2)}) %collective-permute-start.3) | collective-permute-done | bytes 147488 | tf_op jit(solution)/shard_map/ppermute | solution.py:202
  22.1 2.2 %collective-permute-start.4 = (bf16[2,2,4,72,128]{4,3,2,1,0:T(8,128)(2,1)S(1)}, bf16[2,2,4,72,128]{4,3,2,1,0:T(8,128)(2,1)S(1)}, u32[]{:S(2)}, u32[]{:S(2)}) collective-permute-start(bf16[2,2,4,72,128]{4,3,2,1,0:T(8,128)(2,1)S(1)} %pad_maximum_fusion.4), channel_id=1, source_target_pairs={{0,6},{1,25},{2,4},{3,27},{4,2},{5,29},{6,0},{7,31},{8,14},{9,17},... | collective-permute-start | bytes 884744 | tf_op jit(solution)/shard_map/ppermute | solution.py:202
  24.3 4.6 %collective-permute-done.4 = bf16[2,2,4,72,128]{4,3,2,1,0:T(8,128)(2,1)S(1)} collective-permute-done((bf16[2,2,4,72,128]{4,3,2,1,0:T(8,128)(2,1)S(1)}, bf16[2,2,4,72,128]{4,3,2,1,0:T(8,128)(2,1)S(1)}, u32[]{:S(2)}, u32[]{:S(2)}) %collective-permute-start.4) | collective-permute-done | bytes 294944 | tf_op jit(solution)/shard_map/ppermute | solution.py:202
  29.2 2.5 %collective-permute-start.6 = (bf16[4,4,72,128]{3,2,1,0:T(8,128)(2,1)S(1)}, bf16[4,4,72,128]{3,2,1,0:T(8,128)(2,1)S(1)}, u32[]{:S(2)}, u32[]{:S(2)}) collective-permute-start(bf16[4,4,72,128]{3,2,1,0:T(8,128)(2,1)S(1)} %get-tuple-element.24), channel_id=1, source_target_pairs={{0,24},{1,7},{2,26},{3,5},{4,28},{5,3},{6,30},{7,1},{8,16},{9,15},... | collective-permute-start | bytes 884744 | tf_op jit(solution)/shard_map/ppermute | solution.py:202
  31.7 6.4 %collective-permute-done.6.refs_5_ = bf16[4,4,72,128]{3,2,1,0:T(8,128)(2,1)S(1)} collective-permute-done((bf16[4,4,72,128]{3,2,1,0:T(8,128)(2,1)S(1)}, bf16[4,4,72,128]{3,2,1,0:T(8,128)(2,1)S(1)}, u32[]{:S(2)}, u32[]{:S(2)}) %collective-permute-start.6) | collective-permute-done | bytes 294944 | tf_op jit(solution)/shard_map/ppermute | solution.py:202
  38.4 1.9 %collective-permute-start.7 = (bf16[2,4,4,72,128]{4,3,2,1,0:T(8,128)(2,1)S(1)}, bf16[2,4,4,72,128]{4,3,2,1,0:T(8,128)(2,1)S(1)}, u32[]{:S(2)}, u32[]{:S(2)}) collective-permute-start(bf16[2,4,4,72,128]{4,3,2,1,0:T(8,128)(2,1)S(1)} %pad_maximum_fusion.1), channel_id=1, source_target_pairs={{0,24},{1,7},{2,26},{3,5},{4,28},{5,3},{6,30},{7,1},{8,16},{9,15},... | collective-permute-start | bytes 1769480 | tf_op jit(solution)/shard_map/ppermute | solution.py:202
  40.3 8.1 %collective-permute-start.9 = (bf16[2,4,4,72,128]{4,3,2,1,0:T(8,128)(2,1)S(1)}, bf16[2,4,4,72,128]{4,3,2,1,0:T(8,128)(2,1)S(1)}, u32[]{:S(2)}, u32[]{:S(2)}) collective-permute-start(bf16[2,4,4,72,128]{4,3,2,1,0:T(8,128)(2,1)S(1)} %pad_maximum_fusion.refs_3_), channel_id=1, source_target_pairs={{0,1},{1,0},{2,3},{3,2},{4,5},{5,4},{6,7},{7,6},{8,9},{9,8},{10,11... | collective-permute-start | bytes 1769480 | tf_op jit(solution)/shard_map/ppermute | solution.py:202
  48.4 7.6 %collective-permute-start.13 = (bf16[2,4,4,72,128]{4,3,2,1,0:T(8,128)(2,1)S(1)}, bf16[2,4,4,72,128]{4,3,2,1,0:T(8,128)(2,1)}, u32[]{:S(2)}, u32[]{:S(2)}) collective-permute-start(bf16[2,4,4,72,128]{4,3,2,1,0:T(8,128)(2,1)S(1)} %collective-permute-done.8.refs_7_), channel_id=1, source_target_pairs={{0,1},{1,0},{2,3},{3,2},{4,5},{5,4},{6,7},{7,6},{8,9},{9,8},{10,11... | collective-permute-start | bytes 1769480 | tf_op jit(solution)/shard_map/ppermute | solution.py:202
  56.0 1.4 collective-permute-start.12
  57.4 0.5 collective-permute-start.11
  58.0 1.1 constant_dynamic-slice_fusion.1
  59.1 0.5 collective-permute-done.10.refs_9_
  59.6 0.4 collective-permute-done.11.refs_10_
  60.0 19.9 %image_step.1 = (bf16[2,4,4,72,128]{4,3,2,1,0:T(8,128)(2,1)S(1)}, bf16[2,4,4,72,128]{4,3,2,1,0:T(8,128)(2,1)S(1)}, bf16[2,4,4,72,128]{4,3,2,1,0:T(8,128)(2,1)S(1...) custom-call(s32[4]{0:T(128)S(1)} %pad_add_fusion.refs_0_, ...), custom_call_target="tpu_custom_call" | custom-call | tf_op jit(solution)/shard_map/image_step/pallas_call | solution.py:163
  79.9 0.5 collective-permute-start.15
  80.3 0.3 collective-permute-start.19
  80.6 0.2 collective-permute-start.14
  80.9 0.3 collective-permute-start.18
  81.1 0.8 collective-permute-done.15
  82.0 0.2 add_convert_fusion.1
  82.1 2.9 %collective-permute-start.16 = (bf16[2,4,4,72,128]{4,3,2,1,0:T(8,128)(2,1)S(1)}, bf16[2,4,4,72,128]{4,3,2,1,0:T(8,128)(2,1)S(1)}, u32[]{:S(2)}, u32[]{:S(2)}) collective-permute-start(bf16[2,4,4,72,128]{4,3,2,1,0:T(8,128)(2,1)S(1)} %add_convert_fusion.1), channel_id=1, source_target_pairs={{0,24},{1,7},{2,26},{3,5},{4,28},{5,3},{6,30},{7,1},{8,16},{9,15},... | collective-permute-start | bytes 1769480 | tf_op jit(solution)/shard_map/ppermute | solution.py:202
  85.3 7.3 %collective-permute-done.16 = bf16[2,4,4,72,128]{4,3,2,1,0:T(8,128)(2,1)S(1)} collective-permute-done((bf16[2,4,4,72,128]{4,3,2,1,0:T(8,128)(2,1)S(1)}, bf16[2,4,4,72,128]{4,3,2,1,0:T(8,128)(2,1)S(1)}, u32[]{:S(2)}, u32[]{:S(2)}) %collective-permute-start.16) | collective-permute-done | bytes 589856 | tf_op jit(solution)/shard_map/ppermute | solution.py:202
  92.8 1.5 collective-permute-done.20
  94.4 1.3 collective-permute-start.21
  95.7 2.9 %collective-permute-done.17 = bf16[4,4,72,128]{3,2,1,0:T(8,128)(2,1)S(1)} collective-permute-done((bf16[4,4,72,128]{3,2,1,0:T(8,128)(2,1)S(1)}, bf16[4,4,72,128]{3,2,1,0:T(8,128)(2,1)S(1)}, u32[]{:S(2)}, u32[]{:S(2)}) %collective-permute-start.17) | collective-permute-done | bytes 294944 | tf_op jit(solution)/shard_map/ppermute | solution.py:202
  98.7 0.2 fusion.4
  98.8 2.8 %collective-permute-done.21 = bf16[4,4,72,128]{3,2,1,0:T(8,128)(2,1)S(1)} collective-permute-done((bf16[4,4,72,128]{3,2,1,0:T(8,128)(2,1)S(1)}, bf16[4,4,72,128]{3,2,1,0:T(8,128)(2,1)S(1)}, u32[]{:S(2)}, u32[]{:S(2)}) %collective-permute-start.21) | collective-permute-done | bytes 294944 | tf_op jit(solution)/shard_map/ppermute | solution.py:202
  101.6 0.2 fusion.5
  101.8 1.6 %collective-permute-start.22 = (bf16[2,2,4,72,128]{4,3,2,1,0:T(8,128)(2,1)S(1)}, bf16[2,2,4,72,128]{4,3,2,1,0:T(8,128)(2,1)S(1)}, u32[]{:S(2)}, u32[]{:S(2)}) collective-permute-start(bf16[2,2,4,72,128]{4,3,2,1,0:T(8,128)(2,1)S(1)} %pad_maximum_fusion.3), channel_id=1, source_target_pairs={{0,6},{1,25},{2,4},{3,27},{4,2},{5,29},{6,0},{7,31},{8,14},{9,17},... | collective-permute-start | bytes 884744 | tf_op jit(solution)/shard_map/ppermute | solution.py:202
  103.4 5.6 %collective-permute-done.22 = bf16[2,2,4,72,128]{4,3,2,1,0:T(8,128)(2,1)S(1)} collective-permute-done((bf16[2,2,4,72,128]{4,3,2,1,0:T(8,128)(2,1)S(1)}, bf16[2,2,4,72,128]{4,3,2,1,0:T(8,128)(2,1)S(1)}, u32[]{:S(2)}, u32[]{:S(2)}) %collective-permute-start.22) | collective-permute-done | bytes 294944 | tf_op jit(solution)/shard_map/ppermute | solution.py:202
  109.2 4.0 %collective-permute-done.23 = bf16[2,4,72,128]{3,2,1,0:T(8,128)(2,1)S(1)} collective-permute-done((bf16[2,4,72,128]{3,2,1,0:T(8,128)(2,1)S(1)}, bf16[2,4,72,128]{3,2,1,0:T(8,128)(2,1)S(1)}, u32[]{:S(2)}, u32[]{:S(2)}) %collective-permute-start.23) | collective-permute-done | bytes 147488 | tf_op jit(solution)/shard_map/ppermute | solution.py:202
  113.2 0.8 collective-permute-start.24
  114.0 2.5 %collective-permute-done.24 = bf16[4,72,128]{2,1,0:T(8,128)(2,1)S(1)} collective-permute-done((bf16[4,72,128]{2,1,0:T(8,128)(2,1)S(1)}, bf16[4,72,128]{2,1,0:T(8,128)(2,1)S(1)}, u32[]{:S(2)}, u32[]{:S(2)}) %collective-permute-start.24) | collective-permute-done | bytes 73760 | tf_op jit(solution)/shard_map/ppermute | solution.py:192
  116.5 2.2 %collective-permute-start.25 = (bf16[2,72,128]{2,1,0:T(8,128)(2,1)S(1)}, bf16[2,72,128]{2,1,0:T(8,128)(2,1)S(1)}, u32[]{:S(2)}, u32[]{:S(2)}) collective-permute-start(bf16[2,72,128]{2,1,0:T(8,128)(2,1)S(1)} %slice.162), channel_id=1, source_target_pairs={{0,64},{32,96},{64,0},{96,32},{128,192},{160,224},{192,128},{224,1... | collective-permute-start | bytes 110600 | tf_op jit(solution)/shard_map/ppermute | solution.py:192
  118.7 1.7 %collective-permute-done.25 = bf16[2,72,128]{2,1,0:T(8,128)(2,1)S(1)} collective-permute-done((bf16[2,72,128]{2,1,0:T(8,128)(2,1)S(1)}, bf16[2,72,128]{2,1,0:T(8,128)(2,1)S(1)}, u32[]{:S(2)}, u32[]{:S(2)}) %collective-permute-start.25) | collective-permute-done | bytes 36896 | tf_op jit(solution)/shard_map/ppermute | solution.py:192
  120.5 5.9 %collective-permute-start.26 = (bf16[1,72,128]{2,1,0:T(8,128)(2,1)S(1)}, bf16[1,72,128]{2,1,0:T(8,128)(2,1)S(1)}, u32[]{:S(2)}, u32[]{:S(2)}) collective-permute-start(bf16[1,72,128]{2,1,0:T(8,128)(2,1)S(1)} %slice.163), channel_id=1, source_target_pairs={{0,128},{32,160},{64,192},{96,224},{128,0},{160,32},{192,64},{224,... | collective-permute-start | bytes 55304 | tf_op jit(solution)/shard_map/ppermute | solution.py:192
  126.4 1.2 collective-permute-done.26
  127.6 0.6 convert_bitcast_fusion
  128.3 24.5 %all_to_all.5 = bf16[32,72,128]{2,1,0:T(8,128)(2,1)S(1)} all-to-all(bf16[32,72,128]{2,1,0:T(8,128)(2,1)S(1)} %broadcast_in_dim.16), channel_id=1, replica_groups=mesh['section'=8,'dp'=32] {'dp'}, dimensions={0} | all-to-all | bytes 1179648 | tf_op jit(solution)/shard_map/all_to_all | solution.py:286
  152.7 0.8 copy.11
  (43 shorter events, 1.6 us)
Async XLA Ops:
  0.6 1.1 copy-start
  1.7 8.9 %collective-permute-start = (bf16[1,72,128]{2,1,0:T(8,128)(2,1)S(1)}, bf16[1,72,128]{2,1,0:T(8,128)(2,1)S(1)}, u32[]{:S(2)}, u32[]{:S(2)}) collective-permute-start(bf16[1,72,128]{2,1,0:T(8,128)(2,1)S(1)} %constant_dynamic-slice_fusion), channel_id=1, source_target_pairs={{0,128},{32,160},{64,192},{96,224},{128,0},{160,32},{192,64},{224,... | collective-permute-start | bytes 55304 | tf_op jit(solution)/shard_map/ppermute | solution.py:192
  10.6 3.7 %collective-permute-start.1 = (bf16[2,72,128]{2,1,0:T(8,128)(2,1)S(1)}, bf16[2,72,128]{2,1,0:T(8,128)(2,1)S(1)}, u32[]{:S(2)}, u32[]{:S(2)}) collective-permute-start(bf16[2,72,128]{2,1,0:T(8,128)(2,1)S(1)} %pad_maximum_fusion.6), channel_id=1, source_target_pairs={{0,64},{32,96},{64,0},{96,32},{128,192},{160,224},{192,128},{224,1... | collective-permute-start | bytes 110600 | tf_op jit(solution)/shard_map/ppermute | solution.py:192
  14.3 3.6 %collective-permute-start.2 = (bf16[4,72,128]{2,1,0:T(8,128)(2,1)S(1)}, bf16[4,72,128]{2,1,0:T(8,128)(2,1)S(1)}, u32[]{:S(2)}, u32[]{:S(2)}) collective-permute-start(bf16[4,72,128]{2,1,0:T(8,128)(2,1)S(1)} %get-tuple-element.27), channel_id=1, source_target_pairs={{0,32},{32,0},{64,96},{96,64},{128,160},{160,128},{192,224},{224,1... | collective-permute-start | bytes 221192 | tf_op jit(solution)/shard_map/ppermute | solution.py:192
  18.0 4.1 %collective-permute-start.3 = (bf16[2,1,4,72,128]{4,3,2,1,0:T(8,128)(2,1)S(1)}, bf16[2,1,4,72,128]{4,3,2,1,0:T(8,128)(2,1)S(1)}, u32[]{:S(2)}, u32[]{:S(2)}) collective-permute-start(bf16[2,1,4,72,128]{4,3,2,1,0:T(8,128)(2,1)S(1)} %maximum_bitcast_fusion), channel_id=1, source_target_pairs={{0,2},{1,9},{2,0},{3,11},{4,6},{5,13},{6,4},{7,15},{8,10},{9,1},{1... | collective-permute-start | bytes 442376 | tf_op jit(solution)/shard_map/ppermute | solution.py:202
  22.1 6.9 %collective-permute-start.4 = (bf16[2,2,4,72,128]{4,3,2,1,0:T(8,128)(2,1)S(1)}, bf16[2,2,4,72,128]{4,3,2,1,0:T(8,128)(2,1)S(1)}, u32[]{:S(2)}, u32[]{:S(2)}) collective-permute-start(bf16[2,2,4,72,128]{4,3,2,1,0:T(8,128)(2,1)S(1)} %pad_maximum_fusion.4), channel_id=1, source_target_pairs={{0,6},{1,25},{2,4},{3,27},{4,2},{5,29},{6,0},{7,31},{8,14},{9,17},... | collective-permute-start | bytes 884744 | tf_op jit(solution)/shard_map/ppermute | solution.py:202
  29.2 8.9 %collective-permute-start.6 = (bf16[4,4,72,128]{3,2,1,0:T(8,128)(2,1)S(1)}, bf16[4,4,72,128]{3,2,1,0:T(8,128)(2,1)S(1)}, u32[]{:S(2)}, u32[]{:S(2)}) collective-permute-start(bf16[4,4,72,128]{3,2,1,0:T(8,128)(2,1)S(1)} %get-tuple-element.24), channel_id=1, source_target_pairs={{0,24},{1,7},{2,26},{3,5},{4,28},{5,3},{6,30},{7,1},{8,16},{9,15},... | collective-permute-start | bytes 884744 | tf_op jit(solution)/shard_map/ppermute | solution.py:202
  31.7 6.6 %collective-permute-start.5 = (bf16[4,4,72,128]{3,2,1,0:T(8,128)(2,1)S(1)}, bf16[4,4,72,128]{3,2,1,0:T(8,128)(2,1)S(1)}, u32[]{:S(2)}, u32[]{:S(2)}) collective-permute-start(bf16[4,4,72,128]{3,2,1,0:T(8,128)(2,1)S(1)} %get-tuple-element.23), channel_id=1, source_target_pairs={{0,8},{1,3},{2,10},{3,1},{4,12},{5,7},{6,14},{7,5},{8,0},{9,11},{1... | collective-permute-start | bytes 884744 | tf_op jit(solution)/shard_map/ppermute | solution.py:202
  38.2 10.2 %collective-permute-start.8 = (bf16[2,4,4,72,128]{4,3,2,1,0:T(8,128)(2,1)S(1)}, bf16[2,4,4,72,128]{4,3,2,1,0:T(8,128)(2,1)S(1)}, u32[]{:S(2)}, u32[]{:S(2)}) collective-permute-start(bf16[2,4,4,72,128]{4,3,2,1,0:T(8,128)(2,1)S(1)} %pad_maximum_fusion.2), channel_id=1, source_target_pairs={{0,8},{1,3},{2,10},{3,1},{4,12},{5,7},{6,14},{7,5},{8,0},{9,11},{1... | collective-permute-start | bytes 1769480 | tf_op jit(solution)/shard_map/ppermute | solution.py:202
  38.4 17.6 %collective-permute-start.7 = (bf16[2,4,4,72,128]{4,3,2,1,0:T(8,128)(2,1)S(1)}, bf16[2,4,4,72,128]{4,3,2,1,0:T(8,128)(2,1)S(1)}, u32[]{:S(2)}, u32[]{:S(2)}) collective-permute-start(bf16[2,4,4,72,128]{4,3,2,1,0:T(8,128)(2,1)S(1)} %pad_maximum_fusion.1), channel_id=1, source_target_pairs={{0,24},{1,7},{2,26},{3,5},{4,28},{5,3},{6,30},{7,1},{8,16},{9,15},... | collective-permute-start | bytes 1769480 | tf_op jit(solution)/shard_map/ppermute | solution.py:202
  40.3 18.8 %collective-permute-start.9 = (bf16[2,4,4,72,128]{4,3,2,1,0:T(8,128)(2,1)S(1)}, bf16[2,4,4,72,128]{4,3,2,1,0:T(8,128)(2,1)S(1)}, u32[]{:S(2)}, u32[]{:S(2)}) collective-permute-start(bf16[2,4,4,72,128]{4,3,2,1,0:T(8,128)(2,1)S(1)} %pad_maximum_fusion.refs_3_), channel_id=1, source_target_pairs={{0,1},{1,0},{2,3},{3,2},{4,5},{5,4},{6,7},{7,6},{8,9},{9,8},{10,11... | collective-permute-start | bytes 1769480 | tf_op jit(solution)/shard_map/ppermute | solution.py:202
  48.4 11.6 %collective-permute-start.13 = (bf16[2,4,4,72,128]{4,3,2,1,0:T(8,128)(2,1)S(1)}, bf16[2,4,4,72,128]{4,3,2,1,0:T(8,128)(2,1)}, u32[]{:S(2)}, u32[]{:S(2)}) collective-permute-start(bf16[2,4,4,72,128]{4,3,2,1,0:T(8,128)(2,1)S(1)} %collective-permute-done.8.refs_7_), channel_id=1, source_target_pairs={{0,1},{1,0},{2,3},{3,2},{4,5},{5,4},{6,7},{7,6},{8,9},{9,8},{10,11... | collective-permute-start | bytes 1769480 | tf_op jit(solution)/shard_map/ppermute | solution.py:202
  56.0 4.0 %collective-permute-start.12 = (bf16[2,4,4,72,128]{4,3,2,1,0:T(8,128)(2,1)S(1)}, bf16[2,4,4,72,128]{4,3,2,1,0:T(8,128)(2,1)}, u32[]{:S(2)}, u32[]{:S(2)}) collective-permute-start(bf16[2,4,4,72,128]{4,3,2,1,0:T(8,128)(2,1)S(1)} %collective-permute-done.7.refs_6_), channel_id=1, source_target_pairs={{0,1},{1,0},{2,3},{3,2},{4,5},{5,4},{6,7},{7,6},{8,9},{9,8},{10,11... | collective-permute-start | bytes 1769480 | tf_op jit(solution)/shard_map/ppermute | solution.py:202
  57.4 2.2 %collective-permute-start.10 = (bf16[4,4,72,128]{3,2,1,0:T(8,128)(2,1)S(1)}, bf16[4,4,72,128]{3,2,1,0:T(8,128)(2,1)}, u32[]{:S(2)}, u32[]{:S(2)}) collective-permute-start(bf16[4,4,72,128]{3,2,1,0:T(8,128)(2,1)S(1)} %collective-permute-done.5.refs_4_), channel_id=1, source_target_pairs={{0,1},{1,0},{2,3},{3,2},{4,5},{5,4},{6,7},{7,6},{8,9},{9,8},{10,11... | collective-permute-start | bytes 884744 | tf_op jit(solution)/shard_map/ppermute | solution.py:202
  57.4 2.6 %collective-permute-start.11 = (bf16[4,4,72,128]{3,2,1,0:T(8,128)(2,1)S(1)}, bf16[4,4,72,128]{3,2,1,0:T(8,128)(2,1)}, u32[]{:S(2)}, u32[]{:S(2)}) collective-permute-start(bf16[4,4,72,128]{3,2,1,0:T(8,128)(2,1)S(1)} %collective-permute-done.6.refs_5_), channel_id=1, source_target_pairs={{0,1},{1,0},{2,3},{3,2},{4,5},{5,4},{6,7},{7,6},{8,9},{9,8},{10,11... | collective-permute-start | bytes 884744 | tf_op jit(solution)/shard_map/ppermute | solution.py:202
  79.9 2.1 %collective-permute-start.15 = (bf16[2,4,4,72,128]{4,3,2,1,0:T(8,128)(2,1)S(1)}, bf16[2,4,4,72,128]{4,3,2,1,0:T(8,128)(2,1)S(1)}, u32[]{:S(2)}, u32[]{:S(2)}) collective-permute-start(bf16[2,4,4,72,128]{4,3,2,1,0:T(8,128)(2,1)S(1)} %get-tuple-element.14), channel_id=1, source_target_pairs={{0,1},{1,0},{2,3},{3,2},{4,5},{5,4},{6,7},{7,6},{8,9},{9,8},{10,11... | collective-permute-start | bytes 1769480 | tf_op jit(solution)/shard_map/ppermute | solution.py:202
  80.3 4.7 %collective-permute-start.19 = (bf16[2,4,4,72,128]{4,3,2,1,0:T(8,128)(2,1)S(1)}, bf16[2,4,4,72,128]{4,3,2,1,0:T(8,128)(2,1)S(1)}, u32[]{:S(2)}, u32[]{:S(2)}) collective-permute-start(bf16[2,4,4,72,128]{4,3,2,1,0:T(8,128)(2,1)S(1)} %get-tuple-element.18), channel_id=1, source_target_pairs={{0,1},{1,0},{2,3},{3,2},{4,5},{5,4},{6,7},{7,6},{8,9},{9,8},{10,11... | collective-permute-start | bytes 1769480 | tf_op jit(solution)/shard_map/ppermute | solution.py:202
  80.6 4.7 %collective-permute-start.14 = (bf16[2,4,4,72,128]{4,3,2,1,0:T(8,128)(2,1)S(1)}, bf16[2,4,4,72,128]{4,3,2,1,0:T(8,128)(2,1)S(1)}, u32[]{:S(2)}, u32[]{:S(2)}) collective-permute-start(bf16[2,4,4,72,128]{4,3,2,1,0:T(8,128)(2,1)S(1)} %get-tuple-element.12), channel_id=1, source_target_pairs={{0,1},{1,0},{2,3},{3,2},{4,5},{5,4},{6,7},{7,6},{8,9},{9,8},{10,11... | collective-permute-start | bytes 1769480 | tf_op jit(solution)/shard_map/ppermute | solution.py:202
  80.9 12.0 %collective-permute-start.18 = (bf16[2,4,4,72,128]{4,3,2,1,0:T(8,128)(2,1)S(1)}, bf16[2,4,4,72,128]{4,3,2,1,0:T(8,128)(2,1)S(1)}, u32[]{:S(2)}, u32[]{:S(2)}) collective-permute-start(bf16[2,4,4,72,128]{4,3,2,1,0:T(8,128)(2,1)S(1)} %get-tuple-element.16), channel_id=1, source_target_pairs={{0,1},{1,0},{2,3},{3,2},{4,5},{5,4},{6,7},{7,6},{8,9},{9,8},{10,11... | collective-permute-start | bytes 1769480 | tf_op jit(solution)/shard_map/ppermute | solution.py:202
  82.1 10.5 %collective-permute-start.16 = (bf16[2,4,4,72,128]{4,3,2,1,0:T(8,128)(2,1)S(1)}, bf16[2,4,4,72,128]{4,3,2,1,0:T(8,128)(2,1)S(1)}, u32[]{:S(2)}, u32[]{:S(2)}) collective-permute-start(bf16[2,4,4,72,128]{4,3,2,1,0:T(8,128)(2,1)S(1)} %add_convert_fusion.1), channel_id=1, source_target_pairs={{0,24},{1,7},{2,26},{3,5},{4,28},{5,3},{6,30},{7,1},{8,16},{9,15},... | collective-permute-start | bytes 1769480 | tf_op jit(solution)/shard_map/ppermute | solution.py:202
  85.2 9.1 %collective-permute-start.20 = (bf16[2,4,4,72,128]{4,3,2,1,0:T(8,128)(2,1)S(1)}, bf16[2,4,4,72,128]{4,3,2,1,0:T(8,128)(2,1)S(1)}, u32[]{:S(2)}, u32[]{:S(2)}) collective-permute-start(bf16[2,4,4,72,128]{4,3,2,1,0:T(8,128)(2,1)S(1)} %add_convert_fusion), channel_id=1, source_target_pairs={{0,8},{1,3},{2,10},{3,1},{4,12},{5,7},{6,14},{7,5},{8,0},{9,11},{1... | collective-permute-start | bytes 1769480 | tf_op jit(solution)/shard_map/ppermute | solution.py:202
  92.7 6.0 %collective-permute-start.17 = (bf16[4,4,72,128]{3,2,1,0:T(8,128)(2,1)S(1)}, bf16[4,4,72,128]{3,2,1,0:T(8,128)(2,1)S(1)}, u32[]{:S(2)}, u32[]{:S(2)}) collective-permute-start(bf16[4,4,72,128]{3,2,1,0:T(8,128)(2,1)S(1)} %fusion.2), channel_id=1, source_target_pairs={{0,8},{1,3},{2,10},{3,1},{4,12},{5,7},{6,14},{7,5},{8,0},{9,11},{1... | collective-permute-start | bytes 884744 | tf_op jit(solution)/shard_map/ppermute | solution.py:202
  94.4 7.2 %collective-permute-start.21 = (bf16[4,4,72,128]{3,2,1,0:T(8,128)(2,1)S(1)}, bf16[4,4,72,128]{3,2,1,0:T(8,128)(2,1)S(1)}, u32[]{:S(2)}, u32[]{:S(2)}) collective-permute-start(bf16[4,4,72,128]{3,2,1,0:T(8,128)(2,1)S(1)} %fusion.3), channel_id=1, source_target_pairs={{0,24},{1,7},{2,26},{3,5},{4,28},{5,3},{6,30},{7,1},{8,16},{9,15},... | collective-permute-start | bytes 884744 | tf_op jit(solution)/shard_map/ppermute | solution.py:202
  101.8 7.2 %collective-permute-start.22 = (bf16[2,2,4,72,128]{4,3,2,1,0:T(8,128)(2,1)S(1)}, bf16[2,2,4,72,128]{4,3,2,1,0:T(8,128)(2,1)S(1)}, u32[]{:S(2)}, u32[]{:S(2)}) collective-permute-start(bf16[2,2,4,72,128]{4,3,2,1,0:T(8,128)(2,1)S(1)} %pad_maximum_fusion.3), channel_id=1, source_target_pairs={{0,6},{1,25},{2,4},{3,27},{4,2},{5,29},{6,0},{7,31},{8,14},{9,17},... | collective-permute-start | bytes 884744 | tf_op jit(solution)/shard_map/ppermute | solution.py:202
  109.0 18.5 %copy-start.1 = (f32[1,72,128]{2,1,0:T(8,128)S(1)}, f32[1,72,128]{2,1,0:T(8,128)}, u32[]{:S(2)}) copy-start(f32[1,72,128]{2,1,0:T(8,128)} %param.8) | copy-start | bytes 110596
  109.0 18.5 %copy-start.2 = (f32[1,72,128]{2,1,0:T(8,128)S(1)}, f32[1,72,128]{2,1,0:T(8,128)}, u32[]{:S(2)}) copy-start(f32[1,72,128]{2,1,0:T(8,128)} %param.9) | copy-start | bytes 110596
  109.1 4.1 %collective-permute-start.23 = (bf16[2,4,72,128]{3,2,1,0:T(8,128)(2,1)S(1)}, bf16[2,4,72,128]{3,2,1,0:T(8,128)(2,1)S(1)}, u32[]{:S(2)}, u32[]{:S(2)}) collective-permute-start(bf16[2,4,72,128]{3,2,1,0:T(8,128)(2,1)S(1)} %fusion.8), channel_id=1, source_target_pairs={{0,2},{1,9},{2,0},{3,11},{4,6},{5,13},{6,4},{7,15},{8,10},{9,1},{1... | collective-permute-start | bytes 442376 | tf_op jit(solution)/shard_map/ppermute | solution.py:202
  113.2 3.3 %collective-permute-start.24 = (bf16[4,72,128]{2,1,0:T(8,128)(2,1)S(1)}, bf16[4,72,128]{2,1,0:T(8,128)(2,1)S(1)}, u32[]{:S(2)}, u32[]{:S(2)}) collective-permute-start(bf16[4,72,128]{2,1,0:T(8,128)(2,1)S(1)} %fusion.10), channel_id=1, source_target_pairs={{0,32},{32,0},{64,96},{96,64},{128,160},{160,128},{192,224},{224,1... | collective-permute-start | bytes 221192 | tf_op jit(solution)/shard_map/ppermute | solution.py:192
  116.5 3.9 %collective-permute-start.25 = (bf16[2,72,128]{2,1,0:T(8,128)(2,1)S(1)}, bf16[2,72,128]{2,1,0:T(8,128)(2,1)S(1)}, u32[]{:S(2)}, u32[]{:S(2)}) collective-permute-start(bf16[2,72,128]{2,1,0:T(8,128)(2,1)S(1)} %slice.162), channel_id=1, source_target_pairs={{0,64},{32,96},{64,0},{96,32},{128,192},{160,224},{192,128},{224,1... | collective-permute-start | bytes 110600 | tf_op jit(solution)/shard_map/ppermute | solution.py:192
  120.5 7.1 %collective-permute-start.26 = (bf16[1,72,128]{2,1,0:T(8,128)(2,1)S(1)}, bf16[1,72,128]{2,1,0:T(8,128)(2,1)S(1)}, u32[]{:S(2)}, u32[]{:S(2)}) collective-permute-start(bf16[1,72,128]{2,1,0:T(8,128)(2,1)S(1)} %slice.163), channel_id=1, source_target_pairs={{0,128},{32,160},{64,192},{96,224},{128,0},{160,32},{192,64},{224,... | collective-permute-start | bytes 55304 | tf_op jit(solution)/shard_map/ppermute | solution.py:192

commit v4 on v3

v4 whole, which is shorter than its diff:
```python
import jax
import jax.numpy as jnp
from jax import lax
from jax.experimental import pallas as pl
from jax.experimental.pallas import tpu as pltpu
from jax.sharding import PartitionSpec as P

STEP_SIZE = 0.1
INERTIA = 0.9
ROUND = jnp.bfloat16
VMEM = 24
UNROLL = True


ORDERS = ((0, 1, 3, 2), (0, 3, 1, 2))


def slot_of(section, z):
    apart = ((section >> 1) - (z >> 1)) & 3
    pair = jnp.where(apart == 0, 0, jnp.where(apart == 3, 1, apart + 1))
    return 2 * pair + ((section ^ z) & 1)


def image_step(sides, sections, side, share, place, stream, cotangent, *refs):
    gathered, refs = refs[:12], refs[12:]
    outs, refs = refs[:4], refs[4:]
    x_in, d_in, w_all, g_all, saved_p, slopes, fwd_pad, bwd_pad, line_pad, x_sem, w_sem, g_sem = refs
    z, x, y, core = place[0], place[1], place[2], place[3]
    channels = stream.shape[-1]
    pixels = side * side
    rows = w_all.shape[1]
    half = rows // 2
    slots = sections // 2
    x_copy = pltpu.make_async_copy(stream, x_in, x_sem.at[0])
    d_copy = pltpu.make_async_copy(cotangent, d_in, x_sem.at[1])

    def lines(role, first, second):
        px = x ^ jnp.where(role == 0, second, first)
        py = y ^ jnp.where(role == 0, first, second)
        start = pl.multiple_of(((px * sides + py) * 2 + role) * share, 8)
        return pl.ds(start, share)

    copies = []
    for which in range(2):
        role = core if which == 0 else 1 - core
        for part in range(2):
            near, one, two = gathered[6 * which + 3 * part : 6 * which + 3 * part + 3]
            for i in range(sides):
                for j, source in enumerate((near.at[i], one.at[i], two.at[0, i], two.at[1, i])):
                    where = lines(role, ORDERS[part][i], ORDERS[part][j])
                    target = w_all.at[pl.ds(part * slots, slots), where, :]
                    copies.append(pltpu.make_async_copy(source, target, w_sem.at[len(copies)]))

    def send(slot):
        part, place_in = slot // slots, lax.rem(slot, slots)
        for a, role in enumerate((1 - core, core)):
            for j in (2, 3, 0, 1):
                which = 2 * a + (1 if j < 2 else 0)
                second = jnp.where(part == 0, ORDERS[0][j], ORDERS[1][j])
                for i in range(sides):
                    first = jnp.where(part == 0, ORDERS[0][i], ORDERS[1][i])
                    source = g_all.at[slot, lines(role, first, second), :]
                    target = outs[which].at[part, j % 2, i, place_in]
                    pltpu.make_async_copy(source, target, g_sem.at[which]).start()

    x_copy.start()
    for copy in copies:
        copy.start()
    d_copy.start()
    edge = jnp.zeros((side, 3 * channels), ROUND)
    for pad in (fwd_pad, bwd_pad):
        for k in range(2):
            pad[k, 0:side, :] = edge
            pad[k, side + pixels : 2 * side + pixels, :] = edge

    column = lax.broadcasted_iota(jnp.int32, (pixels, channels), 0) & (side - 1)
    not_first = column > 0
    not_last = column < side - 1

    def around(v):
        line_pad[8 : 8 + pixels, :] = v
        low = jnp.where(not_first, line_pad[7 : 7 + pixels, :], 0.0).astype(ROUND)
        high = jnp.where(not_last, line_pad[9 : 9 + pixels, :], 0.0).astype(ROUND)
        return low, high

    def band(pad, k, low, mid, high):
        body = pl.ds(side, pixels)
        pad[k, body, 0:channels] = low
        pad[k, body, channels : 2 * channels] = mid
        pad[k, body, 2 * channels : 3 * channels] = high

    def conv(pad, k, w):
        taps = jnp.concatenate([pad[k, a * side : a * side + pixels, :] for a in range(3)], axis=1)
        return jnp.dot(taps, w, preferred_element_type=jnp.float32)

    def activate(v, at):
        logistic = 1.0 / (1.0 + jnp.exp(-v))
        p = v * logistic
        slopes[at] = logistic + p * (1.0 - logistic)
        saved_p[at] = p.T.astype(ROUND)
        return p

    def forward(s, pair):
        x1, x2 = pair
        w = w_all.at[slot_of(s, z)]
        p = activate(x2, 2 * s)
        low, high = around(p)
        band(fwd_pad, 0, low, p.astype(ROUND), high)
        y1 = x1 + conv(fwd_pad, 0, w[0:half, :])
        p = activate(y1, 2 * s + 1)
        low, high = around(p)
        band(fwd_pad, 1, low, p.astype(ROUND), high)
        y2 = x2 + conv(fwd_pad, 1, w[half:rows, :])
        return y1, y2

    x_copy.wait()
    for copy in copies:
        copy.wait()
    lax.fori_loop(0, sections, forward, (x_in[0], x_in[1]), unroll=UNROLL)

    def spread(k, e, w, g, base, at):
        low, high = around(e)
        band(bwd_pad, k, high, e.astype(ROUND), low)
        total = None
        pieces = []
        for a in range(3):
            lines = bwd_pad[k, (2 - a) * side : (2 - a) * side + pixels, :]
            pieces.append(lines)
            for b in range(3):
                first = base + (3 * a + b) * channels
                part = lax.dot_general(
                    lines[:, b * channels : (b + 1) * channels], w[first : first + channels, :],
                    (((1,), (1,)), ((), ())), preferred_element_type=jnp.float32,
                )
                total = part if total is None else total + part
        wgrad = jnp.dot(
            saved_p[at], jnp.concatenate(pieces, axis=1), preferred_element_type=jnp.float32
        ).astype(ROUND)
        for tap in range(9):
            first = base + tap * channels
            g[first : first + channels, :] = wgrad[:, tap * channels : (tap + 1) * channels]
        return total * slopes[at]

    def backward(step, pair):
        d1, d2 = pair
        s = sections - 1 - step
        slot = slot_of(s, z)
        w = w_all.at[slot]
        g = g_all.at[slot]
        d1 = d1 + spread(0, d2, w, g, half, 2 * s + 1)
        d2 = d2 + spread(1, d1, w, g, 0, 2 * s)
        send(slot)
        return d1, d2

    d_copy.wait()
    lax.fori_loop(0, sections, backward, (d_in[0], d_in[1]), unroll=UNROLL)
    for which, out in enumerate(outs):
        pltpu.make_async_copy(out, out, g_sem.at[which]).wait()


def image_grads(stream, cotangent, gathered, place, sides):
    pixels, channels = stream.shape[1:]
    side = int(round(pixels**0.5))
    share = gathered[0].shape[2]
    sections = 2 * gathered[0].shape[1]
    rows = share * 2 * sides * sides
    far = pl.BlockSpec(memory_space=pl.ANY)
    kernel = lambda *refs: image_step(sides, sections, side, share, *refs)
    piece = (2, 2, sides, sections // 2, share, channels)
    return pl.pallas_call(
        kernel,
        out_shape=[jax.ShapeDtypeStruct(piece, ROUND)] * 4,
        grid_spec=pltpu.PrefetchScalarGridSpec(
            num_scalar_prefetch=1,
            grid=(1,),
            in_specs=[far] * 14,
            out_specs=[far] * 4,
            scratch_shapes=[
                pltpu.VMEM((2, pixels, channels), jnp.float32),
                pltpu.VMEM((2, pixels, channels), jnp.float32),
                pltpu.VMEM((sections, rows, channels), ROUND),
                pltpu.VMEM((sections, rows, channels), ROUND),
                pltpu.VMEM((2 * sections, channels, pixels), ROUND),
                pltpu.VMEM((2 * sections, pixels, channels), jnp.float32),
                pltpu.VMEM((2, pixels + 2 * side, 3 * channels), ROUND),
                pltpu.VMEM((2, pixels + 2 * side, 3 * channels), ROUND),
                pltpu.VMEM((pixels + 16, channels), jnp.float32),
                pltpu.SemaphoreType.DMA((2,)),
                pltpu.SemaphoreType.DMA((4 * sides * sides,)),
                pltpu.SemaphoreType.DMA((4,)),
            ],
        ),
        compiler_params=pltpu.CompilerParams(vmem_limit_bytes=VMEM << 20),
        name="image_step",
    )(place, stream, cotangent, *gathered)


def crossed_z(value):
    n = lax.axis_size("section")
    return lax.ppermute(value, "section", [(i, i ^ 1) for i in range(n)])


def moved_z(value, by):
    n = lax.axis_size("section")
    return lax.ppermute(value, "section", [(i, (i + by) % n) for i in range(n)])


def in_plane(sides, value, to):
    pairs = []
    for x in range(sides):
        for y in range(sides):
            for core in range(2):
                px, py, pc = to(x, y, core)
                pairs.append(((x * sides + y) * 2 + core, (px * sides + py) * 2 + pc))
    return lax.ppermute(value, "dp", pairs)


def along_first(sides, value, mask):
    return in_plane(sides, value, lambda x, y, c: (x, y ^ mask, c) if c == 0 else (x ^ mask, y, c))


def along_second(sides, value, mask):
    return in_plane(sides, value, lambda x, y, c: (x ^ mask, y, c) if c == 0 else (x, y ^ mask, c))


def swapped(sides, value):
    return in_plane(sides, value, lambda x, y, c: (x, y, 1 - c))


def gather_weights(mine, sides):
    pair = jnp.stack([mine, crossed_z(mine)])
    below = moved_z(pair, 2)
    above = moved_z(pair, -2)
    across = moved_z(below, 2)
    own = []
    lines = [jnp.concatenate([pair, below])[None], jnp.concatenate([above, across])[None]]
    for turn in range(2):
        for part in range(2):
            got = along_first(sides, lines[part], (1, 3)[turn ^ part])
            lines[part] = jnp.concatenate([lines[part], got])
    one = [along_second(sides, lines[part], (1, 3)[part]) for part in range(2)]
    two = [along_second(sides, jnp.stack([lines[part], one[part]]), (3, 1)[part]) for part in range(2)]
    own = [lines[0], one[0], two[0], lines[1], one[1], two[1]]
    return own + [swapped(sides, block) for block in own]


def wide(value):
    return value.astype(jnp.float32)


def scatter_grads(blocks, sides):
    passed_far, passed_near, kept_far, kept_near = blocks
    far = swapped(sides, passed_far)
    near = swapped(sides, passed_near)
    came = []
    for part in range(2):
        out = (wide(kept_far[part]) + wide(far[part])).astype(ROUND)
        came.append(along_second(sides, out, (3, 1)[part]))
    lines = []
    for part in range(2):
        out = (wide(kept_near[part, 1]) + wide(near[part, 1]) + wide(came[part][1])).astype(ROUND)
        last = along_second(sides, out, (1, 3)[part])
        lines.append(wide(kept_near[part, 0]) + wide(near[part, 0]) + wide(came[part][0]) + wide(last))
    for turn in range(2):
        for part in range(2):
            line = lines[part]
            middle = line.shape[0] // 2
            got = along_first(sides, line[middle:].astype(ROUND), (3, 1)[turn ^ part])
            lines[part] = line[:middle] + wide(got)
    (here, below), (above, across) = (jnp.split(line[0], 2) for line in lines)
    below = below + wide(moved_z(across.astype(ROUND), -2))
    here = here + wide(moved_z(above.astype(ROUND), 2)) + wide(moved_z(below.astype(ROUND), -2))
    return here[0] + wide(crossed_z(here[1].astype(ROUND)))


def on_device(stream, cotangent, weights, master, momentum):
    dp = lax.axis_size("dp")
    sides = int(round((dp // 2) ** 0.5))
    images = stream.shape[1] * dp
    share = weights.shape[1] // dp
    channels = weights.shape[2]
    z, at = lax.axis_index("section"), lax.axis_index("dp")
    place = jnp.stack([z, at // (2 * sides), at // 2 % sides, at % 2]).astype(jnp.int32)
    mine = lax.dynamic_slice_in_dim(weights[0], at * share, share, 0)
    gathered = gather_weights(mine, sides)
    pair = (2, stream.shape[2] * stream.shape[3], channels)
    first, last = (lax.dynamic_slice_in_dim(v, z, 1, 1).reshape(pair) for v in (stream, cotangent))
    blocks = image_grads(first, last, gathered, place, sides)
    gradient = scatter_grads(blocks, sides) / images
    new_momentum = INERTIA * momentum[0] + gradient
    new_master = master[0] - STEP_SIZE * new_momentum
    copies = jnp.broadcast_to(new_master.astype(ROUND)[None], (dp, share, channels))
    new_weights = lax.all_to_all(copies, "dp", 0, 0, tiled=True).reshape(dp * share, channels)
    return (new_master[None], new_momentum[None], new_weights[None])


def solution(mesh):
    placed = (
        P(None, "dp", None, None, None),
        P(None, "dp", None, None, None),
        P("section", None, None),
        P("section", "dp", None),
        P("section", "dp", None),
    )
    return jax.shard_map(
        on_device,
        mesh=mesh,
        in_specs=placed,
        out_specs=(P("section", "dp", None), P("section", "dp", None), P("section", None, None)),
        check_vma=False,
    )
```

time: 154 us -> 153 us (level)
  blocking collectives: 24.5 us -> 0 us
  starting transfers between devices: 51.6 us -> 63.4 us
  waiting for transfers between devices: 51.6 us -> 58.5 us
  Pallas kernels: 19.9 us -> 23.6 us
    all_to_all x1 -> x0, blocking collectives: 24.5 us -> none  [on_device(): lax.all_to_all(copies, 'dp', 0, 0, tiled=True).reshape(dp * share, channels)]
    all_to_all x0 -> x1, starting transfers between devices: none -> 12.3 us  [on_device(): lax.all_to_all(copies, 'dp', 0, 0, tiled=True).reshape(dp * share, channels)]
    all_to_all x0 -> x1, waiting for transfers between devices: none -> 11.7 us  [on_device(): lax.all_to_all(copies, 'dp', 0, 0, tiled=True).reshape(dp * share, channels)]
    ppermute x21 -> x24, waiting for transfers between devices: 40 us -> 32.5 us  [in_plane(): return lax.ppermute(value, 'dp', pairs)]
    ppermute x6 -> x8, starting transfers between devices: 19 us -> 15.1 us  [the longest x6 12.5 us: moved_z(): return lax.ppermute(value, 'section', [(i, (i + by) % n) for i in range(n)])]
    pallas_call x1, Pallas kernels: 19.9 us -> 23.6 us  [image_grads(): pl.pallas_call(kernel, out_shape=[jax.ShapeDtypeStruct(piece, ROUND)] * 4...]
    ppermute x21 -> x24, starting transfers between devices: 32.7 us -> 35.9 us  [in_plane(): return lax.ppermute(value, 'dp', pairs)]
    ppermute x6 -> x8, waiting for transfers between devices: 11.5 us -> 14.3 us  [the longest x6 10.6 us: moved_z(): return lax.ppermute(value, 'section', [(i, (i + by) % n) for i in range(n)])]
  transfers between devices with their start and end apart: 27 -> 33, of which waited for: 18 -> 20; matrix products, arithmetic and copies ran while one was open for 1% -> 2% of each run, Pallas kernels for 0% -> 0%
where the time goes in v4:
time: 153 us
  starting transfers between devices  63.4 us (41%)
  waiting for transfers between devices  58.5 us (38%)
  Pallas kernels  23.6 us (15%)
  local copies, waits for them, and re-layouts  4.68 us (3%)
  other arithmetic  1.92 us (1%)
    ppermute x24, starting transfers between devices, in_plane(): return lax.ppermute(value, 'dp', pairs)  35.9 us
    ppermute x24, waiting for transfers between devices, in_plane(): return lax.ppermute(value, 'dp', pairs)  32.5 us
    pallas_call x1, Pallas kernels, image_grads(): pl.pallas_call(kernel, out_shape=[jax.ShapeDtypeStruct(piece, ROUND)] * 4...  23.6 us
    ppermute x6, starting transfers between devices, moved_z(): return lax.ppermute(value, 'section', [(i, (i + by) % n) for i in range(n)])  12.5 us
    all_to_all x1, starting transfers between devices, on_device(): lax.all_to_all(copies, 'dp', 0, 0, tiled=True).reshape(dp * share, channels)  12.3 us
    all_to_all x1, waiting for transfers between devices, on_device(): lax.all_to_all(copies, 'dp', 0, 0, tiled=True).reshape(dp * share, channels)  11.7 us
    ppermute x6, waiting for transfers between devices, moved_z(): return lax.ppermute(value, 'section', [(i, (i + by) % n) for i in range(n)])  10.6 us
    ppermute x2, waiting for transfers between devices, crossed_z(): return lax.ppermute(value, 'section', [(i, i ^ 1) for i in range(n)])  3.71 us
  transfers between devices with their start and end apart: 33, of which 20 were waited for; matrix products, arithmetic and copies ran while one was open for 2% of the time, Pallas kernels for 0%

profile of v4, /device:TPU:1, one launch (start us, length us, event | category | flops | bytes accessed | tf_op | source)
XLA Modules:
  0.0 152.9 jit_solution(16573131022820262110)
XLA Ops:
  0.7 1.1 copy-done
  1.7 2.5 %collective-permute-start = (bf16[72,128]{1,0:T(8,128)(2,1)S(1)}, bf16[72,128]{1,0:T(8,128)(2,1)S(1)}, u32[]{:S(2)}, u32[]{:S(2)}) collective-permute-start(bf16[72,128]{1,0:T(8,128)(2,1)S(1)} %fusion.20), channel_id=1, source_target_pairs={{0,32},{32,0},{64,96},{96,64},{128,160},{160,128},{192,224},{224,1... | collective-permute-start | bytes 55304 | tf_op jit(solution)/shard_map/ppermute | solution.py:200
  4.2 1.1 collective-permute-done
  5.3 3.0 %collective-permute-start.1 = (bf16[2,72,128]{2,1,0:T(8,128)(2,1)S(1)}, bf16[2,72,128]{2,1,0:T(8,128)(2,1)S(1)}, u32[]{:S(2)}, u32[]{:S(2)}) collective-permute-start(bf16[2,72,128]{2,1,0:T(8,128)(2,1)S(1)} %pad_maximum_fusion.6), channel_id=1, source_target_pairs={{0,64},{32,96},{64,128},{96,160},{128,192},{160,224},{192,0},{224,... | collective-permute-start | bytes 110600 | tf_op jit(solution)/shard_map/ppermute | solution.py:205
  8.3 2.9 %collective-permute-start.6 = (bf16[2,72,128]{2,1,0:T(8,128)(2,1)S(1)}, bf16[2,72,128]{2,1,0:T(8,128)(2,1)S(1)}, u32[]{:S(2)}, u32[]{:S(2)}) collective-permute-start(bf16[2,72,128]{2,1,0:T(8,128)(2,1)S(1)} %pad_maximum_fusion.6), channel_id=1, source_target_pairs={{0,192},{32,224},{64,0},{96,32},{128,64},{160,96},{192,128},{224,1... | collective-permute-start | bytes 110600 | tf_op jit(solution)/shard_map/ppermute | solution.py:205
  11.3 1.3 collective-permute-done.1
  12.5 0.9 collective-permute-start.7
  13.4 1.3 collective-permute-start.2
  14.7 2.8 %collective-permute-done.7 = bf16[2,72,128]{2,1,0:T(8,128)(2,1)S(1)} collective-permute-done((bf16[2,72,128]{2,1,0:T(8,128)(2,1)S(1)}, bf16[2,72,128]{2,1,0:T(8,128)(2,1)S(1)}, u32[]{:S(2)}, u32[]{:S(2)}) %collective-permute-start.7) | collective-permute-done | bytes 36896 | tf_op jit(solution)/shard_map/ppermute | solution.py:205
  17.5 2.6 %collective-permute-start.8 = (bf16[1,4,72,128]{3,2,1,0:T(8,128)(2,1)S(1)}, bf16[1,4,72,128]{3,2,1,0:T(8,128)(2,1)S(1)}, u32[]{:S(2)}, u32[]{:S(2)}) collective-permute-start(bf16[1,4,72,128]{3,2,1,0:T(8,128)(2,1)S(1)} %maximum_bitcast_fusion.1), channel_id=1, source_target_pairs={{0,6},{1,25},{2,4},{3,27},{4,2},{5,29},{6,0},{7,31},{8,14},{9,17},... | collective-permute-start | bytes 221192 | tf_op jit(solution)/shard_map/ppermute | solution.py:215
  20.4 1.6 %collective-permute-done.8 = bf16[1,4,72,128]{3,2,1,0:T(8,128)(2,1)S(1)} collective-permute-done((bf16[1,4,72,128]{3,2,1,0:T(8,128)(2,1)S(1)}, bf16[1,4,72,128]{3,2,1,0:T(8,128)(2,1)S(1)}, u32[]{:S(2)}, u32[]{:S(2)}) %collective-permute-start.8) | collective-permute-done | bytes 73760 | tf_op jit(solution)/shard_map/ppermute | solution.py:215
  22.2 3.2 %collective-permute-done.3 = bf16[2,4,72,128]{3,2,1,0:T(8,128)(2,1)S(1)} collective-permute-done((bf16[2,4,72,128]{3,2,1,0:T(8,128)(2,1)S(1)}, bf16[2,4,72,128]{3,2,1,0:T(8,128)(2,1)S(1)}, u32[]{:S(2)}, u32[]{:S(2)}) %collective-permute-start.3) | collective-permute-done | bytes 147488 | tf_op jit(solution)/shard_map/ppermute | solution.py:215
  25.4 1.4 collective-permute-start.4
  26.9 2.4 %collective-permute-start.10 = (bf16[4,4,72,128]{3,2,1,0:T(8,128)(2,1)S(1)}, bf16[4,4,72,128]{3,2,1,0:T(8,128)(2,1)S(1)}, u32[]{:S(2)}, u32[]{:S(2)}) collective-permute-start(bf16[4,4,72,128]{3,2,1,0:T(8,128)(2,1)S(1)} %get-tuple-element.18.refs_6_), channel_id=1, source_target_pairs={{0,24},{1,7},{2,26},{3,5},{4,28},{5,3},{6,30},{7,1},{8,16},{9,15},... | collective-permute-start | bytes 884744 | tf_op jit(solution)/shard_map/ppermute | solution.py:215
  29.3 3.2 %collective-permute-done.4.refs_4_ = bf16[4,4,72,128]{3,2,1,0:T(8,128)(2,1)S(1)} collective-permute-done((bf16[4,4,72,128]{3,2,1,0:T(8,128)(2,1)S(1)}, bf16[4,4,72,128]{3,2,1,0:T(8,128)(2,1)S(1)}, u32[]{:S(2)}, u32[]{:S(2)}) %collective-permute-start.4) | collective-permute-done | bytes 294944 | tf_op jit(solution)/shard_map/ppermute | solution.py:215
  32.5 2.8 %collective-permute-start.5 = (bf16[2,4,4,72,128]{4,3,2,1,0:T(8,128)(2,1)S(1)}, bf16[2,4,4,72,128]{4,3,2,1,0:T(8,128)(2,1)S(1)}, u32[]{:S(2)}, u32[]{:S(2)}) collective-permute-start(bf16[2,4,4,72,128]{4,3,2,1,0:T(8,128)(2,1)S(1)} %pad_maximum_fusion), channel_id=1, source_target_pairs={{0,24},{1,7},{2,26},{3,5},{4,28},{5,3},{6,30},{7,1},{8,16},{9,15},... | collective-permute-start | bytes 1769480 | tf_op jit(solution)/shard_map/ppermute | solution.py:215
  35.4 0.5 collective-permute-start.11
  35.9 6.3 %collective-permute-start.12 = (bf16[4,4,72,128]{3,2,1,0:T(8,128)(2,1)S(1)}, bf16[4,4,72,128]{3,2,1,0:T(8,128)(2,1)S(1)}, u32[]{:S(2)}, u32[]{:S(2)}) collective-permute-start(bf16[4,4,72,128]{3,2,1,0:T(8,128)(2,1)S(1)} %get-tuple-element.20.refs_3_), channel_id=1, source_target_pairs={{0,1},{1,0},{2,3},{3,2},{4,5},{5,4},{6,7},{7,6},{8,9},{9,8},{10,11... | collective-permute-start | bytes 884744 | tf_op jit(solution)/shard_map/ppermute | solution.py:215
  42.6 7.2 %collective-permute-start.14 = (bf16[2,4,4,72,128]{4,3,2,1,0:T(8,128)(2,1)S(1)}, bf16[2,4,4,72,128]{4,3,2,1,0:T(8,128)(2,1)S(1)}, u32[]{:S(2)}, u32[]{:S(2)}) collective-permute-start(bf16[2,4,4,72,128]{4,3,2,1,0:T(8,128)(2,1)S(1)} %collective-permute-done.5.refs_5_), channel_id=1, source_target_pairs={{0,1},{1,0},{2,3},{3,2},{4,5},{5,4},{6,7},{7,6},{8,9},{9,8},{10,11... | collective-permute-start | bytes 1769480 | tf_op jit(solution)/shard_map/ppermute | solution.py:215
  49.8 2.2 %collective-permute-start.17 = (bf16[2,4,4,72,128]{4,3,2,1,0:T(8,128)(2,1)S(1)}, bf16[2,4,4,72,128]{4,3,2,1,0:T(8,128)(2,1)}, u32[]{:S(2)}, u32[]{:S(2)}) collective-permute-start(bf16[2,4,4,72,128]{4,3,2,1,0:T(8,128)(2,1)S(1)} %collective-permute-done.11.refs_8_), channel_id=1, source_target_pairs={{0,1},{1,0},{2,3},{3,2},{4,5},{5,4},{6,7},{7,6},{8,9},{9,8},{10,11... | collective-permute-start | bytes 1769480 | tf_op jit(solution)/shard_map/ppermute | solution.py:215
  52.0 0.5 collective-permute-start.13
  52.5 0.7 copy-done.1
  53.3 1.1 constant_dynamic-slice_fusion.1
  55.0 23.6 %image_step.1 = (bf16[2,2,4,4,72,128]{5,4,3,2,1,0:T(8,128)(2,1)S(1)}, bf16[2,2,4,4,72,128]{5,4,3,2,1,0:T(8,128)(2,1)S(1)}, bf16[2,2,4,4,72,128]{5,4,3,2,1,0:T(8,...) custom-call(s32[4]{0:T(128)S(1)} %pad_add_fusion.refs_0_, f32[2,256,128]{2,1,0:T(8,128)S(1)} %bitcast.94, ...), custom_call_target="tpu_custom_call" | custom-call | tf_op jit(solution)/shard_map/image_step/pallas_call | solution.py:170
  78.6 0.5 collective-permute-start.19
  79.2 2.4 %collective-permute-done.19 = bf16[2,2,4,4,72,128]{5,4,3,2,1,0:T(8,128)(2,1)S(1)} collective-permute-done((bf16[2,2,4,4,72,128]{5,4,3,2,1,0:T(8,128)(2,1)S(1)}, bf16[2,2,4,4,72,128]{5,4,3,2,1,0:T(8,128)(2,1)S(1)}, u32[]{:S(2)}, u32[]{:S(2)}) %collective-permute-start.19) | collective-permute-done | bytes 1179680 | tf_op jit(solution)/shard_map/ppermute | solution.py:215
  81.9 2.4 %collective-permute-start.20 = (bf16[2,4,4,72,128]{4,3,2,1,0:T(8,128)(2,1)S(1)}, bf16[2,4,4,72,128]{4,3,2,1,0:T(8,128)(2,1)S(1)}, u32[]{:S(2)}, u32[]{:S(2)}) collective-permute-start(bf16[2,4,4,72,128]{4,3,2,1,0:T(8,128)(2,1)S(1)} %get-tuple-element.16), channel_id=1, source_target_pairs={{0,24},{1,7},{2,26},{3,5},{4,28},{5,3},{6,30},{7,1},{8,16},{9,15},... | collective-permute-start | bytes 1769480 | tf_op jit(solution)/shard_map/ppermute | solution.py:215
  84.4 6.6 %collective-permute-done.24 = bf16[2,4,4,72,128]{4,3,2,1,0:T(8,128)(2,1)S(1)} collective-permute-done((bf16[2,4,4,72,128]{4,3,2,1,0:T(8,128)(2,1)S(1)}, bf16[2,4,4,72,128]{4,3,2,1,0:T(8,128)(2,1)S(1)}, u32[]{:S(2)}, u32[]{:S(2)}) %collective-permute-start.24) | collective-permute-done | bytes 589856 | tf_op jit(solution)/shard_map/ppermute | solution.py:215
  91.1 2.3 %collective-permute-start.25 = (bf16[4,4,72,128]{3,2,1,0:T(8,128)(2,1)S(1)}, bf16[4,4,72,128]{3,2,1,0:T(8,128)(2,1)S(1)}, u32[]{:S(2)}, u32[]{:S(2)}) collective-permute-start(bf16[4,4,72,128]{3,2,1,0:T(8,128)(2,1)S(1)} %fusion.2), channel_id=1, source_target_pairs={{0,24},{1,7},{2,26},{3,5},{4,28},{5,3},{6,30},{7,1},{8,16},{9,15},... | collective-permute-start | bytes 884744 | tf_op jit(solution)/shard_map/ppermute | solution.py:215
  93.4 4.9 %collective-permute-done.25 = bf16[4,4,72,128]{3,2,1,0:T(8,128)(2,1)S(1)} collective-permute-done((bf16[4,4,72,128]{3,2,1,0:T(8,128)(2,1)S(1)}, bf16[4,4,72,128]{3,2,1,0:T(8,128)(2,1)S(1)}, u32[]{:S(2)}, u32[]{:S(2)}) %collective-permute-start.25) | collective-permute-done | bytes 294944 | tf_op jit(solution)/shard_map/ppermute | solution.py:215
  98.7 3.9 %collective-permute-done.26 = bf16[2,4,72,128]{3,2,1,0:T(8,128)(2,1)S(1)} collective-permute-done((bf16[2,4,72,128]{3,2,1,0:T(8,128)(2,1)S(1)}, bf16[2,4,72,128]{3,2,1,0:T(8,128)(2,1)S(1)}, u32[]{:S(2)}, u32[]{:S(2)}) %collective-permute-start.26) | collective-permute-done | bytes 147488 | tf_op jit(solution)/shard_map/ppermute | solution.py:215
  102.7 1.0 collective-permute-start.27
  103.7 1.5 collective-permute-done.21
  105.4 1.0 collective-permute-start.22
  106.5 0.7 collective-permute-done.27
  107.2 3.5 %collective-permute-done.22 = bf16[2,4,72,128]{3,2,1,0:T(8,128)(2,1)S(1)} collective-permute-done((bf16[2,4,72,128]{3,2,1,0:T(8,128)(2,1)S(1)}, bf16[2,4,72,128]{3,2,1,0:T(8,128)(2,1)S(1)}, u32[]{:S(2)}, u32[]{:S(2)}) %collective-permute-start.22) | collective-permute-done | bytes 147488 | tf_op jit(solution)/shard_map/ppermute | solution.py:215
  110.8 0.7 collective-permute-start.23
  111.4 0.8 collective-permute-start.28
  112.3 2.7 %collective-permute-start.29 = (bf16[2,72,128]{2,1,0:T(8,128)(2,1)S(1)}, bf16[2,72,128]{2,1,0:T(8,128)(2,1)S(1)}, u32[]{:S(2)}, u32[]{:S(2)}) collective-permute-start(bf16[2,72,128]{2,1,0:T(8,128)(2,1)S(1)} %get-tuple-element.22), channel_id=1, source_target_pairs={{0,192},{32,224},{64,0},{96,32},{128,64},{160,96},{192,128},{224,1... | collective-permute-start | bytes 110600 | tf_op jit(solution)/shard_map/ppermute | solution.py:205
  115.0 2.9 %collective-permute-done.29 = bf16[2,72,128]{2,1,0:T(8,128)(2,1)S(1)} collective-permute-done((bf16[2,72,128]{2,1,0:T(8,128)(2,1)S(1)}, bf16[2,72,128]{2,1,0:T(8,128)(2,1)S(1)}, u32[]{:S(2)}, u32[]{:S(2)}) %collective-permute-start.29) | collective-permute-done | bytes 36896 | tf_op jit(solution)/shard_map/ppermute | solution.py:205
  117.9 2.1 %collective-permute-start.30 = (bf16[2,72,128]{2,1,0:T(8,128)(2,1)S(1)}, bf16[2,72,128]{2,1,0:T(8,128)(2,1)S(1)}, u32[]{:S(2)}, u32[]{:S(2)}) collective-permute-start(bf16[2,72,128]{2,1,0:T(8,128)(2,1)S(1)} %fusion.8), channel_id=1, source_target_pairs={{0,192},{32,224},{64,0},{96,32},{128,64},{160,96},{192,128},{224,1... | collective-permute-start | bytes 110600 | tf_op jit(solution)/shard_map/ppermute | solution.py:205
  120.0 3.8 %collective-permute-done.30 = bf16[2,72,128]{2,1,0:T(8,128)(2,1)S(1)} collective-permute-done((bf16[2,72,128]{2,1,0:T(8,128)(2,1)S(1)}, bf16[2,72,128]{2,1,0:T(8,128)(2,1)S(1)}, u32[]{:S(2)}, u32[]{:S(2)}) %collective-permute-start.30) | collective-permute-done | bytes 36896 | tf_op jit(solution)/shard_map/ppermute | solution.py:205
  123.9 2.6 %collective-permute-done.31 = bf16[72,128]{1,0:T(8,128)(2,1)S(1)} collective-permute-done((bf16[72,128]{1,0:T(8,128)(2,1)S(1)}, bf16[72,128]{1,0:T(8,128)(2,1)S(1)}, u32[]{:S(2)}, u32[]{:S(2)}) %collective-permute-start.31) | collective-permute-done | bytes 18464 | tf_op jit(solution)/shard_map/ppermute | solution.py:200
  126.6 0.9 broadcast_in_dim.22
  127.4 12.3 %all-to-all-start = ((bf16[32,72,128]{2,1,0:T(8,128)(2,1)}), bf16[32,72,128]{2,1,0:T(8,128)(2,1)S(1)}, u32[]{:S(2)}, u32[]{:S(2)}) async-start(bf16[32,72,128]{2,1,0:T(8,128)(2,1)} %broadcast_in_dim.22), calls=%async_computation | async-start | bytes 1179648 | tf_op jit(solution)/shard_map/all_to_all | solution.py:293
  139.8 0.6 fusion.16
  140.4 11.7 %all-to-all-done = bf16[32,72,128]{2,1,0:T(8,128)(2,1)S(1)} async-done(((bf16[32,72,128]{2,1,0:T(8,128)(2,1)}), bf16[32,72,128]{2,1,0:T(8,128)(2,1)S(1)}, u32[]{:S(2)}, u32[]{:S(2)}) %all-to-all-start) | async-done | bytes 589856 | tf_op jit(solution)/shard_map/all_to_all | solution.py:293
  152.1 0.8 copy.9
  (64 shorter events, 3.5 us)
Async XLA Ops:
  0.6 1.1 copy-start
  1.7 3.6 %collective-permute-start = (bf16[72,128]{1,0:T(8,128)(2,1)S(1)}, bf16[72,128]{1,0:T(8,128)(2,1)S(1)}, u32[]{:S(2)}, u32[]{:S(2)}) collective-permute-start(bf16[72,128]{1,0:T(8,128)(2,1)S(1)} %fusion.20), channel_id=1, source_target_pairs={{0,32},{32,0},{64,96},{96,64},{128,160},{160,128},{192,224},{224,1... | collective-permute-start | bytes 55304 | tf_op jit(solution)/shard_map/ppermute | solution.py:200
  5.3 7.2 %collective-permute-start.1 = (bf16[2,72,128]{2,1,0:T(8,128)(2,1)S(1)}, bf16[2,72,128]{2,1,0:T(8,128)(2,1)S(1)}, u32[]{:S(2)}, u32[]{:S(2)}) collective-permute-start(bf16[2,72,128]{2,1,0:T(8,128)(2,1)S(1)} %pad_maximum_fusion.6), channel_id=1, source_target_pairs={{0,64},{32,96},{64,128},{96,160},{128,192},{160,224},{192,0},{224,... | collective-permute-start | bytes 110600 | tf_op jit(solution)/shard_map/ppermute | solution.py:205
  8.3 6.4 %collective-permute-start.6 = (bf16[2,72,128]{2,1,0:T(8,128)(2,1)S(1)}, bf16[2,72,128]{2,1,0:T(8,128)(2,1)S(1)}, u32[]{:S(2)}, u32[]{:S(2)}) collective-permute-start(bf16[2,72,128]{2,1,0:T(8,128)(2,1)S(1)} %pad_maximum_fusion.6), channel_id=1, source_target_pairs={{0,192},{32,224},{64,0},{96,32},{128,64},{160,96},{192,128},{224,1... | collective-permute-start | bytes 110600 | tf_op jit(solution)/shard_map/ppermute | solution.py:205
  12.5 5.0 %collective-permute-start.7 = (bf16[2,72,128]{2,1,0:T(8,128)(2,1)S(1)}, bf16[2,72,128]{2,1,0:T(8,128)(2,1)S(1)}, u32[]{:S(2)}, u32[]{:S(2)}) collective-permute-start(bf16[2,72,128]{2,1,0:T(8,128)(2,1)S(1)} %collective-permute-done.1), channel_id=1, source_target_pairs={{0,64},{32,96},{64,128},{96,160},{128,192},{160,224},{192,0},{224,... | collective-permute-start | bytes 110600 | tf_op jit(solution)/shard_map/ppermute | solution.py:205
  13.4 6.6 %collective-permute-start.2 = (bf16[1,4,72,128]{3,2,1,0:T(8,128)(2,1)S(1)}, bf16[1,4,72,128]{3,2,1,0:T(8,128)(2,1)S(1)}, u32[]{:S(2)}, u32[]{:S(2)}) collective-permute-start(bf16[1,4,72,128]{3,2,1,0:T(8,128)(2,1)S(1)} %maximum_bitcast_fusion), channel_id=1, source_target_pairs={{0,2},{1,9},{2,0},{3,11},{4,6},{5,13},{6,4},{7,15},{8,10},{9,1},{1... | collective-permute-start | bytes 221192 | tf_op jit(solution)/shard_map/ppermute | solution.py:215
  17.5 4.5 %collective-permute-start.8 = (bf16[1,4,72,128]{3,2,1,0:T(8,128)(2,1)S(1)}, bf16[1,4,72,128]{3,2,1,0:T(8,128)(2,1)S(1)}, u32[]{:S(2)}, u32[]{:S(2)}) collective-permute-start(bf16[1,4,72,128]{3,2,1,0:T(8,128)(2,1)S(1)} %maximum_bitcast_fusion.1), channel_id=1, source_target_pairs={{0,6},{1,25},{2,4},{3,27},{4,2},{5,29},{6,0},{7,31},{8,14},{9,17},... | collective-permute-start | bytes 221192 | tf_op jit(solution)/shard_map/ppermute | solution.py:215
  20.1 5.3 %collective-permute-start.3 = (bf16[2,4,72,128]{3,2,1,0:T(8,128)(2,1)S(1)}, bf16[2,4,72,128]{3,2,1,0:T(8,128)(2,1)S(1)}, u32[]{:S(2)}, u32[]{:S(2)}) collective-permute-start(bf16[2,4,72,128]{3,2,1,0:T(8,128)(2,1)S(1)} %pad_maximum_fusion.4), channel_id=1, source_target_pairs={{0,6},{1,25},{2,4},{3,27},{4,2},{5,29},{6,0},{7,31},{8,14},{9,17},... | collective-permute-start | bytes 442376 | tf_op jit(solution)/shard_map/ppermute | solution.py:215
  22.0 4.8 %collective-permute-start.9 = (bf16[2,4,72,128]{3,2,1,0:T(8,128)(2,1)S(1)}, bf16[2,4,72,128]{3,2,1,0:T(8,128)(2,1)S(1)}, u32[]{:S(2)}, u32[]{:S(2)}) collective-permute-start(bf16[2,4,72,128]{3,2,1,0:T(8,128)(2,1)S(1)} %pad_maximum_fusion.5), channel_id=1, source_target_pairs={{0,2},{1,9},{2,0},{3,11},{4,6},{5,13},{6,4},{7,15},{8,10},{9,1},{1... | collective-permute-start | bytes 442376 | tf_op jit(solution)/shard_map/ppermute | solution.py:215
  25.4 7.0 %collective-permute-start.4 = (bf16[4,4,72,128]{3,2,1,0:T(8,128)(2,1)S(1)}, bf16[4,4,72,128]{3,2,1,0:T(8,128)(2,1)S(1)}, u32[]{:S(2)}, u32[]{:S(2)}) collective-permute-start(bf16[4,4,72,128]{3,2,1,0:T(8,128)(2,1)S(1)} %get-tuple-element.20.refs_3_), channel_id=1, source_target_pairs={{0,8},{1,3},{2,10},{3,1},{4,12},{5,7},{6,14},{7,5},{8,0},{9,11},{1... | collective-permute-start | bytes 884744 | tf_op jit(solution)/shard_map/ppermute | solution.py:215
  26.9 8.5 %collective-permute-start.10 = (bf16[4,4,72,128]{3,2,1,0:T(8,128)(2,1)S(1)}, bf16[4,4,72,128]{3,2,1,0:T(8,128)(2,1)S(1)}, u32[]{:S(2)}, u32[]{:S(2)}) collective-permute-start(bf16[4,4,72,128]{3,2,1,0:T(8,128)(2,1)S(1)} %get-tuple-element.18.refs_6_), channel_id=1, source_target_pairs={{0,24},{1,7},{2,26},{3,5},{4,28},{5,3},{6,30},{7,1},{8,16},{9,15},... | collective-permute-start | bytes 884744 | tf_op jit(solution)/shard_map/ppermute | solution.py:215
  32.5 10.1 %collective-permute-start.5 = (bf16[2,4,4,72,128]{4,3,2,1,0:T(8,128)(2,1)S(1)}, bf16[2,4,4,72,128]{4,3,2,1,0:T(8,128)(2,1)S(1)}, u32[]{:S(2)}, u32[]{:S(2)}) collective-permute-start(bf16[2,4,4,72,128]{4,3,2,1,0:T(8,128)(2,1)S(1)} %pad_maximum_fusion), channel_id=1, source_target_pairs={{0,24},{1,7},{2,26},{3,5},{4,28},{5,3},{6,30},{7,1},{8,16},{9,15},... | collective-permute-start | bytes 1769480 | tf_op jit(solution)/shard_map/ppermute | solution.py:215
  35.4 14.4 %collective-permute-start.11 = (bf16[2,4,4,72,128]{4,3,2,1,0:T(8,128)(2,1)S(1)}, bf16[2,4,4,72,128]{4,3,2,1,0:T(8,128)(2,1)S(1)}, u32[]{:S(2)}, u32[]{:S(2)}) collective-permute-start(bf16[2,4,4,72,128]{4,3,2,1,0:T(8,128)(2,1)S(1)} %pad_maximum_fusion.1), channel_id=1, source_target_pairs={{0,8},{1,3},{2,10},{3,1},{4,12},{5,7},{6,14},{7,5},{8,0},{9,11},{1... | collective-permute-start | bytes 1769480 | tf_op jit(solution)/shard_map/ppermute | solution.py:215
  35.9 16.6 %collective-permute-start.12 = (bf16[4,4,72,128]{3,2,1,0:T(8,128)(2,1)S(1)}, bf16[4,4,72,128]{3,2,1,0:T(8,128)(2,1)S(1)}, u32[]{:S(2)}, u32[]{:S(2)}) collective-permute-start(bf16[4,4,72,128]{3,2,1,0:T(8,128)(2,1)S(1)} %get-tuple-element.20.refs_3_), channel_id=1, source_target_pairs={{0,1},{1,0},{2,3},{3,2},{4,5},{5,4},{6,7},{7,6},{8,9},{9,8},{10,11... | collective-permute-start | bytes 884744 | tf_op jit(solution)/shard_map/ppermute | solution.py:215
  42.6 12.4 %collective-permute-start.14 = (bf16[2,4,4,72,128]{4,3,2,1,0:T(8,128)(2,1)S(1)}, bf16[2,4,4,72,128]{4,3,2,1,0:T(8,128)(2,1)S(1)}, u32[]{:S(2)}, u32[]{:S(2)}) collective-permute-start(bf16[2,4,4,72,128]{4,3,2,1,0:T(8,128)(2,1)S(1)} %collective-permute-done.5.refs_5_), channel_id=1, source_target_pairs={{0,1},{1,0},{2,3},{3,2},{4,5},{5,4},{6,7},{7,6},{8,9},{9,8},{10,11... | collective-permute-start | bytes 1769480 | tf_op jit(solution)/shard_map/ppermute | solution.py:215
  49.8 5.2 %collective-permute-start.17 = (bf16[2,4,4,72,128]{4,3,2,1,0:T(8,128)(2,1)S(1)}, bf16[2,4,4,72,128]{4,3,2,1,0:T(8,128)(2,1)}, u32[]{:S(2)}, u32[]{:S(2)}) collective-permute-start(bf16[2,4,4,72,128]{4,3,2,1,0:T(8,128)(2,1)S(1)} %collective-permute-done.11.refs_8_), channel_id=1, source_target_pairs={{0,1},{1,0},{2,3},{3,2},{4,5},{5,4},{6,7},{7,6},{8,9},{9,8},{10,11... | collective-permute-start | bytes 1769480 | tf_op jit(solution)/shard_map/ppermute | solution.py:215
  52.0 2.4 %collective-permute-start.15 = (bf16[4,4,72,128]{3,2,1,0:T(8,128)(2,1)S(1)}, bf16[4,4,72,128]{3,2,1,0:T(8,128)(2,1)}, u32[]{:S(2)}, u32[]{:S(2)}) collective-permute-start(bf16[4,4,72,128]{3,2,1,0:T(8,128)(2,1)S(1)} %get-tuple-element.18.refs_6_), channel_id=1, source_target_pairs={{0,1},{1,0},{2,3},{3,2},{4,5},{5,4},{6,7},{7,6},{8,9},{9,8},{10,11... | collective-permute-start | bytes 884744 | tf_op jit(solution)/shard_map/ppermute | solution.py:215
  52.0 2.6 %collective-permute-start.13 = (bf16[4,4,72,128]{3,2,1,0:T(8,128)(2,1)S(1)}, bf16[4,4,72,128]{3,2,1,0:T(8,128)(2,1)}, u32[]{:S(2)}, u32[]{:S(2)}) collective-permute-start(bf16[4,4,72,128]{3,2,1,0:T(8,128)(2,1)S(1)} %collective-permute-done.4.refs_4_), channel_id=1, source_target_pairs={{0,1},{1,0},{2,3},{3,2},{4,5},{5,4},{6,7},{7,6},{8,9},{9,8},{10,11... | collective-permute-start | bytes 884744 | tf_op jit(solution)/shard_map/ppermute | solution.py:215
  52.5 0.7 copy-start.1
  53.2 1.8 %collective-permute-start.16 = (bf16[4,4,72,128]{3,2,1,0:T(8,128)(2,1)S(1)}, bf16[4,4,72,128]{3,2,1,0:T(8,128)(2,1)}, u32[]{:S(2)}, u32[]{:S(2)}) collective-permute-start(bf16[4,4,72,128]{3,2,1,0:T(8,128)(2,1)S(1)} %collective-permute-done.10.refs_7_), channel_id=1, source_target_pairs={{0,1},{1,0},{2,3},{3,2},{4,5},{5,4},{6,7},{7,6},{8,9},{9,8},{10,11... | collective-permute-start | bytes 884744 | tf_op jit(solution)/shard_map/ppermute | solution.py:215
  53.2 1.8 %copy-start.2 = (bf16[4,4,72,128]{3,2,1,0:T(8,128)(2,1)S(1)}, bf16[4,4,72,128]{3,2,1,0:T(8,128)(2,1)}, u32[]{:S(2)}) copy-start(bf16[4,4,72,128]{3,2,1,0:T(8,128)(2,1)} %copy-done.1) | copy-start | bytes 884740
  78.6 3.0 %collective-permute-start.19 = (bf16[2,2,4,4,72,128]{5,4,3,2,1,0:T(8,128)(2,1)S(1)}, bf16[2,2,4,4,72,128]{5,4,3,2,1,0:T(8,128)(2,1)S(1)}, u32[]{:S(2)}, u32[]{:S(2)}) collective-permute-start(bf16[2,2,4,4,72,128]{5,4,3,2,1,0:T(8,128)(2,1)S(1)} %get-tuple-element.10), channel_id=1, source_target_pairs={{0,1},{1,0},{2,3},{3,2},{4,5},{5,4},{6,7},{7,6},{8,9},{9,8},{10,11... | collective-permute-start | bytes 3538952 | tf_op jit(solution)/shard_map/ppermute | solution.py:215
  79.1 5.3 %collective-permute-start.18 = (bf16[2,2,4,4,72,128]{5,4,3,2,1,0:T(8,128)(2,1)S(1)}, bf16[2,2,4,4,72,128]{5,4,3,2,1,0:T(8,128)(2,1)S(1)}, u32[]{:S(2)}, u32[]{:S(2)}) collective-permute-start(bf16[2,2,4,4,72,128]{5,4,3,2,1,0:T(8,128)(2,1)S(1)} %get-tuple-element.8), channel_id=1, source_target_pairs={{0,1},{1,0},{2,3},{3,2},{4,5},{5,4},{6,7},{7,6},{8,9},{9,8},{10,11... | collective-permute-start | bytes 3538952 | tf_op jit(solution)/shard_map/ppermute | solution.py:215
  81.8 9.1 %collective-permute-start.24 = (bf16[2,4,4,72,128]{4,3,2,1,0:T(8,128)(2,1)S(1)}, bf16[2,4,4,72,128]{4,3,2,1,0:T(8,128)(2,1)S(1)}, u32[]{:S(2)}, u32[]{:S(2)}) collective-permute-start(bf16[2,4,4,72,128]{4,3,2,1,0:T(8,128)(2,1)S(1)} %get-tuple-element.15), channel_id=1, source_target_pairs={{0,8},{1,3},{2,10},{3,1},{4,12},{5,7},{6,14},{7,5},{8,0},{9,11},{1... | collective-permute-start | bytes 1769480 | tf_op jit(solution)/shard_map/ppermute | solution.py:215
  81.9 11.4 %collective-permute-start.20 = (bf16[2,4,4,72,128]{4,3,2,1,0:T(8,128)(2,1)S(1)}, bf16[2,4,4,72,128]{4,3,2,1,0:T(8,128)(2,1)S(1)}, u32[]{:S(2)}, u32[]{:S(2)}) collective-permute-start(bf16[2,4,4,72,128]{4,3,2,1,0:T(8,128)(2,1)S(1)} %get-tuple-element.16), channel_id=1, source_target_pairs={{0,24},{1,7},{2,26},{3,5},{4,28},{5,3},{6,30},{7,1},{8,16},{9,15},... | collective-permute-start | bytes 1769480 | tf_op jit(solution)/shard_map/ppermute | solution.py:215
  91.1 7.2 %collective-permute-start.25 = (bf16[4,4,72,128]{3,2,1,0:T(8,128)(2,1)S(1)}, bf16[4,4,72,128]{3,2,1,0:T(8,128)(2,1)S(1)}, u32[]{:S(2)}, u32[]{:S(2)}) collective-permute-start(bf16[4,4,72,128]{3,2,1,0:T(8,128)(2,1)S(1)} %fusion.2), channel_id=1, source_target_pairs={{0,24},{1,7},{2,26},{3,5},{4,28},{5,3},{6,30},{7,1},{8,16},{9,15},... | collective-permute-start | bytes 884744 | tf_op jit(solution)/shard_map/ppermute | solution.py:215
  98.5 4.1 %collective-permute-start.26 = (bf16[2,4,72,128]{3,2,1,0:T(8,128)(2,1)S(1)}, bf16[2,4,72,128]{3,2,1,0:T(8,128)(2,1)S(1)}, u32[]{:S(2)}, u32[]{:S(2)}) collective-permute-start(bf16[2,4,72,128]{3,2,1,0:T(8,128)(2,1)S(1)} %slice.179), channel_id=1, source_target_pairs={{0,2},{1,9},{2,0},{3,11},{4,6},{5,13},{6,4},{7,15},{8,10},{9,1},{1... | collective-permute-start | bytes 442376 | tf_op jit(solution)/shard_map/ppermute | solution.py:215
  98.6 6.6 %collective-permute-start.21 = (bf16[4,4,72,128]{3,2,1,0:T(8,128)(2,1)S(1)}, bf16[4,4,72,128]{3,2,1,0:T(8,128)(2,1)S(1)}, u32[]{:S(2)}, u32[]{:S(2)}) collective-permute-start(bf16[4,4,72,128]{3,2,1,0:T(8,128)(2,1)S(1)} %get-tuple-element.14), channel_id=1, source_target_pairs={{0,8},{1,3},{2,10},{3,1},{4,12},{5,7},{6,14},{7,5},{8,0},{9,11},{1... | collective-permute-start | bytes 884744 | tf_op jit(solution)/shard_map/ppermute | solution.py:215
  102.7 4.5 %collective-permute-start.27 = (bf16[1,4,72,128]{3,2,1,0:T(8,128)(2,1)S(1)}, bf16[1,4,72,128]{3,2,1,0:T(8,128)(2,1)S(1)}, u32[]{:S(2)}, u32[]{:S(2)}) collective-permute-start(bf16[1,4,72,128]{3,2,1,0:T(8,128)(2,1)S(1)} %slice.181), channel_id=1, source_target_pairs={{0,6},{1,25},{2,4},{3,27},{4,2},{5,29},{6,0},{7,31},{8,14},{9,17},... | collective-permute-start | bytes 221192 | tf_op jit(solution)/shard_map/ppermute | solution.py:215
  105.4 21.1 %copy-start.3 = (f32[1,72,128]{2,1,0:T(8,128)S(1)}, f32[1,72,128]{2,1,0:T(8,128)}, u32[]{:S(2)}) copy-start(f32[1,72,128]{2,1,0:T(8,128)} %param.8) | copy-start | bytes 110596
  105.4 21.1 %copy-start.5 = (f32[1,72,128]{2,1,0:T(8,128)S(1)}, f32[1,72,128]{2,1,0:T(8,128)}, u32[]{:S(2)}) copy-start(f32[1,72,128]{2,1,0:T(8,128)} %param.9) | copy-start | bytes 110596
  105.4 5.3 %collective-permute-start.22 = (bf16[2,4,72,128]{3,2,1,0:T(8,128)(2,1)S(1)}, bf16[2,4,72,128]{3,2,1,0:T(8,128)(2,1)S(1)}, u32[]{:S(2)}, u32[]{:S(2)}) collective-permute-start(bf16[2,4,72,128]{3,2,1,0:T(8,128)(2,1)S(1)} %slice.180), channel_id=1, source_target_pairs={{0,6},{1,25},{2,4},{3,27},{4,2},{5,29},{6,0},{7,31},{8,14},{9,17},... | collective-permute-start | bytes 442376 | tf_op jit(solution)/shard_map/ppermute | solution.py:215
  110.8 4.2 %collective-permute-start.23 = (bf16[1,4,72,128]{3,2,1,0:T(8,128)(2,1)S(1)}, bf16[1,4,72,128]{3,2,1,0:T(8,128)(2,1)S(1)}, u32[]{:S(2)}, u32[]{:S(2)}) collective-permute-start(bf16[1,4,72,128]{3,2,1,0:T(8,128)(2,1)S(1)} %slice.182), channel_id=1, source_target_pairs={{0,2},{1,9},{2,0},{3,11},{4,6},{5,13},{6,4},{7,15},{8,10},{9,1},{1... | collective-permute-start | bytes 221192 | tf_op jit(solution)/shard_map/ppermute | solution.py:215
  111.4 8.6 %collective-permute-start.28 = (bf16[2,72,128]{2,1,0:T(8,128)(2,1)S(1)}, bf16[2,72,128]{2,1,0:T(8,128)(2,1)S(1)}, u32[]{:S(2)}, u32[]{:S(2)}) collective-permute-start(bf16[2,72,128]{2,1,0:T(8,128)(2,1)S(1)} %get-tuple-element.21), channel_id=1, source_target_pairs={{0,64},{32,96},{64,128},{96,160},{128,192},{160,224},{192,0},{224,... | collective-permute-start | bytes 110600 | tf_op jit(solution)/shard_map/ppermute | solution.py:205
  112.3 5.6 %collective-permute-start.29 = (bf16[2,72,128]{2,1,0:T(8,128)(2,1)S(1)}, bf16[2,72,128]{2,1,0:T(8,128)(2,1)S(1)}, u32[]{:S(2)}, u32[]{:S(2)}) collective-permute-start(bf16[2,72,128]{2,1,0:T(8,128)(2,1)S(1)} %get-tuple-element.22), channel_id=1, source_target_pairs={{0,192},{32,224},{64,0},{96,32},{128,64},{160,96},{192,128},{224,1... | collective-permute-start | bytes 110600 | tf_op jit(solution)/shard_map/ppermute | solution.py:205
  117.9 5.9 %collective-permute-start.30 = (bf16[2,72,128]{2,1,0:T(8,128)(2,1)S(1)}, bf16[2,72,128]{2,1,0:T(8,128)(2,1)S(1)}, u32[]{:S(2)}, u32[]{:S(2)}) collective-permute-start(bf16[2,72,128]{2,1,0:T(8,128)(2,1)S(1)} %fusion.8), channel_id=1, source_target_pairs={{0,192},{32,224},{64,0},{96,32},{128,64},{160,96},{192,128},{224,1... | collective-permute-start | bytes 110600 | tf_op jit(solution)/shard_map/ppermute | solution.py:205
  123.8 2.7 %collective-permute-start.31 = (bf16[72,128]{1,0:T(8,128)(2,1)S(1)}, bf16[72,128]{1,0:T(8,128)(2,1)S(1)}, u32[]{:S(2)}, u32[]{:S(2)}) collective-permute-start(bf16[72,128]{1,0:T(8,128)(2,1)S(1)} %fusion.14), channel_id=1, source_target_pairs={{0,32},{32,0},{64,96},{96,64},{128,160},{160,128},{192,224},{224,1... | collective-permute-start | bytes 55304 | tf_op jit(solution)/shard_map/ppermute | solution.py:200
  126.5 26.3 %copy-start.4 = (f32[72,128]{1,0:T(8,128)}, f32[72,128]{1,0:T(8,128)S(1)}, u32[]{:S(2)}) copy-start(f32[72,128]{1,0:T(8,128)S(1)} %get-tuple-element.12) | copy-start | bytes 110596
  127.4 24.6 %all-to-all-start = ((bf16[32,72,128]{2,1,0:T(8,128)(2,1)}), bf16[32,72,128]{2,1,0:T(8,128)(2,1)S(1)}, u32[]{:S(2)}, u32[]{:S(2)}) async-start(bf16[32,72,128]{2,1,0:T(8,128)(2,1)} %broadcast_in_dim.22), calls=%async_computation | async-start | bytes 1179648 | tf_op jit(solution)/shard_map/all_to_all | solution.py:293

commit v5 on v4

--- a/solution.py
+++ b/solution.py
@@ -9,10 +9,29 @@
 INERTIA = 0.9
 ROUND = jnp.bfloat16
 VMEM = 24
-UNROLL = True
 
 
 ORDERS = ((0, 1, 3, 2), (0, 3, 1, 2))
+
+
+def rank_in(part, distance):
+    if part == 0:
+        return distance ^ (distance >> 1)
+    return ((distance << 1) & 3) ^ (3 * (distance >> 1))
+
+
+def block_table(sides, x, y, core):
+    block = jnp.arange(2 * sides * sides)
+    role = block % 2
+    px, py = (block // (2 * sides)) ^ x, (block // 2 % sides) ^ y
+    first, second = jnp.where(role == 0, py, px), jnp.where(role == 0, px, py)
+    stays = (role == core).astype(jnp.int32)
+    tables = []
+    for part in range(2):
+        rank = rank_in(part, second)
+        late = 1 - rank // 2
+        tables.append((((stays * 2 + late) * 2 + part) * 2 + rank % 2) * sides + first)
+    return jnp.concatenate(tables).astype(jnp.int32)
 
 
 def slot_of(section, z):
@@ -21,16 +40,17 @@
     return 2 * pair + ((section ^ z) & 1)
 
 
-def image_step(sides, sections, side, share, place, stream, cotangent, *refs):
+def image_step(sides, sections, side, share, place, table, stream, cotangent, *refs):
     gathered, refs = refs[:12], refs[12:]
-    outs, refs = refs[:4], refs[4:]
-    x_in, d_in, w_all, g_all, saved_p, slopes, fwd_pad, bwd_pad, line_pad, x_sem, w_sem, g_sem = refs
+    out, refs = refs[0], refs[1:]
+    x_in, d_in, w_all, saved_p, slopes, fwd_pad, bwd_pad, line_pad, x_sem, w_sem = refs
     z, x, y, core = place[0], place[1], place[2], place[3]
     channels = stream.shape[-1]
     pixels = side * side
     rows = w_all.shape[1]
     half = rows // 2
     slots = sections // 2
+    blocks = 2 * sides * sides
     x_copy = pltpu.make_async_copy(stream, x_in, x_sem.at[0])
     d_copy = pltpu.make_async_copy(cotangent, d_in, x_sem.at[1])
 
@@ -47,21 +67,9 @@
             near, one, two = gathered[6 * which + 3 * part : 6 * which + 3 * part + 3]
             for i in range(sides):
                 for j, source in enumerate((near.at[i], one.at[i], two.at[0, i], two.at[1, i])):
-                    where = lines(role, ORDERS[part][i], ORDERS[part][j])
+                    where = lines(role, i, ORDERS[part][j])
                     target = w_all.at[pl.ds(part * slots, slots), where, :]
                     copies.append(pltpu.make_async_copy(source, target, w_sem.at[len(copies)]))
-
-    def send(slot):
-        part, place_in = slot // slots, lax.rem(slot, slots)
-        for a, role in enumerate((1 - core, core)):
-            for j in (2, 3, 0, 1):
-                which = 2 * a + (1 if j < 2 else 0)
-                second = jnp.where(part == 0, ORDERS[0][j], ORDERS[1][j])
-                for i in range(sides):
-                    first = jnp.where(part == 0, ORDERS[0][i], ORDERS[1][i])
-                    source = g_all.at[slot, lines(role, first, second), :]
-                    target = outs[which].at[part, j % 2, i, place_in]
-                    pltpu.make_async_copy(source, target, g_sem.at[which]).start()
 
     x_copy.start()
     for copy in copies:
@@ -116,49 +124,46 @@
     x_copy.wait()
     for copy in copies:
         copy.wait()
-    lax.fori_loop(0, sections, forward, (x_in[0], x_in[1]), unroll=UNROLL)
-
-    def spread(k, e, w, g, base, at):
+    lax.fori_loop(0, sections, forward, (x_in[0], x_in[1]), unroll=True)
+
+    def spread(k, e, w, s, base, at):
         low, high = around(e)
         band(bwd_pad, k, high, e.astype(ROUND), low)
-        total = None
-        pieces = []
-        for a in range(3):
-            lines = bwd_pad[k, (2 - a) * side : (2 - a) * side + pixels, :]
-            pieces.append(lines)
-            for b in range(3):
-                first = base + (3 * a + b) * channels
-                part = lax.dot_general(
-                    lines[:, b * channels : (b + 1) * channels], w[first : first + channels, :],
-                    (((1,), (1,)), ((), ())), preferred_element_type=jnp.float32,
-                )
-                total = part if total is None else total + part
-        wgrad = jnp.dot(
-            saved_p[at], jnp.concatenate(pieces, axis=1), preferred_element_type=jnp.float32
-        ).astype(ROUND)
+        taps = jnp.concatenate(
+            [bwd_pad[k, (2 - a) * side : (2 - a) * side + pixels, :] for a in range(3)], axis=1
+        )
+        across = jnp.concatenate(
+            [w[base + tap * channels : base + (tap + 1) * channels, :] for tap in range(9)], axis=1
+        )
+        total = lax.dot_general(taps, across, (((1,), (1,)), ((), ())), preferred_element_type=jnp.float32)
+        wgrad = jnp.dot(saved_p[at], taps, preferred_element_type=jnp.float32)
         for tap in range(9):
-            first = base + tap * channels
-            g[first : first + channels, :] = wgrad[:, tap * channels : (tap + 1) * channels]
+            row, end = base + tap * channels, base + (tap + 1) * channels
+            while row < end:
+                block = row // share
+                stop = min(end, (block + 1) * share)
+                n = table[s // slots * blocks + block] * slots + s % slots
+                c = row - base - tap * channels
+                piece = wgrad[c : c + stop - row, tap * channels : (tap + 1) * channels].astype(ROUND)
+                out[n, row - block * share : stop - block * share, :] = piece
+                row = stop
         return total * slopes[at]
 
     def backward(step, pair):
         d1, d2 = pair
         s = sections - 1 - step
-        slot = slot_of(s, z)
-        w = w_all.at[slot]
-        g = g_all.at[slot]
-        d1 = d1 + spread(0, d2, w, g, half, 2 * s + 1)
-        d2 = d2 + spread(1, d1, w, g, 0, 2 * s)
-        send(slot)
+        w = w_all.at[slot_of(s, z)]
+        d1 = d1 + spread(0, d2, w, s, half, 2 * s + 1)
+        d2 = d2 + spread(1, d1, w, s, 0, 2 * s)
         return d1, d2
 
     d_copy.wait()
-    lax.fori_loop(0, sections, backward, (d_in[0], d_in[1]), unroll=UNROLL)
-    for which, out in enumerate(outs):
-        pltpu.make_async_copy(out, out, g_sem.at[which]).wait()
-
-
-def image_grads(stream, cotangent, gathered, place, sides):
+    pair = d_in[0], d_in[1]
+    for step in range(sections):
+        pair = backward(step, pair)
+
+
+def image_grads(stream, cotangent, gathered, place, table, sides):
     pixels, channels = stream.shape[1:]
     side = int(round(pixels**0.5))
     share = gathered[0].shape[2]
@@ -166,19 +171,18 @@
     rows = share * 2 * sides * sides
     far = pl.BlockSpec(memory_space=pl.ANY)
     kernel = lambda *refs: image_step(sides, sections, side, share, *refs)
-    piece = (2, 2, sides, sections // 2, share, channels)
+    whole = 2 * sides * sides * sections
     return pl.pallas_call(
         kernel,
-        out_shape=[jax.ShapeDtypeStruct(piece, ROUND)] * 4,
+        out_shape=jax.ShapeDtypeStruct((whole, share, channels), ROUND),
         grid_spec=pltpu.PrefetchScalarGridSpec(
-            num_scalar_prefetch=1,
+            num_scalar_prefetch=2,
             grid=(1,),
             in_specs=[far] * 14,
-            out_specs=[far] * 4,
+            out_specs=pl.BlockSpec(memory_space=pltpu.VMEM),
             scratch_shapes=[
                 pltpu.VMEM((2, pixels, channels), jnp.float32),
                 pltpu.VMEM((2, pixels, channels), jnp.float32),
-                pltpu.VMEM((sections, rows, channels), ROUND),
                 pltpu.VMEM((sections, rows, channels), ROUND),
                 pltpu.VMEM((2 * sections, channels, pixels), ROUND),
                 pltpu.VMEM((2 * sections, pixels, channels), jnp.float32),
@@ -187,12 +191,11 @@
                 pltpu.VMEM((pixels + 16, channels), jnp.float32),
                 pltpu.SemaphoreType.DMA((2,)),
                 pltpu.SemaphoreType.DMA((4 * sides * sides,)),
-                pltpu.SemaphoreType.DMA((4,)),
             ],
         ),
         compiler_params=pltpu.CompilerParams(vmem_limit_bytes=VMEM << 20),
         name="image_step",
-    )(place, stream, cotangent, *gathered)
+    )(place, table, stream, cotangent, *gathered)
 
 
 def crossed_z(value):
@@ -232,12 +235,9 @@
     below = moved_z(pair, 2)
     above = moved_z(pair, -2)
     across = moved_z(below, 2)
-    own = []
-    lines = [jnp.concatenate([pair, below])[None], jnp.concatenate([above, across])[None]]
-    for turn in range(2):
-        for part in range(2):
-            got = along_first(sides, lines[part], (1, 3)[turn ^ part])
-            lines[part] = jnp.concatenate([lines[part], got])
+    line = jnp.stack([jnp.concatenate([pair, below]), jnp.concatenate([above, across])])
+    came = [line] + [along_first(sides, line, mask) for mask in range(1, sides)]
+    lines = [jnp.stack([got[part] for got in came]) for part in range(2)]
     one = [along_second(sides, lines[part], (1, 3)[part]) for part in range(2)]
     two = [along_second(sides, jnp.stack([lines[part], one[part]]), (3, 1)[part]) for part in range(2)]
     own = [lines[0], one[0], two[0], lines[1], one[1], two[1]]
@@ -249,7 +249,7 @@
 
 
 def scatter_grads(blocks, sides):
-    passed_far, passed_near, kept_far, kept_near = blocks
+    (passed_far, passed_near), (kept_far, kept_near) = blocks
     far = swapped(sides, passed_far)
     near = swapped(sides, passed_near)
     came = []
@@ -261,16 +261,13 @@
         out = (wide(kept_near[part, 1]) + wide(near[part, 1]) + wide(came[part][1])).astype(ROUND)
         last = along_second(sides, out, (1, 3)[part])
         lines.append(wide(kept_near[part, 0]) + wide(near[part, 0]) + wide(came[part][0]) + wide(last))
-    for turn in range(2):
-        for part in range(2):
-            line = lines[part]
-            middle = line.shape[0] // 2
-            got = along_first(sides, line[middle:].astype(ROUND), (3, 1)[turn ^ part])
-            lines[part] = line[:middle] + wide(got)
-    (here, below), (above, across) = (jnp.split(line[0], 2) for line in lines)
-    below = below + wide(moved_z(across.astype(ROUND), -2))
-    here = here + wide(moved_z(above.astype(ROUND), 2)) + wide(moved_z(below.astype(ROUND), -2))
-    return here[0] + wide(crossed_z(here[1].astype(ROUND)))
+    line = jnp.concatenate(lines, axis=1)
+    total = line[0]
+    line = line.astype(ROUND)
+    for mask in range(1, sides):
+        total = total + wide(along_first(sides, line[mask], mask))
+    tiles = lax.all_to_all(total.astype(ROUND), "section", 0, 0, tiled=True)
+    return jnp.sum(wide(tiles), axis=0)
 
 
 def on_device(stream, cotangent, weights, master, momentum):
@@ -285,7 +282,9 @@
     gathered = gather_weights(mine, sides)
     pair = (2, stream.shape[2] * stream.shape[3], channels)
     first, last = (lax.dynamic_slice_in_dim(v, z, 1, 1).reshape(pair) for v in (stream, cotangent))
-    blocks = image_grads(first, last, gathered, place, sides)
+    table = block_table(sides, *place[1:])
+    blocks = image_grads(first, last, gathered, place, table, sides)
+    blocks = blocks.reshape(2, 2, 2, 2, sides, -1, share, channels)
     gradient = scatter_grads(blocks, sides) / images
     new_momentum = INERTIA * momentum[0] + gradient
     new_master = master[0] - STEP_SIZE * new_momentum

time: 153 us -> 144 us (0.941)
  blocking collectives: 0 us -> 38 us
  waiting for transfers between devices: 58.5 us -> 39.3 us
  starting transfers between devices: 63.4 us -> 45 us
  Pallas kernels: 23.6 us -> 15 us
    all_to_all x0 -> x2, blocking collectives: none -> 38 us  [the longest x1 23.6 us: on_device(): lax.all_to_all(copies, 'dp', 0, 0, tiled=True).reshape(dp * share, channels)]
    all_to_all x1 -> x0, starting transfers between devices: 12.3 us -> none  [on_device(): lax.all_to_all(copies, 'dp', 0, 0, tiled=True).reshape(dp * share, channels)]
    all_to_all x1 -> x0, waiting for transfers between devices: 11.7 us -> none  [on_device(): lax.all_to_all(copies, 'dp', 0, 0, tiled=True).reshape(dp * share, channels)]
    pallas_call x1, Pallas kernels: 23.6 us -> 15 us  [image_grads(): pl.pallas_call(kernel, out_shape=jax.ShapeDtypeStruct((whole, share, chan...]
    ppermute x6 -> x3, starting transfers between devices: 12.5 us -> 6.82 us  [moved_z(): return lax.ppermute(value, 'section', [(i, (i + by) % n) for i in range(n)])]
    ppermute x6 -> x3, waiting for transfers between devices: 10.6 us -> 5.33 us  [moved_z(): return lax.ppermute(value, 'section', [(i, (i + by) % n) for i in range(n)])]
    ppermute x2 -> x1, waiting for transfers between devices: 3.71 us -> 1.14 us  [crossed_z(): return lax.ppermute(value, 'section', [(i, i ^ 1) for i in range(n)])]
    ppermute x24 -> x22, waiting for transfers between devices: 32.5 us -> 32.9 us  [in_plane(): return lax.ppermute(value, 'dp', pairs)]
  transfers between devices with their start and end apart: 33 -> 26, of which waited for: 20 -> 18; matrix products, arithmetic and copies ran while one was open for 2% -> 1% of each run, Pallas kernels for 0% -> 0%
where the time goes in v5:
time: 144 us
  starting transfers between devices  45 us (31%)
  waiting for transfers between devices  39.3 us (27%)
  blocking collectives  38 us (26%)
  Pallas kernels  15 us (10%)
  local copies, waits for them, and re-layouts  3.81 us (3%)
  other arithmetic  2.07 us (1%)
    ppermute x22, starting transfers between devices, in_plane(): return lax.ppermute(value, 'dp', pairs)  35.7 us
    ppermute x22, waiting for transfers between devices, in_plane(): return lax.ppermute(value, 'dp', pairs)  32.9 us
    all_to_all x1, blocking collectives, on_device(): lax.all_to_all(copies, 'dp', 0, 0, tiled=True).reshape(dp * share, channels)  23.6 us
    pallas_call x1, Pallas kernels, image_grads(): pl.pallas_call(kernel, out_shape=jax.ShapeDtypeStruct((whole, share, chan...  15 us
    all_to_all x1, blocking collectives, scatter_grads(): tiles = lax.all_to_all(total.astype(ROUND), 'section', 0, 0, tiled=True)  14.4 us
    ppermute x3, starting transfers between devices, moved_z(): return lax.ppermute(value, 'section', [(i, (i + by) % n) for i in range(n)])  6.82 us
    ppermute x3, waiting for transfers between devices, moved_z(): return lax.ppermute(value, 'section', [(i, (i + by) % n) for i in range(n)])  5.33 us
  transfers between devices with their start and end apart: 26, of which 18 were waited for; matrix products, arithmetic and copies ran while one was open for 1% of the time, Pallas kernels for 0%

profile of v5, /device:TPU:1, one launch (start us, length us, event | category | flops | bytes accessed | tf_op | source)
XLA Modules:
  0.0 144.1 jit_solution(17055642561146907897)
XLA Ops:
  0.7 1.1 copy-done
  1.7 2.5 %collective-permute-start = (bf16[72,128]{1,0:T(8,128)(2,1)S(1)}, bf16[72,128]{1,0:T(8,128)(2,1)S(1)}, u32[]{:S(2)}, u32[]{:S(2)}) collective-permute-start(bf16[72,128]{1,0:T(8,128)(2,1)S(1)} %fusion.26), channel_id=1, source_target_pairs={{0,32},{32,0},{64,96},{96,64},{128,160},{160,128},{192,224},{224,1... | collective-permute-start | bytes 55304 | tf_op jit(solution)/shard_map/ppermute | solution.py:203
  4.2 1.1 collective-permute-done
  5.3 3.0 %collective-permute-start.1 = (bf16[2,72,128]{2,1,0:T(8,128)(2,1)S(1)}, bf16[2,72,128]{2,1,0:T(8,128)(2,1)S(1)}, u32[]{:S(2)}, u32[]{:S(2)}) collective-permute-start(bf16[2,72,128]{2,1,0:T(8,128)(2,1)S(1)} %pad_maximum_fusion.6), channel_id=1, source_target_pairs={{0,64},{32,96},{64,128},{96,160},{128,192},{160,224},{192,0},{224,... | collective-permute-start | bytes 110600 | tf_op jit(solution)/shard_map/ppermute | solution.py:208
  8.3 2.9 %collective-permute-start.2 = (bf16[2,72,128]{2,1,0:T(8,128)(2,1)S(1)}, bf16[2,72,128]{2,1,0:T(8,128)(2,1)S(1)}, u32[]{:S(2)}, u32[]{:S(2)}) collective-permute-start(bf16[2,72,128]{2,1,0:T(8,128)(2,1)S(1)} %pad_maximum_fusion.6), channel_id=1, source_target_pairs={{0,192},{32,224},{64,0},{96,32},{128,64},{160,96},{192,128},{224,1... | collective-permute-start | bytes 110600 | tf_op jit(solution)/shard_map/ppermute | solution.py:208
  11.3 1.3 collective-permute-done.1
  12.5 0.9 collective-permute-start.3
  13.4 0.3 collective-permute-done.2
  13.7 3.8 %collective-permute-done.3 = bf16[2,72,128]{2,1,0:T(8,128)(2,1)S(1)} collective-permute-done((bf16[2,72,128]{2,1,0:T(8,128)(2,1)S(1)}, bf16[2,72,128]{2,1,0:T(8,128)(2,1)S(1)}, u32[]{:S(2)}, u32[]{:S(2)}) %collective-permute-start.3) | collective-permute-done | bytes 36896 | tf_op jit(solution)/shard_map/ppermute | solution.py:208
  17.5 2.6 %collective-permute-start.6 = (bf16[2,4,72,128]{3,2,1,0:T(8,128)(2,1)S(1)}, bf16[2,4,72,128]{3,2,1,0:T(8,128)(2,1)S(1)}, u32[]{:S(2)}, u32[]{:S(2)}) collective-permute-start(bf16[2,4,72,128]{3,2,1,0:T(8,128)(2,1)S(1)} %pad_maximum_fusion.5), channel_id=1, source_target_pairs={{0,6},{1,25},{2,4},{3,27},{4,2},{5,29},{6,0},{7,31},{8,14},{9,17},... | collective-permute-start | bytes 442376 | tf_op jit(solution)/shard_map/ppermute | solution.py:218
  20.1 0.5 collective-permute-start.5
  20.6 0.3 collective-permute-start.4
  20.9 2.9 %collective-permute-done.6 = bf16[2,4,72,128]{3,2,1,0:T(8,128)(2,1)S(1)} collective-permute-done((bf16[2,4,72,128]{3,2,1,0:T(8,128)(2,1)S(1)}, bf16[2,4,72,128]{3,2,1,0:T(8,128)(2,1)S(1)}, u32[]{:S(2)}, u32[]{:S(2)}) %collective-permute-start.6) | collective-permute-done | bytes 147488 | tf_op jit(solution)/shard_map/ppermute | solution.py:218
  23.8 1.8 %collective-permute-done.5 = bf16[2,4,72,128]{3,2,1,0:T(8,128)(2,1)S(1)} collective-permute-done((bf16[2,4,72,128]{3,2,1,0:T(8,128)(2,1)S(1)}, bf16[2,4,72,128]{3,2,1,0:T(8,128)(2,1)S(1)}, u32[]{:S(2)}, u32[]{:S(2)}) %collective-permute-start.5) | collective-permute-done | bytes 147488 | tf_op jit(solution)/shard_map/ppermute | solution.py:218
  25.7 1.4 collective-permute-start.7
  27.1 2.0 %collective-permute-start.9 = (bf16[4,4,72,128]{3,2,1,0:T(8,128)(2,1)S(1)}, bf16[4,4,72,128]{3,2,1,0:T(8,128)(2,1)S(1)}, u32[]{:S(2)}, u32[]{:S(2)}) collective-permute-start(bf16[4,4,72,128]{3,2,1,0:T(8,128)(2,1)S(1)} %get-tuple-element.19.refs_7_), channel_id=1, source_target_pairs={{0,24},{1,7},{2,26},{3,5},{4,28},{5,3},{6,30},{7,1},{8,16},{9,15},... | collective-permute-start | bytes 884744 | tf_op jit(solution)/shard_map/ppermute | solution.py:218
  29.1 3.6 %collective-permute-done.7.refs_5_ = bf16[4,4,72,128]{3,2,1,0:T(8,128)(2,1)S(1)} collective-permute-done((bf16[4,4,72,128]{3,2,1,0:T(8,128)(2,1)S(1)}, bf16[4,4,72,128]{3,2,1,0:T(8,128)(2,1)S(1)}, u32[]{:S(2)}, u32[]{:S(2)}) %collective-permute-start.7) | collective-permute-done | bytes 294944 | tf_op jit(solution)/shard_map/ppermute | solution.py:218
  32.8 2.8 %collective-permute-start.8 = (bf16[2,4,4,72,128]{4,3,2,1,0:T(8,128)(2,1)S(1)}, bf16[2,4,4,72,128]{4,3,2,1,0:T(8,128)(2,1)S(1)}, u32[]{:S(2)}, u32[]{:S(2)}) collective-permute-start(bf16[2,4,4,72,128]{4,3,2,1,0:T(8,128)(2,1)S(1)} %pad_maximum_fusion.1), channel_id=1, source_target_pairs={{0,24},{1,7},{2,26},{3,5},{4,28},{5,3},{6,30},{7,1},{8,16},{9,15},... | collective-permute-start | bytes 1769480 | tf_op jit(solution)/shard_map/ppermute | solution.py:218
  35.7 6.5 %collective-permute-start.14 = (bf16[4,4,72,128]{3,2,1,0:T(8,128)(2,1)S(1)}, bf16[4,4,72,128]{3,2,1,0:T(8,128)(2,1)}, u32[]{:S(2)}, u32[]{:S(2)}) collective-permute-start(bf16[4,4,72,128]{3,2,1,0:T(8,128)(2,1)S(1)} %get-tuple-element.19.refs_7_), channel_id=1, source_target_pairs={{0,1},{1,0},{2,3},{3,2},{4,5},{5,4},{6,7},{7,6},{8,9},{9,8},{10,11... | collective-permute-start | bytes 884744 | tf_op jit(solution)/shard_map/ppermute | solution.py:218
  42.3 0.9 collective-permute-done.8.refs_6_
  43.1 6.6 %collective-permute-start.13 = (bf16[2,4,4,72,128]{4,3,2,1,0:T(8,128)(2,1)S(1)}, bf16[2,4,4,72,128]{4,3,2,1,0:T(8,128)(2,1)S(1)}, u32[]{:S(2)}, u32[]{:S(2)}) collective-permute-start(bf16[2,4,4,72,128]{4,3,2,1,0:T(8,128)(2,1)S(1)} %collective-permute-done.8.refs_6_), channel_id=1, source_target_pairs={{0,1},{1,0},{2,3},{3,2},{4,5},{5,4},{6,7},{7,6},{8,9},{9,8},{10,11... | collective-permute-start | bytes 1769480 | tf_op jit(solution)/shard_map/ppermute | solution.py:218
  49.8 2.2 %collective-permute-start.16 = (bf16[2,4,4,72,128]{4,3,2,1,0:T(8,128)(2,1)S(1)}, bf16[2,4,4,72,128]{4,3,2,1,0:T(8,128)(2,1)}, u32[]{:S(2)}, u32[]{:S(2)}) collective-permute-start(bf16[2,4,4,72,128]{4,3,2,1,0:T(8,128)(2,1)S(1)} %collective-permute-done.10.refs_9_), channel_id=1, source_target_pairs={{0,1},{1,0},{2,3},{3,2},{4,5},{5,4},{6,7},{7,6},{8,9},{9,8},{10,11... | collective-permute-start | bytes 1769480 | tf_op jit(solution)/shard_map/ppermute | solution.py:218
  52.1 0.5 collective-permute-start.15
  52.8 1.1 constant_dynamic-slice_fusion.1
  54.0 0.4 collective-permute-done.15.refs_14_
  54.4 0.4 collective-permute-done.12.refs_11_
  54.8 15.0 %image_step.1 = bf16[256,72,128]{2,1,0:T(8,128)(2,1)S(1)} custom-call(s32[4]{0:T(128)S(1)} %pad_add_fusion.refs_0_, s32[64]{0:T(128)S(1)} %pad_add_fusion.1.refs_1_, f32[2,256,128]{2,1,0:T(8,128)S(1)} %bitcast.89, f32[2,256,128]{2,1,0:T(8,128)S(1)} %bitcast.88, bf16[4,4,72,128]{3,2,1,0:T(8,128)(2,1)S(1)} %get-tuple-element.21.refs_4_, ...), custom_call_target="tpu_custom_call" | custom-call | tf_op jit(solution)/shard_map/image_step/pallas_call | solution.py:175
  69.9 0.6 fusion.22
  70.5 0.5 collective-permute-start.18
  71.2 2.2 %collective-permute-done.18 = bf16[2,2,4,4,72,128]{5,4,3,2,1,0:T(8,128)(2,1)S(1)} collective-permute-done((bf16[2,2,4,4,72,128]{5,4,3,2,1,0:T(8,128)(2,1)S(1)}, bf16[2,2,4,4,72,128]{5,4,3,2,1,0:T(8,128)(2,1)S(1)}, u32[]{:S(2)}, u32[]{:S(2)}) %collective-permute-start.18) | collective-permute-done | bytes 1179680 | tf_op jit(solution)/shard_map/ppermute | solution.py:218
  73.4 0.3 fusion.1
  73.7 1.3 collective-permute-start.21
  75.1 1.9 %collective-permute-start.19 = (bf16[2,4,4,72,128]{4,3,2,1,0:T(8,128)(2,1)S(1)}, bf16[2,4,4,72,128]{4,3,2,1,0:T(8,128)(2,1)S(1)}, u32[]{:S(2)}, u32[]{:S(2)}) collective-permute-start(bf16[2,4,4,72,128]{4,3,2,1,0:T(8,128)(2,1)S(1)} %get-tuple-element.14), channel_id=1, source_target_pairs={{0,24},{1,7},{2,26},{3,5},{4,28},{5,3},{6,30},{7,1},{8,16},{9,15},... | collective-permute-start | bytes 1769480 | tf_op jit(solution)/shard_map/ppermute | solution.py:218
  77.0 6.1 %collective-permute-done.21 = bf16[2,4,4,72,128]{4,3,2,1,0:T(8,128)(2,1)S(1)} collective-permute-done((bf16[2,4,4,72,128]{4,3,2,1,0:T(8,128)(2,1)S(1)}, bf16[2,4,4,72,128]{4,3,2,1,0:T(8,128)(2,1)S(1)}, u32[]{:S(2)}, u32[]{:S(2)}) %collective-permute-start.21) | collective-permute-done | bytes 589856 | tf_op jit(solution)/shard_map/ppermute | solution.py:218
  83.2 2.9 %collective-permute-start.22 = (bf16[4,4,72,128]{3,2,1,0:T(8,128)(2,1)S(1)}, bf16[4,4,72,128]{3,2,1,0:T(8,128)(2,1)S(1)}, u32[]{:S(2)}, u32[]{:S(2)}) collective-permute-start(bf16[4,4,72,128]{3,2,1,0:T(8,128)(2,1)S(1)} %fusion.3), channel_id=1, source_target_pairs={{0,24},{1,7},{2,26},{3,5},{4,28},{5,3},{6,30},{7,1},{8,16},{9,15},... | collective-permute-start | bytes 884744 | tf_op jit(solution)/shard_map/ppermute | solution.py:218
  86.1 4.4 %collective-permute-done.22 = bf16[4,4,72,128]{3,2,1,0:T(8,128)(2,1)S(1)} collective-permute-done((bf16[4,4,72,128]{3,2,1,0:T(8,128)(2,1)S(1)}, bf16[4,4,72,128]{3,2,1,0:T(8,128)(2,1)S(1)}, u32[]{:S(2)}, u32[]{:S(2)}) %collective-permute-start.22) | collective-permute-done | bytes 294944 | tf_op jit(solution)/shard_map/ppermute | solution.py:218
  90.5 0.3 fusion.4
  90.8 5.9 %collective-permute-done.20 = bf16[4,4,72,128]{3,2,1,0:T(8,128)(2,1)S(1)} collective-permute-done((bf16[4,4,72,128]{3,2,1,0:T(8,128)(2,1)S(1)}, bf16[4,4,72,128]{3,2,1,0:T(8,128)(2,1)S(1)}, u32[]{:S(2)}, u32[]{:S(2)}) %collective-permute-start.20) | collective-permute-done | bytes 294944 | tf_op jit(solution)/shard_map/ppermute | solution.py:218
  96.7 0.1 fusion.6
  97.1 1.8 %collective-permute-start.25 = (bf16[8,72,128]{2,1,0:T(8,128)(2,1)S(1)}, bf16[8,72,128]{2,1,0:T(8,128)(2,1)S(1)}, u32[]{:S(2)}, u32[]{:S(2)}) collective-permute-start(bf16[8,72,128]{2,1,0:T(8,128)(2,1)S(1)} %get-tuple-element.16), channel_id=1, source_target_pairs={{0,6},{1,25},{2,4},{3,27},{4,2},{5,29},{6,0},{7,31},{8,14},{9,17},... | collective-permute-start | bytes 442376 | tf_op jit(solution)/shard_map/ppermute | solution.py:218
  98.9 1.4 collective-permute-start.24
  100.3 0.7 collective-permute-done.23
  101.1 1.5 %collective-permute-done.25 = bf16[8,72,128]{2,1,0:T(8,128)(2,1)S(1)} collective-permute-done((bf16[8,72,128]{2,1,0:T(8,128)(2,1)S(1)}, bf16[8,72,128]{2,1,0:T(8,128)(2,1)S(1)}, u32[]{:S(2)}, u32[]{:S(2)}) %collective-permute-start.25) | collective-permute-done | bytes 147488 | tf_op jit(solution)/shard_map/ppermute | solution.py:218
  102.6 1.8 %collective-permute-done.24 = bf16[8,72,128]{2,1,0:T(8,128)(2,1)S(1)} collective-permute-done((bf16[8,72,128]{2,1,0:T(8,128)(2,1)S(1)}, bf16[8,72,128]{2,1,0:T(8,128)(2,1)S(1)}, u32[]{:S(2)}, u32[]{:S(2)}) %collective-permute-start.24) | collective-permute-done | bytes 147488 | tf_op jit(solution)/shard_map/ppermute | solution.py:218
  104.5 14.4 %all_to_all.10 = bf16[8,72,128]{2,1,0:T(8,128)(2,1)S(1)} all-to-all(bf16[8,72,128]{2,1,0:T(8,128)(2,1)S(1)} %fusion.12), channel_id=1, replica_groups=mesh['section'=8,'dp'=32] {'section'}, dimensions={0} | all-to-all | bytes 294912 | tf_op jit(solution)/shard_map/all_to_all | solution.py:269
  118.9 0.6 convert_bitcast_fusion
  119.6 23.6 %all_to_all.11 = bf16[32,72,128]{2,1,0:T(8,128)(2,1)S(1)} all-to-all(bf16[32,72,128]{2,1,0:T(8,128)(2,1)S(1)} %broadcast_in_dim.5), channel_id=1, replica_groups=mesh['section'=8,'dp'=32] {'dp'}, dimensions={0} | all-to-all | bytes 1179648 | tf_op jit(solution)/shard_map/all_to_all | solution.py:292
  143.2 0.8 copy.9
  (43 shorter events, 1.7 us)
Async XLA Ops:
  0.6 1.1 copy-start
  1.7 3.6 %collective-permute-start = (bf16[72,128]{1,0:T(8,128)(2,1)S(1)}, bf16[72,128]{1,0:T(8,128)(2,1)S(1)}, u32[]{:S(2)}, u32[]{:S(2)}) collective-permute-start(bf16[72,128]{1,0:T(8,128)(2,1)S(1)} %fusion.26), channel_id=1, source_target_pairs={{0,32},{32,0},{64,96},{96,64},{128,160},{160,128},{192,224},{224,1... | collective-permute-start | bytes 55304 | tf_op jit(solution)/shard_map/ppermute | solution.py:203
  5.3 7.2 %collective-permute-start.1 = (bf16[2,72,128]{2,1,0:T(8,128)(2,1)S(1)}, bf16[2,72,128]{2,1,0:T(8,128)(2,1)S(1)}, u32[]{:S(2)}, u32[]{:S(2)}) collective-permute-start(bf16[2,72,128]{2,1,0:T(8,128)(2,1)S(1)} %pad_maximum_fusion.6), channel_id=1, source_target_pairs={{0,64},{32,96},{64,128},{96,160},{128,192},{160,224},{192,0},{224,... | collective-permute-start | bytes 110600 | tf_op jit(solution)/shard_map/ppermute | solution.py:208
  8.3 5.4 %collective-permute-start.2 = (bf16[2,72,128]{2,1,0:T(8,128)(2,1)S(1)}, bf16[2,72,128]{2,1,0:T(8,128)(2,1)S(1)}, u32[]{:S(2)}, u32[]{:S(2)}) collective-permute-start(bf16[2,72,128]{2,1,0:T(8,128)(2,1)S(1)} %pad_maximum_fusion.6), channel_id=1, source_target_pairs={{0,192},{32,224},{64,0},{96,32},{128,64},{160,96},{192,128},{224,1... | collective-permute-start | bytes 110600 | tf_op jit(solution)/shard_map/ppermute | solution.py:208
  12.5 5.0 %collective-permute-start.3 = (bf16[2,72,128]{2,1,0:T(8,128)(2,1)S(1)}, bf16[2,72,128]{2,1,0:T(8,128)(2,1)S(1)}, u32[]{:S(2)}, u32[]{:S(2)}) collective-permute-start(bf16[2,72,128]{2,1,0:T(8,128)(2,1)S(1)} %collective-permute-done.1), channel_id=1, source_target_pairs={{0,64},{32,96},{64,128},{96,160},{128,192},{160,224},{192,0},{224,... | collective-permute-start | bytes 110600 | tf_op jit(solution)/shard_map/ppermute | solution.py:208
  17.5 6.2 %collective-permute-start.6 = (bf16[2,4,72,128]{3,2,1,0:T(8,128)(2,1)S(1)}, bf16[2,4,72,128]{3,2,1,0:T(8,128)(2,1)S(1)}, u32[]{:S(2)}, u32[]{:S(2)}) collective-permute-start(bf16[2,4,72,128]{3,2,1,0:T(8,128)(2,1)S(1)} %pad_maximum_fusion.5), channel_id=1, source_target_pairs={{0,6},{1,25},{2,4},{3,27},{4,2},{5,29},{6,0},{7,31},{8,14},{9,17},... | collective-permute-start | bytes 442376 | tf_op jit(solution)/shard_map/ppermute | solution.py:218
  20.1 5.5 %collective-permute-start.5 = (bf16[2,4,72,128]{3,2,1,0:T(8,128)(2,1)S(1)}, bf16[2,4,72,128]{3,2,1,0:T(8,128)(2,1)S(1)}, u32[]{:S(2)}, u32[]{:S(2)}) collective-permute-start(bf16[2,4,72,128]{3,2,1,0:T(8,128)(2,1)S(1)} %pad_maximum_fusion.5), channel_id=1, source_target_pairs={{0,4},{1,17},{2,6},{3,19},{4,0},{5,21},{6,2},{7,23},{8,12},{9,25},... | collective-permute-start | bytes 442376 | tf_op jit(solution)/shard_map/ppermute | solution.py:218
  20.6 5.0 %collective-permute-start.4 = (bf16[2,4,72,128]{3,2,1,0:T(8,128)(2,1)S(1)}, bf16[2,4,72,128]{3,2,1,0:T(8,128)(2,1)S(1)}, u32[]{:S(2)}, u32[]{:S(2)}) collective-permute-start(bf16[2,4,72,128]{3,2,1,0:T(8,128)(2,1)S(1)} %pad_maximum_fusion.5), channel_id=1, source_target_pairs={{0,2},{1,9},{2,0},{3,11},{4,6},{5,13},{6,4},{7,15},{8,10},{9,1},{1... | collective-permute-start | bytes 442376 | tf_op jit(solution)/shard_map/ppermute | solution.py:218
  25.7 7.0 %collective-permute-start.7 = (bf16[4,4,72,128]{3,2,1,0:T(8,128)(2,1)S(1)}, bf16[4,4,72,128]{3,2,1,0:T(8,128)(2,1)S(1)}, u32[]{:S(2)}, u32[]{:S(2)}) collective-permute-start(bf16[4,4,72,128]{3,2,1,0:T(8,128)(2,1)S(1)} %get-tuple-element.21.refs_4_), channel_id=1, source_target_pairs={{0,8},{1,3},{2,10},{3,1},{4,12},{5,7},{6,14},{7,5},{8,0},{9,11},{1... | collective-permute-start | bytes 884744 | tf_op jit(solution)/shard_map/ppermute | solution.py:218
  27.1 8.4 %collective-permute-start.9 = (bf16[4,4,72,128]{3,2,1,0:T(8,128)(2,1)S(1)}, bf16[4,4,72,128]{3,2,1,0:T(8,128)(2,1)S(1)}, u32[]{:S(2)}, u32[]{:S(2)}) collective-permute-start(bf16[4,4,72,128]{3,2,1,0:T(8,128)(2,1)S(1)} %get-tuple-element.19.refs_7_), channel_id=1, source_target_pairs={{0,24},{1,7},{2,26},{3,5},{4,28},{5,3},{6,30},{7,1},{8,16},{9,15},... | collective-permute-start | bytes 884744 | tf_op jit(solution)/shard_map/ppermute | solution.py:218
  32.8 10.3 %collective-permute-start.8 = (bf16[2,4,4,72,128]{4,3,2,1,0:T(8,128)(2,1)S(1)}, bf16[2,4,4,72,128]{4,3,2,1,0:T(8,128)(2,1)S(1)}, u32[]{:S(2)}, u32[]{:S(2)}) collective-permute-start(bf16[2,4,4,72,128]{4,3,2,1,0:T(8,128)(2,1)S(1)} %pad_maximum_fusion.1), channel_id=1, source_target_pairs={{0,24},{1,7},{2,26},{3,5},{4,28},{5,3},{6,30},{7,1},{8,16},{9,15},... | collective-permute-start | bytes 1769480 | tf_op jit(solution)/shard_map/ppermute | solution.py:218
  35.6 14.1 %collective-permute-start.10 = (bf16[2,4,4,72,128]{4,3,2,1,0:T(8,128)(2,1)S(1)}, bf16[2,4,4,72,128]{4,3,2,1,0:T(8,128)(2,1)S(1)}, u32[]{:S(2)}, u32[]{:S(2)}) collective-permute-start(bf16[2,4,4,72,128]{4,3,2,1,0:T(8,128)(2,1)S(1)} %pad_maximum_fusion.2), channel_id=1, source_target_pairs={{0,8},{1,3},{2,10},{3,1},{4,12},{5,7},{6,14},{7,5},{8,0},{9,11},{1... | collective-permute-start | bytes 1769480 | tf_op jit(solution)/shard_map/ppermute | solution.py:218
  35.7 16.8 %collective-permute-start.14 = (bf16[4,4,72,128]{3,2,1,0:T(8,128)(2,1)S(1)}, bf16[4,4,72,128]{3,2,1,0:T(8,128)(2,1)}, u32[]{:S(2)}, u32[]{:S(2)}) collective-permute-start(bf16[4,4,72,128]{3,2,1,0:T(8,128)(2,1)S(1)} %get-tuple-element.19.refs_7_), channel_id=1, source_target_pairs={{0,1},{1,0},{2,3},{3,2},{4,5},{5,4},{6,7},{7,6},{8,9},{9,8},{10,11... | collective-permute-start | bytes 884744 | tf_op jit(solution)/shard_map/ppermute | solution.py:218
  43.1 11.7 %collective-permute-start.13 = (bf16[2,4,4,72,128]{4,3,2,1,0:T(8,128)(2,1)S(1)}, bf16[2,4,4,72,128]{4,3,2,1,0:T(8,128)(2,1)S(1)}, u32[]{:S(2)}, u32[]{:S(2)}) collective-permute-start(bf16[2,4,4,72,128]{4,3,2,1,0:T(8,128)(2,1)S(1)} %collective-permute-done.8.refs_6_), channel_id=1, source_target_pairs={{0,1},{1,0},{2,3},{3,2},{4,5},{5,4},{6,7},{7,6},{8,9},{9,8},{10,11... | collective-permute-start | bytes 1769480 | tf_op jit(solution)/shard_map/ppermute | solution.py:218
  49.8 5.1 %collective-permute-start.16 = (bf16[2,4,4,72,128]{4,3,2,1,0:T(8,128)(2,1)S(1)}, bf16[2,4,4,72,128]{4,3,2,1,0:T(8,128)(2,1)}, u32[]{:S(2)}, u32[]{:S(2)}) collective-permute-start(bf16[2,4,4,72,128]{4,3,2,1,0:T(8,128)(2,1)S(1)} %collective-permute-done.10.refs_9_), channel_id=1, source_target_pairs={{0,1},{1,0},{2,3},{3,2},{4,5},{5,4},{6,7},{7,6},{8,9},{9,8},{10,11... | collective-permute-start | bytes 1769480 | tf_op jit(solution)/shard_map/ppermute | solution.py:218
  52.0 2.0 %collective-permute-start.11 = (bf16[4,4,72,128]{3,2,1,0:T(8,128)(2,1)S(1)}, bf16[4,4,72,128]{3,2,1,0:T(8,128)(2,1)S(1)}, u32[]{:S(2)}, u32[]{:S(2)}) collective-permute-start(bf16[4,4,72,128]{3,2,1,0:T(8,128)(2,1)S(1)} %get-tuple-element.21.refs_4_), channel_id=1, source_target_pairs={{0,1},{1,0},{2,3},{3,2},{4,5},{5,4},{6,7},{7,6},{8,9},{9,8},{10,11... | collective-permute-start | bytes 884744 | tf_op jit(solution)/shard_map/ppermute | solution.py:218
  52.1 2.3 %collective-permute-start.15 = (bf16[4,4,72,128]{3,2,1,0:T(8,128)(2,1)S(1)}, bf16[4,4,72,128]{3,2,1,0:T(8,128)(2,1)S(1)}, u32[]{:S(2)}, u32[]{:S(2)}) collective-permute-start(bf16[4,4,72,128]{3,2,1,0:T(8,128)(2,1)S(1)} %collective-permute-done.9.refs_8_), channel_id=1, source_target_pairs={{0,1},{1,0},{2,3},{3,2},{4,5},{5,4},{6,7},{7,6},{8,9},{9,8},{10,11... | collective-permute-start | bytes 884744 | tf_op jit(solution)/shard_map/ppermute | solution.py:218
  52.6 2.3 %collective-permute-start.12 = (bf16[4,4,72,128]{3,2,1,0:T(8,128)(2,1)S(1)}, bf16[4,4,72,128]{3,2,1,0:T(8,128)(2,1)S(1)}, u32[]{:S(2)}, u32[]{:S(2)}) collective-permute-start(bf16[4,4,72,128]{3,2,1,0:T(8,128)(2,1)S(1)} %collective-permute-done.7.refs_5_), channel_id=1, source_target_pairs={{0,1},{1,0},{2,3},{3,2},{4,5},{5,4},{6,7},{7,6},{8,9},{9,8},{10,11... | collective-permute-start | bytes 884744 | tf_op jit(solution)/shard_map/ppermute | solution.py:218
  70.5 2.9 %collective-permute-start.18 = (bf16[2,2,4,4,72,128]{5,4,3,2,1,0:T(8,128)(2,1)S(1)}, bf16[2,2,4,4,72,128]{5,4,3,2,1,0:T(8,128)(2,1)S(1)}, u32[]{:S(2)}, u32[]{:S(2)}) collective-permute-start(bf16[2,2,4,4,72,128]{5,4,3,2,1,0:T(8,128)(2,1)S(1)} %bitcast.97), channel_id=1, source_target_pairs={{0,1},{1,0},{2,3},{3,2},{4,5},{5,4},{6,7},{7,6},{8,9},{9,8},{10,11... | collective-permute-start | bytes 3538952 | tf_op jit(solution)/shard_map/ppermute | solution.py:218
  70.9 6.0 %collective-permute-start.17 = (bf16[2,2,4,4,72,128]{5,4,3,2,1,0:T(8,128)(2,1)S(1)}, bf16[2,2,4,4,72,128]{5,4,3,2,1,0:T(8,128)(2,1)S(1)}, u32[]{:S(2)}, u32[]{:S(2)}) collective-permute-start(bf16[2,2,4,4,72,128]{5,4,3,2,1,0:T(8,128)(2,1)S(1)} %bitcast.96), channel_id=1, source_target_pairs={{0,1},{1,0},{2,3},{3,2},{4,5},{5,4},{6,7},{7,6},{8,9},{9,8},{10,11... | collective-permute-start | bytes 3538952 | tf_op jit(solution)/shard_map/ppermute | solution.py:218
  73.7 9.3 %collective-permute-start.21 = (bf16[2,4,4,72,128]{4,3,2,1,0:T(8,128)(2,1)S(1)}, bf16[2,4,4,72,128]{4,3,2,1,0:T(8,128)(2,1)S(1)}, u32[]{:S(2)}, u32[]{:S(2)}) collective-permute-start(bf16[2,4,4,72,128]{4,3,2,1,0:T(8,128)(2,1)S(1)} %get-tuple-element.13), channel_id=1, source_target_pairs={{0,8},{1,3},{2,10},{3,1},{4,12},{5,7},{6,14},{7,5},{8,0},{9,11},{1... | collective-permute-start | bytes 1769480 | tf_op jit(solution)/shard_map/ppermute | solution.py:218
  75.1 11.0 %collective-permute-start.19 = (bf16[2,4,4,72,128]{4,3,2,1,0:T(8,128)(2,1)S(1)}, bf16[2,4,4,72,128]{4,3,2,1,0:T(8,128)(2,1)S(1)}, u32[]{:S(2)}, u32[]{:S(2)}) collective-permute-start(bf16[2,4,4,72,128]{4,3,2,1,0:T(8,128)(2,1)S(1)} %get-tuple-element.14), channel_id=1, source_target_pairs={{0,24},{1,7},{2,26},{3,5},{4,28},{5,3},{6,30},{7,1},{8,16},{9,15},... | collective-permute-start | bytes 1769480 | tf_op jit(solution)/shard_map/ppermute | solution.py:218
  83.2 7.3 %collective-permute-start.22 = (bf16[4,4,72,128]{3,2,1,0:T(8,128)(2,1)S(1)}, bf16[4,4,72,128]{3,2,1,0:T(8,128)(2,1)S(1)}, u32[]{:S(2)}, u32[]{:S(2)}) collective-permute-start(bf16[4,4,72,128]{3,2,1,0:T(8,128)(2,1)S(1)} %fusion.3), channel_id=1, source_target_pairs={{0,24},{1,7},{2,26},{3,5},{4,28},{5,3},{6,30},{7,1},{8,16},{9,15},... | collective-permute-start | bytes 884744 | tf_op jit(solution)/shard_map/ppermute | solution.py:218
  90.7 6.0 %collective-permute-start.20 = (bf16[4,4,72,128]{3,2,1,0:T(8,128)(2,1)S(1)}, bf16[4,4,72,128]{3,2,1,0:T(8,128)(2,1)S(1)}, u32[]{:S(2)}, u32[]{:S(2)}) collective-permute-start(bf16[4,4,72,128]{3,2,1,0:T(8,128)(2,1)S(1)} %get-tuple-element.12), channel_id=1, source_target_pairs={{0,8},{1,3},{2,10},{3,1},{4,12},{5,7},{6,14},{7,5},{8,0},{9,11},{1... | collective-permute-start | bytes 884744 | tf_op jit(solution)/shard_map/ppermute | solution.py:218
  96.9 21.9 %copy-start.1 = (f32[1,72,128]{2,1,0:T(8,128)S(1)}, f32[1,72,128]{2,1,0:T(8,128)}, u32[]{:S(2)}) copy-start(f32[1,72,128]{2,1,0:T(8,128)} %param.8) | copy-start | bytes 110596
  97.0 21.9 %copy-start.2 = (f32[1,72,128]{2,1,0:T(8,128)S(1)}, f32[1,72,128]{2,1,0:T(8,128)}, u32[]{:S(2)}) copy-start(f32[1,72,128]{2,1,0:T(8,128)} %param.9) | copy-start | bytes 110596
  97.0 4.1 %collective-permute-start.23 = (bf16[8,72,128]{2,1,0:T(8,128)(2,1)S(1)}, bf16[8,72,128]{2,1,0:T(8,128)(2,1)S(1)}, u32[]{:S(2)}, u32[]{:S(2)}) collective-permute-start(bf16[8,72,128]{2,1,0:T(8,128)(2,1)S(1)} %get-tuple-element.15), channel_id=1, source_target_pairs={{0,2},{1,9},{2,0},{3,11},{4,6},{5,13},{6,4},{7,15},{8,10},{9,1},{1... | collective-permute-start | bytes 442376 | tf_op jit(solution)/shard_map/ppermute | solution.py:218
  97.1 5.5 %collective-permute-start.25 = (bf16[8,72,128]{2,1,0:T(8,128)(2,1)S(1)}, bf16[8,72,128]{2,1,0:T(8,128)(2,1)S(1)}, u32[]{:S(2)}, u32[]{:S(2)}) collective-permute-start(bf16[8,72,128]{2,1,0:T(8,128)(2,1)S(1)} %get-tuple-element.16), channel_id=1, source_target_pairs={{0,6},{1,25},{2,4},{3,27},{4,2},{5,29},{6,0},{7,31},{8,14},{9,17},... | collective-permute-start | bytes 442376 | tf_op jit(solution)/shard_map/ppermute | solution.py:218
  98.9 5.5 %collective-permute-start.24 = (bf16[8,72,128]{2,1,0:T(8,128)(2,1)S(1)}, bf16[8,72,128]{2,1,0:T(8,128)(2,1)S(1)}, u32[]{:S(2)}, u32[]{:S(2)}) collective-permute-start(bf16[8,72,128]{2,1,0:T(8,128)(2,1)S(1)} %get-tuple-element.17), channel_id=1, source_target_pairs={{0,4},{1,17},{2,6},{3,19},{4,0},{5,21},{6,2},{7,23},{8,12},{9,25},... | collective-permute-start | bytes 442376 | tf_op jit(solution)/shard_map/ppermute | solution.py:218

commit v6 on v5

--- a/solution.py
+++ b/solution.py
@@ -9,6 +9,7 @@
 INERTIA = 0.9
 ROUND = jnp.bfloat16
 VMEM = 24
+SMALL = 16
 
 
 ORDERS = ((0, 1, 3, 2), (0, 3, 1, 2))
@@ -28,20 +29,13 @@
     stays = (role == core).astype(jnp.int32)
     tables = []
     for part in range(2):
-        rank = rank_in(part, second)
-        late = 1 - rank // 2
-        tables.append((((stays * 2 + late) * 2 + part) * 2 + rank % 2) * sides + first)
+        turn = sides - 1 - rank_in(part, second)
+        tables.append(((stays * sides + turn) * 2 + part) * sides + first)
     return jnp.concatenate(tables).astype(jnp.int32)
 
 
-def slot_of(section, z):
-    apart = ((section >> 1) - (z >> 1)) & 3
-    pair = jnp.where(apart == 0, 0, jnp.where(apart == 3, 1, apart + 1))
-    return 2 * pair + ((section ^ z) & 1)
-
-
 def image_step(sides, sections, side, share, place, table, stream, cotangent, *refs):
-    gathered, refs = refs[:12], refs[12:]
+    gathered, refs = refs[:16], refs[16:]
     out, refs = refs[0], refs[1:]
     x_in, d_in, w_all, saved_p, slopes, fwd_pad, bwd_pad, line_pad, x_sem, w_sem = refs
     z, x, y, core = place[0], place[1], place[2], place[3]
@@ -64,9 +58,10 @@
     for which in range(2):
         role = core if which == 0 else 1 - core
         for part in range(2):
-            near, one, two = gathered[6 * which + 3 * part : 6 * which + 3 * part + 3]
+            sources = gathered[8 * which + 4 * part : 8 * which + 4 * part + 4]
             for i in range(sides):
-                for j, source in enumerate((near.at[i], one.at[i], two.at[0, i], two.at[1, i])):
+                for j in range(sides):
+                    source = sources[j].at[i]
                     where = lines(role, i, ORDERS[part][j])
                     target = w_all.at[pl.ds(part * slots, slots), where, :]
                     copies.append(pltpu.make_async_copy(source, target, w_sem.at[len(copies)]))
@@ -110,7 +105,7 @@
 
     def forward(s, pair):
         x1, x2 = pair
-        w = w_all.at[slot_of(s, z)]
+        w = w_all.at[s]
         p = activate(x2, 2 * s)
         low, high = around(p)
         band(fwd_pad, 0, low, p.astype(ROUND), high)
@@ -152,7 +147,7 @@
     def backward(step, pair):
         d1, d2 = pair
         s = sections - 1 - step
-        w = w_all.at[slot_of(s, z)]
+        w = w_all.at[s]
         d1 = d1 + spread(0, d2, w, s, half, 2 * s + 1)
         d2 = d2 + spread(1, d1, w, s, 0, 2 * s)
         return d1, d2
@@ -178,7 +173,7 @@
         grid_spec=pltpu.PrefetchScalarGridSpec(
             num_scalar_prefetch=2,
             grid=(1,),
-            in_specs=[far] * 14,
+            in_specs=[far] * 18,
             out_specs=pl.BlockSpec(memory_space=pltpu.VMEM),
             scratch_shapes=[
                 pltpu.VMEM((2, pixels, channels), jnp.float32),
@@ -198,16 +193,6 @@
     )(place, table, stream, cotangent, *gathered)
 
 
-def crossed_z(value):
-    n = lax.axis_size("section")
-    return lax.ppermute(value, "section", [(i, i ^ 1) for i in range(n)])
-
-
-def moved_z(value, by):
-    n = lax.axis_size("section")
-    return lax.ppermute(value, "section", [(i, (i + by) % n) for i in range(n)])
-
-
 def in_plane(sides, value, to):
     pairs = []
     for x in range(sides):
@@ -230,37 +215,79 @@
     return in_plane(sides, value, lambda x, y, c: (x, y, 1 - c))
 
 
-def gather_weights(mine, sides):
-    pair = jnp.stack([mine, crossed_z(mine)])
-    below = moved_z(pair, 2)
-    above = moved_z(pair, -2)
-    across = moved_z(below, 2)
-    line = jnp.stack([jnp.concatenate([pair, below]), jnp.concatenate([above, across])])
+def gather_weights(mine, early, sides):
+    sections = lax.axis_size("section")
+    line = jnp.broadcast_to(mine, (sections, *mine.shape))
+    line = lax.all_to_all(line, "section", 0, 0, tiled=True).reshape(2, -1, *mine.shape)
     came = [line] + [along_first(sides, line, mask) for mask in range(1, sides)]
     lines = [jnp.stack([got[part] for got in came]) for part in range(2)]
-    one = [along_second(sides, lines[part], (1, 3)[part]) for part in range(2)]
-    two = [along_second(sides, jnp.stack([lines[part], one[part]]), (3, 1)[part]) for part in range(2)]
-    own = [lines[0], one[0], two[0], lines[1], one[1], two[1]]
-    return own + [swapped(sides, block) for block in own]
+    wait = sum(nothing(value[0, : mine.shape[0]]) for value in early).astype(ROUND)
+    lines = [block + wait for block in lines]
+    with jax.named_scope("get_one"):
+        one = [along_second(sides, lines[part], ORDERS[part][1]) for part in range(2)]
+    with jax.named_scope("get_three"):
+        three = [along_second(sides, lines[part], ORDERS[part][2]) for part in range(2)]
+    with jax.named_scope("get_two"):
+        two = [along_second(sides, one[part], ORDERS[part][2]) for part in range(2)]
+    own = [block for part in range(2) for block in (lines[part], one[part], three[part], two[part])]
+    with jax.named_scope("share"):
+        theirs = []
+        for part in range(2):
+            line = lines[part] + nothing(one[part]).astype(ROUND)
+            theirs += [swapped(sides, block) for block in (line, one[part], three[part], two[part])]
+    return own + theirs
+
+
+def nothing(value):
+    return jnp.minimum(jnp.abs(value.astype(jnp.float32)), 0.0)
 
 
 def wide(value):
     return value.astype(jnp.float32)
 
 
+def added(blocks, which, swap, *came):
+    first = which[0][0]
+
+    def kernel(blocks, swap, *refs):
+        for at, (turn, part) in enumerate(which):
+            total = wide(blocks[1, turn, part]) + wide(swap[turn - first, part])
+            if came:
+                total = total + wide(refs[at][...])
+            refs[len(came) + at][...] = total.astype(ROUND)
+
+    near = pl.BlockSpec(memory_space=pltpu.VMEM)
+    return pl.pallas_call(
+        kernel,
+        out_shape=[jax.ShapeDtypeStruct(blocks.shape[3:], ROUND)] * len(which),
+        in_specs=[near] * (2 + len(came)),
+        out_specs=[near] * len(which),
+        compiler_params=pltpu.CompilerParams(vmem_limit_bytes=SMALL << 20),
+        name="added",
+    )(blocks, swap, *came)
+
+
 def scatter_grads(blocks, sides):
-    (passed_far, passed_near), (kept_far, kept_near) = blocks
-    far = swapped(sides, passed_far)
-    near = swapped(sides, passed_near)
-    came = []
-    for part in range(2):
-        out = (wide(kept_far[part]) + wide(far[part])).astype(ROUND)
-        came.append(along_second(sides, out, (3, 1)[part]))
+    passed = blocks[0]
+    with jax.named_scope("swap_far"):
+        far = swapped(sides, passed[:2])
+    with jax.named_scope("swap_near"):
+        near = swapped(sides, passed[2:])
+    two, three, one = [None] * 2, [None] * 2, [None] * 2
+    two[0], two[1], three[0], three[1] = added(blocks, ((0, 0), (0, 1), (1, 0), (1, 1)), far)
+    for part in range(2):
+        with jax.named_scope("sum_two"):
+            two[part] = along_second(sides, two[part], ORDERS[part][2])
+    for part in range(2):
+        with jax.named_scope("sum_three"):
+            three[part] = along_second(sides, three[part], ORDERS[part][2])
+    one = list(added(blocks, ((2, 0), (2, 1)), near, *two))
+    for part in range(2):
+        with jax.named_scope("sum_one"):
+            one[part] = along_second(sides, one[part], ORDERS[part][1])
     lines = []
     for part in range(2):
-        out = (wide(kept_near[part, 1]) + wide(near[part, 1]) + wide(came[part][1])).astype(ROUND)
-        last = along_second(sides, out, (1, 3)[part])
-        lines.append(wide(kept_near[part, 0]) + wide(near[part, 0]) + wide(came[part][0]) + wide(last))
+        lines.append(wide(blocks[1, 3, part]) + wide(near[1, part]) + wide(three[part]) + wide(one[part]))
     line = jnp.concatenate(lines, axis=1)
     total = line[0]
     line = line.astype(ROUND)
@@ -279,17 +306,23 @@
     z, at = lax.axis_index("section"), lax.axis_index("dp")
     place = jnp.stack([z, at // (2 * sides), at // 2 % sides, at % 2]).astype(jnp.int32)
     mine = lax.dynamic_slice_in_dim(weights[0], at * share, share, 0)
-    gathered = gather_weights(mine, sides)
     pair = (2, stream.shape[2] * stream.shape[3], channels)
     first, last = (lax.dynamic_slice_in_dim(v, z, 1, 1).reshape(pair) for v in (stream, cotangent))
+    gathered = gather_weights(mine, (first, last), sides)
     table = block_table(sides, *place[1:])
     blocks = image_grads(first, last, gathered, place, table, sides)
-    blocks = blocks.reshape(2, 2, 2, 2, sides, -1, share, channels)
+    blocks = blocks.reshape(2, sides, 2, sides, -1, share, channels)
     gradient = scatter_grads(blocks, sides) / images
     new_momentum = INERTIA * momentum[0] + gradient
     new_master = master[0] - STEP_SIZE * new_momentum
-    copies = jnp.broadcast_to(new_master.astype(ROUND)[None], (dp, share, channels))
-    new_weights = lax.all_to_all(copies, "dp", 0, 0, tiled=True).reshape(dp * share, channels)
+    chips = dp // 2
+    copies = jnp.broadcast_to(new_master.astype(ROUND)[None], (chips, share, channels))
+    same_core = [[2 * chip + core for chip in range(chips)] for core in range(2)]
+    own = lax.all_to_all(copies, "dp", 0, 0, tiled=True, axis_index_groups=same_core)
+    other = swapped(sides, own)
+    even = (at % 2 == 0)
+    both = [jnp.where(even, own, other), jnp.where(even, other, own)]
+    new_weights = jnp.stack(both, axis=1).reshape(dp * share, channels)
     return (new_master[None], new_momentum[None], new_weights[None])
 
 

time: 144 us -> 127 us (0.88)
  blocking collectives: 38 us -> 21.4 us
  waiting for transfers between devices: 39.3 us -> 33.3 us
  starting transfers between devices: 45 us -> 49.2 us
    all_to_all x1, blocking collectives: 23.6 us -> 10.9 us  [on_device(): lax.all_to_all(copies, 'dp', 0, 0, tiled=True, axis_index_groups=same_core)]
    ppermute x4 -> x0, starting transfers between devices: 9.29 us -> none  [the longest x3 6.82 us: moved_z(): return lax.ppermute(value, 'section', [(i, (i + by) % n) for i in range(n)])]
    all_to_all x0 -> x1, starting transfers between devices: none -> 9.01 us  [gather_weights(): lax.all_to_all(line, 'section', 0, 0, tiled=True)]
    all_to_all x0 -> x1, waiting for transfers between devices: none -> 6.83 us  [gather_weights(): lax.all_to_all(line, 'section', 0, 0, tiled=True)]
    ppermute x4 -> x0, waiting for transfers between devices: 6.47 us -> none  [the longest x3 5.33 us: moved_z(): return lax.ppermute(value, 'section', [(i, (i + by) % n) for i in range(n)])]
    ppermute x22 -> x29, waiting for transfers between devices: 32.9 us -> 26.5 us  [in_plane(): return lax.ppermute(value, 'dp', pairs)]
    ppermute x22 -> x29, starting transfers between devices: 35.7 us -> 40.2 us  [in_plane(): return lax.ppermute(value, 'dp', pairs)]
    all_to_all x1, blocking collectives: 14.4 us -> 10.5 us  [scatter_grads(): tiles = lax.all_to_all(total.astype(ROUND), 'section', 0, 0, tiled=True)]
  transfers between devices with their start and end apart: 26 -> 30, of which waited for: 18 -> 17; matrix products, arithmetic and copies ran while one was open for 1% -> 2% of each run, Pallas kernels for 0% -> 0%
where the time goes in v6:
time: 127 us; the launch traced here: 126 us
  starting transfers between devices  49.2 us (39%)
  waiting for transfers between devices  33.3 us (26%)
  blocking collectives  21.4 us (17%)
  Pallas kernels  15.2 us (12%)
  other arithmetic  3.22 us (3%)
  local copies, waits for them, and re-layouts  3.13 us (2%)
    ppermute x29, starting transfers between devices, in_plane(): return lax.ppermute(value, 'dp', pairs)  40.2 us
    ppermute x29, waiting for transfers between devices, in_plane(): return lax.ppermute(value, 'dp', pairs)  26.5 us
    pallas_call x1, Pallas kernels, image_grads(): pl.pallas_call(kernel, out_shape=jax.ShapeDtypeStruct((whole, share, chan...  14.8 us
    all_to_all x1, blocking collectives, on_device(): lax.all_to_all(copies, 'dp', 0, 0, tiled=True, axis_index_groups=same_core)  10.9 us
    all_to_all x1, blocking collectives, scatter_grads(): tiles = lax.all_to_all(total.astype(ROUND), 'section', 0, 0, tiled=True)  10.5 us
    all_to_all x1, starting transfers between devices, gather_weights(): lax.all_to_all(line, 'section', 0, 0, tiled=True)  9.01 us
    all_to_all x1, waiting for transfers between devices, gather_weights(): lax.all_to_all(line, 'section', 0, 0, tiled=True)  6.83 us
  transfers between devices with their start and end apart: 30, of which 17 were waited for; matrix products, arithmetic and copies ran while one was open for 2% of the time, Pallas kernels for 0%

profile of v6, /device:TPU:1, one launch (start us, length us, event | category | flops | bytes accessed | tf_op | source)
XLA Modules:
  0.0 126.3 jit_solution(883834059130085761)
XLA Ops:
  0.7 1.0 copy-done
  1.7 0.7 broadcast_in_dim.6
  2.4 9.0 %all-to-all-start = ((bf16[8,72,128]{2,1,0:T(8,128)(2,1)}), bf16[8,72,128]{2,1,0:T(8,128)(2,1)S(1)}, u32[]{:S(2)}, u32[]{:S(2)}) async-start(bf16[8,72,128]{2,1,0:T(8,128)(2,1)} %broadcast_in_dim.6), calls=%async_computation | async-start | bytes 294912 | tf_op jit(solution)/shard_map/all_to_all | solution.py:221
  11.4 1.1 constant_dynamic-slice_fusion
  12.5 6.8 %all-to-all-done = bf16[8,72,128]{2,1,0:T(8,128)(2,1)S(1)} async-done(((bf16[8,72,128]{2,1,0:T(8,128)(2,1)}), bf16[8,72,128]{2,1,0:T(8,128)(2,1)S(1)}, u32[]{:S(2)}, u32[]{:S(2)}) %all-to-all-start) | async-done | bytes 147488 | tf_op jit(solution)/shard_map/all_to_all | solution.py:221
  19.3 2.5 %collective-permute-start.2 = (bf16[2,4,72,128]{3,2,1,0:T(8,128)(2,1)S(1)}, bf16[2,4,72,128]{3,2,1,0:T(8,128)(2,1)S(1)}, u32[]{:S(2)}, u32[]{:S(2)}) collective-permute-start(bf16[2,4,72,128]{3,2,1,0:T(8,128)(2,1)S(1)} %bitcast.76), channel_id=1, source_target_pairs={{0,6},{1,25},{2,4},{3,27},{4,2},{5,29},{6,0},{7,31},{8,14},{9,17},... | collective-permute-start | bytes 442376 | tf_op jit(solution)/shard_map/ppermute | solution.py:203
  21.8 0.5 collective-permute-start.1
  22.6 2.9 %collective-permute-done.2 = bf16[2,4,72,128]{3,2,1,0:T(8,128)(2,1)S(1)} collective-permute-done((bf16[2,4,72,128]{3,2,1,0:T(8,128)(2,1)S(1)}, bf16[2,4,72,128]{3,2,1,0:T(8,128)(2,1)S(1)}, u32[]{:S(2)}, u32[]{:S(2)}) %collective-permute-start.2) | collective-permute-done | bytes 147488 | tf_op jit(solution)/shard_map/ppermute | solution.py:203
  25.5 1.8 %collective-permute-done.1 = bf16[2,4,72,128]{3,2,1,0:T(8,128)(2,1)S(1)} collective-permute-done((bf16[2,4,72,128]{3,2,1,0:T(8,128)(2,1)S(1)}, bf16[2,4,72,128]{3,2,1,0:T(8,128)(2,1)S(1)}, u32[]{:S(2)}, u32[]{:S(2)}) %collective-permute-start.1) | collective-permute-done | bytes 147488 | tf_op jit(solution)/shard_map/ppermute | solution.py:203
  27.4 1.4 %collective-permute-start.7 = (bf16[4,4,72,128]{3,2,1,0:T(8,128)(2,1)S(1)}, bf16[4,4,72,128]{3,2,1,0:T(8,128)(2,1)S(1)}, u32[]{:S(2)}, u32[]{:S(2)}) collective-permute-start(bf16[4,4,72,128]{3,2,1,0:T(8,128)(2,1)S(1)} %get-tuple-element.35.refs_8_), channel_id=1, source_target_pairs={{0,8},{1,3},{2,10},{3,1},{4,12},{5,7},{6,14},{7,5},{8,0},{9,11},{1... | collective-permute-start | bytes 884744 | tf_op jit(solution)/shard_map/get_three/ppermute | solution.py:203
  28.8 1.9 %collective-permute-start.6 = (bf16[4,4,72,128]{3,2,1,0:T(8,128)(2,1)S(1)}, bf16[4,4,72,128]{3,2,1,0:T(8,128)(2,1)S(1)}, u32[]{:S(2)}, u32[]{:S(2)}) collective-permute-start(bf16[4,4,72,128]{3,2,1,0:T(8,128)(2,1)S(1)} %get-tuple-element.35.refs_8_), channel_id=1, source_target_pairs={{0,24},{1,7},{2,26},{3,5},{4,28},{5,3},{6,30},{7,1},{8,16},{9,15},... | collective-permute-start | bytes 884744 | tf_op jit(solution)/shard_map/get_one/ppermute | solution.py:203
  30.7 0.8 collective-permute-start.4
  31.5 1.6 %collective-permute-done.7.refs_10_ = bf16[4,4,72,128]{3,2,1,0:T(8,128)(2,1)S(1)} collective-permute-done((bf16[4,4,72,128]{3,2,1,0:T(8,128)(2,1)S(1)}, bf16[4,4,72,128]{3,2,1,0:T(8,128)(2,1)S(1)}, u32[]{:S(2)}, u32[]{:S(2)}) %collective-permute-start.7) | collective-permute-done | bytes 294944 | tf_op jit(solution)/shard_map/get_three/ppermute | solution.py:203
  33.1 5.3 %collective-permute-start.15 = (bf16[4,4,72,128]{3,2,1,0:T(8,128)(2,1)S(1)}, bf16[4,4,72,128]{3,2,1,0:T(8,128)(2,1)S(1)}, u32[]{:S(2)}, u32[]{:S(2)}) collective-permute-start(bf16[4,4,72,128]{3,2,1,0:T(8,128)(2,1)S(1)} %collective-permute-done.7.refs_10_), channel_id=1, source_target_pairs={{0,1},{1,0},{2,3},{3,2},{4,5},{5,4},{6,7},{7,6},{8,9},{9,8},{10,11... | collective-permute-start | bytes 884744 | tf_op jit(solution)/shard_map/share/ppermute | solution.py:203
  38.4 0.8 fusion.6
  39.2 2.7 %collective-permute-start.13 = (bf16[4,4,72,128]{3,2,1,0:T(8,128)(2,1)}, bf16[4,4,72,128]{3,2,1,0:T(8,128)(2,1)S(1)}, u32[]{:S(2)}, u32[]{:S(2)}) collective-permute-start(bf16[4,4,72,128]{3,2,1,0:T(8,128)(2,1)} %fusion.6), channel_id=1, source_target_pairs={{0,1},{1,0},{2,3},{3,2},{4,5},{5,4},{6,7},{7,6},{8,9},{9,8},{10,11... | collective-permute-start | bytes 884744 | tf_op jit(solution)/shard_map/share/ppermute | solution.py:203
  41.9 0.9 collective-permute-start.8
  42.8 1.6 %collective-permute-start.5 = (bf16[4,4,72,128]{3,2,1,0:T(8,128)(2,1)S(1)}, bf16[4,4,72,128]{3,2,1,0:T(8,128)(2,1)}, u32[]{:S(2)}, u32[]{:S(2)}) collective-permute-start(bf16[4,4,72,128]{3,2,1,0:T(8,128)(2,1)S(1)} %collective-permute-done.3.refs_5_), channel_id=1, source_target_pairs={{0,24},{1,7},{2,26},{3,5},{4,28},{5,3},{6,30},{7,1},{8,16},{9,15},... | collective-permute-start | bytes 884744 | tf_op jit(solution)/shard_map/get_two/ppermute | solution.py:203
  44.6 2.0 %collective-permute-start.9 = (bf16[4,4,72,128]{3,2,1,0:T(8,128)(2,1)S(1)}, bf16[4,4,72,128]{3,2,1,0:T(8,128)(2,1)S(1)}, u32[]{:S(2)}, u32[]{:S(2)}) collective-permute-start(bf16[4,4,72,128]{3,2,1,0:T(8,128)(2,1)S(1)} %fusion.5), channel_id=1, source_target_pairs={{0,1},{1,0},{2,3},{3,2},{4,5},{5,4},{6,7},{7,6},{8,9},{9,8},{10,11... | collective-permute-start | bytes 884744 | tf_op jit(solution)/shard_map/share/ppermute | solution.py:203
  46.7 0.4 collective-permute-start.11
  47.1 0.8 collective-permute-done.8.refs_11_
  47.9 3.2 %collective-permute-start.16 = (bf16[4,4,72,128]{3,2,1,0:T(8,128)(2,1)}, bf16[4,4,72,128]{3,2,1,0:T(8,128)(2,1)S(1)}, u32[]{:S(2)}, u32[]{:S(2)}) collective-permute-start(bf16[4,4,72,128]{3,2,1,0:T(8,128)(2,1)} %collective-permute-done.8.refs_11_), channel_id=1, source_target_pairs={{0,1},{1,0},{2,3},{3,2},{4,5},{5,4},{6,7},{7,6},{8,9},{9,8},{10,11... | collective-permute-start | bytes 884744 | tf_op jit(solution)/shard_map/share/ppermute | solution.py:203
  51.1 1.2 collective-permute-start.12
  52.5 1.2 collective-permute-done.12.refs_15_
  53.7 14.8 %image_step.1 = bf16[256,72,128]{2,1,0:T(8,128)(2,1)S(1)} custom-call(s32[4]{0:T(128)S(1)} %pad_add_fusion.refs_0_, s32[64]{0:T(128)S(1)} %pad_add_fusion.1.refs_1_, f32[2,256,128]{2,1,0:T(8,128)S(1)} %bitcast.72, f32[2,256,128]{2,1,0:T(8,128)S(1)} %bitcast.70, bf16[4,4,72,128]{3,2,1,0:T(8,128)(2,1)S(1)} %get-tuple-element.36.refs_4_, ...), custom_call_target="tpu_custom_call" | custom-call | tf_op jit(solution)/shard_map/image_step/pallas_call | solution.py:170
  68.7 0.5 collective-permute-start.18
  69.3 2.3 %collective-permute-done.18.swap = bf16[2,2,4,4,72,128]{5,4,3,2,1,0:T(8,128)(2,1)S(1)} collective-permute-done((bf16[2,2,4,4,72,128]{5,4,3,2,1,0:T(8,128)(2,1)S(1)}, bf16[2,2,4,4,72,128]{5,4,3,2,1,0:T(8,128)(2,1)S(1)}, u32[]{:S(2)}, u32[]{:S(2)}) %collective-permute-start.18) | collective-permute-done | bytes 1179680 | tf_op jit(solution)/shard_map/swap_far/ppermute | solution.py:203
  71.9 2.1 %collective-permute-start.20 = (bf16[4,4,72,128]{3,2,1,0:T(8,128)(2,1)S(1)}, bf16[4,4,72,128]{3,2,1,0:T(8,128)(2,1)S(1)}, u32[]{:S(2)}, u32[]{:S(2)}) collective-permute-start(bf16[4,4,72,128]{3,2,1,0:T(8,128)(2,1)S(1)} %get-tuple-element.10), channel_id=1, source_target_pairs={{0,24},{1,7},{2,26},{3,5},{4,28},{5,3},{6,30},{7,1},{8,16},{9,15},... | collective-permute-start | bytes 884744 | tf_op jit(solution)/shard_map/sum_two/ppermute | solution.py:203
  74.0 0.9 collective-permute-start.19
  75.0 0.6 collective-permute-start.23
  75.5 3.5 %collective-permute-done.20.refs_0_ = bf16[4,4,72,128]{3,2,1,0:T(8,128)(2,1)S(1)} collective-permute-done((bf16[4,4,72,128]{3,2,1,0:T(8,128)(2,1)S(1)}, bf16[4,4,72,128]{3,2,1,0:T(8,128)(2,1)S(1)}, u32[]{:S(2)}, u32[]{:S(2)}) %collective-permute-start.20) | collective-permute-done | bytes 294944 | tf_op jit(solution)/shard_map/sum_two/ppermute | solution.py:203
  79.1 0.8 collective-permute-done.21.refs_1_
  80.2 1.3 %collective-permute-start.24 = (bf16[4,4,72,128]{3,2,1,0:T(8,128)(2,1)S(1)}, bf16[4,4,72,128]{3,2,1,0:T(8,128)(2,1)S(1)}, u32[]{:S(2)}, u32[]{:S(2)}) collective-permute-start(bf16[4,4,72,128]{3,2,1,0:T(8,128)(2,1)S(1)} %get-tuple-element.14), channel_id=1, source_target_pairs={{0,24},{1,7},{2,26},{3,5},{4,28},{5,3},{6,30},{7,1},{8,16},{9,15},... | collective-permute-start | bytes 884744 | tf_op jit(solution)/shard_map/sum_one/ppermute | solution.py:203
  81.5 0.7 collective-permute-done.19
  82.2 0.8 collective-permute-done.23
  83.1 3.2 %collective-permute-done.22 = bf16[4,4,72,128]{3,2,1,0:T(8,128)(2,1)S(1)} collective-permute-done((bf16[4,4,72,128]{3,2,1,0:T(8,128)(2,1)S(1)}, bf16[4,4,72,128]{3,2,1,0:T(8,128)(2,1)S(1)}, u32[]{:S(2)}, u32[]{:S(2)}) %collective-permute-start.22) | collective-permute-done | bytes 294944 | tf_op jit(solution)/shard_map/sum_one/ppermute | solution.py:203
  86.2 1.2 collective-permute-done.24
  88.1 1.8 %collective-permute-start.27 = (bf16[8,72,128]{2,1,0:T(8,128)(2,1)S(1)}, bf16[8,72,128]{2,1,0:T(8,128)(2,1)S(1)}, u32[]{:S(2)}, u32[]{:S(2)}) collective-permute-start(bf16[8,72,128]{2,1,0:T(8,128)(2,1)S(1)} %get-tuple-element.25), channel_id=1, source_target_pairs={{0,6},{1,25},{2,4},{3,27},{4,2},{5,29},{6,0},{7,31},{8,14},{9,17},... | collective-permute-start | bytes 442376 | tf_op jit(solution)/shard_map/ppermute | solution.py:203
  90.0 1.2 collective-permute-start.26
  91.1 0.7 collective-permute-done.25
  91.9 1.7 %collective-permute-done.27 = bf16[8,72,128]{2,1,0:T(8,128)(2,1)S(1)} collective-permute-done((bf16[8,72,128]{2,1,0:T(8,128)(2,1)S(1)}, bf16[8,72,128]{2,1,0:T(8,128)(2,1)S(1)}, u32[]{:S(2)}, u32[]{:S(2)}) %collective-permute-start.27) | collective-permute-done | bytes 147488 | tf_op jit(solution)/shard_map/ppermute | solution.py:203
  93.6 1.8 %collective-permute-done.26 = bf16[8,72,128]{2,1,0:T(8,128)(2,1)S(1)} collective-permute-done((bf16[8,72,128]{2,1,0:T(8,128)(2,1)S(1)}, bf16[8,72,128]{2,1,0:T(8,128)(2,1)S(1)}, u32[]{:S(2)}, u32[]{:S(2)}) %collective-permute-start.26) | collective-permute-done | bytes 147488 | tf_op jit(solution)/shard_map/ppermute | solution.py:203
  95.5 10.5 %all_to_all.15 = bf16[8,72,128]{2,1,0:T(8,128)(2,1)S(1)} all-to-all(bf16[8,72,128]{2,1,0:T(8,128)(2,1)S(1)} %fusion.12), channel_id=1, replica_groups=mesh['section'=8,'dp'=32] {'section'}, dimensions={0} | all-to-all | bytes 294912 | tf_op jit(solution)/shard_map/all_to_all | solution.py:296
  106.1 0.6 convert_bitcast_fusion
  106.8 10.9 %all_to_all.16 = bf16[16,72,128]{2,1,0:T(8,128)(2,1)S(1)} all-to-all(bf16[16,72,128]{2,1,0:T(8,128)(2,1)S(1)} %broadcast_in_dim.8), channel_id=1, replica_groups={{0,2,4,6,8,10,12,14,16,18,20,22,24,26,28,30},{1,3,5,7,9,11,13,15,17,19,..., dimensions={0} | all-to-all | bytes 589824 | tf_op jit(solution)/shard_map/all_to_all | solution.py:321
  117.6 6.6 %collective-permute-start.28 = (bf16[16,72,128]{2,1,0:T(8,128)(2,1)S(1)}, bf16[16,72,128]{2,1,0:T(8,128)(2,1)S(1)}, u32[]{:S(2)}, u32[]{:S(2)}) collective-permute-start(bf16[16,72,128]{2,1,0:T(8,128)(2,1)S(1)} %all_to_all.16), channel_id=1, source_target_pairs={{0,1},{1,0},{2,3},{3,2},{4,5},{5,4},{6,7},{7,6},{8,9},{9,8},{10,11... | collective-permute-start | bytes 884744 | tf_op jit(solution)/shard_map/ppermute | solution.py:203
  124.2 1.2 collective-permute-done.28
  125.5 0.9 pad_maximum_fusion.1
  (47 shorter events, 2.7 us)
Async XLA Ops:
  0.6 1.1 copy-start
  2.4 16.9 %all-to-all-start = ((bf16[8,72,128]{2,1,0:T(8,128)(2,1)}), bf16[8,72,128]{2,1,0:T(8,128)(2,1)S(1)}, u32[]{:S(2)}, u32[]{:S(2)}) async-start(bf16[8,72,128]{2,1,0:T(8,128)(2,1)} %broadcast_in_dim.6), calls=%async_computation | async-start | bytes 294912 | tf_op jit(solution)/shard_map/all_to_all | solution.py:221
  19.3 6.1 %collective-permute-start.2 = (bf16[2,4,72,128]{3,2,1,0:T(8,128)(2,1)S(1)}, bf16[2,4,72,128]{3,2,1,0:T(8,128)(2,1)S(1)}, u32[]{:S(2)}, u32[]{:S(2)}) collective-permute-start(bf16[2,4,72,128]{3,2,1,0:T(8,128)(2,1)S(1)} %bitcast.76), channel_id=1, source_target_pairs={{0,6},{1,25},{2,4},{3,27},{4,2},{5,29},{6,0},{7,31},{8,14},{9,17},... | collective-permute-start | bytes 442376 | tf_op jit(solution)/shard_map/ppermute | solution.py:203
  21.8 5.5 %collective-permute-start.1 = (bf16[2,4,72,128]{3,2,1,0:T(8,128)(2,1)S(1)}, bf16[2,4,72,128]{3,2,1,0:T(8,128)(2,1)S(1)}, u32[]{:S(2)}, u32[]{:S(2)}) collective-permute-start(bf16[2,4,72,128]{3,2,1,0:T(8,128)(2,1)S(1)} %bitcast.77), channel_id=1, source_target_pairs={{0,4},{1,17},{2,6},{3,19},{4,0},{5,21},{6,2},{7,23},{8,12},{9,25},... | collective-permute-start | bytes 442376 | tf_op jit(solution)/shard_map/ppermute | solution.py:203
  22.3 5.0 %collective-permute-start = (bf16[2,4,72,128]{3,2,1,0:T(8,128)(2,1)S(1)}, bf16[2,4,72,128]{3,2,1,0:T(8,128)(2,1)S(1)}, u32[]{:S(2)}, u32[]{:S(2)}) collective-permute-start(bf16[2,4,72,128]{3,2,1,0:T(8,128)(2,1)S(1)} %bitcast.78), channel_id=1, source_target_pairs={{0,2},{1,9},{2,0},{3,11},{4,6},{5,13},{6,4},{7,15},{8,10},{9,1},{1... | collective-permute-start | bytes 442376 | tf_op jit(solution)/shard_map/ppermute | solution.py:203
  27.4 5.7 %collective-permute-start.7 = (bf16[4,4,72,128]{3,2,1,0:T(8,128)(2,1)S(1)}, bf16[4,4,72,128]{3,2,1,0:T(8,128)(2,1)S(1)}, u32[]{:S(2)}, u32[]{:S(2)}) collective-permute-start(bf16[4,4,72,128]{3,2,1,0:T(8,128)(2,1)S(1)} %get-tuple-element.35.refs_8_), channel_id=1, source_target_pairs={{0,8},{1,3},{2,10},{3,1},{4,12},{5,7},{6,14},{7,5},{8,0},{9,11},{1... | collective-permute-start | bytes 884744 | tf_op jit(solution)/shard_map/get_three/ppermute | solution.py:203
  28.8 9.6 %collective-permute-start.6 = (bf16[4,4,72,128]{3,2,1,0:T(8,128)(2,1)S(1)}, bf16[4,4,72,128]{3,2,1,0:T(8,128)(2,1)S(1)}, u32[]{:S(2)}, u32[]{:S(2)}) collective-permute-start(bf16[4,4,72,128]{3,2,1,0:T(8,128)(2,1)S(1)} %get-tuple-element.35.refs_8_), channel_id=1, source_target_pairs={{0,24},{1,7},{2,26},{3,5},{4,28},{5,3},{6,30},{7,1},{8,16},{9,15},... | collective-permute-start | bytes 884744 | tf_op jit(solution)/shard_map/get_one/ppermute | solution.py:203
  30.7 11.2 %collective-permute-start.4 = (bf16[4,4,72,128]{3,2,1,0:T(8,128)(2,1)S(1)}, bf16[4,4,72,128]{3,2,1,0:T(8,128)(2,1)S(1)}, u32[]{:S(2)}, u32[]{:S(2)}) collective-permute-start(bf16[4,4,72,128]{3,2,1,0:T(8,128)(2,1)S(1)} %get-tuple-element.36.refs_4_), channel_id=1, source_target_pairs={{0,24},{1,7},{2,26},{3,5},{4,28},{5,3},{6,30},{7,1},{8,16},{9,15},... | collective-permute-start | bytes 884744 | tf_op jit(solution)/shard_map/get_three/ppermute | solution.py:203
  31.5 11.3 %collective-permute-start.3 = (bf16[4,4,72,128]{3,2,1,0:T(8,128)(2,1)S(1)}, bf16[4,4,72,128]{3,2,1,0:T(8,128)(2,1)S(1)}, u32[]{:S(2)}, u32[]{:S(2)}) collective-permute-start(bf16[4,4,72,128]{3,2,1,0:T(8,128)(2,1)S(1)} %get-tuple-element.36.refs_4_), channel_id=1, source_target_pairs={{0,8},{1,3},{2,10},{3,1},{4,12},{5,7},{6,14},{7,5},{8,0},{9,11},{1... | collective-permute-start | bytes 884744 | tf_op jit(solution)/shard_map/get_one/ppermute | solution.py:203
  33.1 11.5 %collective-permute-start.15 = (bf16[4,4,72,128]{3,2,1,0:T(8,128)(2,1)S(1)}, bf16[4,4,72,128]{3,2,1,0:T(8,128)(2,1)S(1)}, u32[]{:S(2)}, u32[]{:S(2)}) collective-permute-start(bf16[4,4,72,128]{3,2,1,0:T(8,128)(2,1)S(1)} %collective-permute-done.7.refs_10_), channel_id=1, source_target_pairs={{0,1},{1,0},{2,3},{3,2},{4,5},{5,4},{6,7},{7,6},{8,9},{9,8},{10,11... | collective-permute-start | bytes 884744 | tf_op jit(solution)/shard_map/share/ppermute | solution.py:203
  39.2 7.4 %collective-permute-start.13 = (bf16[4,4,72,128]{3,2,1,0:T(8,128)(2,1)}, bf16[4,4,72,128]{3,2,1,0:T(8,128)(2,1)S(1)}, u32[]{:S(2)}, u32[]{:S(2)}) collective-permute-start(bf16[4,4,72,128]{3,2,1,0:T(8,128)(2,1)} %fusion.6), channel_id=1, source_target_pairs={{0,1},{1,0},{2,3},{3,2},{4,5},{5,4},{6,7},{7,6},{8,9},{9,8},{10,11... | collective-permute-start | bytes 884744 | tf_op jit(solution)/shard_map/share/ppermute | solution.py:203
  41.9 4.8 %collective-permute-start.14 = (bf16[4,4,72,128]{3,2,1,0:T(8,128)(2,1)S(1)}, bf16[4,4,72,128]{3,2,1,0:T(8,128)(2,1)}, u32[]{:S(2)}, u32[]{:S(2)}) collective-permute-start(bf16[4,4,72,128]{3,2,1,0:T(8,128)(2,1)S(1)} %collective-permute-done.6.refs_9_), channel_id=1, source_target_pairs={{0,1},{1,0},{2,3},{3,2},{4,5},{5,4},{6,7},{7,6},{8,9},{9,8},{10,11... | collective-permute-start | bytes 884744 | tf_op jit(solution)/shard_map/share/ppermute | solution.py:203
  41.9 6.0 %collective-permute-start.8 = (bf16[4,4,72,128]{3,2,1,0:T(8,128)(2,1)S(1)}, bf16[4,4,72,128]{3,2,1,0:T(8,128)(2,1)}, u32[]{:S(2)}, u32[]{:S(2)}) collective-permute-start(bf16[4,4,72,128]{3,2,1,0:T(8,128)(2,1)S(1)} %collective-permute-done.6.refs_9_), channel_id=1, source_target_pairs={{0,8},{1,3},{2,10},{3,1},{4,12},{5,7},{6,14},{7,5},{8,0},{9,11},{1... | collective-permute-start | bytes 884744 | tf_op jit(solution)/shard_map/get_two/ppermute | solution.py:203
  42.8 8.2 %collective-permute-start.5 = (bf16[4,4,72,128]{3,2,1,0:T(8,128)(2,1)S(1)}, bf16[4,4,72,128]{3,2,1,0:T(8,128)(2,1)}, u32[]{:S(2)}, u32[]{:S(2)}) collective-permute-start(bf16[4,4,72,128]{3,2,1,0:T(8,128)(2,1)S(1)} %collective-permute-done.3.refs_5_), channel_id=1, source_target_pairs={{0,24},{1,7},{2,26},{3,5},{4,28},{5,3},{6,30},{7,1},{8,16},{9,15},... | collective-permute-start | bytes 884744 | tf_op jit(solution)/shard_map/get_two/ppermute | solution.py:203
  44.6 7.9 %collective-permute-start.9 = (bf16[4,4,72,128]{3,2,1,0:T(8,128)(2,1)S(1)}, bf16[4,4,72,128]{3,2,1,0:T(8,128)(2,1)S(1)}, u32[]{:S(2)}, u32[]{:S(2)}) collective-permute-start(bf16[4,4,72,128]{3,2,1,0:T(8,128)(2,1)S(1)} %fusion.5), channel_id=1, source_target_pairs={{0,1},{1,0},{2,3},{3,2},{4,5},{5,4},{6,7},{7,6},{8,9},{9,8},{10,11... | collective-permute-start | bytes 884744 | tf_op jit(solution)/shard_map/share/ppermute | solution.py:203
  46.6 5.9 %collective-permute-start.10 = (bf16[4,4,72,128]{3,2,1,0:T(8,128)(2,1)S(1)}, bf16[4,4,72,128]{3,2,1,0:T(8,128)(2,1)S(1)}, u32[]{:S(2)}, u32[]{:S(2)}) collective-permute-start(bf16[4,4,72,128]{3,2,1,0:T(8,128)(2,1)S(1)} %collective-permute-done.3.refs_5_), channel_id=1, source_target_pairs={{0,1},{1,0},{2,3},{3,2},{4,5},{5,4},{6,7},{7,6},{8,9},{9,8},{10,11... | collective-permute-start | bytes 884744 | tf_op jit(solution)/shard_map/share/ppermute | solution.py:203
  46.7 5.8 %collective-permute-start.11 = (bf16[4,4,72,128]{3,2,1,0:T(8,128)(2,1)S(1)}, bf16[4,4,72,128]{3,2,1,0:T(8,128)(2,1)S(1)}, u32[]{:S(2)}, u32[]{:S(2)}) collective-permute-start(bf16[4,4,72,128]{3,2,1,0:T(8,128)(2,1)S(1)} %collective-permute-done.4.refs_6_), channel_id=1, source_target_pairs={{0,1},{1,0},{2,3},{3,2},{4,5},{5,4},{6,7},{7,6},{8,9},{9,8},{10,11... | collective-permute-start | bytes 884744 | tf_op jit(solution)/shard_map/share/ppermute | solution.py:203
  47.9 4.6 %collective-permute-start.16 = (bf16[4,4,72,128]{3,2,1,0:T(8,128)(2,1)}, bf16[4,4,72,128]{3,2,1,0:T(8,128)(2,1)S(1)}, u32[]{:S(2)}, u32[]{:S(2)}) collective-permute-start(bf16[4,4,72,128]{3,2,1,0:T(8,128)(2,1)} %collective-permute-done.8.refs_11_), channel_id=1, source_target_pairs={{0,1},{1,0},{2,3},{3,2},{4,5},{5,4},{6,7},{7,6},{8,9},{9,8},{10,11... | collective-permute-start | bytes 884744 | tf_op jit(solution)/shard_map/share/ppermute | solution.py:203
  51.1 2.6 %collective-permute-start.12 = (bf16[4,4,72,128]{3,2,1,0:T(8,128)(2,1)}, bf16[4,4,72,128]{3,2,1,0:T(8,128)(2,1)S(1)}, u32[]{:S(2)}, u32[]{:S(2)}) collective-permute-start(bf16[4,4,72,128]{3,2,1,0:T(8,128)(2,1)} %collective-permute-done.5.refs_7_), channel_id=1, source_target_pairs={{0,1},{1,0},{2,3},{3,2},{4,5},{5,4},{6,7},{7,6},{8,9},{9,8},{10,11... | collective-permute-start | bytes 884744 | tf_op jit(solution)/shard_map/share/ppermute | solution.py:203
  68.7 2.9 %collective-permute-start.18 = (bf16[2,2,4,4,72,128]{5,4,3,2,1,0:T(8,128)(2,1)S(1)}, bf16[2,2,4,4,72,128]{5,4,3,2,1,0:T(8,128)(2,1)S(1)}, u32[]{:S(2)}, u32[]{:S(2)}) collective-permute-start(bf16[2,2,4,4,72,128]{5,4,3,2,1,0:T(8,128)(2,1)S(1)} %bitcast.74), channel_id=1, source_target_pairs={{0,1},{1,0},{2,3},{3,2},{4,5},{5,4},{6,7},{7,6},{8,9},{9,8},{10,11... | collective-permute-start | bytes 3538952 | tf_op jit(solution)/shard_map/swap_far/ppermute | solution.py:203
  69.1 6.4 %collective-permute-start.17 = (bf16[2,2,4,4,72,128]{5,4,3,2,1,0:T(8,128)(2,1)S(1)}, bf16[2,2,4,4,72,128]{5,4,3,2,1,0:T(8,128)(2,1)S(1)}, u32[]{:S(2)}, u32[]{:S(2)}) collective-permute-start(bf16[2,2,4,4,72,128]{5,4,3,2,1,0:T(8,128)(2,1)S(1)} %bitcast.73), channel_id=1, source_target_pairs={{0,1},{1,0},{2,3},{3,2},{4,5},{5,4},{6,7},{7,6},{8,9},{9,8},{10,11... | collective-permute-start | bytes 3538952 | tf_op jit(solution)/shard_map/swap_near/ppermute | solution.py:203
  71.9 7.2 %collective-permute-start.20 = (bf16[4,4,72,128]{3,2,1,0:T(8,128)(2,1)S(1)}, bf16[4,4,72,128]{3,2,1,0:T(8,128)(2,1)S(1)}, u32[]{:S(2)}, u32[]{:S(2)}) collective-permute-start(bf16[4,4,72,128]{3,2,1,0:T(8,128)(2,1)S(1)} %get-tuple-element.10), channel_id=1, source_target_pairs={{0,24},{1,7},{2,26},{3,5},{4,28},{5,3},{6,30},{7,1},{8,16},{9,15},... | collective-permute-start | bytes 884744 | tf_op jit(solution)/shard_map/sum_two/ppermute | solution.py:203
  74.0 5.9 %collective-permute-start.21 = (bf16[4,4,72,128]{3,2,1,0:T(8,128)(2,1)S(1)}, bf16[4,4,72,128]{3,2,1,0:T(8,128)(2,1)S(1)}, u32[]{:S(2)}, u32[]{:S(2)}) collective-permute-start(bf16[4,4,72,128]{3,2,1,0:T(8,128)(2,1)S(1)} %get-tuple-element.11), channel_id=1, source_target_pairs={{0,8},{1,3},{2,10},{3,1},{4,12},{5,7},{6,14},{7,5},{8,0},{9,11},{1... | collective-permute-start | bytes 884744 | tf_op jit(solution)/shard_map/sum_two/ppermute | solution.py:203
  74.0 8.2 %collective-permute-start.19 = (bf16[4,4,72,128]{3,2,1,0:T(8,128)(2,1)S(1)}, bf16[4,4,72,128]{3,2,1,0:T(8,128)(2,1)S(1)}, u32[]{:S(2)}, u32[]{:S(2)}) collective-permute-start(bf16[4,4,72,128]{3,2,1,0:T(8,128)(2,1)S(1)} %get-tuple-element.9), channel_id=1, source_target_pairs={{0,24},{1,7},{2,26},{3,5},{4,28},{5,3},{6,30},{7,1},{8,16},{9,15},... | collective-permute-start | bytes 884744 | tf_op jit(solution)/shard_map/sum_three/ppermute | solution.py:203
  75.0 8.1 %collective-permute-start.23 = (bf16[4,4,72,128]{3,2,1,0:T(8,128)(2,1)S(1)}, bf16[4,4,72,128]{3,2,1,0:T(8,128)(2,1)S(1)}, u32[]{:S(2)}, u32[]{:S(2)}) collective-permute-start(bf16[4,4,72,128]{3,2,1,0:T(8,128)(2,1)S(1)} %get-tuple-element.13), channel_id=1, source_target_pairs={{0,8},{1,3},{2,10},{3,1},{4,12},{5,7},{6,14},{7,5},{8,0},{9,11},{1... | collective-permute-start | bytes 884744 | tf_op jit(solution)/shard_map/sum_three/ppermute | solution.py:203
  80.1 6.1 %collective-permute-start.22 = (bf16[4,4,72,128]{3,2,1,0:T(8,128)(2,1)S(1)}, bf16[4,4,72,128]{3,2,1,0:T(8,128)(2,1)S(1)}, u32[]{:S(2)}, u32[]{:S(2)}) collective-permute-start(bf16[4,4,72,128]{3,2,1,0:T(8,128)(2,1)S(1)} %get-tuple-element.12), channel_id=1, source_target_pairs={{0,8},{1,3},{2,10},{3,1},{4,12},{5,7},{6,14},{7,5},{8,0},{9,11},{1... | collective-permute-start | bytes 884744 | tf_op jit(solution)/shard_map/sum_one/ppermute | solution.py:203
  80.2 7.2 %collective-permute-start.24 = (bf16[4,4,72,128]{3,2,1,0:T(8,128)(2,1)S(1)}, bf16[4,4,72,128]{3,2,1,0:T(8,128)(2,1)S(1)}, u32[]{:S(2)}, u32[]{:S(2)}) collective-permute-start(bf16[4,4,72,128]{3,2,1,0:T(8,128)(2,1)S(1)} %get-tuple-element.14), channel_id=1, source_target_pairs={{0,24},{1,7},{2,26},{3,5},{4,28},{5,3},{6,30},{7,1},{8,16},{9,15},... | collective-permute-start | bytes 884744 | tf_op jit(solution)/shard_map/sum_one/ppermute | solution.py:203
  87.8 18.3 %copy-start.1 = (f32[1,72,128]{2,1,0:T(8,128)S(1)}, f32[1,72,128]{2,1,0:T(8,128)}, u32[]{:S(2)}) copy-start(f32[1,72,128]{2,1,0:T(8,128)} %param.8) | copy-start | bytes 110596
  87.8 18.3 %copy-start.2 = (f32[1,72,128]{2,1,0:T(8,128)S(1)}, f32[1,72,128]{2,1,0:T(8,128)}, u32[]{:S(2)}) copy-start(f32[1,72,128]{2,1,0:T(8,128)} %param.9) | copy-start | bytes 110596
  87.8 4.1 %collective-permute-start.25 = (bf16[8,72,128]{2,1,0:T(8,128)(2,1)S(1)}, bf16[8,72,128]{2,1,0:T(8,128)(2,1)S(1)}, u32[]{:S(2)}, u32[]{:S(2)}) collective-permute-start(bf16[8,72,128]{2,1,0:T(8,128)(2,1)S(1)} %get-tuple-element.24), channel_id=1, source_target_pairs={{0,2},{1,9},{2,0},{3,11},{4,6},{5,13},{6,4},{7,15},{8,10},{9,1},{1... | collective-permute-start | bytes 442376 | tf_op jit(solution)/shard_map/ppermute | solution.py:203
  88.1 5.5 %collective-permute-start.27 = (bf16[8,72,128]{2,1,0:T(8,128)(2,1)S(1)}, bf16[8,72,128]{2,1,0:T(8,128)(2,1)S(1)}, u32[]{:S(2)}, u32[]{:S(2)}) collective-permute-start(bf16[8,72,128]{2,1,0:T(8,128)(2,1)S(1)} %get-tuple-element.25), channel_id=1, source_target_pairs={{0,6},{1,25},{2,4},{3,27},{4,2},{5,29},{6,0},{7,31},{8,14},{9,17},... | collective-permute-start | bytes 442376 | tf_op jit(solution)/shard_map/ppermute | solution.py:203
  90.0 5.5 %collective-permute-start.26 = (bf16[8,72,128]{2,1,0:T(8,128)(2,1)S(1)}, bf16[8,72,128]{2,1,0:T(8,128)(2,1)S(1)}, u32[]{:S(2)}, u32[]{:S(2)}) collective-permute-start(bf16[8,72,128]{2,1,0:T(8,128)(2,1)S(1)} %get-tuple-element.26), channel_id=1, source_target_pairs={{0,4},{1,17},{2,6},{3,19},{4,0},{5,21},{6,2},{7,23},{8,12},{9,25},... | collective-permute-start | bytes 442376 | tf_op jit(solution)/shard_map/ppermute | solution.py:203
  117.6 7.8 %collective-permute-start.28 = (bf16[16,72,128]{2,1,0:T(8,128)(2,1)S(1)}, bf16[16,72,128]{2,1,0:T(8,128)(2,1)S(1)}, u32[]{:S(2)}, u32[]{:S(2)}) collective-permute-start(bf16[16,72,128]{2,1,0:T(8,128)(2,1)S(1)} %all_to_all.16), channel_id=1, source_target_pairs={{0,1},{1,0},{2,3},{3,2},{4,5},{5,4},{6,7},{7,6},{8,9},{9,8},{10,11... | collective-permute-start | bytes 884744 | tf_op jit(solution)/shard_map/ppermute | solution.py:203

commit v7 on v6

--- a/solution.py
+++ b/solution.py
@@ -34,8 +34,12 @@
     return jnp.concatenate(tables).astype(jnp.int32)
 
 
+def in_strips(value, product):
+    return jnp.concatenate([product(part) for part in jnp.split(value, 2)], axis=0)
+
+
 def image_step(sides, sections, side, share, place, table, stream, cotangent, *refs):
-    gathered, refs = refs[:16], refs[16:]
+    gathered, refs = refs[:8], refs[8:]
     out, refs = refs[0], refs[1:]
     x_in, d_in, w_all, saved_p, slopes, fwd_pad, bwd_pad, line_pad, x_sem, w_sem = refs
     z, x, y, core = place[0], place[1], place[2], place[3]
@@ -55,16 +59,15 @@
         return pl.ds(start, share)
 
     copies = []
-    for which in range(2):
-        role = core if which == 0 else 1 - core
-        for part in range(2):
-            sources = gathered[8 * which + 4 * part : 8 * which + 4 * part + 4]
+    for part in range(2):
+        for which, role in ((0, core), (4, 1 - core)):
+            early, late = gathered[which + part], gathered[which + 2 + part]
+            sources = early.at[0], early.at[1], late.at[0], late.at[1]
             for i in range(sides):
                 for j in range(sides):
-                    source = sources[j].at[i]
                     where = lines(role, i, ORDERS[part][j])
                     target = w_all.at[pl.ds(part * slots, slots), where, :]
-                    copies.append(pltpu.make_async_copy(source, target, w_sem.at[len(copies)]))
+                    copies.append(pltpu.make_async_copy(sources[j].at[i], target, w_sem.at[len(copies)]))
 
     x_copy.start()
     for copy in copies:
@@ -94,7 +97,7 @@
 
     def conv(pad, k, w):
         taps = jnp.concatenate([pad[k, a * side : a * side + pixels, :] for a in range(3)], axis=1)
-        return jnp.dot(taps, w, preferred_element_type=jnp.float32)
+        return in_strips(taps, lambda v: jnp.dot(v, w, preferred_element_type=jnp.float32))
 
     def activate(v, at):
         logistic = 1.0 / (1.0 + jnp.exp(-v))
@@ -117,9 +120,12 @@
         return y1, y2
 
     x_copy.wait()
-    for copy in copies:
-        copy.wait()
-    lax.fori_loop(0, sections, forward, (x_in[0], x_in[1]), unroll=True)
+    pair = x_in[0], x_in[1]
+    for s in range(sections):
+        if s % slots == 0:
+            for copy in copies[s // slots * len(copies) // 2 : (s // slots + 1) * len(copies) // 2]:
+                copy.wait()
+        pair = forward(s, pair)
 
     def spread(k, e, w, s, base, at):
         low, high = around(e)
@@ -130,7 +136,10 @@
         across = jnp.concatenate(
             [w[base + tap * channels : base + (tap + 1) * channels, :] for tap in range(9)], axis=1
         )
-        total = lax.dot_general(taps, across, (((1,), (1,)), ((), ())), preferred_element_type=jnp.float32)
+        total = in_strips(
+            taps,
+            lambda v: lax.dot_general(v, across, (((1,), (1,)), ((), ())), preferred_element_type=jnp.float32),
+        )
         wgrad = jnp.dot(saved_p[at], taps, preferred_element_type=jnp.float32)
         for tap in range(9):
             row, end = base + tap * channels, base + (tap + 1) * channels
@@ -161,8 +170,8 @@
 def image_grads(stream, cotangent, gathered, place, table, sides):
     pixels, channels = stream.shape[1:]
     side = int(round(pixels**0.5))
-    share = gathered[0].shape[2]
-    sections = 2 * gathered[0].shape[1]
+    share = gathered[0].shape[3]
+    sections = 2 * gathered[0].shape[2]
     rows = share * 2 * sides * sides
     far = pl.BlockSpec(memory_space=pl.ANY)
     kernel = lambda *refs: image_step(sides, sections, side, share, *refs)
@@ -173,7 +182,7 @@
         grid_spec=pltpu.PrefetchScalarGridSpec(
             num_scalar_prefetch=2,
             grid=(1,),
-            in_specs=[far] * 18,
+            in_specs=[far] * 10,
             out_specs=pl.BlockSpec(memory_space=pltpu.VMEM),
             scratch_shapes=[
                 pltpu.VMEM((2, pixels, channels), jnp.float32),
@@ -225,17 +234,32 @@
     lines = [block + wait for block in lines]
     with jax.named_scope("get_one"):
         one = [along_second(sides, lines[part], ORDERS[part][1]) for part in range(2)]
-    with jax.named_scope("get_three"):
-        three = [along_second(sides, lines[part], ORDERS[part][2]) for part in range(2)]
-    with jax.named_scope("get_two"):
-        two = [along_second(sides, one[part], ORDERS[part][2]) for part in range(2)]
-    own = [block for part in range(2) for block in (lines[part], one[part], three[part], two[part])]
+    pairs = paired(lines, one)
+    with jax.named_scope("get_pair"):
+        far = [along_second(sides, pairs[part], ORDERS[part][2]) for part in range(2)]
     with jax.named_scope("share"):
-        theirs = []
+        early = [swapped(sides, block) for block in pairs]
+        late = [swapped(sides, block) for block in far]
+    return list(pairs) + far + early + late
+
+
+def paired(kept, came):
+    shape = kept[0].shape
+
+    def kernel(*refs):
         for part in range(2):
-            line = lines[part] + nothing(one[part]).astype(ROUND)
-            theirs += [swapped(sides, block) for block in (line, one[part], three[part], two[part])]
-    return own + theirs
+            for k in range(2):
+                refs[4 + part][k] = refs[2 * k + part][...]
+
+    near = pl.BlockSpec(memory_space=pltpu.VMEM)
+    return pl.pallas_call(
+        kernel,
+        out_shape=[jax.ShapeDtypeStruct((2, *shape), ROUND)] * 2,
+        in_specs=[near] * 4,
+        out_specs=[near] * 2,
+        compiler_params=pltpu.CompilerParams(vmem_limit_bytes=SMALL << 20),
+        name="paired",
+    )(*kept, *came)
 
 
 def nothing(value):

time: 127 us -> 125 us (0.984)
  waiting for transfers between devices: 33.3 us -> 41.7 us
  starting transfers between devices: 49.2 us -> 42.4 us
  Pallas kernels: 15.2 us -> 12.6 us
    ppermute x29 -> x23, waiting for transfers between devices: 26.5 us -> 34.9 us  [in_plane(): return lax.ppermute(value, 'dp', pairs)]
    ppermute x29 -> x23, starting transfers between devices: 40.2 us -> 33.4 us  [in_plane(): return lax.ppermute(value, 'dp', pairs)]
    pallas_call x1, Pallas kernels: 14.8 us -> 12 us  [image_grads(): pl.pallas_call(kernel, out_shape=jax.ShapeDtypeStruct((whole, share, chan...]
  transfers between devices with their start and end apart: 30 -> 24, of which waited for: 17 -> 18; matrix products, arithmetic and copies ran while one was open for 2% -> 1% of each run, Pallas kernels for 0% -> 0%
where the time goes in v7:
time: 125 us
  starting transfers between devices  42.4 us (34%)
  waiting for transfers between devices  41.7 us (33%)
  blocking collectives  21.7 us (17%)
  Pallas kernels  12.6 us (10%)
  local copies, waits for them, and re-layouts  3.13 us (3%)
  other arithmetic  2.27 us (2%)
    ppermute x23, waiting for transfers between devices, in_plane(): return lax.ppermute(value, 'dp', pairs)  34.9 us
    ppermute x23, starting transfers between devices, in_plane(): return lax.ppermute(value, 'dp', pairs)  33.4 us
    pallas_call x1, Pallas kernels, image_grads(): pl.pallas_call(kernel, out_shape=jax.ShapeDtypeStruct((whole, share, chan...  12 us
    all_to_all x1, blocking collectives, on_device(): lax.all_to_all(copies, 'dp', 0, 0, tiled=True, axis_index_groups=same_core)  11.2 us
    all_to_all x1, blocking collectives, scatter_grads(): tiles = lax.all_to_all(total.astype(ROUND), 'section', 0, 0, tiled=True)  10.5 us
    all_to_all x1, starting transfers between devices, gather_weights(): lax.all_to_all(line, 'section', 0, 0, tiled=True)  9.01 us
    all_to_all x1, waiting for transfers between devices, gather_weights(): lax.all_to_all(line, 'section', 0, 0, tiled=True)  6.83 us
  transfers between devices with their start and end apart: 24, of which 18 were waited for; matrix products, arithmetic and copies ran while one was open for 1% of the time, Pallas kernels for 0%

profile of v7, /device:TPU:1, one launch (start us, length us, event | category | flops | bytes accessed | tf_op | source)
XLA Modules:
  0.0 124.7 jit_solution(17608413841651436601)
XLA Ops:
  0.7 1.0 copy-done
  1.7 0.7 broadcast_in_dim.6
  2.4 9.0 %all-to-all-start = ((bf16[8,72,128]{2,1,0:T(8,128)(2,1)}), bf16[8,72,128]{2,1,0:T(8,128)(2,1)S(1)}, u32[]{:S(2)}, u32[]{:S(2)}) async-start(bf16[8,72,128]{2,1,0:T(8,128)(2,1)} %broadcast_in_dim.6), calls=%async_computation | async-start | bytes 294912 | tf_op jit(solution)/shard_map/all_to_all | solution.py:230
  11.4 1.1 constant_dynamic-slice_fusion
  12.5 6.8 %all-to-all-done = bf16[8,72,128]{2,1,0:T(8,128)(2,1)S(1)} async-done(((bf16[8,72,128]{2,1,0:T(8,128)(2,1)}), bf16[8,72,128]{2,1,0:T(8,128)(2,1)S(1)}, u32[]{:S(2)}, u32[]{:S(2)}) %all-to-all-start) | async-done | bytes 147488 | tf_op jit(solution)/shard_map/all_to_all | solution.py:230
  19.3 2.5 %collective-permute-start.2 = (bf16[2,4,72,128]{3,2,1,0:T(8,128)(2,1)S(1)}, bf16[2,4,72,128]{3,2,1,0:T(8,128)(2,1)S(1)}, u32[]{:S(2)}, u32[]{:S(2)}) collective-permute-start(bf16[2,4,72,128]{3,2,1,0:T(8,128)(2,1)S(1)} %bitcast.76), channel_id=1, source_target_pairs={{0,6},{1,25},{2,4},{3,27},{4,2},{5,29},{6,0},{7,31},{8,14},{9,17},... | collective-permute-start | bytes 442376 | tf_op jit(solution)/shard_map/ppermute | solution.py:212
  21.8 0.5 collective-permute-start.1
  22.3 0.3 collective-permute-start
  22.6 2.9 %collective-permute-done.2 = bf16[2,4,72,128]{3,2,1,0:T(8,128)(2,1)S(1)} collective-permute-done((bf16[2,4,72,128]{3,2,1,0:T(8,128)(2,1)S(1)}, bf16[2,4,72,128]{3,2,1,0:T(8,128)(2,1)S(1)}, u32[]{:S(2)}, u32[]{:S(2)}) %collective-permute-start.2) | collective-permute-done | bytes 147488 | tf_op jit(solution)/shard_map/ppermute | solution.py:212
  25.5 1.8 %collective-permute-done.1 = bf16[2,4,72,128]{3,2,1,0:T(8,128)(2,1)S(1)} collective-permute-done((bf16[2,4,72,128]{3,2,1,0:T(8,128)(2,1)S(1)}, bf16[2,4,72,128]{3,2,1,0:T(8,128)(2,1)S(1)}, u32[]{:S(2)}, u32[]{:S(2)}) %collective-permute-start.1) | collective-permute-done | bytes 147488 | tf_op jit(solution)/shard_map/ppermute | solution.py:212
  27.4 3.1 %collective-permute-start.4 = (bf16[4,4,72,128]{3,2,1,0:T(8,128)(2,1)S(1)}, bf16[4,4,72,128]{3,2,1,0:T(8,128)(2,1)S(1)}, u32[]{:S(2)}, u32[]{:S(2)}) collective-permute-start(bf16[4,4,72,128]{3,2,1,0:T(8,128)(2,1)S(1)} %get-tuple-element.39.refs_1_), channel_id=1, source_target_pairs={{0,24},{1,7},{2,26},{3,5},{4,28},{5,3},{6,30},{7,1},{8,16},{9,15},... | collective-permute-start | bytes 884744 | tf_op jit(solution)/shard_map/get_one/ppermute | solution.py:212
  30.6 4.1 %collective-permute-done.4.refs_3_ = bf16[4,4,72,128]{3,2,1,0:T(8,128)(2,1)S(1)} collective-permute-done((bf16[4,4,72,128]{3,2,1,0:T(8,128)(2,1)S(1)}, bf16[4,4,72,128]{3,2,1,0:T(8,128)(2,1)S(1)}, u32[]{:S(2)}, u32[]{:S(2)}) %collective-permute-start.4) | collective-permute-done | bytes 294944 | tf_op jit(solution)/shard_map/get_one/ppermute | solution.py:212
  34.7 1.8 %collective-permute-done.3.refs_2_ = bf16[4,4,72,128]{3,2,1,0:T(8,128)(2,1)S(1)} collective-permute-done((bf16[4,4,72,128]{3,2,1,0:T(8,128)(2,1)S(1)}, bf16[4,4,72,128]{3,2,1,0:T(8,128)(2,1)S(1)}, u32[]{:S(2)}, u32[]{:S(2)}) %collective-permute-start.3) | collective-permute-done | bytes 294944 | tf_op jit(solution)/shard_map/get_one/ppermute | solution.py:212
  36.5 1.0 collective-permute-start.5
  37.5 5.0 %collective-permute-start.7 = (bf16[2,4,4,72,128]{4,3,2,1,0:T(8,128)(2,1)S(1)}, bf16[2,4,4,72,128]{4,3,2,1,0:T(8,128)(2,1)}, u32[]{:S(2)}, u32[]{:S(2)}) collective-permute-start(bf16[2,4,4,72,128]{4,3,2,1,0:T(8,128)(2,1)S(1)} %get-tuple-element.11.refs_4_), channel_id=1, source_target_pairs={{0,1},{1,0},{2,3},{3,2},{4,5},{5,4},{6,7},{7,6},{8,9},{9,8},{10,11... | collective-permute-start | bytes 1769480 | tf_op jit(solution)/shard_map/share/ppermute | solution.py:212
  42.5 4.3 %collective-permute-done.5.refs_6_ = bf16[2,4,4,72,128]{4,3,2,1,0:T(8,128)(2,1)S(1)} collective-permute-done((bf16[2,4,4,72,128]{4,3,2,1,0:T(8,128)(2,1)S(1)}, bf16[2,4,4,72,128]{4,3,2,1,0:T(8,128)(2,1)S(1)}, u32[]{:S(2)}, u32[]{:S(2)}) %collective-permute-start.5) | collective-permute-done | bytes 589856 | tf_op jit(solution)/shard_map/get_pair/ppermute | solution.py:212
  46.8 5.6 %collective-permute-start.9 = (bf16[2,4,4,72,128]{4,3,2,1,0:T(8,128)(2,1)S(1)}, bf16[2,4,4,72,128]{4,3,2,1,0:T(8,128)(2,1)}, u32[]{:S(2)}, u32[]{:S(2)}) collective-permute-start(bf16[2,4,4,72,128]{4,3,2,1,0:T(8,128)(2,1)S(1)} %collective-permute-done.5.refs_6_), channel_id=1, source_target_pairs={{0,1},{1,0},{2,3},{3,2},{4,5},{5,4},{6,7},{7,6},{8,9},{9,8},{10,11... | collective-permute-start | bytes 1769480 | tf_op jit(solution)/shard_map/share/ppermute | solution.py:212
  52.6 1.6 %collective-permute-done.9.refs_10_ = bf16[2,4,4,72,128]{4,3,2,1,0:T(8,128)(2,1)} collective-permute-done((bf16[2,4,4,72,128]{4,3,2,1,0:T(8,128)(2,1)S(1)}, bf16[2,4,4,72,128]{4,3,2,1,0:T(8,128)(2,1)}, u32[]{:S(2)}, u32[]{:S(2)}) %collective-permute-start.9) | collective-permute-done | bytes 589856 | tf_op jit(solution)/shard_map/share/ppermute | solution.py:212
  54.2 0.8 collective-permute-done.10.refs_11_
  55.0 12.0 %image_step.1 = bf16[256,72,128]{2,1,0:T(8,128)(2,1)S(1)} custom-call(s32[4]{0:T(128)S(1)} %pad_add_fusion.refs_0_, s32[64]{0:T(128)S(1)} %pad_add_fusion.1.refs_1_, f32[2,256,128]{2,1,0:T(8,128)S(1)} %bitcast.72, f32[2,256,128]{2,1,0:T(8,128)S(1)} %bitcast.70, bf16[2,4,4,72,128]{4,3,2,1,0:T(8,128)(2,1)S(1)} %get-tuple-element.11.refs_4_, ...), custom_call_target="tpu_custom_call" | custom-call | tf_op jit(solution)/shard_map/image_step/pallas_call | solution.py:179
  67.0 0.2 fusion.22
  67.2 0.5 collective-permute-start.12
  67.7 0.1 collective-permute-start.11
  67.8 2.3 %collective-permute-done.12.swap = bf16[2,2,4,4,72,128]{5,4,3,2,1,0:T(8,128)(2,1)S(1)} collective-permute-done((bf16[2,2,4,4,72,128]{5,4,3,2,1,0:T(8,128)(2,1)S(1)}, bf16[2,2,4,4,72,128]{5,4,3,2,1,0:T(8,128)(2,1)S(1)}, u32[]{:S(2)}, u32[]{:S(2)}) %collective-permute-start.12) | collective-permute-done | bytes 1179680 | tf_op jit(solution)/shard_map/swap_far/ppermute | solution.py:212
  70.2 0.3 added.2
  70.5 2.0 %collective-permute-start.14 = (bf16[4,4,72,128]{3,2,1,0:T(8,128)(2,1)S(1)}, bf16[4,4,72,128]{3,2,1,0:T(8,128)(2,1)S(1)}, u32[]{:S(2)}, u32[]{:S(2)}) collective-permute-start(bf16[4,4,72,128]{3,2,1,0:T(8,128)(2,1)S(1)} %get-tuple-element.14), channel_id=1, source_target_pairs={{0,24},{1,7},{2,26},{3,5},{4,28},{5,3},{6,30},{7,1},{8,16},{9,15},... | collective-permute-start | bytes 884744 | tf_op jit(solution)/shard_map/sum_two/ppermute | solution.py:212
  72.5 0.7 collective-permute-start.13
  73.2 0.9 collective-permute-start.17
  74.1 3.5 %collective-permute-done.14.refs_0_ = bf16[4,4,72,128]{3,2,1,0:T(8,128)(2,1)S(1)} collective-permute-done((bf16[4,4,72,128]{3,2,1,0:T(8,128)(2,1)S(1)}, bf16[4,4,72,128]{3,2,1,0:T(8,128)(2,1)S(1)}, u32[]{:S(2)}, u32[]{:S(2)}) %collective-permute-start.14) | collective-permute-done | bytes 294944 | tf_op jit(solution)/shard_map/sum_two/ppermute | solution.py:212
  77.6 0.7 collective-permute-done.15.refs_1_
  78.4 0.2 added.3
  78.6 0.1 collective-permute-start.16
  78.7 1.3 %collective-permute-start.18 = (bf16[4,4,72,128]{3,2,1,0:T(8,128)(2,1)S(1)}, bf16[4,4,72,128]{3,2,1,0:T(8,128)(2,1)S(1)}, u32[]{:S(2)}, u32[]{:S(2)}) collective-permute-start(bf16[4,4,72,128]{3,2,1,0:T(8,128)(2,1)S(1)} %get-tuple-element.18), channel_id=1, source_target_pairs={{0,24},{1,7},{2,26},{3,5},{4,28},{5,3},{6,30},{7,1},{8,16},{9,15},... | collective-permute-start | bytes 884744 | tf_op jit(solution)/shard_map/sum_one/ppermute | solution.py:212
  80.0 0.8 collective-permute-done.13
  80.8 0.7 collective-permute-done.17
  81.5 3.2 %collective-permute-done.16 = bf16[4,4,72,128]{3,2,1,0:T(8,128)(2,1)S(1)} collective-permute-done((bf16[4,4,72,128]{3,2,1,0:T(8,128)(2,1)S(1)}, bf16[4,4,72,128]{3,2,1,0:T(8,128)(2,1)S(1)}, u32[]{:S(2)}, u32[]{:S(2)}) %collective-permute-start.16) | collective-permute-done | bytes 294944 | tf_op jit(solution)/shard_map/sum_one/ppermute | solution.py:212
  84.7 1.2 collective-permute-done.18
  85.9 0.3 fusion.2
  86.4 1.0 collective-permute-start.21
  87.4 2.2 %collective-permute-start.20 = (bf16[8,72,128]{2,1,0:T(8,128)(2,1)S(1)}, bf16[8,72,128]{2,1,0:T(8,128)(2,1)S(1)}, u32[]{:S(2)}, u32[]{:S(2)}) collective-permute-start(bf16[8,72,128]{2,1,0:T(8,128)(2,1)S(1)} %get-tuple-element.30), channel_id=1, source_target_pairs={{0,4},{1,17},{2,6},{3,19},{4,0},{5,21},{6,2},{7,23},{8,12},{9,25},... | collective-permute-start | bytes 442376 | tf_op jit(solution)/shard_map/ppermute | solution.py:212
  89.6 0.7 collective-permute-done.19
  90.4 3.2 %collective-permute-done.21 = bf16[8,72,128]{2,1,0:T(8,128)(2,1)S(1)} collective-permute-done((bf16[8,72,128]{2,1,0:T(8,128)(2,1)S(1)}, bf16[8,72,128]{2,1,0:T(8,128)(2,1)S(1)}, u32[]{:S(2)}, u32[]{:S(2)}) %collective-permute-start.21) | collective-permute-done | bytes 147488 | tf_op jit(solution)/shard_map/ppermute | solution.py:212
  93.6 10.5 %all_to_all.15 = bf16[8,72,128]{2,1,0:T(8,128)(2,1)S(1)} all-to-all(bf16[8,72,128]{2,1,0:T(8,128)(2,1)S(1)} %fusion.10), channel_id=1, replica_groups=mesh['section'=8,'dp'=32] {'section'}, dimensions={0} | all-to-all | bytes 294912 | tf_op jit(solution)/shard_map/all_to_all | solution.py:320
  104.2 0.6 convert_bitcast_fusion
  104.9 11.2 %all_to_all.16 = bf16[16,72,128]{2,1,0:T(8,128)(2,1)S(1)} all-to-all(bf16[16,72,128]{2,1,0:T(8,128)(2,1)S(1)} %broadcast_in_dim.8), channel_id=1, replica_groups={{0,2,4,6,8,10,12,14,16,18,20,22,24,26,28,30},{1,3,5,7,9,11,13,15,17,19,..., dimensions={0} | all-to-all | bytes 589824 | tf_op jit(solution)/shard_map/all_to_all | solution.py:345
  116.1 6.5 %collective-permute-start.22 = (bf16[16,72,128]{2,1,0:T(8,128)(2,1)S(1)}, bf16[16,72,128]{2,1,0:T(8,128)(2,1)S(1)}, u32[]{:S(2)}, u32[]{:S(2)}) collective-permute-start(bf16[16,72,128]{2,1,0:T(8,128)(2,1)S(1)} %all_to_all.16), channel_id=1, source_target_pairs={{0,1},{1,0},{2,3},{3,2},{4,5},{5,4},{6,7},{7,6},{8,9},{9,8},{10,11... | collective-permute-start | bytes 884744 | tf_op jit(solution)/shard_map/ppermute | solution.py:212
  122.6 1.2 collective-permute-done.22
  123.8 0.9 pad_maximum_fusion.1
  (34 shorter events, 0.8 us)
Async XLA Ops:
  0.6 1.1 copy-start
  2.4 16.9 %all-to-all-start = ((bf16[8,72,128]{2,1,0:T(8,128)(2,1)}), bf16[8,72,128]{2,1,0:T(8,128)(2,1)S(1)}, u32[]{:S(2)}, u32[]{:S(2)}) async-start(bf16[8,72,128]{2,1,0:T(8,128)(2,1)} %broadcast_in_dim.6), calls=%async_computation | async-start | bytes 294912 | tf_op jit(solution)/shard_map/all_to_all | solution.py:230
  19.3 6.1 %collective-permute-start.2 = (bf16[2,4,72,128]{3,2,1,0:T(8,128)(2,1)S(1)}, bf16[2,4,72,128]{3,2,1,0:T(8,128)(2,1)S(1)}, u32[]{:S(2)}, u32[]{:S(2)}) collective-permute-start(bf16[2,4,72,128]{3,2,1,0:T(8,128)(2,1)S(1)} %bitcast.76), channel_id=1, source_target_pairs={{0,6},{1,25},{2,4},{3,27},{4,2},{5,29},{6,0},{7,31},{8,14},{9,17},... | collective-permute-start | bytes 442376 | tf_op jit(solution)/shard_map/ppermute | solution.py:212
  21.8 5.5 %collective-permute-start.1 = (bf16[2,4,72,128]{3,2,1,0:T(8,128)(2,1)S(1)}, bf16[2,4,72,128]{3,2,1,0:T(8,128)(2,1)S(1)}, u32[]{:S(2)}, u32[]{:S(2)}) collective-permute-start(bf16[2,4,72,128]{3,2,1,0:T(8,128)(2,1)S(1)} %bitcast.77), channel_id=1, source_target_pairs={{0,4},{1,17},{2,6},{3,19},{4,0},{5,21},{6,2},{7,23},{8,12},{9,25},... | collective-permute-start | bytes 442376 | tf_op jit(solution)/shard_map/ppermute | solution.py:212
  22.3 5.0 %collective-permute-start = (bf16[2,4,72,128]{3,2,1,0:T(8,128)(2,1)S(1)}, bf16[2,4,72,128]{3,2,1,0:T(8,128)(2,1)S(1)}, u32[]{:S(2)}, u32[]{:S(2)}) collective-permute-start(bf16[2,4,72,128]{3,2,1,0:T(8,128)(2,1)S(1)} %bitcast.78), channel_id=1, source_target_pairs={{0,2},{1,9},{2,0},{3,11},{4,6},{5,13},{6,4},{7,15},{8,10},{9,1},{1... | collective-permute-start | bytes 442376 | tf_op jit(solution)/shard_map/ppermute | solution.py:212
  27.4 7.2 %collective-permute-start.4 = (bf16[4,4,72,128]{3,2,1,0:T(8,128)(2,1)S(1)}, bf16[4,4,72,128]{3,2,1,0:T(8,128)(2,1)S(1)}, u32[]{:S(2)}, u32[]{:S(2)}) collective-permute-start(bf16[4,4,72,128]{3,2,1,0:T(8,128)(2,1)S(1)} %get-tuple-element.39.refs_1_), channel_id=1, source_target_pairs={{0,24},{1,7},{2,26},{3,5},{4,28},{5,3},{6,30},{7,1},{8,16},{9,15},... | collective-permute-start | bytes 884744 | tf_op jit(solution)/shard_map/get_one/ppermute | solution.py:212
  30.6 5.9 %collective-permute-start.3 = (bf16[4,4,72,128]{3,2,1,0:T(8,128)(2,1)S(1)}, bf16[4,4,72,128]{3,2,1,0:T(8,128)(2,1)S(1)}, u32[]{:S(2)}, u32[]{:S(2)}) collective-permute-start(bf16[4,4,72,128]{3,2,1,0:T(8,128)(2,1)S(1)} %get-tuple-element.40.refs_0_), channel_id=1, source_target_pairs={{0,8},{1,3},{2,10},{3,1},{4,12},{5,7},{6,14},{7,5},{8,0},{9,11},{1... | collective-permute-start | bytes 884744 | tf_op jit(solution)/shard_map/get_one/ppermute | solution.py:212
  36.5 10.3 %collective-permute-start.5 = (bf16[2,4,4,72,128]{4,3,2,1,0:T(8,128)(2,1)S(1)}, bf16[2,4,4,72,128]{4,3,2,1,0:T(8,128)(2,1)S(1)}, u32[]{:S(2)}, u32[]{:S(2)}) collective-permute-start(bf16[2,4,4,72,128]{4,3,2,1,0:T(8,128)(2,1)S(1)} %get-tuple-element.11.refs_4_), channel_id=1, source_target_pairs={{0,24},{1,7},{2,26},{3,5},{4,28},{5,3},{6,30},{7,1},{8,16},{9,15},... | collective-permute-start | bytes 1769480 | tf_op jit(solution)/shard_map/get_pair/ppermute | solution.py:212
  37.5 14.9 %collective-permute-start.6 = (bf16[2,4,4,72,128]{4,3,2,1,0:T(8,128)(2,1)S(1)}, bf16[2,4,4,72,128]{4,3,2,1,0:T(8,128)(2,1)S(1)}, u32[]{:S(2)}, u32[]{:S(2)}) collective-permute-start(bf16[2,4,4,72,128]{4,3,2,1,0:T(8,128)(2,1)S(1)} %get-tuple-element.12.refs_5_), channel_id=1, source_target_pairs={{0,8},{1,3},{2,10},{3,1},{4,12},{5,7},{6,14},{7,5},{8,0},{9,11},{1... | collective-permute-start | bytes 1769480 | tf_op jit(solution)/shard_map/get_pair/ppermute | solution.py:212
  37.5 15.1 %collective-permute-start.7 = (bf16[2,4,4,72,128]{4,3,2,1,0:T(8,128)(2,1)S(1)}, bf16[2,4,4,72,128]{4,3,2,1,0:T(8,128)(2,1)}, u32[]{:S(2)}, u32[]{:S(2)}) collective-permute-start(bf16[2,4,4,72,128]{4,3,2,1,0:T(8,128)(2,1)S(1)} %get-tuple-element.11.refs_4_), channel_id=1, source_target_pairs={{0,1},{1,0},{2,3},{3,2},{4,5},{5,4},{6,7},{7,6},{8,9},{9,8},{10,11... | collective-permute-start | bytes 1769480 | tf_op jit(solution)/shard_map/share/ppermute | solution.py:212
  42.5 10.1 %collective-permute-start.8 = (bf16[2,4,4,72,128]{4,3,2,1,0:T(8,128)(2,1)S(1)}, bf16[2,4,4,72,128]{4,3,2,1,0:T(8,128)(2,1)}, u32[]{:S(2)}, u32[]{:S(2)}) collective-permute-start(bf16[2,4,4,72,128]{4,3,2,1,0:T(8,128)(2,1)S(1)} %get-tuple-element.12.refs_5_), channel_id=1, source_target_pairs={{0,1},{1,0},{2,3},{3,2},{4,5},{5,4},{6,7},{7,6},{8,9},{9,8},{10,11... | collective-permute-start | bytes 1769480 | tf_op jit(solution)/shard_map/share/ppermute | solution.py:212
  46.8 7.3 %collective-permute-start.9 = (bf16[2,4,4,72,128]{4,3,2,1,0:T(8,128)(2,1)S(1)}, bf16[2,4,4,72,128]{4,3,2,1,0:T(8,128)(2,1)}, u32[]{:S(2)}, u32[]{:S(2)}) collective-permute-start(bf16[2,4,4,72,128]{4,3,2,1,0:T(8,128)(2,1)S(1)} %collective-permute-done.5.refs_6_), channel_id=1, source_target_pairs={{0,1},{1,0},{2,3},{3,2},{4,5},{5,4},{6,7},{7,6},{8,9},{9,8},{10,11... | collective-permute-start | bytes 1769480 | tf_op jit(solution)/shard_map/share/ppermute | solution.py:212
  52.4 2.6 %collective-permute-start.10 = (bf16[2,4,4,72,128]{4,3,2,1,0:T(8,128)(2,1)S(1)}, bf16[2,4,4,72,128]{4,3,2,1,0:T(8,128)(2,1)}, u32[]{:S(2)}, u32[]{:S(2)}) collective-permute-start(bf16[2,4,4,72,128]{4,3,2,1,0:T(8,128)(2,1)S(1)} %collective-permute-done.6.refs_7_), channel_id=1, source_target_pairs={{0,1},{1,0},{2,3},{3,2},{4,5},{5,4},{6,7},{7,6},{8,9},{9,8},{10,11... | collective-permute-start | bytes 1769480 | tf_op jit(solution)/shard_map/share/ppermute | solution.py:212
  67.2 2.9 %collective-permute-start.12 = (bf16[2,2,4,4,72,128]{5,4,3,2,1,0:T(8,128)(2,1)S(1)}, bf16[2,2,4,4,72,128]{5,4,3,2,1,0:T(8,128)(2,1)S(1)}, u32[]{:S(2)}, u32[]{:S(2)}) collective-permute-start(bf16[2,2,4,4,72,128]{5,4,3,2,1,0:T(8,128)(2,1)S(1)} %bitcast.74), channel_id=1, source_target_pairs={{0,1},{1,0},{2,3},{3,2},{4,5},{5,4},{6,7},{7,6},{8,9},{9,8},{10,11... | collective-permute-start | bytes 3538952 | tf_op jit(solution)/shard_map/swap_far/ppermute | solution.py:212
  67.7 6.4 %collective-permute-start.11 = (bf16[2,2,4,4,72,128]{5,4,3,2,1,0:T(8,128)(2,1)S(1)}, bf16[2,2,4,4,72,128]{5,4,3,2,1,0:T(8,128)(2,1)S(1)}, u32[]{:S(2)}, u32[]{:S(2)}) collective-permute-start(bf16[2,2,4,4,72,128]{5,4,3,2,1,0:T(8,128)(2,1)S(1)} %bitcast.73), channel_id=1, source_target_pairs={{0,1},{1,0},{2,3},{3,2},{4,5},{5,4},{6,7},{7,6},{8,9},{9,8},{10,11... | collective-permute-start | bytes 3538952 | tf_op jit(solution)/shard_map/swap_near/ppermute | solution.py:212
  70.5 7.2 %collective-permute-start.14 = (bf16[4,4,72,128]{3,2,1,0:T(8,128)(2,1)S(1)}, bf16[4,4,72,128]{3,2,1,0:T(8,128)(2,1)S(1)}, u32[]{:S(2)}, u32[]{:S(2)}) collective-permute-start(bf16[4,4,72,128]{3,2,1,0:T(8,128)(2,1)S(1)} %get-tuple-element.14), channel_id=1, source_target_pairs={{0,24},{1,7},{2,26},{3,5},{4,28},{5,3},{6,30},{7,1},{8,16},{9,15},... | collective-permute-start | bytes 884744 | tf_op jit(solution)/shard_map/sum_two/ppermute | solution.py:212
  72.5 5.9 %collective-permute-start.15 = (bf16[4,4,72,128]{3,2,1,0:T(8,128)(2,1)S(1)}, bf16[4,4,72,128]{3,2,1,0:T(8,128)(2,1)S(1)}, u32[]{:S(2)}, u32[]{:S(2)}) collective-permute-start(bf16[4,4,72,128]{3,2,1,0:T(8,128)(2,1)S(1)} %get-tuple-element.15), channel_id=1, source_target_pairs={{0,8},{1,3},{2,10},{3,1},{4,12},{5,7},{6,14},{7,5},{8,0},{9,11},{1... | collective-permute-start | bytes 884744 | tf_op jit(solution)/shard_map/sum_two/ppermute | solution.py:212
  72.5 8.3 %collective-permute-start.13 = (bf16[4,4,72,128]{3,2,1,0:T(8,128)(2,1)S(1)}, bf16[4,4,72,128]{3,2,1,0:T(8,128)(2,1)S(1)}, u32[]{:S(2)}, u32[]{:S(2)}) collective-permute-start(bf16[4,4,72,128]{3,2,1,0:T(8,128)(2,1)S(1)} %get-tuple-element.13), channel_id=1, source_target_pairs={{0,24},{1,7},{2,26},{3,5},{4,28},{5,3},{6,30},{7,1},{8,16},{9,15},... | collective-permute-start | bytes 884744 | tf_op jit(solution)/shard_map/sum_three/ppermute | solution.py:212
  73.2 8.3 %collective-permute-start.17 = (bf16[4,4,72,128]{3,2,1,0:T(8,128)(2,1)S(1)}, bf16[4,4,72,128]{3,2,1,0:T(8,128)(2,1)S(1)}, u32[]{:S(2)}, u32[]{:S(2)}) collective-permute-start(bf16[4,4,72,128]{3,2,1,0:T(8,128)(2,1)S(1)} %get-tuple-element.17), channel_id=1, source_target_pairs={{0,8},{1,3},{2,10},{3,1},{4,12},{5,7},{6,14},{7,5},{8,0},{9,11},{1... | collective-permute-start | bytes 884744 | tf_op jit(solution)/shard_map/sum_three/ppermute | solution.py:212
  78.6 6.1 %collective-permute-start.16 = (bf16[4,4,72,128]{3,2,1,0:T(8,128)(2,1)S(1)}, bf16[4,4,72,128]{3,2,1,0:T(8,128)(2,1)S(1)}, u32[]{:S(2)}, u32[]{:S(2)}) collective-permute-start(bf16[4,4,72,128]{3,2,1,0:T(8,128)(2,1)S(1)} %get-tuple-element.16), channel_id=1, source_target_pairs={{0,8},{1,3},{2,10},{3,1},{4,12},{5,7},{6,14},{7,5},{8,0},{9,11},{1... | collective-permute-start | bytes 884744 | tf_op jit(solution)/shard_map/sum_one/ppermute | solution.py:212
  78.7 7.2 %collective-permute-start.18 = (bf16[4,4,72,128]{3,2,1,0:T(8,128)(2,1)S(1)}, bf16[4,4,72,128]{3,2,1,0:T(8,128)(2,1)S(1)}, u32[]{:S(2)}, u32[]{:S(2)}) collective-permute-start(bf16[4,4,72,128]{3,2,1,0:T(8,128)(2,1)S(1)} %get-tuple-element.18), channel_id=1, source_target_pairs={{0,24},{1,7},{2,26},{3,5},{4,28},{5,3},{6,30},{7,1},{8,16},{9,15},... | collective-permute-start | bytes 884744 | tf_op jit(solution)/shard_map/sum_one/ppermute | solution.py:212
  86.3 17.9 %copy-start.1 = (f32[1,72,128]{2,1,0:T(8,128)S(1)}, f32[1,72,128]{2,1,0:T(8,128)}, u32[]{:S(2)}) copy-start(f32[1,72,128]{2,1,0:T(8,128)} %param.8) | copy-start | bytes 110596
  86.3 17.9 %copy-start.2 = (f32[1,72,128]{2,1,0:T(8,128)S(1)}, f32[1,72,128]{2,1,0:T(8,128)}, u32[]{:S(2)}) copy-start(f32[1,72,128]{2,1,0:T(8,128)} %param.9) | copy-start | bytes 110596
  86.3 4.1 %collective-permute-start.19 = (bf16[8,72,128]{2,1,0:T(8,128)(2,1)S(1)}, bf16[8,72,128]{2,1,0:T(8,128)(2,1)S(1)}, u32[]{:S(2)}, u32[]{:S(2)}) collective-permute-start(bf16[8,72,128]{2,1,0:T(8,128)(2,1)S(1)} %get-tuple-element.28), channel_id=1, source_target_pairs={{0,2},{1,9},{2,0},{3,11},{4,6},{5,13},{6,4},{7,15},{8,10},{9,1},{1... | collective-permute-start | bytes 442376 | tf_op jit(solution)/shard_map/ppermute | solution.py:212
  86.4 7.2 %collective-permute-start.21 = (bf16[8,72,128]{2,1,0:T(8,128)(2,1)S(1)}, bf16[8,72,128]{2,1,0:T(8,128)(2,1)S(1)}, u32[]{:S(2)}, u32[]{:S(2)}) collective-permute-start(bf16[8,72,128]{2,1,0:T(8,128)(2,1)S(1)} %get-tuple-element.29), channel_id=1, source_target_pairs={{0,6},{1,25},{2,4},{3,27},{4,2},{5,29},{6,0},{7,31},{8,14},{9,17},... | collective-permute-start | bytes 442376 | tf_op jit(solution)/shard_map/ppermute | solution.py:212
  87.4 6.1 %collective-permute-start.20 = (bf16[8,72,128]{2,1,0:T(8,128)(2,1)S(1)}, bf16[8,72,128]{2,1,0:T(8,128)(2,1)S(1)}, u32[]{:S(2)}, u32[]{:S(2)}) collective-permute-start(bf16[8,72,128]{2,1,0:T(8,128)(2,1)S(1)} %get-tuple-element.30), channel_id=1, source_target_pairs={{0,4},{1,17},{2,6},{3,19},{4,0},{5,21},{6,2},{7,23},{8,12},{9,25},... | collective-permute-start | bytes 442376 | tf_op jit(solution)/shard_map/ppermute | solution.py:212
  116.1 7.7 %collective-permute-start.22 = (bf16[16,72,128]{2,1,0:T(8,128)(2,1)S(1)}, bf16[16,72,128]{2,1,0:T(8,128)(2,1)S(1)}, u32[]{:S(2)}, u32[]{:S(2)}) collective-permute-start(bf16[16,72,128]{2,1,0:T(8,128)(2,1)S(1)} %all_to_all.16), channel_id=1, source_target_pairs={{0,1},{1,0},{2,3},{3,2},{4,5},{5,4},{6,7},{7,6},{8,9},{9,8},{10,11... | collective-permute-start | bytes 884744 | tf_op jit(solution)/shard_map/ppermute | solution.py:212

commit v8 on v7

--- a/solution.py
+++ b/solution.py
@@ -103,7 +103,7 @@
         logistic = 1.0 / (1.0 + jnp.exp(-v))
         p = v * logistic
         slopes[at] = logistic + p * (1.0 - logistic)
-        saved_p[at] = p.T.astype(ROUND)
+        saved_p[at] = p.astype(ROUND)
         return p
 
     def forward(s, pair):
@@ -140,7 +140,7 @@
             taps,
             lambda v: lax.dot_general(v, across, (((1,), (1,)), ((), ())), preferred_element_type=jnp.float32),
         )
-        wgrad = jnp.dot(saved_p[at], taps, preferred_element_type=jnp.float32)
+        wgrad = lax.dot_general(saved_p[at], taps, (((0,), (0,)), ((), ())), preferred_element_type=jnp.float32)
         for tap in range(9):
             row, end = base + tap * channels, base + (tap + 1) * channels
             while row < end:
@@ -188,7 +188,7 @@
                 pltpu.VMEM((2, pixels, channels), jnp.float32),
                 pltpu.VMEM((2, pixels, channels), jnp.float32),
                 pltpu.VMEM((sections, rows, channels), ROUND),
-                pltpu.VMEM((2 * sections, channels, pixels), ROUND),
+                pltpu.VMEM((2 * sections, pixels, channels), ROUND),
                 pltpu.VMEM((2 * sections, pixels, channels), jnp.float32),
                 pltpu.VMEM((2, pixels + 2 * side, 3 * channels), ROUND),
                 pltpu.VMEM((2, pixels + 2 * side, 3 * channels), ROUND),
@@ -345,6 +345,9 @@
     own = lax.all_to_all(copies, "dp", 0, 0, tiled=True, axis_index_groups=same_core)
     other = swapped(sides, own)
     even = (at % 2 == 0)
+    gradient = gradient + nothing(own[0])
+    new_momentum = INERTIA * momentum[0] + gradient
+    new_master = master[0] - STEP_SIZE * new_momentum
     both = [jnp.where(even, own, other), jnp.where(even, other, own)]
     new_weights = jnp.stack(both, axis=1).reshape(dp * share, channels)
     return (new_master[None], new_momentum[None], new_weights[None])

time: 125 us -> 124 us (level)
  transfers between devices with their start and end apart: 24 -> 24, of which waited for: 18 -> 18; matrix products, arithmetic and copies ran while one was open for 1% -> 2% of each run, Pallas kernels for 0% -> 0%
where the time goes in v8:
time: 124 us
  starting transfers between devices  42.4 us (34%)
  waiting for transfers between devices  41.1 us (33%)
  blocking collectives  21.7 us (18%)
  Pallas kernels  12.5 us (10%)
  local copies, waits for them, and re-layouts  3.99 us (3%)
  other arithmetic  1.51 us (1%)
    ppermute x23, waiting for transfers between devices, in_plane(): return lax.ppermute(value, 'dp', pairs)  34.3 us
    ppermute x23, starting transfers between devices, in_plane(): return lax.ppermute(value, 'dp', pairs)  33.4 us
    pallas_call x1, Pallas kernels, image_grads(): pl.pallas_call(kernel, out_shape=jax.ShapeDtypeStruct((whole, share, chan...  11.9 us
    all_to_all x1, blocking collectives, on_device(): lax.all_to_all(copies, 'dp', 0, 0, tiled=True, axis_index_groups=same_core)  11.2 us
    all_to_all x1, blocking collectives, scatter_grads(): tiles = lax.all_to_all(total.astype(ROUND), 'section', 0, 0, tiled=True)  10.5 us
    all_to_all x1, starting transfers between devices, gather_weights(): lax.all_to_all(line, 'section', 0, 0, tiled=True)  9.01 us
    all_to_all x1, waiting for transfers between devices, gather_weights(): lax.all_to_all(line, 'section', 0, 0, tiled=True)  6.83 us
  transfers between devices with their start and end apart: 24, of which 18 were waited for; matrix products, arithmetic and copies ran while one was open for 2% of the time, Pallas kernels for 0%

profile of v8, /device:TPU:1, one launch (start us, length us, event | category | flops | bytes accessed | tf_op | source)
XLA Modules:
  0.0 124.0 jit_solution(1502640505588036235)
XLA Ops:
  0.7 1.0 copy-done
  1.7 0.7 broadcast_in_dim.6
  2.4 9.0 %all-to-all-start = ((bf16[8,72,128]{2,1,0:T(8,128)(2,1)}), bf16[8,72,128]{2,1,0:T(8,128)(2,1)S(1)}, u32[]{:S(2)}, u32[]{:S(2)}) async-start(bf16[8,72,128]{2,1,0:T(8,128)(2,1)} %broadcast_in_dim.6), calls=%async_computation | async-start | bytes 294912 | tf_op jit(solution)/shard_map/all_to_all | solution.py:230
  11.4 1.1 constant_dynamic-slice_fusion
  12.5 6.8 %all-to-all-done = bf16[8,72,128]{2,1,0:T(8,128)(2,1)S(1)} async-done(((bf16[8,72,128]{2,1,0:T(8,128)(2,1)}), bf16[8,72,128]{2,1,0:T(8,128)(2,1)S(1)}, u32[]{:S(2)}, u32[]{:S(2)}) %all-to-all-start) | async-done | bytes 147488 | tf_op jit(solution)/shard_map/all_to_all | solution.py:230
  19.3 2.5 %collective-permute-start.2 = (bf16[2,4,72,128]{3,2,1,0:T(8,128)(2,1)S(1)}, bf16[2,4,72,128]{3,2,1,0:T(8,128)(2,1)S(1)}, u32[]{:S(2)}, u32[]{:S(2)}) collective-permute-start(bf16[2,4,72,128]{3,2,1,0:T(8,128)(2,1)S(1)} %bitcast.85), channel_id=1, source_target_pairs={{0,6},{1,25},{2,4},{3,27},{4,2},{5,29},{6,0},{7,31},{8,14},{9,17},... | collective-permute-start | bytes 442376 | tf_op jit(solution)/shard_map/ppermute | solution.py:212
  21.8 0.5 collective-permute-start.1
  22.3 0.3 collective-permute-start
  22.6 2.9 %collective-permute-done.2 = bf16[2,4,72,128]{3,2,1,0:T(8,128)(2,1)S(1)} collective-permute-done((bf16[2,4,72,128]{3,2,1,0:T(8,128)(2,1)S(1)}, bf16[2,4,72,128]{3,2,1,0:T(8,128)(2,1)S(1)}, u32[]{:S(2)}, u32[]{:S(2)}) %collective-permute-start.2) | collective-permute-done | bytes 147488 | tf_op jit(solution)/shard_map/ppermute | solution.py:212
  25.5 1.8 %collective-permute-done.1 = bf16[2,4,72,128]{3,2,1,0:T(8,128)(2,1)S(1)} collective-permute-done((bf16[2,4,72,128]{3,2,1,0:T(8,128)(2,1)S(1)}, bf16[2,4,72,128]{3,2,1,0:T(8,128)(2,1)S(1)}, u32[]{:S(2)}, u32[]{:S(2)}) %collective-permute-start.1) | collective-permute-done | bytes 147488 | tf_op jit(solution)/shard_map/ppermute | solution.py:212
  27.4 3.1 %collective-permute-start.4 = (bf16[4,4,72,128]{3,2,1,0:T(8,128)(2,1)S(1)}, bf16[4,4,72,128]{3,2,1,0:T(8,128)(2,1)S(1)}, u32[]{:S(2)}, u32[]{:S(2)}) collective-permute-start(bf16[4,4,72,128]{3,2,1,0:T(8,128)(2,1)S(1)} %get-tuple-element.38.refs_1_), channel_id=1, source_target_pairs={{0,24},{1,7},{2,26},{3,5},{4,28},{5,3},{6,30},{7,1},{8,16},{9,15},... | collective-permute-start | bytes 884744 | tf_op jit(solution)/shard_map/get_one/ppermute | solution.py:212
  30.6 4.1 %collective-permute-done.4.refs_3_ = bf16[4,4,72,128]{3,2,1,0:T(8,128)(2,1)S(1)} collective-permute-done((bf16[4,4,72,128]{3,2,1,0:T(8,128)(2,1)S(1)}, bf16[4,4,72,128]{3,2,1,0:T(8,128)(2,1)S(1)}, u32[]{:S(2)}, u32[]{:S(2)}) %collective-permute-start.4) | collective-permute-done | bytes 294944 | tf_op jit(solution)/shard_map/get_one/ppermute | solution.py:212
  34.7 1.8 %collective-permute-done.3.refs_2_ = bf16[4,4,72,128]{3,2,1,0:T(8,128)(2,1)S(1)} collective-permute-done((bf16[4,4,72,128]{3,2,1,0:T(8,128)(2,1)S(1)}, bf16[4,4,72,128]{3,2,1,0:T(8,128)(2,1)S(1)}, u32[]{:S(2)}, u32[]{:S(2)}) %collective-permute-start.3) | collective-permute-done | bytes 294944 | tf_op jit(solution)/shard_map/get_one/ppermute | solution.py:212
  36.5 1.0 collective-permute-start.5
  37.5 5.0 %collective-permute-start.7 = (bf16[2,4,4,72,128]{4,3,2,1,0:T(8,128)(2,1)S(1)}, bf16[2,4,4,72,128]{4,3,2,1,0:T(8,128)(2,1)}, u32[]{:S(2)}, u32[]{:S(2)}) collective-permute-start(bf16[2,4,4,72,128]{4,3,2,1,0:T(8,128)(2,1)S(1)} %get-tuple-element.11.refs_4_), channel_id=1, source_target_pairs={{0,1},{1,0},{2,3},{3,2},{4,5},{5,4},{6,7},{7,6},{8,9},{9,8},{10,11... | collective-permute-start | bytes 1769480 | tf_op jit(solution)/shard_map/share/ppermute | solution.py:212
  42.5 4.3 %collective-permute-done.5.refs_6_ = bf16[2,4,4,72,128]{4,3,2,1,0:T(8,128)(2,1)S(1)} collective-permute-done((bf16[2,4,4,72,128]{4,3,2,1,0:T(8,128)(2,1)S(1)}, bf16[2,4,4,72,128]{4,3,2,1,0:T(8,128)(2,1)S(1)}, u32[]{:S(2)}, u32[]{:S(2)}) %collective-permute-start.5) | collective-permute-done | bytes 589856 | tf_op jit(solution)/shard_map/get_pair/ppermute | solution.py:212
  46.8 5.6 %collective-permute-start.9 = (bf16[2,4,4,72,128]{4,3,2,1,0:T(8,128)(2,1)S(1)}, bf16[2,4,4,72,128]{4,3,2,1,0:T(8,128)(2,1)}, u32[]{:S(2)}, u32[]{:S(2)}) collective-permute-start(bf16[2,4,4,72,128]{4,3,2,1,0:T(8,128)(2,1)S(1)} %collective-permute-done.5.refs_6_), channel_id=1, source_target_pairs={{0,1},{1,0},{2,3},{3,2},{4,5},{5,4},{6,7},{7,6},{8,9},{9,8},{10,11... | collective-permute-start | bytes 1769480 | tf_op jit(solution)/shard_map/share/ppermute | solution.py:212
  52.6 1.6 %collective-permute-done.9.refs_10_ = bf16[2,4,4,72,128]{4,3,2,1,0:T(8,128)(2,1)} collective-permute-done((bf16[2,4,4,72,128]{4,3,2,1,0:T(8,128)(2,1)S(1)}, bf16[2,4,4,72,128]{4,3,2,1,0:T(8,128)(2,1)}, u32[]{:S(2)}, u32[]{:S(2)}) %collective-permute-start.9) | collective-permute-done | bytes 589856 | tf_op jit(solution)/shard_map/share/ppermute | solution.py:212
  54.2 0.8 collective-permute-done.10.refs_11_
  55.0 11.9 %image_step.1 = bf16[256,72,128]{2,1,0:T(8,128)(2,1)S(1)} custom-call(s32[4]{0:T(128)S(1)} %pad_add_fusion.refs_0_, s32[64]{0:T(128)S(1)} %pad_add_fusion.1.refs_1_, f32[2,256,128]{2,1,0:T(8,128)S(1)} %bitcast.81, f32[2,256,128]{2,1,0:T(8,128)S(1)} %bitcast.79, bf16[2,4,4,72,128]{4,3,2,1,0:T(8,128)(2,1)S(1)} %get-tuple-element.11.refs_4_, ...), custom_call_target="tpu_custom_call" | custom-call | tf_op jit(solution)/shard_map/image_step/pallas_call | solution.py:179
  66.9 0.2 fusion.28
  67.1 0.5 collective-permute-start.12
  67.6 0.1 collective-permute-start.11
  67.7 2.3 %collective-permute-done.12.swap = bf16[2,2,4,4,72,128]{5,4,3,2,1,0:T(8,128)(2,1)S(1)} collective-permute-done((bf16[2,2,4,4,72,128]{5,4,3,2,1,0:T(8,128)(2,1)S(1)}, bf16[2,2,4,4,72,128]{5,4,3,2,1,0:T(8,128)(2,1)S(1)}, u32[]{:S(2)}, u32[]{:S(2)}) %collective-permute-start.12) | collective-permute-done | bytes 1179680 | tf_op jit(solution)/shard_map/swap_far/ppermute | solution.py:212
  70.1 0.3 added.2
  70.4 2.0 %collective-permute-start.14 = (bf16[4,4,72,128]{3,2,1,0:T(8,128)(2,1)S(1)}, bf16[4,4,72,128]{3,2,1,0:T(8,128)(2,1)S(1)}, u32[]{:S(2)}, u32[]{:S(2)}) collective-permute-start(bf16[4,4,72,128]{3,2,1,0:T(8,128)(2,1)S(1)} %get-tuple-element.14), channel_id=1, source_target_pairs={{0,24},{1,7},{2,26},{3,5},{4,28},{5,3},{6,30},{7,1},{8,16},{9,15},... | collective-permute-start | bytes 884744 | tf_op jit(solution)/shard_map/sum_two/ppermute | solution.py:212
  72.4 0.7 collective-permute-start.13
  73.1 0.9 collective-permute-start.17
  74.0 3.5 %collective-permute-done.14.refs_0_ = bf16[4,4,72,128]{3,2,1,0:T(8,128)(2,1)S(1)} collective-permute-done((bf16[4,4,72,128]{3,2,1,0:T(8,128)(2,1)S(1)}, bf16[4,4,72,128]{3,2,1,0:T(8,128)(2,1)S(1)}, u32[]{:S(2)}, u32[]{:S(2)}) %collective-permute-start.14) | collective-permute-done | bytes 294944 | tf_op jit(solution)/shard_map/sum_two/ppermute | solution.py:212
  77.5 0.7 collective-permute-done.15.refs_1_
  78.3 0.2 added.3
  78.6 1.3 %collective-permute-start.18 = (bf16[4,4,72,128]{3,2,1,0:T(8,128)(2,1)S(1)}, bf16[4,4,72,128]{3,2,1,0:T(8,128)(2,1)S(1)}, u32[]{:S(2)}, u32[]{:S(2)}) collective-permute-start(bf16[4,4,72,128]{3,2,1,0:T(8,128)(2,1)S(1)} %get-tuple-element.18), channel_id=1, source_target_pairs={{0,24},{1,7},{2,26},{3,5},{4,28},{5,3},{6,30},{7,1},{8,16},{9,15},... | collective-permute-start | bytes 884744 | tf_op jit(solution)/shard_map/sum_one/ppermute | solution.py:212
  79.9 0.8 collective-permute-done.13
  80.7 0.7 collective-permute-done.17
  81.4 3.2 %collective-permute-done.16 = bf16[4,4,72,128]{3,2,1,0:T(8,128)(2,1)S(1)} collective-permute-done((bf16[4,4,72,128]{3,2,1,0:T(8,128)(2,1)S(1)}, bf16[4,4,72,128]{3,2,1,0:T(8,128)(2,1)S(1)}, u32[]{:S(2)}, u32[]{:S(2)}) %collective-permute-start.16) | collective-permute-done | bytes 294944 | tf_op jit(solution)/shard_map/sum_one/ppermute | solution.py:212
  84.6 1.2 collective-permute-done.18
  85.8 0.3 fusion.2
  86.2 0.1 collective-permute-start.19
  86.3 1.0 collective-permute-start.21
  87.3 2.2 %collective-permute-start.20 = (bf16[8,72,128]{2,1,0:T(8,128)(2,1)S(1)}, bf16[8,72,128]{2,1,0:T(8,128)(2,1)S(1)}, u32[]{:S(2)}, u32[]{:S(2)}) collective-permute-start(bf16[8,72,128]{2,1,0:T(8,128)(2,1)S(1)} %get-tuple-element.29), channel_id=1, source_target_pairs={{0,4},{1,17},{2,6},{3,19},{4,0},{5,21},{6,2},{7,23},{8,12},{9,25},... | collective-permute-start | bytes 442376 | tf_op jit(solution)/shard_map/ppermute | solution.py:212
  89.5 0.7 collective-permute-done.19
  90.3 3.2 %collective-permute-done.21 = bf16[8,72,128]{2,1,0:T(8,128)(2,1)S(1)} collective-permute-done((bf16[8,72,128]{2,1,0:T(8,128)(2,1)S(1)}, bf16[8,72,128]{2,1,0:T(8,128)(2,1)S(1)}, u32[]{:S(2)}, u32[]{:S(2)}) %collective-permute-start.21) | collective-permute-done | bytes 147488 | tf_op jit(solution)/shard_map/ppermute | solution.py:212
  93.5 10.5 %all_to_all.15 = bf16[8,72,128]{2,1,0:T(8,128)(2,1)S(1)} all-to-all(bf16[8,72,128]{2,1,0:T(8,128)(2,1)S(1)} %fusion.10), channel_id=1, replica_groups=mesh['section'=8,'dp'=32] {'section'}, dimensions={0} | all-to-all | bytes 294912 | tf_op jit(solution)/shard_map/all_to_all | solution.py:320
  104.1 11.2 %all_to_all.16 = bf16[16,72,128]{2,1,0:T(8,128)(2,1)S(1)} all-to-all(bf16[16,72,128]{2,1,0:T(8,128)(2,1)S(1)} %broadcast_in_dim.8), channel_id=1, replica_groups={{0,2,4,6,8,10,12,14,16,18,20,22,24,26,28,30},{1,3,5,7,9,11,13,15,17,19,..., dimensions={0} | all-to-all | bytes 589824 | tf_op jit(solution)/shard_map/all_to_all | solution.py:345
  115.3 6.5 %collective-permute-start.22 = (bf16[16,72,128]{2,1,0:T(8,128)(2,1)S(1)}, bf16[16,72,128]{2,1,0:T(8,128)(2,1)S(1)}, u32[]{:S(2)}, u32[]{:S(2)}) collective-permute-start(bf16[16,72,128]{2,1,0:T(8,128)(2,1)S(1)} %all_to_all.16), channel_id=1, source_target_pairs={{0,1},{1,0},{2,3},{3,2},{4,5},{5,4},{6,7},{7,6},{8,9},{9,8},{10,11... | collective-permute-start | bytes 884744 | tf_op jit(solution)/shard_map/ppermute | solution.py:212
  121.8 0.6 multiply_subtract_fusion
  122.5 0.6 collective-permute-done.22
  123.2 0.9 copy.8
  (36 shorter events, 0.9 us)
Async XLA Ops:
  0.6 1.1 copy-start
  2.4 16.9 %all-to-all-start = ((bf16[8,72,128]{2,1,0:T(8,128)(2,1)}), bf16[8,72,128]{2,1,0:T(8,128)(2,1)S(1)}, u32[]{:S(2)}, u32[]{:S(2)}) async-start(bf16[8,72,128]{2,1,0:T(8,128)(2,1)} %broadcast_in_dim.6), calls=%async_computation | async-start | bytes 294912 | tf_op jit(solution)/shard_map/all_to_all | solution.py:230
  19.3 6.1 %collective-permute-start.2 = (bf16[2,4,72,128]{3,2,1,0:T(8,128)(2,1)S(1)}, bf16[2,4,72,128]{3,2,1,0:T(8,128)(2,1)S(1)}, u32[]{:S(2)}, u32[]{:S(2)}) collective-permute-start(bf16[2,4,72,128]{3,2,1,0:T(8,128)(2,1)S(1)} %bitcast.85), channel_id=1, source_target_pairs={{0,6},{1,25},{2,4},{3,27},{4,2},{5,29},{6,0},{7,31},{8,14},{9,17},... | collective-permute-start | bytes 442376 | tf_op jit(solution)/shard_map/ppermute | solution.py:212
  21.8 5.5 %collective-permute-start.1 = (bf16[2,4,72,128]{3,2,1,0:T(8,128)(2,1)S(1)}, bf16[2,4,72,128]{3,2,1,0:T(8,128)(2,1)S(1)}, u32[]{:S(2)}, u32[]{:S(2)}) collective-permute-start(bf16[2,4,72,128]{3,2,1,0:T(8,128)(2,1)S(1)} %bitcast.86), channel_id=1, source_target_pairs={{0,4},{1,17},{2,6},{3,19},{4,0},{5,21},{6,2},{7,23},{8,12},{9,25},... | collective-permute-start | bytes 442376 | tf_op jit(solution)/shard_map/ppermute | solution.py:212
  22.3 5.0 %collective-permute-start = (bf16[2,4,72,128]{3,2,1,0:T(8,128)(2,1)S(1)}, bf16[2,4,72,128]{3,2,1,0:T(8,128)(2,1)S(1)}, u32[]{:S(2)}, u32[]{:S(2)}) collective-permute-start(bf16[2,4,72,128]{3,2,1,0:T(8,128)(2,1)S(1)} %bitcast.87), channel_id=1, source_target_pairs={{0,2},{1,9},{2,0},{3,11},{4,6},{5,13},{6,4},{7,15},{8,10},{9,1},{1... | collective-permute-start | bytes 442376 | tf_op jit(solution)/shard_map/ppermute | solution.py:212
  27.4 7.2 %collective-permute-start.4 = (bf16[4,4,72,128]{3,2,1,0:T(8,128)(2,1)S(1)}, bf16[4,4,72,128]{3,2,1,0:T(8,128)(2,1)S(1)}, u32[]{:S(2)}, u32[]{:S(2)}) collective-permute-start(bf16[4,4,72,128]{3,2,1,0:T(8,128)(2,1)S(1)} %get-tuple-element.38.refs_1_), channel_id=1, source_target_pairs={{0,24},{1,7},{2,26},{3,5},{4,28},{5,3},{6,30},{7,1},{8,16},{9,15},... | collective-permute-start | bytes 884744 | tf_op jit(solution)/shard_map/get_one/ppermute | solution.py:212
  30.6 5.9 %collective-permute-start.3 = (bf16[4,4,72,128]{3,2,1,0:T(8,128)(2,1)S(1)}, bf16[4,4,72,128]{3,2,1,0:T(8,128)(2,1)S(1)}, u32[]{:S(2)}, u32[]{:S(2)}) collective-permute-start(bf16[4,4,72,128]{3,2,1,0:T(8,128)(2,1)S(1)} %get-tuple-element.39.refs_0_), channel_id=1, source_target_pairs={{0,8},{1,3},{2,10},{3,1},{4,12},{5,7},{6,14},{7,5},{8,0},{9,11},{1... | collective-permute-start | bytes 884744 | tf_op jit(solution)/shard_map/get_one/ppermute | solution.py:212
  36.5 10.3 %collective-permute-start.5 = (bf16[2,4,4,72,128]{4,3,2,1,0:T(8,128)(2,1)S(1)}, bf16[2,4,4,72,128]{4,3,2,1,0:T(8,128)(2,1)S(1)}, u32[]{:S(2)}, u32[]{:S(2)}) collective-permute-start(bf16[2,4,4,72,128]{4,3,2,1,0:T(8,128)(2,1)S(1)} %get-tuple-element.11.refs_4_), channel_id=1, source_target_pairs={{0,24},{1,7},{2,26},{3,5},{4,28},{5,3},{6,30},{7,1},{8,16},{9,15},... | collective-permute-start | bytes 1769480 | tf_op jit(solution)/shard_map/get_pair/ppermute | solution.py:212
  37.5 14.9 %collective-permute-start.6 = (bf16[2,4,4,72,128]{4,3,2,1,0:T(8,128)(2,1)S(1)}, bf16[2,4,4,72,128]{4,3,2,1,0:T(8,128)(2,1)S(1)}, u32[]{:S(2)}, u32[]{:S(2)}) collective-permute-start(bf16[2,4,4,72,128]{4,3,2,1,0:T(8,128)(2,1)S(1)} %get-tuple-element.12.refs_5_), channel_id=1, source_target_pairs={{0,8},{1,3},{2,10},{3,1},{4,12},{5,7},{6,14},{7,5},{8,0},{9,11},{1... | collective-permute-start | bytes 1769480 | tf_op jit(solution)/shard_map/get_pair/ppermute | solution.py:212
  37.5 15.1 %collective-permute-start.7 = (bf16[2,4,4,72,128]{4,3,2,1,0:T(8,128)(2,1)S(1)}, bf16[2,4,4,72,128]{4,3,2,1,0:T(8,128)(2,1)}, u32[]{:S(2)}, u32[]{:S(2)}) collective-permute-start(bf16[2,4,4,72,128]{4,3,2,1,0:T(8,128)(2,1)S(1)} %get-tuple-element.11.refs_4_), channel_id=1, source_target_pairs={{0,1},{1,0},{2,3},{3,2},{4,5},{5,4},{6,7},{7,6},{8,9},{9,8},{10,11... | collective-permute-start | bytes 1769480 | tf_op jit(solution)/shard_map/share/ppermute | solution.py:212
  42.5 10.1 %collective-permute-start.8 = (bf16[2,4,4,72,128]{4,3,2,1,0:T(8,128)(2,1)S(1)}, bf16[2,4,4,72,128]{4,3,2,1,0:T(8,128)(2,1)}, u32[]{:S(2)}, u32[]{:S(2)}) collective-permute-start(bf16[2,4,4,72,128]{4,3,2,1,0:T(8,128)(2,1)S(1)} %get-tuple-element.12.refs_5_), channel_id=1, source_target_pairs={{0,1},{1,0},{2,3},{3,2},{4,5},{5,4},{6,7},{7,6},{8,9},{9,8},{10,11... | collective-permute-start | bytes 1769480 | tf_op jit(solution)/shard_map/share/ppermute | solution.py:212
  46.8 7.3 %collective-permute-start.9 = (bf16[2,4,4,72,128]{4,3,2,1,0:T(8,128)(2,1)S(1)}, bf16[2,4,4,72,128]{4,3,2,1,0:T(8,128)(2,1)}, u32[]{:S(2)}, u32[]{:S(2)}) collective-permute-start(bf16[2,4,4,72,128]{4,3,2,1,0:T(8,128)(2,1)S(1)} %collective-permute-done.5.refs_6_), channel_id=1, source_target_pairs={{0,1},{1,0},{2,3},{3,2},{4,5},{5,4},{6,7},{7,6},{8,9},{9,8},{10,11... | collective-permute-start | bytes 1769480 | tf_op jit(solution)/shard_map/share/ppermute | solution.py:212
  52.4 2.6 %collective-permute-start.10 = (bf16[2,4,4,72,128]{4,3,2,1,0:T(8,128)(2,1)S(1)}, bf16[2,4,4,72,128]{4,3,2,1,0:T(8,128)(2,1)}, u32[]{:S(2)}, u32[]{:S(2)}) collective-permute-start(bf16[2,4,4,72,128]{4,3,2,1,0:T(8,128)(2,1)S(1)} %collective-permute-done.6.refs_7_), channel_id=1, source_target_pairs={{0,1},{1,0},{2,3},{3,2},{4,5},{5,4},{6,7},{7,6},{8,9},{9,8},{10,11... | collective-permute-start | bytes 1769480 | tf_op jit(solution)/shard_map/share/ppermute | solution.py:212
  67.1 2.9 %collective-permute-start.12 = (bf16[2,2,4,4,72,128]{5,4,3,2,1,0:T(8,128)(2,1)S(1)}, bf16[2,2,4,4,72,128]{5,4,3,2,1,0:T(8,128)(2,1)S(1)}, u32[]{:S(2)}, u32[]{:S(2)}) collective-permute-start(bf16[2,2,4,4,72,128]{5,4,3,2,1,0:T(8,128)(2,1)S(1)} %bitcast.83), channel_id=1, source_target_pairs={{0,1},{1,0},{2,3},{3,2},{4,5},{5,4},{6,7},{7,6},{8,9},{9,8},{10,11... | collective-permute-start | bytes 3538952 | tf_op jit(solution)/shard_map/swap_far/ppermute | solution.py:212
  67.6 6.4 %collective-permute-start.11 = (bf16[2,2,4,4,72,128]{5,4,3,2,1,0:T(8,128)(2,1)S(1)}, bf16[2,2,4,4,72,128]{5,4,3,2,1,0:T(8,128)(2,1)S(1)}, u32[]{:S(2)}, u32[]{:S(2)}) collective-permute-start(bf16[2,2,4,4,72,128]{5,4,3,2,1,0:T(8,128)(2,1)S(1)} %bitcast.82), channel_id=1, source_target_pairs={{0,1},{1,0},{2,3},{3,2},{4,5},{5,4},{6,7},{7,6},{8,9},{9,8},{10,11... | collective-permute-start | bytes 3538952 | tf_op jit(solution)/shard_map/swap_near/ppermute | solution.py:212
  70.4 7.2 %collective-permute-start.14 = (bf16[4,4,72,128]{3,2,1,0:T(8,128)(2,1)S(1)}, bf16[4,4,72,128]{3,2,1,0:T(8,128)(2,1)S(1)}, u32[]{:S(2)}, u32[]{:S(2)}) collective-permute-start(bf16[4,4,72,128]{3,2,1,0:T(8,128)(2,1)S(1)} %get-tuple-element.14), channel_id=1, source_target_pairs={{0,24},{1,7},{2,26},{3,5},{4,28},{5,3},{6,30},{7,1},{8,16},{9,15},... | collective-permute-start | bytes 884744 | tf_op jit(solution)/shard_map/sum_two/ppermute | solution.py:212
  72.4 5.9 %collective-permute-start.15 = (bf16[4,4,72,128]{3,2,1,0:T(8,128)(2,1)S(1)}, bf16[4,4,72,128]{3,2,1,0:T(8,128)(2,1)S(1)}, u32[]{:S(2)}, u32[]{:S(2)}) collective-permute-start(bf16[4,4,72,128]{3,2,1,0:T(8,128)(2,1)S(1)} %get-tuple-element.15), channel_id=1, source_target_pairs={{0,8},{1,3},{2,10},{3,1},{4,12},{5,7},{6,14},{7,5},{8,0},{9,11},{1... | collective-permute-start | bytes 884744 | tf_op jit(solution)/shard_map/sum_two/ppermute | solution.py:212
  72.4 8.3 %collective-permute-start.13 = (bf16[4,4,72,128]{3,2,1,0:T(8,128)(2,1)S(1)}, bf16[4,4,72,128]{3,2,1,0:T(8,128)(2,1)S(1)}, u32[]{:S(2)}, u32[]{:S(2)}) collective-permute-start(bf16[4,4,72,128]{3,2,1,0:T(8,128)(2,1)S(1)} %get-tuple-element.13), channel_id=1, source_target_pairs={{0,24},{1,7},{2,26},{3,5},{4,28},{5,3},{6,30},{7,1},{8,16},{9,15},... | collective-permute-start | bytes 884744 | tf_op jit(solution)/shard_map/sum_three/ppermute | solution.py:212
  73.1 8.3 %collective-permute-start.17 = (bf16[4,4,72,128]{3,2,1,0:T(8,128)(2,1)S(1)}, bf16[4,4,72,128]{3,2,1,0:T(8,128)(2,1)S(1)}, u32[]{:S(2)}, u32[]{:S(2)}) collective-permute-start(bf16[4,4,72,128]{3,2,1,0:T(8,128)(2,1)S(1)} %get-tuple-element.17), channel_id=1, source_target_pairs={{0,8},{1,3},{2,10},{3,1},{4,12},{5,7},{6,14},{7,5},{8,0},{9,11},{1... | collective-permute-start | bytes 884744 | tf_op jit(solution)/shard_map/sum_three/ppermute | solution.py:212
  78.5 6.1 %collective-permute-start.16 = (bf16[4,4,72,128]{3,2,1,0:T(8,128)(2,1)S(1)}, bf16[4,4,72,128]{3,2,1,0:T(8,128)(2,1)S(1)}, u32[]{:S(2)}, u32[]{:S(2)}) collective-permute-start(bf16[4,4,72,128]{3,2,1,0:T(8,128)(2,1)S(1)} %get-tuple-element.16), channel_id=1, source_target_pairs={{0,8},{1,3},{2,10},{3,1},{4,12},{5,7},{6,14},{7,5},{8,0},{9,11},{1... | collective-permute-start | bytes 884744 | tf_op jit(solution)/shard_map/sum_one/ppermute | solution.py:212
  78.6 7.2 %collective-permute-start.18 = (bf16[4,4,72,128]{3,2,1,0:T(8,128)(2,1)S(1)}, bf16[4,4,72,128]{3,2,1,0:T(8,128)(2,1)S(1)}, u32[]{:S(2)}, u32[]{:S(2)}) collective-permute-start(bf16[4,4,72,128]{3,2,1,0:T(8,128)(2,1)S(1)} %get-tuple-element.18), channel_id=1, source_target_pairs={{0,24},{1,7},{2,26},{3,5},{4,28},{5,3},{6,30},{7,1},{8,16},{9,15},... | collective-permute-start | bytes 884744 | tf_op jit(solution)/shard_map/sum_one/ppermute | solution.py:212
  86.2 17.9 %copy-start.1 = (f32[1,72,128]{2,1,0:T(8,128)S(1)}, f32[1,72,128]{2,1,0:T(8,128)}, u32[]{:S(2)}) copy-start(f32[1,72,128]{2,1,0:T(8,128)} %param.8) | copy-start | bytes 110596
  86.2 17.9 %copy-start.2 = (f32[1,72,128]{2,1,0:T(8,128)S(1)}, f32[1,72,128]{2,1,0:T(8,128)}, u32[]{:S(2)}) copy-start(f32[1,72,128]{2,1,0:T(8,128)} %param.9) | copy-start | bytes 110596
  86.2 4.1 %collective-permute-start.19 = (bf16[8,72,128]{2,1,0:T(8,128)(2,1)S(1)}, bf16[8,72,128]{2,1,0:T(8,128)(2,1)S(1)}, u32[]{:S(2)}, u32[]{:S(2)}) collective-permute-start(bf16[8,72,128]{2,1,0:T(8,128)(2,1)S(1)} %get-tuple-element.27), channel_id=1, source_target_pairs={{0,2},{1,9},{2,0},{3,11},{4,6},{5,13},{6,4},{7,15},{8,10},{9,1},{1... | collective-permute-start | bytes 442376 | tf_op jit(solution)/shard_map/ppermute | solution.py:212
  86.3 7.2 %collective-permute-start.21 = (bf16[8,72,128]{2,1,0:T(8,128)(2,1)S(1)}, bf16[8,72,128]{2,1,0:T(8,128)(2,1)S(1)}, u32[]{:S(2)}, u32[]{:S(2)}) collective-permute-start(bf16[8,72,128]{2,1,0:T(8,128)(2,1)S(1)} %get-tuple-element.28), channel_id=1, source_target_pairs={{0,6},{1,25},{2,4},{3,27},{4,2},{5,29},{6,0},{7,31},{8,14},{9,17},... | collective-permute-start | bytes 442376 | tf_op jit(solution)/shard_map/ppermute | solution.py:212
  87.3 6.1 %collective-permute-start.20 = (bf16[8,72,128]{2,1,0:T(8,128)(2,1)S(1)}, bf16[8,72,128]{2,1,0:T(8,128)(2,1)S(1)}, u32[]{:S(2)}, u32[]{:S(2)}) collective-permute-start(bf16[8,72,128]{2,1,0:T(8,128)(2,1)S(1)} %get-tuple-element.29), channel_id=1, source_target_pairs={{0,4},{1,17},{2,6},{3,19},{4,0},{5,21},{6,2},{7,23},{8,12},{9,25},... | collective-permute-start | bytes 442376 | tf_op jit(solution)/shard_map/ppermute | solution.py:212
  115.3 7.7 %collective-permute-start.22 = (bf16[16,72,128]{2,1,0:T(8,128)(2,1)S(1)}, bf16[16,72,128]{2,1,0:T(8,128)(2,1)S(1)}, u32[]{:S(2)}, u32[]{:S(2)}) collective-permute-start(bf16[16,72,128]{2,1,0:T(8,128)(2,1)S(1)} %all_to_all.16), channel_id=1, source_target_pairs={{0,1},{1,0},{2,3},{3,2},{4,5},{5,4},{6,7},{7,6},{8,9},{9,8},{10,11... | collective-permute-start | bytes 884744 | tf_op jit(solution)/shard_map/ppermute | solution.py:212
